TPU v7x, 256 devices: a whole 4x4x8 slice. The times are simulated.
256 devices in a mesh: query: 4 (over y), corpus: 64 (over x, z, core).
Axes of the slice: x: 4, y: 4, z: 8, core: 2. Of those that a mesh axis runs over, the one named last changes fastest.
Arguments:
- hidden_in: bfloat16 [512, 4096], P('query', 'corpus'), may hold values from -6 to 6
- lengths: int32 [16], P('query'), may hold values from 1 to 32, 320 in all
- gate_weight: bfloat16 [4096, 14336], P('query', 'corpus'), may hold values from -0.09375 to 0.09375
- up_weight: bfloat16 [4096, 14336], P('query', 'corpus'), may hold values from -0.09375 to 0.09375
- down_weight: bfloat16 [14336, 4096], P('corpus', 'query'), may hold values from -0.04175957 to 0.04175957
- code_weight: bfloat16 [4096, 1024], P('corpus'), may hold values from -0.03125 to 0.03125
- corpus_codes: bfloat16 [131072, 1024], P(('query', 'corpus')), may hold values from -1 to 1, as said below
Outputs:
- top_scores: float32 [16, 100], replicated
Inputs may be any that keep to these rules, and one draw needn't show every extreme that they name: `corpus_codes`: every entry is +1 or -1. `lengths`: at least one query has all 32 slots real.
All inputs are finite; a program needn't handle non-finite values. No bound on the sum of `lengths` on one device may be relied on, other than what follows from the above.
Results may differ from a plain program's by a relative error of at most 0.00067.
Values may be sent and summed in bfloat16 or wider, within the bound.
No kernel may reach another device: no remote copies, remote signals or barrier semaphores. Data moves between devices by JAX's collectives and lax.ppermute only.
A program may use at most 64 MiB of HBM per device.

v0:
```python
import math

import jax
import jax.numpy as jnp
from jax import lax
from jax.sharding import Mesh
from jax.sharding import PartitionSpec as P

D = 4096
SEQ = 32
TOPK = 100
CORPUS = ("corpus_0", "corpus_1", "corpus_2")
QUERY_CORPUS = ("query", "corpus_0", "corpus_1", "corpus_2")


epsilon = 1e-05


def copy_for_each(x, axis):
    peers = lax.axis_size(axis)
    return lax.all_to_all(jnp.broadcast_to(x[None], (peers, *x.shape)), axis, 0, 0, tiled=True)


def in_order(parts, dim):
    shape = list(parts.shape[1:])
    shape[dim] *= parts.shape[0]
    return jnp.moveaxis(parts, 0, dim).reshape(shape)


def collect(x, axis, dim):
    parts = copy_for_each(x, axis)
    return in_order(parts, dim)


def sent_together(arrays, axis, dim, along):
    ends, at = ([], 0)
    for a in arrays[:-1]:
        at += a.shape[along]
        ends.append(at)
    both = jnp.concatenate(arrays, axis=along)
    return tuple(jnp.split(lax.all_gather(both, axis, axis=dim, tiled=True), ends, axis=along))


def in_blocks(x, dim, peers):
    before, after = (x.shape[:dim], x.shape[dim + 1 :])
    return jnp.moveaxis(x.reshape(*before, peers, -1, *after), dim, 0)


def sum_at_owner(x, axis, dim):
    parts = in_blocks(x, dim, lax.axis_size(axis))
    arrived = lax.all_to_all(parts, axis, split_axis=0, concat_axis=0, tiled=True)
    return arrived.sum(axis=0)


def over_copies(x, axis):
    return copy_for_each(x, axis).sum(axis=0)


def merged_by_axis(x, axes, combine):
    for axis in axes:
        pieces = lax.all_gather(x, axis)
        x = pieces[0]
        for k in range(1, lax.axis_size(axis)):
            x = combine(x, pieces[k])
    return x


def keep_best(first, second):
    return lax.top_k(jnp.concatenate([first, second], axis=1), first.shape[1])[0]


def per_device(hidden_in, lengths, gate_weight, up_weight, down_weight, code_weight, corpus_codes):
    gathered = collect(hidden_in, CORPUS, 1)
    widened = gathered.astype(jnp.float32)
    normed = (
        widened * lax.rsqrt(jnp.mean(widened * widened, axis=1, keepdims=True) + epsilon)
    ).astype(jnp.bfloat16)
    pieces = sent_together((gate_weight, up_weight), "query", 0, 1)
    gate_sum = jnp.dot(normed, pieces[0], preferred_element_type=jnp.float32)
    up_sum = jnp.dot(normed, pieces[1], preferred_element_type=jnp.float32)
    hidden_units = (jax.nn.silu(gate_sum) * up_sum).astype(jnp.bfloat16)
    branch_part = jnp.dot(
        hidden_units, collect(down_weight, "query", 1), preferred_element_type=jnp.float32
    )
    feat_width = hidden_in.shape[1]
    branch_out = sum_at_owner(branch_part, CORPUS, 1)
    residual = hidden_in.astype(jnp.float32) + branch_out
    total_sq = over_copies(jnp.sum(residual * residual, axis=1), CORPUS)
    final_rows = residual * lax.rsqrt(total_sq / D + epsilon)[:, None]
    group_count = lengths.shape[0]
    grouped = final_rows.reshape(group_count, SEQ, feat_width)
    valid_mask = (jnp.arange(SEQ, dtype=jnp.int32)[None, :] < lengths[:, None]).astype(jnp.float32)
    pooled = jnp.sum(grouped * valid_mask[:, :, None], axis=1) / lengths[:, None].astype(
        jnp.float32
    )
    pooled = pooled.astype(jnp.bfloat16)
    code_part = jnp.dot(pooled, code_weight, preferred_element_type=jnp.float32)
    group_codes = over_copies(code_part, CORPUS).astype(jnp.bfloat16)
    query_codes = collect(group_codes, "query", 0)
    scale = 1.0 / math.sqrt(corpus_codes.shape[1])
    scores = (
        lax.dot_general(
            query_codes, corpus_codes, (((1,), (1,)), ((), ())), preferred_element_type=jnp.float32
        )
        * scale
    )
    local_best = lax.top_k(scores, TOPK)[0]
    top_scores = merged_by_axis(local_best, QUERY_CORPUS, keep_best)
    return top_scores


def solution(mesh):
    split = Mesh(
        mesh.devices.reshape(mesh.shape["query"], 4, 8, 2),
        ("query", "corpus_0", "corpus_1", "corpus_2"),
    )
    return jax.shard_map(
        per_device,
        mesh=split,
        in_specs=(
            P("query", CORPUS),
            P("query"),
            P("query", CORPUS),
            P("query", CORPUS),
            P(CORPUS, "query"),
            P(CORPUS, None),
            P(QUERY_CORPUS, None),
        ),
        out_specs=P(),
        check_vma=False,
    )
```

profile of v0, /device:TPU:32, one launch (start us, length us, event | category | flops | bytes accessed | tf_op | source)
XLA Modules:
  0.0 321.6 jit_solution(3866231962825095288)
XLA Ops:
  6.5 2.3 pad_maximum_fusion
  9.2 37.5 %all_to_all.31 = bf16[4,224,1024]{2,1,0:T(8,128)(2,1)} all-to-all(bf16[4,224,1024]{2,1,0:T(8,128)(2,1)S(1)} %broadcast_in_dim.11), channel_id=1, replica_groups=mesh['query'=4,'corpus_0'=4,'corpus_1'=8,'corpus_2'=2] {'query'}, dimensions={0} | all-to-all | bytes 3670016 | tf_op jit(solution)/shard_map/all_to_all | solution.py:21
  47.9 12.7 %all-to-all-start = ((bf16[64,128,64]{1,2,0:T(8,128)(2,1)}), bf16[64,128,64]{1,2,0:T(8,128)(2,1)S(1)}, u32[]{:S(2)}, u32[]{:S(2)}) async-start(bf16[64,128,64]{1,2,0:T(8,128)(2,1)} %broadcast_in_dim.10), calls=%async_computation | async-start | bytes 2097152 | tf_op jit(solution)/shard_map/all_to_all | solution.py:21
  60.6 3.0 copy.25
  63.6 4.0 %copy.20 = bf16[4096,224]{1,0:T(8,128)(2,1)} copy(bf16[4096,224]{0,1:T(8,128)(2,1)} %bitcast.29) | data formatting | bytes 3670016 | tf_op jit(solution)/shard_map/dot_general | solution.py:82
  67.6 20.9 %all-to-all-done = bf16[64,128,64]{1,2,0:T(8,128)(2,1)S(1)} async-done(((bf16[64,128,64]{1,2,0:T(8,128)(2,1)}), bf16[64,128,64]{1,2,0:T(8,128)(2,1)S(1)}, u32[]{:S(2)}, u32[]{:S(2)}) %all-to-all-start) | async-done | bytes 1048608 | tf_op jit(solution)/shard_map/all_to_all | solution.py:21
  89.3 2.5 fusion.3
  91.8 3.8 %convolution_bitcast_fusion = f32[64,128,64]{1,2,0:T(8,128)S(1)} fusion(bf16[64,64,224]{2,1,0:T(8,128)(2,1)} %bitcast.27, bf16[128,4096]{0,1:T(8,128)(2,1)} %copy-done.1, bf16[4096,448]{0,1:T(8,128)(2,1)} %all-gather.6.cloned.1.call-done, f32[128,224]{0,1:T(8,128)S(1)} %fusion.3), kind=kOutput, calls=%fused_computation.7 | convolution fusion | flops 469934080 | bytes 7192576 | tf_op jit(solution)/shard_map/dot_general | solution.py:82
  95.6 56.6 %all_to_all.32 = f32[64,128,64]{1,2,0:T(8,128)} all-to-all(f32[64,128,64]{1,2,0:T(8,128)S(1)} %convolution_bitcast_fusion), channel_id=1, replica_groups=mesh['query'=4,'corpus_0'=4,'corpus_1'=8,'corpus_2'=2] {'corpus_0','corp..., dimensions={0} | all-to-all | bytes 4194304 | tf_op jit(solution)/shard_map/all_to_all | solution.py:51
  154.6 7.3 %all-to-all-start.3 = ((f32[64,1,128]{2,1,0:T(1,128)}), f32[64,1,128]{2,1,0:T(1,128)S(1)}, u32[]{:S(2)}, u32[]{:S(2)}) async-start(f32[64,1,128]{2,1,0:T(1,128)} %broadcast_in_dim.12), calls=%async_computation.3 | async-start | bytes 65536 | tf_op jit(solution)/shard_map/all_to_all | solution.py:21
  162.0 8.5 %all-to-all-done.3 = f32[64,1,128]{2,1,0:T(1,128)S(1)} async-done(((f32[64,1,128]{2,1,0:T(1,128)}), f32[64,1,128]{2,1,0:T(1,128)S(1)}, u32[]{:S(2)}, u32[]{:S(2)}) %all-to-all-start.3) | async-done | bytes 32800 | tf_op jit(solution)/shard_map/all_to_all | solution.py:21
  171.1 32.6 %all_to_all.33 = f32[64,4,1024]{2,1,0:T(4,128)S(1)} all-to-all(f32[64,4,1024]{2,1,0:T(4,128)S(1)} %broadcast_in_dim.13), channel_id=1, replica_groups=mesh['query'=4,'corpus_0'=4,'corpus_1'=8,'corpus_2'=2] {'corpus_0','corp..., dimensions={0} | all-to-all | bytes 2097152 | tf_op jit(solution)/shard_map/all_to_all | solution.py:21
  204.0 7.8 %all_to_all.34 = bf16[4,4,1024]{2,1,0:T(4,128)(2,1)S(1)} all-to-all(bf16[4,4,1024]{2,1,0:T(4,128)(2,1)S(1)} %broadcast_in_dim.14), channel_id=1, replica_groups=mesh['query'=4,'corpus_0'=4,'corpus_1'=8,'corpus_2'=2] {'query'}, dimensions={0} | all-to-all | bytes 65536 | tf_op jit(solution)/shard_map/all_to_all | solution.py:21
  212.2 3.1 sort_prefixfusion
  215.3 11.9 %all-gather = f32[64,100]{1,0:T(8,128)S(1)} all-gather(f32[16,100]{1,0:T(8,128)S(1)} %sort_prefixfusion), channel_id=2, replica_groups=mesh['query'=4,'corpus_0'=4,'corpus_1'=8,'corpus_2'=2] {'query'}, dimensions={0}, use_global_device_ids=true | all-gather | bytes 32000 | tf_op jit(solution)/shard_map/all_gather | solution.py:61
  227.4 3.4 %top_k.117 = (f32[16,200]{1,0:T(8,128)S(1)}, s32[16,200]{1,0:T(8,128)}) sort(f32[16,200]{1,0:T(8,128)S(1)} %pad_maximum_fusion.1, s32[16,200]{1,0:T(8,128)S(1)} %iota.53), dimensions={1}, to_apply=%region_7.8 | sort | flops 38400 | bytes 51200 | tf_op jit(solution)/shard_map/top_k | solution.py:69
  230.9 3.4 %top_k.119 = (f32[16,200]{1,0:T(8,128)S(1)}, s32[16,200]{1,0:T(8,128)}) sort(f32[16,200]{1,0:T(8,128)S(1)} %pad_maximum_fusion.2, s32[16,200]{1,0:T(8,128)S(1)} %iota.54), dimensions={1}, to_apply=%region_8.9 | sort | flops 38400 | bytes 51200 | tf_op jit(solution)/shard_map/top_k | solution.py:69
  234.4 3.4 %top_k.121 = (f32[16,200]{1,0:T(8,128)S(1)}, s32[16,200]{1,0:T(8,128)}) sort(f32[16,200]{1,0:T(8,128)S(1)} %pad_maximum_fusion.3, s32[16,200]{1,0:T(8,128)S(1)} %iota.55), dimensions={1}, to_apply=%region_9.10 | sort | flops 38400 | bytes 51200 | tf_op jit(solution)/shard_map/top_k | solution.py:69
  237.8 12.1 %all-gather.1 = f32[64,100]{1,0:T(8,128)S(1)} all-gather(f32[16,100]{1,0:T(8,128)S(1)} %top_k.122), channel_id=3, replica_groups=mesh['query'=4,'corpus_0'=4,'corpus_1'=8,'corpus_2'=2] {'corpus_0'}, dimensions={0}, use_global_device_ids=true | all-gather | bytes 32000 | tf_op jit(solution)/shard_map/all_gather | solution.py:61
  250.0 3.4 %top_k.123 = (f32[16,200]{1,0:T(8,128)S(1)}, s32[16,200]{1,0:T(8,128)}) sort(f32[16,200]{1,0:T(8,128)S(1)} %pad_maximum_fusion.4, s32[16,200]{1,0:T(8,128)S(1)} %iota.56), dimensions={1}, to_apply=%region_10.11 | sort | flops 38400 | bytes 51200 | tf_op jit(solution)/shard_map/top_k | solution.py:69
  253.5 3.4 %top_k.129 = (f32[16,200]{1,0:T(8,128)S(1)}, s32[16,200]{1,0:T(8,128)}) sort(f32[16,200]{1,0:T(8,128)S(1)} %pad_maximum_fusion.5, s32[16,200]{1,0:T(8,128)S(1)} %iota.57), dimensions={1}, to_apply=%region_11.12 | sort | flops 38400 | bytes 51200 | tf_op jit(solution)/shard_map/top_k | solution.py:69
  257.1 3.4 %top_k.131 = (f32[16,200]{1,0:T(8,128)S(1)}, s32[16,200]{1,0:T(8,128)}) sort(f32[16,200]{1,0:T(8,128)S(1)} %pad_maximum_fusion.6, s32[16,200]{1,0:T(8,128)S(1)} %iota.58), dimensions={1}, to_apply=%region_12.13 | sort | flops 38400 | bytes 51200 | tf_op jit(solution)/shard_map/top_k | solution.py:69
  260.5 23.7 %all-gather.2 = f32[128,100]{1,0:T(8,128)S(1)} all-gather(f32[16,100]{1,0:T(8,128)S(1)} %top_k.132), channel_id=4, replica_groups=mesh['query'=4,'corpus_0'=4,'corpus_1'=8,'corpus_2'=2] {'corpus_1'}, dimensions={0}, use_global_device_ids=true | all-gather | bytes 57600 | tf_op jit(solution)/shard_map/all_gather | solution.py:61
  284.3 3.4 %top_k.133 = (f32[16,200]{1,0:T(8,128)S(1)}, s32[16,200]{1,0:T(8,128)}) sort(f32[16,200]{1,0:T(8,128)S(1)} %pad_maximum_fusion.7, s32[16,200]{1,0:T(8,128)S(1)} %iota.59), dimensions={1}, to_apply=%region_13.14 | sort | flops 38400 | bytes 51200 | tf_op jit(solution)/shard_map/top_k | solution.py:69
  287.8 3.4 %top_k.135 = (f32[16,200]{1,0:T(8,128)S(1)}, s32[16,200]{1,0:T(8,128)}) sort(f32[16,200]{1,0:T(8,128)S(1)} %pad_maximum_fusion.8, s32[16,200]{1,0:T(8,128)S(1)} %iota.60), dimensions={1}, to_apply=%region_14.15 | sort | flops 38400 | bytes 51200 | tf_op jit(solution)/shard_map/top_k | solution.py:69
  291.3 3.4 %top_k.141 = (f32[16,200]{1,0:T(8,128)S(1)}, s32[16,200]{1,0:T(8,128)}) sort(f32[16,200]{1,0:T(8,128)S(1)} %pad_maximum_fusion.9, s32[16,200]{1,0:T(8,128)S(1)} %iota.61), dimensions={1}, to_apply=%region_15.16 | sort | flops 38400 | bytes 51200 | tf_op jit(solution)/shard_map/top_k | solution.py:69
  294.8 3.4 %top_k.143 = (f32[16,200]{1,0:T(8,128)S(1)}, s32[16,200]{1,0:T(8,128)}) sort(f32[16,200]{1,0:T(8,128)S(1)} %pad_maximum_fusion.10, s32[16,200]{1,0:T(8,128)S(1)} %iota.62), dimensions={1}, to_apply=%region_16.17 | sort | flops 38400 | bytes 51200 | tf_op jit(solution)/shard_map/top_k | solution.py:69
  298.4 3.4 %top_k.145 = (f32[16,200]{1,0:T(8,128)S(1)}, s32[16,200]{1,0:T(8,128)}) sort(f32[16,200]{1,0:T(8,128)S(1)} %pad_maximum_fusion.11, s32[16,200]{1,0:T(8,128)S(1)} %iota.63), dimensions={1}, to_apply=%region_17.18 | sort | flops 38400 | bytes 51200 | tf_op jit(solution)/shard_map/top_k | solution.py:69
  301.9 3.4 %top_k.147 = (f32[16,200]{1,0:T(8,128)S(1)}, s32[16,200]{1,0:T(8,128)}) sort(f32[16,200]{1,0:T(8,128)S(1)} %pad_maximum_fusion.12, s32[16,200]{1,0:T(8,128)S(1)} %iota.64), dimensions={1}, to_apply=%region_18.19 | sort | flops 38400 | bytes 51200 | tf_op jit(solution)/shard_map/top_k | solution.py:69
  305.4 3.4 %top_k.153 = (f32[16,200]{1,0:T(8,128)S(1)}, s32[16,200]{1,0:T(8,128)}) sort(f32[16,200]{1,0:T(8,128)S(1)} %pad_maximum_fusion.13, s32[16,200]{1,0:T(8,128)S(1)} %iota.65), dimensions={1}, to_apply=%region_19.20 | sort | flops 38400 | bytes 51200 | tf_op jit(solution)/shard_map/top_k | solution.py:69
  308.8 1.8 all-gather.3
  310.7 3.4 %top_k.155 = (f32[16,200]{1,0:T(8,128)S(1)}, s32[16,200]{1,0:T(8,128)}) sort(f32[16,200]{1,0:T(8,128)S(1)} %pad_maximum_fusion.14, s32[16,200]{1,0:T(8,128)S(1)} %iota.66), dimensions={1}, to_apply=%region_20.21 | sort | flops 38400 | bytes 51200 | tf_op jit(solution)/shard_map/top_k | solution.py:69
  (82 shorter events, 7.9 us)
Async XLA Ops:
  6.5 205.3 %copy-start = (bf16[512,1024]{1,0:T(8,128)(2,1)S(1)}, bf16[512,1024]{1,0:T(8,128)(2,1)}, u32[]{:S(2)}) copy-start(bf16[512,1024]{1,0:T(8,128)(2,1)} %param.13) | copy-start | bytes 3145732
  6.5 2.4 copy-start.2
  6.5 82.8 %all-gather.6.cloned.1.call-start = ((), (), s32[]{:S(2)}) async-start(), calls=%async_computation.6 | async-start | bytes 4587520 | tf_op jit(solution)/shard_map/all_gather | solution.py:41
  9.1 37.5 %copy-start.3 = (bf16[128,64]{0,1:T(8,128)(2,1)S(1)}, bf16[128,64]{0,1:T(8,128)(2,1)}, u32[]{:S(2)}) copy-start(bf16[128,64]{0,1:T(8,128)(2,1)} %param.7) | copy-start | bytes 49156
  47.9 40.6 %all-to-all-start = ((bf16[64,128,64]{1,2,0:T(8,128)(2,1)}), bf16[64,128,64]{1,2,0:T(8,128)(2,1)S(1)}, u32[]{:S(2)}, u32[]{:S(2)}) async-start(bf16[64,128,64]{1,2,0:T(8,128)(2,1)} %broadcast_in_dim.10), calls=%async_computation | async-start | bytes 2097152 | tf_op jit(solution)/shard_map/all_to_all | solution.py:21
  89.3 2.5 copy-start.1
  152.2 9.7 %copy-start.4 = (s32[4]{0:T(128)S(1)}, s32[4]{0:T(128)}, u32[]{:S(2)}) copy-start(s32[4]{0:T(128)} %param.8) | copy-start | bytes 52
  152.2 18.5 %copy-start.5 = (bf16[64,1024]{1,0:T(8,128)(2,1)S(1)}, bf16[64,1024]{1,0:T(8,128)(2,1)}, u32[]{:S(2)}) copy-start(bf16[64,1024]{1,0:T(8,128)(2,1)} %param.12) | copy-start | bytes 393220
  154.6 15.8 %all-to-all-start.3 = ((f32[64,1,128]{2,1,0:T(1,128)}), f32[64,1,128]{2,1,0:T(1,128)S(1)}, u32[]{:S(2)}, u32[]{:S(2)}) async-start(f32[64,1,128]{2,1,0:T(1,128)} %broadcast_in_dim.12), calls=%async_computation.3 | async-start | bytes 65536 | tf_op jit(solution)/shard_map/all_to_all | solution.py:21
Sparse Core Ops, SparseCore 0:
  9.2 57.3 all-gather.5
where the time goes:
time: 325 us; the launch traced here: 322 us
  blocking collectives  184 us (57%)
  other arithmetic  57.7 us (18%)
  waiting for transfers between devices  29.5 us (9%)
  starting transfers between devices  20 us (6%)
  between operations  13.6 us (4%)
  local copies, waits for them, and re-layouts  10.1 us (3%)
  matrix products  6.82 us (2%)
    all_to_all x3, blocking collectives, copy_for_each(): lax.all_to_all(jnp.broadcast_to(x[None], (peers, *x.shape)), axis, 0, 0,...  77.9 us
    all_to_all x1, blocking collectives, sum_at_owner(): lax.all_to_all(parts, axis, split_axis=0, concat_axis=0, tiled=True)  56.6 us
    all_gather x4, blocking collectives, merged_by_axis(): pieces = lax.all_gather(x, axis)  49.5 us
    top_k x14, other arithmetic, keep_best(): lax.top_k(jnp.concatenate([first, second], axis=1), first.shape[1])[0]  48.1 us
    all_to_all x2, waiting for transfers between devices, copy_for_each(): lax.all_to_all(jnp.broadcast_to(x[None], (peers, *x.shape)), axis, 0, 0,...  29.4 us
    all_to_all x2, starting transfers between devices, copy_for_each(): lax.all_to_all(jnp.broadcast_to(x[None], (peers, *x.shape)), axis, 0, 0,...  20 us
  transfers between devices with their start and end apart: 3, of which 2 were waited for; matrix products, arithmetic and copies ran while one was open for 3% of the time, Pallas kernels for 0%

commit v1 on v0

v1 whole, which is shorter than its diff:
```python
import math

import jax
import jax.numpy as jnp
from jax import lax
from jax.experimental import pallas as pl
from jax.experimental.pallas import tpu as pltpu
from jax.sharding import Mesh
from jax.sharding import PartitionSpec as P

D = 4096
SEQ = 32
TOPK = 100
Z = ("zh", "zb")
XZ = ("x", "zh", "zb")
YXZ = ("y", "x", "zh", "zb")
CORPUS = ("x", "zh", "zb", "k")
QUERY_CORPUS = ("y", "x", "zh", "zb", "k")
EPS = 1e-05
F32 = jnp.float32
BF16 = jnp.bfloat16
PARAMS = pltpu.CompilerParams(vmem_limit_bytes=32 * 1024 * 1024)
VMEM = pl.BlockSpec(memory_space=pltpu.VMEM)
SMEM = pl.BlockSpec(memory_space=pltpu.SMEM)


def shape(dims, dtype):
    return jax.ShapeDtypeStruct(dims, dtype)


def to_peer(x):
    return lax.ppermute(x, "k", [(0, 1), (1, 0)])


def shifted(x, d):
    return lax.ppermute(x, "y", [(i, (i + d) % 4) for i in range(4)])


def spread(x, axes, peers):
    copies = jnp.broadcast_to(x[None], (peers, *x.shape))
    return lax.all_to_all(copies, axes, 0, 0, tiled=True)


def lanes(like):
    return lax.broadcasted_iota(jnp.int32, like, 1)


def gate_up_kernel(place, h, g0, u0, g1, u1, o0, o1, o2, o3, lhs, wide):
    y = place[0]
    for d in range(4):
        i = (y + d) % 4
        for z in range(8):
            lhs[d * 64 : d * 64 + 64, z * 128 : z * 128 + 128] = h[i * 8 + z]
    left = lhs[...]
    widened = left.astype(F32)
    sq = jnp.sum(widened * widened, axis=1, keepdims=True)
    top = sq.astype(BF16).astype(F32)
    mid = (sq - top).astype(BF16).astype(F32)
    low = sq - top - mid
    col = lanes((256, 256))
    wide[...] = jnp.zeros((256, 256), F32)
    for b, w in enumerate((g0, u0, g1, u1)):
        wide[:, 0:224] = jnp.dot(left, w[...], preferred_element_type=F32)
        block = wide[...]
        if b == 0:
            block = jnp.where(col == 224, top, block)
            block = jnp.where(col == 225, mid, block)
            block = jnp.where(col == 226, low, block)
        block = block.astype(BF16)
        for d, o in enumerate((o0, o1, o2, o3)):
            o[:, b * 256 : b * 256 + 256] = block[d * 64 : d * 64 + 64]


def gate_up(place, h, g0, u0, g1, u1):
    part = shape((64, 1024), BF16)
    return pl.pallas_call(
        gate_up_kernel,
        out_shape=(part,) * 4,
        in_specs=[SMEM] + [VMEM] * 5,
        out_specs=(VMEM,) * 4,
        scratch_shapes=[pltpu.VMEM((256, 1024), BF16), pltpu.VMEM((256, 256), F32)],
        compiler_params=PARAMS,
        name="gate_up",
    )(place, h, g0, u0, g1, u1)


def hidden_kernel(a, b, c, d, out):
    total = a[...].astype(F32) + b[...].astype(F32) + c[...].astype(F32) + d[...].astype(F32)
    col = lanes((64, 256))
    first = total[:, 0:256]
    sq = jnp.sum(jnp.where((col >= 224) & (col < 227), first, 0.0), axis=1, keepdims=True)
    r = lax.rsqrt(sq / D + EPS)
    for b in range(2):
        gate = total[:, b * 512 : b * 512 + 256] * r
        up = total[:, b * 512 + 256 : b * 512 + 512] * r
        units = gate / (1.0 + jnp.exp(-gate)) * up
        out[:, b * 256 : b * 256 + 256] = jnp.where(col < 224, units, 0.0).astype(BF16)


def hidden_of(a, b, c, d):
    return pl.pallas_call(
        hidden_kernel,
        out_shape=shape((64, 512), BF16),
        in_specs=[VMEM] * 4,
        out_specs=VMEM,
        compiler_params=PARAMS,
        name="hidden_units",
    )(a, b, c, d)


def down_kernel(place, a, b, c, d, w0, w1, out, lhs):
    y = place[0]
    for s, part in enumerate((a, b, c, d)):
        at = pl.multiple_of(((y - s + 4) % 4) * 64, 64)
        lhs[pl.ds(at, 64), :] = part[...]
    total = jnp.dot(lhs[:, 0:224], w0[...], preferred_element_type=F32)
    total += jnp.dot(lhs[:, 256:480], w1[...], preferred_element_type=F32)
    out[...] = total.astype(BF16)


def down(place, parts, w0, w1):
    return pl.pallas_call(
        down_kernel,
        out_shape=shape((256, 1024), BF16),
        in_specs=[SMEM] + [VMEM] * 6,
        out_specs=VMEM,
        scratch_shapes=[pltpu.VMEM((256, 512), BF16)],
        compiler_params=PARAMS,
        name="down",
    )(place, *parts, w0, w1)


def residual_kernel(parts, h, res, sq):
    total = h[...].astype(F32)
    for p in range(32):
        total += parts[p].astype(F32)
    res[...] = total
    sq[...] = jnp.broadcast_to(jnp.sum(total * total, axis=1, keepdims=True), (8, 128))


def residual_of(parts, h):
    return pl.pallas_call(
        residual_kernel,
        out_shape=(shape((8, 1024), F32), shape((8, 128), F32)),
        in_specs=[VMEM] * 2,
        out_specs=(VMEM,) * 2,
        compiler_params=PARAMS,
        name="residual",
    )(parts, h)


def pool_kernel(place, length, res, a, b, c, d, keep, send):
    k, first = place[1], place[2]
    sq = (a[...] + b[...] + c[...] + d[...])[:, 0:1]
    rows = lax.broadcasted_iota(jnp.int32, (8, 1), 0) + first
    count = length[0]
    weight = jnp.where(rows < count, lax.rsqrt(sq / D + EPS), 0.0)
    pooled = jnp.sum(res[...] * weight, axis=0, keepdims=True) / count.astype(F32)
    low, high = pooled[:, 0:512], pooled[:, 512:1024]
    keep[...] = jnp.where(k == 0, low, high)
    send[...] = jnp.where(k == 0, high, low)


def pool(place, length, res, sqs):
    half = shape((1, 512), F32)
    return pl.pallas_call(
        pool_kernel,
        out_shape=(half, half),
        in_specs=[SMEM] * 2 + [VMEM] * 5,
        out_specs=(VMEM,) * 2,
        compiler_params=PARAMS,
        name="pool",
    )(place, length, res, *sqs)


def code_kernel(place, a, b, w, keep, send):
    k = place[1]
    pooled = a[...] + b[...]
    top = pooled.astype(BF16).astype(F32)
    row = lax.broadcasted_iota(jnp.int32, (8, 512), 0)
    left = jnp.where(row == 0, top, jnp.where(row == 1, pooled - top, 0.0)).astype(BF16)
    both = jnp.dot(left, w[...], preferred_element_type=F32)
    part = both[0:1] + both[1:2]
    low, high = part[:, 0:512], part[:, 512:1024]
    keep[...] = jnp.where(k == 0, low, high)
    send[...] = jnp.where(k == 0, high, low)


def code_part(place, a, b, w):
    half = shape((1, 512), F32)
    return pl.pallas_call(
        code_kernel,
        out_shape=(half, half),
        in_specs=[SMEM] + [VMEM] * 3,
        out_specs=(VMEM,) * 2,
        compiler_params=PARAMS,
        name="code_part",
    )(place, a, b, w)


def exchange(x, step, falling):
    col = lanes(x.shape)
    upper = (col & step) != 0
    other = jnp.where(upper, pltpu.roll(x, step, 1), pltpu.roll(x, 128 - step, 1))
    return jnp.where(upper ^ falling, jnp.maximum(x, other), jnp.minimum(x, other))


def bitonic_merge(x, falling):
    for step in (64, 32, 16, 8, 4, 2, 1):
        x = exchange(x, step, falling)
    return x


def bitonic_sort(x, falling):
    col = lanes(x.shape)
    for size in (2, 4, 8, 16, 32, 64, 128):
        way = falling if size == 128 else falling ^ ((col & size) != 0)
        step = size // 2
        while step:
            x = exchange(x, step, way)
            step //= 2
    return x


def rows_of(like):
    return lax.broadcasted_iota(jnp.int32, like, 0)


def score_kernel(place, mine, theirs, docs, keep, send, *, scale):
    k = place[1]
    own, peer = mine[...], theirs[...]
    low = jnp.where(k == 0, own, peer)
    high = jnp.where(k == 0, peer, own)
    dims = (((1,), (1,)), ((), ()))
    scores = lax.dot_general(low, docs[:, 0:512], dims, preferred_element_type=F32)
    scores += lax.dot_general(high, docs[:, 512:1024], dims, preferred_element_type=F32)
    scores = scores * scale
    x = jnp.concatenate([scores[:, c * 128 : c * 128 + 128] for c in range(4)], axis=0)
    x = bitonic_sort(x, rows_of((64, 128)) < 32)
    x = jnp.maximum(x[0:32], x[32:64])
    x = bitonic_merge(x, rows_of((32, 128)) < 16)
    x = jnp.maximum(x[0:16], x[16:32])
    kept = (rows_of((16, 128)) // 8) == k
    x = bitonic_merge(x, kept)
    keep[...] = jnp.where(k == 0, x[0:8], x[8:16])
    send[...] = jnp.where(k == 0, x[8:16], x[0:8])


def local_lists(place, mine, theirs, docs):
    half = shape((8, 128), F32)

    def body(*refs):
        score_kernel(*refs, scale=1.0 / math.sqrt(docs.shape[1]))

    return pl.pallas_call(
        body,
        out_shape=(half, half),
        in_specs=[SMEM] + [VMEM] * 3,
        out_specs=(VMEM,) * 2,
        compiler_params=PARAMS,
        name="scores",
    )(place, mine, theirs, docs)


def pair_kernel(place, a, b, o0, o1, o2, o3, held):
    y = place[0]
    x = jnp.maximum(a[...], b[...])
    turn = (rows_of((8, 128)) // 2 - y + 4) % 4
    held[...] = bitonic_merge(x, turn % 2 == 0)
    for d, o in enumerate((o0, o1, o2, o3)):
        q = (y + d) % 4
        for r in range(2):
            o[r : r + 1, :] = held[pl.ds(q * 2 + r, 1), :]


def pair_lists(place, a, b):
    two = shape((2, 128), F32)
    return pl.pallas_call(
        pair_kernel,
        out_shape=(two,) * 4,
        in_specs=[SMEM] + [VMEM] * 2,
        out_specs=(VMEM,) * 4,
        scratch_shapes=[pltpu.VMEM((8, 128), F32)],
        compiler_params=PARAMS,
        name="pair_lists",
    )(place, a, b)


def four_kernel(place, a, b, c, d, out, held):
    odd = place[3]
    held[0:2] = jnp.maximum(a[...], b[...])
    held[2:4] = jnp.maximum(c[...], d[...])
    held[4:8] = jnp.zeros((4, 128), F32)
    x = bitonic_merge(held[...], rows_of((8, 128)) < 2)
    held[...] = x
    held[0:2] = jnp.maximum(held[0:2], held[2:4])
    x = bitonic_merge(held[...], (rows_of((8, 128)) * 0 + odd) == 0)
    held[...] = x
    for p in range(128):
        out[p] = held[0:2]


def four_lists(place, lists):
    return pl.pallas_call(
        four_kernel,
        out_shape=shape((128, 2, 128), F32),
        in_specs=[SMEM] + [VMEM] * 4,
        out_specs=VMEM,
        scratch_shapes=[pltpu.VMEM((8, 128), F32)],
        compiler_params=PARAMS,
        name="four_lists",
    )(place, *lists)


def final_kernel(x_ref, out):
    x = x_ref[...]
    lists = 32
    while lists > 1:
        x = x.reshape(lists // 2, 2, 8, 128)
        x = jnp.maximum(x[:, 0], x[:, 1])
        lists //= 2
        x = x.reshape(lists * 8, 128)
        falling = (rows_of(x.shape) // 8) % 2 == 0
        x = bitonic_merge(x, falling)
    out[...] = x


def final_lists(x):
    return pl.pallas_call(
        final_kernel,
        out_shape=shape((8, 128), F32),
        in_specs=[VMEM],
        out_specs=VMEM,
        compiler_params=PARAMS,
        name="final_lists",
    )(x)


def per_device(hidden_in, lengths, gate_weight, up_weight, down_weight, code_weight, corpus_codes):
    y, x, zh, zb, k = (lax.axis_index(a) for a in QUERY_CORPUS)
    place = jnp.stack([y, k, 16 * k + 8 * zb, zb]).astype(jnp.int32)

    halves = hidden_in.reshape(4, 2, 16, 64)
    first, second = halves[:, 0].reshape(64, 64), halves[:, 1].reshape(64, 64)
    counts = jnp.broadcast_to(jnp.repeat(lengths.astype(BF16), 4)[:, None], (16, 64))
    own = jnp.concatenate([jnp.where(k == 0, first, second), counts], axis=0)
    other = jnp.where(k == 0, second, first)
    swap = [(a * 4 + b, b * 4 + a) for a in range(4) for b in range(4)]
    straight = [(s * 2 + c, t * 2 + c) for s, t in swap for c in range(2)]
    crossed = [(s * 2 + c, t * 2 + 1 - c) for s, t in swap for c in range(2)]
    own = lax.ppermute(own, ("y", "x", "k"), straight)
    other = lax.ppermute(other, ("y", "x", "k"), crossed)
    length = lax.dynamic_slice(own[:, 0], (64 + 4 * zh,), (1,)).astype(jnp.int32)
    own = own[:64]
    block = jnp.where(
        k == 0, jnp.concatenate([own, other], axis=1), jnp.concatenate([other, own], axis=1)
    )
    gathered = spread(block, XZ, 32)

    gate_peer, up_peer, down_peer = (to_peer(w) for w in (gate_weight, up_weight, down_weight))

    moves = []
    for i in range(4):
        for j in range(4):
            for z in range(8):
                for c in range(2):
                    source = ((i * 4 + j) * 8 + z) * 2 + c
                    target = ((j * 4 + i) * 8 + (z % 4) * 2 + c) * 2 + z // 4
                    moves.append((source, target))
    code_rows = lax.ppermute(code_weight, QUERY_CORPUS, moves)
    code_rows = lax.all_gather(code_rows, Z, axis=0, tiled=True)

    parts = gate_up(place, gathered, gate_weight, up_weight, gate_peer, up_peer)
    units = hidden_of(parts[0], *(shifted(parts[d], d) for d in (1, 2, 3)))
    groups = (units, *(shifted(units, d) for d in (1, 2, 3)))
    branch = down(place, groups, down_weight, down_peer)
    branch = lax.all_to_all(branch.reshape(32, 8, 1024), XZ, 0, 0, tiled=True)
    here = lax.dynamic_slice(
        gathered.reshape(4, 8, 64, 128), (x, 0, zh * 16 + zb * 8, 0), (1, 8, 8, 128)
    )[0]
    here = jnp.moveaxis(here, 0, 1).reshape(8, 1024)
    res, sq = residual_of(branch, here)
    sqs = (sq, *(shifted(sq, d) for d in (1, 2, 3)))
    keep, send = pool(place, length, res, sqs)
    keep, send = code_part(place, keep, to_peer(send), code_rows)
    part = (keep + to_peer(send)).reshape(4, 128)
    codes = spread(part, YXZ, 128).reshape(4, 4, 4, 2, 512).sum(axis=(0, 3))
    codes = codes.reshape(16, 512).astype(BF16)

    keep, send = local_lists(place, codes, to_peer(codes), corpus_codes)
    lists = pair_lists(place, keep, to_peer(send))
    lists = (lists[0], *(shifted(lists[d], d) for d in (1, 2, 3)))
    lists = four_lists(place, lists)
    arrived = lax.all_to_all(lists, YXZ, 0, 0, tiled=True)
    arrived = jnp.moveaxis(arrived.reshape(4, 32, 2, 128), 0, 1).reshape(256, 128)
    best = final_lists(arrived)
    peer = to_peer(best)
    best = jnp.where(
        k == 0, jnp.concatenate([best, peer], axis=0), jnp.concatenate([peer, best], axis=0)
    )
    return best[:, :TOPK]


def solution(mesh):
    split = Mesh(mesh.devices.reshape(4, 4, 4, 2, 2), QUERY_CORPUS)
    return jax.shard_map(
        per_device,
        mesh=split,
        in_specs=(
            P("y", CORPUS),
            P("y"),
            P("y", CORPUS),
            P("y", CORPUS),
            P(CORPUS, "y"),
            P(CORPUS, None),
            P(QUERY_CORPUS, None),
        ),
        out_specs=P(),
        check_vma=False,
    )
```

time: 325 us -> 188 us (0.58)
  blocking collectives: 184 us -> 42.4 us
  other arithmetic: 57.7 us -> 1 us
  starting transfers between devices: 20 us -> 61.2 us
  waiting for transfers between devices: 29.5 us -> 45.8 us
  Pallas kernels: 0 us -> 14 us
  matrix products: 6.82 us -> 0 us
  local copies, waits for them, and re-layouts: 10.1 us -> 5.8 us
    all_to_all x4 -> x2, blocking collectives: 134 us -> 42.4 us  [the longest x1 22.8 us: spread(): return lax.all_to_all(copies, axes, 0, 0, tiled=True)]
    top_k x15 -> x0, other arithmetic: 51.3 us -> none  [the longest x14 48.1 us: keep_best(): lax.top_k(jnp.concatenate([first, second], axis=1), first.shape[1])[0]]
    all_gather x4 -> x0, blocking collectives: 49.5 us -> none  [merged_by_axis(): pieces = lax.all_gather(x, axis)]
    ppermute x0 -> x23, starting transfers between devices: none -> 32 us  [the longest x12 21.2 us: shifted(): return lax.ppermute(x, 'y', [(i, (i + d) % 4) for i in range(4)])]
    ppermute x0 -> x23, waiting for transfers between devices: none -> 28.3 us  [the longest x12 10.3 us: shifted(): return lax.ppermute(x, 'y', [(i, (i + d) % 4) for i in range(4)])]
    pallas_call x0 -> x10, Pallas kernels: none -> 14 us  [the longest x1 3.95 us: local_lists(): pl.pallas_call(body, out_shape=(half, half), in_specs=[SMEM] + [VMEM] * 3...]
    all_to_all x2, waiting for transfers between devices: 29.4 us -> 17.5 us  [the longest x1 17.5 us: per_device(): branch = lax.all_to_all(branch.reshape(32, 8, 1024), XZ, 0, 0, tiled=True)]
    all_to_all x2, starting transfers between devices: 20 us -> 29.1 us  [the longest x1 21.6 us: spread(): return lax.all_to_all(copies, axes, 0, 0, tiled=True)]
  transfers between devices with their start and end apart: 3 -> 26, of which waited for: 2 -> 19; matrix products, arithmetic and copies ran while one was open for 3% -> 1% of each run, Pallas kernels for 0% -> 2%
where the time goes in v1:
time: 188 us; the launch traced here: 184 us
  starting transfers between devices  61.2 us (33%)
  waiting for transfers between devices  45.8 us (24%)
  blocking collectives  42.4 us (23%)
  between operations  14.3 us (8%)
  Pallas kernels  14 us (7%)
  local copies, waits for them, and re-layouts  5.8 us (3%)
    all_to_all x1, blocking collectives, spread(): return lax.all_to_all(copies, axes, 0, 0, tiled=True)  22.8 us
    all_to_all x1, starting transfers between devices, spread(): return lax.all_to_all(copies, axes, 0, 0, tiled=True)  21.6 us
    ppermute x12, starting transfers between devices, shifted(): return lax.ppermute(x, 'y', [(i, (i + d) % 4) for i in range(4)])  21.2 us
    all_to_all x1, blocking collectives, per_device(): arrived = lax.all_to_all(lists, YXZ, 0, 0, tiled=True)  19.6 us
    all_to_all x1, waiting for transfers between devices, per_device(): branch = lax.all_to_all(branch.reshape(32, 8, 1024), XZ, 0, 0, tiled=True)  17.5 us
    ppermute x12, waiting for transfers between devices, shifted(): return lax.ppermute(x, 'y', [(i, (i + d) % 4) for i in range(4)])  10.3 us
    ppermute x1, waiting for transfers between devices, per_device(): code_rows = lax.ppermute(code_weight, QUERY_CORPUS, moves)  9.92 us
    all_to_all x1, starting transfers between devices, per_device(): branch = lax.all_to_all(branch.reshape(32, 8, 1024), XZ, 0, 0, tiled=True)  7.56 us
  transfers between devices with their start and end apart: 26, of which 19 were waited for; matrix products, arithmetic and copies ran while one was open for 1% of the time, Pallas kernels for 2%

profile of v1, /device:TPU:32, one launch (start us, length us, event | category | flops | bytes accessed | tf_op | source)
XLA Modules:
  0.0 184.5 jit_solution(7014851202807379104)
XLA Ops:
  8.5 1.1 collective-permute-done.1
  10.7 21.6 %all-to-all-start = ((bf16[32,64,128]{2,1,0:T(8,128)(2,1)}), bf16[32,64,128]{2,1,0:T(8,128)(2,1)S(1)}, u32[]{:S(2)}, u32[]{:S(2)}) async-start(bf16[32,64,128]{2,1,0:T(8,128)(2,1)} %broadcast_in_dim.26), calls=%async_computation | async-start | bytes 1048576 | tf_op jit(solution)/shard_map/all_to_all | solution.py:41
  32.3 3.4 %collective-permute-start.15 = (bf16[64,1024]{1,0:T(8,128)(2,1)S(1)}, bf16[64,1024]{1,0:T(8,128)(2,1)S(1)}, u32[]{:S(2)}, u32[]{:S(2)}) collective-permute-start(bf16[64,1024]{1,0:T(8,128)(2,1)S(1)} %copy-done.7), channel_id=1, source_target_pairs={{0,0},{1,2},{2,4},{3,6},{4,8},{5,10},{6,12},{7,14},{8,1},{9,3},{10... | collective-permute-start | bytes 393224 | tf_op jit(solution)/shard_map/ppermute | solution.py:370
  35.7 9.9 %collective-permute-done.15 = bf16[64,1024]{1,0:T(8,128)(2,1)S(1)} collective-permute-done((bf16[64,1024]{1,0:T(8,128)(2,1)S(1)}, bf16[64,1024]{1,0:T(8,128)(2,1)S(1)}, u32[]{:S(2)}, u32[]{:S(2)}) %collective-permute-start.15) | collective-permute-done | bytes 131104 | tf_op jit(solution)/shard_map/ppermute | solution.py:370
  46.5 4.9 %collective-permute-start.2 = (bf16[1024,224]{1,0:T(8,128)(2,1)S(1)}, bf16[1024,224]{1,0:T(8,128)(2,1)S(1)}, u32[]{:S(2)}, u32[]{:S(2)}) collective-permute-start(bf16[1024,224]{1,0:T(8,128)(2,1)S(1)} %copy.30.g0), channel_id=1, source_target_pairs={{0,1},{1,0},{2,3},{3,2},{4,5},{5,4},{6,7},{7,6},{8,9},{9,8},{10,11... | collective-permute-start | bytes 1376264 | tf_op jit(solution)/shard_map/ppermute | solution.py:32
  54.0 1.3 gate_up.1
  55.3 2.9 %collective-permute-start.4 = (bf16[64,1024]{1,0:T(8,128)(2,1)S(1)}, bf16[64,1024]{1,0:T(8,128)(2,1)S(1)}, u32[]{:S(2)}, u32[]{:S(2)}) collective-permute-start(bf16[64,1024]{1,0:T(8,128)(2,1)S(1)} %get-tuple-element.22), channel_id=1, source_target_pairs={{0,64},{64,128},{128,192},{192,0},{1,65},{65,129},{129,193},{193,1... | collective-permute-start | bytes 393224 | tf_op jit(solution)/shard_map/ppermute | solution.py:36
  58.2 4.2 %collective-permute-start.5 = (bf16[64,1024]{1,0:T(8,128)(2,1)S(1)}, bf16[64,1024]{1,0:T(8,128)(2,1)S(1)}, u32[]{:S(2)}, u32[]{:S(2)}) collective-permute-start(bf16[64,1024]{1,0:T(8,128)(2,1)S(1)} %get-tuple-element.23), channel_id=1, source_target_pairs={{0,128},{64,192},{128,0},{192,64},{1,129},{65,193},{129,1},{193,65... | collective-permute-start | bytes 393224 | tf_op jit(solution)/shard_map/ppermute | solution.py:36
  62.4 1.6 collective-permute-start.6
  65.0 4.0 %collective-permute-done.5.c = bf16[64,1024]{1,0:T(8,128)(2,1)S(1)} collective-permute-done((bf16[64,1024]{1,0:T(8,128)(2,1)S(1)}, bf16[64,1024]{1,0:T(8,128)(2,1)S(1)}, u32[]{:S(2)}, u32[]{:S(2)}) %collective-permute-start.5) | collective-permute-done | bytes 131104 | tf_op jit(solution)/shard_map/ppermute | solution.py:36
  69.1 1.3 collective-permute-start.7
  70.4 2.4 %collective-permute-start.8 = (bf16[64,512]{1,0:T(8,128)(2,1)S(1)}, bf16[64,512]{1,0:T(8,128)(2,1)S(1)}, u32[]{:S(2)}, u32[]{:S(2)}) collective-permute-start(bf16[64,512]{1,0:T(8,128)(2,1)S(1)} %hidden_units.1.a), channel_id=1, source_target_pairs={{0,128},{64,192},{128,0},{192,64},{1,129},{65,193},{129,1},{193,65... | collective-permute-start | bytes 196616 | tf_op jit(solution)/shard_map/ppermute | solution.py:36
  72.8 1.8 collective-permute-start.9
  75.1 1.1 collective-permute-done.8.c
  77.1 1.8 down.1
  78.8 7.6 %all-to-all-start.1 = ((bf16[32,8,1024]{2,1,0:T(8,128)(2,1)}), bf16[32,8,1024]{2,1,0:T(8,128)(2,1)S(1)}, u32[]{:S(2)}, u32[]{:S(2)}) async-start(bf16[32,8,1024]{2,1,0:T(8,128)(2,1)} %bitcast.8), calls=%async_computation.1 | async-start | bytes 1048576 | tf_op jit(solution)/shard_map/all_to_all | solution.py:377
  86.4 17.5 %all-to-all-done.1.parts = bf16[32,8,1024]{2,1,0:T(8,128)(2,1)S(1)} async-done(((bf16[32,8,1024]{2,1,0:T(8,128)(2,1)}), bf16[32,8,1024]{2,1,0:T(8,128)(2,1)S(1)}, u32[]{:S(2)}, u32[]{:S(2)}) %all-to-all-start.1) | async-done | bytes 524320 | tf_op jit(solution)/shard_map/all_to_all | solution.py:377
  104.2 2.6 %collective-permute-start.12 = (f32[8,128]{1,0:T(8,128)S(1)}, f32[8,128]{1,0:T(8,128)S(1)}, u32[]{:S(2)}, u32[]{:S(2)}) collective-permute-start(f32[8,128]{1,0:T(8,128)S(1)} %get-tuple-element.26.a), channel_id=1, source_target_pairs={{0,128},{64,192},{128,0},{192,64},{1,129},{65,193},{129,1},{193,65... | collective-permute-start | bytes 12296 | tf_op jit(solution)/shard_map/ppermute | solution.py:36
  107.7 1.2 constant_dynamic-slice_fusion
  111.3 1.1 collective-permute-done.14.b
  112.4 1.2 copy-done.1
  115.7 22.8 %all_to_all.20 = f32[128,4,128]{2,1,0:T(4,128)S(1)} all-to-all(f32[128,4,128]{2,1,0:T(4,128)S(1)} %broadcast_in_dim.28), channel_id=1, replica_groups=mesh['y'=4,'x'=4,'zh'=4,'zb'=2,'k'=2] {'y','x','zh','zb'}, dimensions={0} | all-to-all | bytes 524288 | tf_op jit(solution)/shard_map/all_to_all | solution.py:41
  138.9 1.2 collective-permute-done.17.refs_2_
  140.1 4.0 %scores.1 = (f32[8,128]{1,0:T(8,128)S(1)}, f32[8,128]{1,0:T(8,128)S(1)}) custom-call(s32[4]{0:T(128)S(1)} %pad_add_fusion.place.refs_0_, bf16[16,512]{1,0:T(8,128)(2,1)S(1)} %convert_element_type.17.refs_1_, bf16[16,512]{1,0:T(8,128)(2,1)S(1)} %collective-permute-done.17.refs_2_, bf16[512,1024]{1,0:T(8,128)(2,1)S(1)} %copy-done), custom_call_target="tpu_custom_call" | custom-call | tf_op jit(solution)/shard_map/scores/pallas_call | solution.py:255
  145.3 1.0 pair_lists.1
  146.3 2.1 %collective-permute-start.20 = (f32[2,128]{1,0:T(2,128)S(1)}, f32[2,128]{1,0:T(2,128)S(1)}, u32[]{:S(2)}, u32[]{:S(2)}) collective-permute-start(f32[2,128]{1,0:T(2,128)S(1)} %get-tuple-element.35), channel_id=1, source_target_pairs={{0,128},{64,192},{128,0},{192,64},{1,129},{65,193},{129,1},{193,65... | collective-permute-start | bytes 3080 | tf_op jit(solution)/shard_map/ppermute | solution.py:36
  148.4 1.5 collective-permute-start.21
  149.9 1.2 collective-permute-done.19.b
  152.0 1.6 four_lists.1
  153.6 19.6 %all_to_all.21 = f32[128,2,128]{2,1,0:T(2,128)S(1)} all-to-all(f32[128,2,128]{2,1,0:T(2,128)S(1)} %four_lists.1), channel_id=1, replica_groups=mesh['y'=4,'x'=4,'zh'=4,'zb'=2,'k'=2] {'y','x','zh','zb'}, dimensions={0} | all-to-all | bytes 262144 | tf_op jit(solution)/shard_map/all_to_all | solution.py:394
  173.2 2.6 %final_lists.1 = f32[8,128]{1,0:T(8,128)S(1)} custom-call(f32[256,128]{1,0:T(8,128)S(1)} %bitcast.24), custom_call_target="tpu_custom_call" | custom-call | tf_op jit(solution)/shard_map/final_lists/pallas_call | solution.py:329
  175.8 1.2 collective-permute-done.22
  (73 shorter events, 17.0 us)
Async XLA Ops:
  7.7 0.8 collective-permute-start
  8.4 1.3 collective-permute-start.1
  10.7 21.7 %copy-start.7 = (bf16[64,1024]{1,0:T(8,128)(2,1)S(1)}, bf16[64,1024]{1,0:T(8,128)(2,1)}, u32[]{:S(2)}) copy-start(bf16[64,1024]{1,0:T(8,128)(2,1)} %param.12) | copy-start | bytes 393220
  10.7 35.6 %copy-start.3 = (bf16[1024,224]{0,1:T(8,128)(2,1)S(1)}, bf16[1024,224]{0,1:T(8,128)(2,1)}, u32[]{:S(2)}) copy-start(bf16[1024,224]{0,1:T(8,128)(2,1)} %param.9) | copy-start | bytes 1376260
  10.7 43.3 %all-to-all-start = ((bf16[32,64,128]{2,1,0:T(8,128)(2,1)}), bf16[32,64,128]{2,1,0:T(8,128)(2,1)S(1)}, u32[]{:S(2)}, u32[]{:S(2)}) async-start(bf16[32,64,128]{2,1,0:T(8,128)(2,1)} %broadcast_in_dim.26), calls=%async_computation | async-start | bytes 1048576 | tf_op jit(solution)/shard_map/all_to_all | solution.py:41
  32.3 79.0 %all-gather.2.cloned.1.call-start = ((), (), s32[]{:S(2)}) async-start(), calls=%async_computation.4 | async-start | bytes 1179648 | tf_op jit(solution)/shard_map/all_gather | solution.py:371
  32.3 13.3 %collective-permute-start.15 = (bf16[64,1024]{1,0:T(8,128)(2,1)S(1)}, bf16[64,1024]{1,0:T(8,128)(2,1)S(1)}, u32[]{:S(2)}, u32[]{:S(2)}) collective-permute-start(bf16[64,1024]{1,0:T(8,128)(2,1)S(1)} %copy-done.7), channel_id=1, source_target_pairs={{0,0},{1,2},{2,4},{3,6},{4,8},{5,10},{6,12},{7,14},{8,1},{9,3},{10... | collective-permute-start | bytes 393224 | tf_op jit(solution)/shard_map/ppermute | solution.py:370
  46.3 5.1 %copy-start.4 = (bf16[1024,224]{0,1:T(8,128)(2,1)S(1)}, bf16[1024,224]{0,1:T(8,128)(2,1)}, u32[]{:S(2)}) copy-start(bf16[1024,224]{0,1:T(8,128)(2,1)} %param.10) | copy-start | bytes 1376260
  46.5 5.9 %copy-start.2 = (bf16[224,1024]{1,0:T(8,128)(2,1)S(1)}, bf16[224,1024]{1,0:T(8,128)(2,1)}, u32[]{:S(2)}) copy-start(bf16[224,1024]{1,0:T(8,128)(2,1)} %w0.1) | copy-start | bytes 1376260
  46.5 6.4 %collective-permute-start.2 = (bf16[1024,224]{1,0:T(8,128)(2,1)S(1)}, bf16[1024,224]{1,0:T(8,128)(2,1)S(1)}, u32[]{:S(2)}, u32[]{:S(2)}) collective-permute-start(bf16[1024,224]{1,0:T(8,128)(2,1)S(1)} %copy.30.g0), channel_id=1, source_target_pairs={{0,1},{1,0},{2,3},{3,2},{4,5},{5,4},{6,7},{7,6},{8,9},{9,8},{10,11... | collective-permute-start | bytes 1376264 | tf_op jit(solution)/shard_map/ppermute | solution.py:32
  51.6 2.3 %collective-permute-start.3 = (bf16[1024,224]{1,0:T(8,128)(2,1)S(1)}, bf16[1024,224]{1,0:T(8,128)(2,1)S(1)}, u32[]{:S(2)}, u32[]{:S(2)}) collective-permute-start(bf16[1024,224]{1,0:T(8,128)(2,1)S(1)} %copy.31.u0), channel_id=1, source_target_pairs={{0,1},{1,0},{2,3},{3,2},{4,5},{5,4},{6,7},{7,6},{8,9},{9,8},{10,11... | collective-permute-start | bytes 1376264 | tf_op jit(solution)/shard_map/ppermute | solution.py:32
  52.4 22.2 %collective-permute-start.10 = (bf16[224,1024]{1,0:T(8,128)(2,1)S(1)}, bf16[224,1024]{1,0:T(8,128)(2,1)S(1)}, u32[]{:S(2)}, u32[]{:S(2)}) collective-permute-start(bf16[224,1024]{1,0:T(8,128)(2,1)S(1)} %copy-done.2), channel_id=1, source_target_pairs={{0,1},{1,0},{2,3},{3,2},{4,5},{5,4},{6,7},{7,6},{8,9},{9,8},{10,11... | collective-permute-start | bytes 1376264 | tf_op jit(solution)/shard_map/ppermute | solution.py:32
  55.3 9.7 %collective-permute-start.4 = (bf16[64,1024]{1,0:T(8,128)(2,1)S(1)}, bf16[64,1024]{1,0:T(8,128)(2,1)S(1)}, u32[]{:S(2)}, u32[]{:S(2)}) collective-permute-start(bf16[64,1024]{1,0:T(8,128)(2,1)S(1)} %get-tuple-element.22), channel_id=1, source_target_pairs={{0,64},{64,128},{128,192},{192,0},{1,65},{65,129},{129,193},{193,1... | collective-permute-start | bytes 393224 | tf_op jit(solution)/shard_map/ppermute | solution.py:36
  58.2 10.8 %collective-permute-start.5 = (bf16[64,1024]{1,0:T(8,128)(2,1)S(1)}, bf16[64,1024]{1,0:T(8,128)(2,1)S(1)}, u32[]{:S(2)}, u32[]{:S(2)}) collective-permute-start(bf16[64,1024]{1,0:T(8,128)(2,1)S(1)} %get-tuple-element.23), channel_id=1, source_target_pairs={{0,128},{64,192},{128,0},{192,64},{1,129},{65,193},{129,1},{193,65... | collective-permute-start | bytes 393224 | tf_op jit(solution)/shard_map/ppermute | solution.py:36
  62.4 6.5 %collective-permute-start.6 = (bf16[64,1024]{1,0:T(8,128)(2,1)S(1)}, bf16[64,1024]{1,0:T(8,128)(2,1)S(1)}, u32[]{:S(2)}, u32[]{:S(2)}) collective-permute-start(bf16[64,1024]{1,0:T(8,128)(2,1)S(1)} %get-tuple-element.24), channel_id=1, source_target_pairs={{0,192},{64,0},{128,64},{192,128},{1,193},{65,1},{129,65},{193,129... | collective-permute-start | bytes 393224 | tf_op jit(solution)/shard_map/ppermute | solution.py:36
  69.1 6.0 %collective-permute-start.7 = (bf16[64,512]{1,0:T(8,128)(2,1)S(1)}, bf16[64,512]{1,0:T(8,128)(2,1)S(1)}, u32[]{:S(2)}, u32[]{:S(2)}) collective-permute-start(bf16[64,512]{1,0:T(8,128)(2,1)S(1)} %hidden_units.1.a), channel_id=1, source_target_pairs={{0,64},{64,128},{128,192},{192,0},{1,65},{65,129},{129,193},{193,1... | collective-permute-start | bytes 196616 | tf_op jit(solution)/shard_map/ppermute | solution.py:36
  70.4 5.8 %collective-permute-start.8 = (bf16[64,512]{1,0:T(8,128)(2,1)S(1)}, bf16[64,512]{1,0:T(8,128)(2,1)S(1)}, u32[]{:S(2)}, u32[]{:S(2)}) collective-permute-start(bf16[64,512]{1,0:T(8,128)(2,1)S(1)} %hidden_units.1.a), channel_id=1, source_target_pairs={{0,128},{64,192},{128,0},{192,64},{1,129},{65,193},{129,1},{193,65... | collective-permute-start | bytes 196616 | tf_op jit(solution)/shard_map/ppermute | solution.py:36
  72.8 4.3 %collective-permute-start.9 = (bf16[64,512]{1,0:T(8,128)(2,1)S(1)}, bf16[64,512]{1,0:T(8,128)(2,1)S(1)}, u32[]{:S(2)}, u32[]{:S(2)}) collective-permute-start(bf16[64,512]{1,0:T(8,128)(2,1)S(1)} %hidden_units.1.a), channel_id=1, source_target_pairs={{0,192},{64,0},{128,64},{192,128},{1,193},{65,1},{129,65},{193,129... | collective-permute-start | bytes 196616 | tf_op jit(solution)/shard_map/ppermute | solution.py:36
  78.8 25.1 %all-to-all-start.1 = ((bf16[32,8,1024]{2,1,0:T(8,128)(2,1)}), bf16[32,8,1024]{2,1,0:T(8,128)(2,1)S(1)}, u32[]{:S(2)}, u32[]{:S(2)}) async-start(bf16[32,8,1024]{2,1,0:T(8,128)(2,1)} %bitcast.8), calls=%async_computation.1 | async-start | bytes 1048576 | tf_op jit(solution)/shard_map/all_to_all | solution.py:377
  104.1 5.4 %collective-permute-start.11 = (f32[8,128]{1,0:T(8,128)S(1)}, f32[8,128]{1,0:T(8,128)S(1)}, u32[]{:S(2)}, u32[]{:S(2)}) collective-permute-start(f32[8,128]{1,0:T(8,128)S(1)} %get-tuple-element.26.a), channel_id=1, source_target_pairs={{0,64},{64,128},{128,192},{192,0},{1,65},{65,129},{129,193},{193,1... | collective-permute-start | bytes 12296 | tf_op jit(solution)/shard_map/ppermute | solution.py:36
  104.2 5.4 %collective-permute-start.12 = (f32[8,128]{1,0:T(8,128)S(1)}, f32[8,128]{1,0:T(8,128)S(1)}, u32[]{:S(2)}, u32[]{:S(2)}) collective-permute-start(f32[8,128]{1,0:T(8,128)S(1)} %get-tuple-element.26.a), channel_id=1, source_target_pairs={{0,128},{64,192},{128,0},{192,64},{1,129},{65,193},{129,1},{193,65... | collective-permute-start | bytes 12296 | tf_op jit(solution)/shard_map/ppermute | solution.py:36
  106.7 3.6 %collective-permute-start.13 = (f32[8,128]{1,0:T(8,128)S(1)}, f32[8,128]{1,0:T(8,128)S(1)}, u32[]{:S(2)}, u32[]{:S(2)}) collective-permute-start(f32[8,128]{1,0:T(8,128)S(1)} %get-tuple-element.26.a), channel_id=1, source_target_pairs={{0,192},{64,0},{128,64},{192,128},{1,193},{65,1},{129,65},{193,129... | collective-permute-start | bytes 12296 | tf_op jit(solution)/shard_map/ppermute | solution.py:36
  111.0 1.4 collective-permute-start.14
  112.4 1.2 copy-start.1
  114.4 25.7 %copy-start = (bf16[512,1024]{1,0:T(8,128)(2,1)S(1)}, bf16[512,1024]{1,0:T(8,128)(2,1)}, u32[]{:S(2)}) copy-start(bf16[512,1024]{1,0:T(8,128)(2,1)} %refs_3_.1) | copy-start | bytes 3145732
  114.4 1.2 collective-permute-start.16
  138.8 1.3 collective-permute-start.17
  144.1 1.2 collective-permute-start.18
  146.3 4.8 %collective-permute-start.19 = (f32[2,128]{1,0:T(2,128)S(1)}, f32[2,128]{1,0:T(2,128)S(1)}, u32[]{:S(2)}, u32[]{:S(2)}) collective-permute-start(f32[2,128]{1,0:T(2,128)S(1)} %get-tuple-element.34), channel_id=1, source_target_pairs={{0,64},{64,128},{128,192},{192,0},{1,65},{65,129},{129,193},{193,1... | collective-permute-start | bytes 3080 | tf_op jit(solution)/shard_map/ppermute | solution.py:36
  146.3 5.1 %collective-permute-start.20 = (f32[2,128]{1,0:T(2,128)S(1)}, f32[2,128]{1,0:T(2,128)S(1)}, u32[]{:S(2)}, u32[]{:S(2)}) collective-permute-start(f32[2,128]{1,0:T(2,128)S(1)} %get-tuple-element.35), channel_id=1, source_target_pairs={{0,128},{64,192},{128,0},{192,64},{1,129},{65,193},{129,1},{193,65... | collective-permute-start | bytes 3080 | tf_op jit(solution)/shard_map/ppermute | solution.py:36
  148.4 3.6 %collective-permute-start.21 = (f32[2,128]{1,0:T(2,128)S(1)}, f32[2,128]{1,0:T(2,128)S(1)}, u32[]{:S(2)}, u32[]{:S(2)}) collective-permute-start(f32[2,128]{1,0:T(2,128)S(1)} %get-tuple-element.36), channel_id=1, source_target_pairs={{0,192},{64,0},{128,64},{192,128},{1,193},{65,1},{129,65},{193,129... | collective-permute-start | bytes 3080 | tf_op jit(solution)/shard_map/ppermute | solution.py:36
  175.8 1.2 collective-permute-start.22
  (3 other events, 2.7 us)
Sparse Core Ops, SparseCore 0:
  46.4 46.1 all-gather.1

commit v2 on v1

--- a/solution.py
+++ b/solution.py
@@ -60,7 +60,9 @@
     col = lanes((256, 256))
     wide[...] = jnp.zeros((256, 256), F32)
     for b, w in enumerate((g0, u0, g1, u1)):
-        wide[:, 0:224] = jnp.dot(left, w[...], preferred_element_type=F32)
+        wide[:, 0:224] = lax.dot_general(
+            left, w[...], (((1,), (1,)), ((), ())), preferred_element_type=F32
+        )
         block = wide[...]
         if b == 0:
             block = jnp.where(col == 224, top, block)
@@ -149,28 +151,35 @@
     )(parts, h)
 
 
-def pool_kernel(place, length, res, a, b, c, d, keep, send):
-    k, first = place[1], place[2]
+def pool_kernel(place, counts, res, a, b, c, d, keep, send):
+    k, first, row = place[1], place[2], place[4]
     sq = (a[...] + b[...] + c[...] + d[...])[:, 0:1]
-    rows = lax.broadcasted_iota(jnp.int32, (8, 1), 0) + first
-    count = length[0]
-    weight = jnp.where(rows < count, lax.rsqrt(sq / D + EPS), 0.0)
-    pooled = jnp.sum(res[...] * weight, axis=0, keepdims=True) / count.astype(F32)
-    low, high = pooled[:, 0:512], pooled[:, 512:1024]
-    keep[...] = jnp.where(k == 0, low, high)
-    send[...] = jnp.where(k == 0, high, low)
-
-
-def pool(place, length, res, sqs):
+    slots = lax.broadcasted_iota(jnp.int32, (8, 1), 0) + first
+    held = counts[...].astype(F32)
+    held = jnp.where(lax.broadcasted_iota(jnp.int32, (16, 64), 0) == row, held, 0.0)
+    count = jnp.max(jnp.max(held, axis=1, keepdims=True), axis=0, keepdims=True)
+    weight = jnp.where(slots.astype(F32) < count, lax.rsqrt(sq / D + EPS), 0.0)
+    pooled = jnp.sum(res[...] * weight, axis=0, keepdims=True) / count
+    low = lanes((1, 128)) < 64
+    for t in range(4):
+        one = pooled[:, t * 256 : t * 256 + 128]
+        two = pooled[:, t * 256 + 128 : t * 256 + 256]
+        even = jnp.where(low, one, pltpu.roll(two, 64, 1))
+        odd = jnp.where(low, pltpu.roll(one, 64, 1), two)
+        keep[:, t * 128 : t * 128 + 128] = jnp.where(k == 0, even, odd)
+        send[:, t * 128 : t * 128 + 128] = jnp.where(k == 0, odd, even)
+
+
+def pool(place, counts, res, sqs):
     half = shape((1, 512), F32)
     return pl.pallas_call(
         pool_kernel,
         out_shape=(half, half),
-        in_specs=[SMEM] * 2 + [VMEM] * 5,
+        in_specs=[SMEM] + [VMEM] * 6,
         out_specs=(VMEM,) * 2,
         compiler_params=PARAMS,
         name="pool",
-    )(place, length, res, *sqs)
+    )(place, counts, res, *sqs)
 
 
 def code_kernel(place, a, b, w, keep, send):
@@ -226,7 +235,7 @@
     return lax.broadcasted_iota(jnp.int32, like, 0)
 
 
-def score_kernel(place, mine, theirs, docs, keep, send, *, scale):
+def score_kernel(place, mine, theirs, docs, lists, *, scale):
     k = place[1]
     own, peer = mine[...], theirs[...]
     low = jnp.where(k == 0, own, peer)
@@ -240,23 +249,18 @@
     x = jnp.maximum(x[0:32], x[32:64])
     x = bitonic_merge(x, rows_of((32, 128)) < 16)
     x = jnp.maximum(x[0:16], x[16:32])
-    kept = (rows_of((16, 128)) // 8) == k
-    x = bitonic_merge(x, kept)
-    keep[...] = jnp.where(k == 0, x[0:8], x[8:16])
-    send[...] = jnp.where(k == 0, x[8:16], x[0:8])
+    lists[...] = bitonic_merge(x, rows_of((16, 128)) * 0 + k == 0)
 
 
 def local_lists(place, mine, theirs, docs):
-    half = shape((8, 128), F32)
-
     def body(*refs):
         score_kernel(*refs, scale=1.0 / math.sqrt(docs.shape[1]))
 
     return pl.pallas_call(
         body,
-        out_shape=(half, half),
+        out_shape=shape((16, 128), F32),
         in_specs=[SMEM] + [VMEM] * 3,
-        out_specs=(VMEM,) * 2,
+        out_specs=VMEM,
         compiler_params=PARAMS,
         name="scores",
     )(place, mine, theirs, docs)
@@ -265,48 +269,42 @@
 def pair_kernel(place, a, b, o0, o1, o2, o3, held):
     y = place[0]
     x = jnp.maximum(a[...], b[...])
-    turn = (rows_of((8, 128)) // 2 - y + 4) % 4
+    turn = (rows_of((16, 128)) // 4 - y + 4) % 4
     held[...] = bitonic_merge(x, turn % 2 == 0)
     for d, o in enumerate((o0, o1, o2, o3)):
-        q = (y + d) % 4
-        for r in range(2):
-            o[r : r + 1, :] = held[pl.ds(q * 2 + r, 1), :]
+        o[...] = held[pl.ds(pl.multiple_of(((y + d) % 4) * 4, 4), 4), :]
 
 
 def pair_lists(place, a, b):
-    two = shape((2, 128), F32)
+    four = shape((4, 128), F32)
     return pl.pallas_call(
         pair_kernel,
-        out_shape=(two,) * 4,
+        out_shape=(four,) * 4,
         in_specs=[SMEM] + [VMEM] * 2,
         out_specs=(VMEM,) * 4,
-        scratch_shapes=[pltpu.VMEM((8, 128), F32)],
+        scratch_shapes=[pltpu.VMEM((16, 128), F32)],
         compiler_params=PARAMS,
         name="pair_lists",
     )(place, a, b)
 
 
-def four_kernel(place, a, b, c, d, out, held):
+def four_kernel(place, a, b, c, d, out):
     odd = place[3]
-    held[0:2] = jnp.maximum(a[...], b[...])
-    held[2:4] = jnp.maximum(c[...], d[...])
-    held[4:8] = jnp.zeros((4, 128), F32)
-    x = bitonic_merge(held[...], rows_of((8, 128)) < 2)
-    held[...] = x
-    held[0:2] = jnp.maximum(held[0:2], held[2:4])
-    x = bitonic_merge(held[...], (rows_of((8, 128)) * 0 + odd) == 0)
-    held[...] = x
-    for p in range(128):
-        out[p] = held[0:2]
+    x = jnp.concatenate(
+        [jnp.maximum(a[...], b[...]), jnp.maximum(c[...], d[...])], axis=0
+    )
+    x = bitonic_merge(x, rows_of((8, 128)) < 4)
+    x = jnp.maximum(x, pltpu.roll(x, 4, 0))
+    x = bitonic_merge(x, (rows_of((8, 128)) * 0 + odd) == 0)
+    out[...] = jnp.broadcast_to(x[0:4][None], (128, 4, 128))
 
 
 def four_lists(place, lists):
     return pl.pallas_call(
         four_kernel,
-        out_shape=shape((128, 2, 128), F32),
+        out_shape=shape((128, 4, 128), F32),
         in_specs=[SMEM] + [VMEM] * 4,
         out_specs=VMEM,
-        scratch_shapes=[pltpu.VMEM((8, 128), F32)],
         compiler_params=PARAMS,
         name="four_lists",
     )(place, *lists)
@@ -314,21 +312,21 @@
 
 def final_kernel(x_ref, out):
     x = x_ref[...]
-    lists = 32
-    while lists > 1:
-        x = x.reshape(lists // 2, 2, 8, 128)
-        x = jnp.maximum(x[:, 0], x[:, 1])
-        lists //= 2
-        x = x.reshape(lists * 8, 128)
-        falling = (rows_of(x.shape) // 8) % 2 == 0
-        x = bitonic_merge(x, falling)
-    out[...] = x
+    for groups in (32, 16, 8, 4):
+        x = x.reshape(groups, 2, 8, 128)
+        x = jnp.maximum(x[:, 0], x[:, 1]).reshape(groups * 8, 128)
+        row = rows_of(x.shape)
+        x = bitonic_merge(x, row % 8 < 4 if groups == 4 else (row // 8) % 2 == 0)
+    x = jnp.maximum(x, pltpu.roll(x, 4, 0))
+    x = bitonic_merge(x, rows_of(x.shape) >= 0)
+    for y in range(4):
+        out[y * 4 : y * 4 + 4, :] = x[y * 8 + 4 : y * 8 + 8, 0:TOPK]
 
 
 def final_lists(x):
     return pl.pallas_call(
         final_kernel,
-        out_shape=shape((8, 128), F32),
+        out_shape=shape((16, TOPK), F32),
         in_specs=[VMEM],
         out_specs=VMEM,
         compiler_params=PARAMS,
@@ -338,7 +336,7 @@
 
 def per_device(hidden_in, lengths, gate_weight, up_weight, down_weight, code_weight, corpus_codes):
     y, x, zh, zb, k = (lax.axis_index(a) for a in QUERY_CORPUS)
-    place = jnp.stack([y, k, 16 * k + 8 * zb, zb]).astype(jnp.int32)
+    place = jnp.stack([y, k, 16 * k + 8 * zb, zh % 2, 4 * zh]).astype(jnp.int32)
 
     halves = hidden_in.reshape(4, 2, 16, 64)
     first, second = halves[:, 0].reshape(64, 64), halves[:, 1].reshape(64, 64)
@@ -350,27 +348,22 @@
     crossed = [(s * 2 + c, t * 2 + 1 - c) for s, t in swap for c in range(2)]
     own = lax.ppermute(own, ("y", "x", "k"), straight)
     other = lax.ppermute(other, ("y", "x", "k"), crossed)
-    length = lax.dynamic_slice(own[:, 0], (64 + 4 * zh,), (1,)).astype(jnp.int32)
-    own = own[:64]
+    counts, own = own[64:], own[:64]
     block = jnp.where(
         k == 0, jnp.concatenate([own, other], axis=1), jnp.concatenate([other, own], axis=1)
     )
+    gate_rows, up_rows = gate_weight.T, up_weight.T
+    gate_peer, up_peer, down_peer = (to_peer(w) for w in (gate_rows, up_rows, down_weight))
+    block, gate_peer, up_peer, down_peer = lax.optimization_barrier(
+        (block, gate_peer, up_peer, down_peer)
+    )
     gathered = spread(block, XZ, 32)
 
-    gate_peer, up_peer, down_peer = (to_peer(w) for w in (gate_weight, up_weight, down_weight))
-
-    moves = []
-    for i in range(4):
-        for j in range(4):
-            for z in range(8):
-                for c in range(2):
-                    source = ((i * 4 + j) * 8 + z) * 2 + c
-                    target = ((j * 4 + i) * 8 + (z % 4) * 2 + c) * 2 + z // 4
-                    moves.append((source, target))
-    code_rows = lax.ppermute(code_weight, QUERY_CORPUS, moves)
+    code_rows = lax.ppermute(code_weight, ("y", "x"), swap)
+    code_rows, gathered = lax.optimization_barrier((code_rows, gathered))
     code_rows = lax.all_gather(code_rows, Z, axis=0, tiled=True)
 
-    parts = gate_up(place, gathered, gate_weight, up_weight, gate_peer, up_peer)
+    parts = gate_up(place, gathered, gate_rows, up_rows, gate_peer, up_peer)
     units = hidden_of(parts[0], *(shifted(parts[d], d) for d in (1, 2, 3)))
     groups = (units, *(shifted(units, d) for d in (1, 2, 3)))
     branch = down(place, groups, down_weight, down_peer)
@@ -381,24 +374,18 @@
     here = jnp.moveaxis(here, 0, 1).reshape(8, 1024)
     res, sq = residual_of(branch, here)
     sqs = (sq, *(shifted(sq, d) for d in (1, 2, 3)))
-    keep, send = pool(place, length, res, sqs)
+    keep, send = pool(place, counts, res, sqs)
     keep, send = code_part(place, keep, to_peer(send), code_rows)
     part = (keep + to_peer(send)).reshape(4, 128)
     codes = spread(part, YXZ, 128).reshape(4, 4, 4, 2, 512).sum(axis=(0, 3))
     codes = codes.reshape(16, 512).astype(BF16)
 
-    keep, send = local_lists(place, codes, to_peer(codes), corpus_codes)
-    lists = pair_lists(place, keep, to_peer(send))
+    lists = local_lists(place, codes, to_peer(codes), corpus_codes)
+    lists = pair_lists(place, lists, to_peer(lists))
     lists = (lists[0], *(shifted(lists[d], d) for d in (1, 2, 3)))
     lists = four_lists(place, lists)
     arrived = lax.all_to_all(lists, YXZ, 0, 0, tiled=True)
-    arrived = jnp.moveaxis(arrived.reshape(4, 32, 2, 128), 0, 1).reshape(256, 128)
-    best = final_lists(arrived)
-    peer = to_peer(best)
-    best = jnp.where(
-        k == 0, jnp.concatenate([best, peer], axis=0), jnp.concatenate([peer, best], axis=0)
-    )
-    return best[:, :TOPK]
+    return final_lists(arrived.reshape(512, 128))
 
 
 def solution(mesh):

time: 188 us -> 180 us (0.957); the launches traced: 184 us -> 180 us
  starting transfers between devices: 61.2 us -> 48.8 us
  waiting for transfers between devices: 45.8 us -> 54.6 us
    all_to_all x1, waiting for transfers between devices: 0.01 us -> 17.3 us  [spread(): return lax.all_to_all(copies, axes, 0, 0, tiled=True)]
    ppermute x1, waiting for transfers between devices: 9.92 us -> 0.01 us  [per_device(): code_rows = lax.ppermute(code_weight, ('y', 'x'), swap)]
    ppermute x12, starting transfers between devices: 21.2 us -> 15.3 us  [shifted(): return lax.ppermute(x, 'y', [(i, (i + d) % 4) for i in range(4)])]
    ppermute x12, waiting for transfers between devices: 10.3 us -> 15.8 us  [shifted(): return lax.ppermute(x, 'y', [(i, (i + d) % 4) for i in range(4)])]
    ppermute x8 -> x7, starting transfers between devices: 6.63 us -> 1.38 us  [to_peer(): return lax.ppermute(x, 'k', [(0, 1), (1, 0)])]
    ppermute x1, starting transfers between devices: 3.37 us -> 0.67 us  [per_device(): code_rows = lax.ppermute(code_weight, ('y', 'x'), swap)]
    ppermute x8 -> x7, waiting for transfers between devices: 6.86 us -> 4.31 us  [to_peer(): return lax.ppermute(x, 'k', [(0, 1), (1, 0)])]
  transfers between devices with their start and end apart: 26 -> 25, of which waited for: 19 -> 17; matrix products, arithmetic and copies ran while one was open for 1% -> 1% of each run, Pallas kernels for 2% -> 2%
where the time goes in v2:
time: 180 us
  waiting for transfers between devices  54.6 us (30%)
  starting transfers between devices  48.8 us (27%)
  blocking collectives  42.9 us (24%)
  Pallas kernels  15 us (8%)
  between operations  13.6 us (8%)
  local copies, waits for them, and re-layouts  4.22 us (2%)
    all_to_all x1, blocking collectives, spread(): return lax.all_to_all(copies, axes, 0, 0, tiled=True)  21.9 us
    all_to_all x1, starting transfers between devices, spread(): return lax.all_to_all(copies, axes, 0, 0, tiled=True)  21.4 us
    all_to_all x1, blocking collectives, per_device(): arrived = lax.all_to_all(lists, YXZ, 0, 0, tiled=True)  21 us
    all_to_all x1, waiting for transfers between devices, spread(): return lax.all_to_all(copies, axes, 0, 0, tiled=True)  17.3 us
    all_to_all x1, waiting for transfers between devices, per_device(): branch = lax.all_to_all(branch.reshape(32, 8, 1024), XZ, 0, 0, tiled=True)  16.3 us
    ppermute x12, waiting for transfers between devices, shifted(): return lax.ppermute(x, 'y', [(i, (i + d) % 4) for i in range(4)])  15.8 us
    ppermute x12, starting transfers between devices, shifted(): return lax.ppermute(x, 'y', [(i, (i + d) % 4) for i in range(4)])  15.3 us
    all_to_all x1, starting transfers between devices, per_device(): branch = lax.all_to_all(branch.reshape(32, 8, 1024), XZ, 0, 0, tiled=True)  8.78 us
  transfers between devices with their start and end apart: 25, of which 17 were waited for; matrix products, arithmetic and copies ran while one was open for 1% of the time, Pallas kernels for 2%

profile of v2, /device:TPU:32, one launch (start us, length us, event | category | flops | bytes accessed | tf_op | source)
XLA Modules:
  0.0 179.5 jit_solution(654935606800544945)
XLA Ops:
  11.1 0.9 broadcast_in_dim.26
  12.0 21.4 %all-to-all-start = ((bf16[32,64,128]{2,1,0:T(8,128)(2,1)}), bf16[32,64,128]{2,1,0:T(8,128)(2,1)S(1)}, u32[]{:S(2)}, u32[]{:S(2)}) async-start(bf16[32,64,128]{2,1,0:T(8,128)(2,1)} %broadcast_in_dim.26), calls=%async_computation | async-start | bytes 1048576 | tf_op jit(solution)/shard_map/all_to_all | solution.py:41
  34.2 17.3 %all-to-all-done.h = bf16[32,64,128]{2,1,0:T(8,128)(2,1)S(1)} async-done(((bf16[32,64,128]{2,1,0:T(8,128)(2,1)}), bf16[32,64,128]{2,1,0:T(8,128)(2,1)S(1)}, u32[]{:S(2)}, u32[]{:S(2)}) %all-to-all-start) | async-done | bytes 524320 | tf_op jit(solution)/shard_map/all_to_all | solution.py:41
  51.6 1.4 gate_up.1
  53.0 1.4 collective-permute-start.6
  54.4 1.3 collective-permute-start.7
  55.7 1.5 collective-permute-start.8
  57.1 3.9 %collective-permute-done.6.b = bf16[64,1024]{1,0:T(8,128)(2,1)S(1)} collective-permute-done((bf16[64,1024]{1,0:T(8,128)(2,1)S(1)}, bf16[64,1024]{1,0:T(8,128)(2,1)S(1)}, u32[]{:S(2)}, u32[]{:S(2)}) %collective-permute-start.6) | collective-permute-done | bytes 131104 | tf_op jit(solution)/shard_map/ppermute | solution.py:36
  61.9 2.5 %collective-permute-start.11 = (bf16[64,512]{1,0:T(8,128)(2,1)S(1)}, bf16[64,512]{1,0:T(8,128)(2,1)S(1)}, u32[]{:S(2)}, u32[]{:S(2)}) collective-permute-start(bf16[64,512]{1,0:T(8,128)(2,1)S(1)} %hidden_units.1.a), channel_id=1, source_target_pairs={{0,192},{64,0},{128,64},{192,128},{1,193},{65,1},{129,65},{193,129... | collective-permute-start | bytes 196616 | tf_op jit(solution)/shard_map/ppermute | solution.py:36
  65.4 1.6 collective-permute-done.11.d
  66.9 3.4 %collective-permute-done.10.c = bf16[64,512]{1,0:T(8,128)(2,1)S(1)} collective-permute-done((bf16[64,512]{1,0:T(8,128)(2,1)S(1)}, bf16[64,512]{1,0:T(8,128)(2,1)S(1)}, u32[]{:S(2)}, u32[]{:S(2)}) %collective-permute-start.10) | collective-permute-done | bytes 65568 | tf_op jit(solution)/shard_map/ppermute | solution.py:36
  70.8 1.8 down.1
  72.6 8.8 %all-to-all-start.1 = ((bf16[32,8,1024]{2,1,0:T(8,128)(2,1)}), bf16[32,8,1024]{2,1,0:T(8,128)(2,1)S(1)}, u32[]{:S(2)}, u32[]{:S(2)}) async-start(bf16[32,8,1024]{2,1,0:T(8,128)(2,1)} %bitcast.10), calls=%async_computation.1 | async-start | bytes 1048576 | tf_op jit(solution)/shard_map/all_to_all | solution.py:370
  81.4 16.3 %all-to-all-done.1.parts = bf16[32,8,1024]{2,1,0:T(8,128)(2,1)S(1)} async-done(((bf16[32,8,1024]{2,1,0:T(8,128)(2,1)}), bf16[32,8,1024]{2,1,0:T(8,128)(2,1)S(1)}, u32[]{:S(2)}, u32[]{:S(2)}) %all-to-all-start.1) | async-done | bytes 524320 | tf_op jit(solution)/shard_map/all_to_all | solution.py:370
  97.9 1.9 %collective-permute-start.14 = (f32[8,128]{1,0:T(8,128)S(1)}, f32[8,128]{1,0:T(8,128)S(1)}, u32[]{:S(2)}, u32[]{:S(2)}) collective-permute-start(f32[8,128]{1,0:T(8,128)S(1)} %get-tuple-element.35.a), channel_id=1, source_target_pairs={{0,192},{64,0},{128,64},{192,128},{1,193},{65,1},{129,65},{193,129... | collective-permute-start | bytes 12296 | tf_op jit(solution)/shard_map/ppermute | solution.py:36
  99.8 0.9 collective-permute-start.13
  100.8 1.1 collective-permute-start.12
  101.9 3.1 %collective-permute-done.13.c = f32[8,128]{1,0:T(8,128)S(1)} collective-permute-done((f32[8,128]{1,0:T(8,128)S(1)}, f32[8,128]{1,0:T(8,128)S(1)}, u32[]{:S(2)}, u32[]{:S(2)}) %collective-permute-start.13) | collective-permute-done | bytes 4128 | tf_op jit(solution)/shard_map/ppermute | solution.py:36
  106.5 1.1 collective-permute-done.15.b
  107.6 1.2 copy-done.1
  110.1 1.0 collective-permute-done.16
  111.1 21.9 %all_to_all.20 = f32[128,4,128]{2,1,0:T(4,128)S(1)} all-to-all(f32[128,4,128]{2,1,0:T(4,128)S(1)} %broadcast_in_dim.28), channel_id=1, replica_groups=mesh['y'=4,'x'=4,'zh'=4,'zb'=2,'k'=2] {'y','x','zh','zb'}, dimensions={0} | all-to-all | bytes 524288 | tf_op jit(solution)/shard_map/all_to_all | solution.py:41
  133.5 1.2 collective-permute-done.17.refs_2_
  134.7 3.9 %scores.1.a = f32[16,128]{1,0:T(8,128)S(1)} custom-call(s32[5]{0:T(128)S(1)} %stack.23.place.refs_0_, bf16[16,512]{1,0:T(8,128)(2,1)S(1)} %convert_element_type.10.refs_1_, bf16[16,512]{1,0:T(8,128)(2,1)S(1)} %collective-permute-done.17.refs_2_, bf16[512,1024]{1,0:T(8,128)(2,1)S(1)} %copy-done), custom_call_target="tpu_custom_call" | custom-call | tf_op jit(solution)/shard_map/scores/pallas_call | solution.py:259
  138.9 1.0 collective-permute-done.18.b
  139.9 1.0 pair_lists.1
  141.0 2.1 %collective-permute-start.20 = (f32[4,128]{1,0:T(4,128)S(1)}, f32[4,128]{1,0:T(4,128)S(1)}, u32[]{:S(2)}, u32[]{:S(2)}) collective-permute-start(f32[4,128]{1,0:T(4,128)S(1)} %get-tuple-element.43), channel_id=1, source_target_pairs={{0,128},{64,192},{128,0},{192,64},{1,129},{65,193},{129,1},{193,65... | collective-permute-start | bytes 6152 | tf_op jit(solution)/shard_map/ppermute | solution.py:36
  143.1 1.5 collective-permute-start.21
  144.5 1.2 collective-permute-done.19.b
  146.7 1.6 four_lists.1
  148.2 21.0 %all_to_all.21 = f32[128,4,128]{2,1,0:T(4,128)S(1)} all-to-all(f32[128,4,128]{2,1,0:T(4,128)S(1)} %four_lists.1), channel_id=1, replica_groups=mesh['y'=4,'x'=4,'zh'=4,'zb'=2,'k'=2] {'y','x','zh','zb'}, dimensions={0} | all-to-all | bytes 524288 | tf_op jit(solution)/shard_map/all_to_all | solution.py:387
  169.2 3.5 %final_lists.1 = f32[16,100]{1,0:T(8,128)} custom-call(f32[512,128]{1,0:T(8,128)S(1)} %bitcast.21), custom_call_target="tpu_custom_call" | custom-call | tf_op jit(solution)/shard_map/final_lists/pallas_call | solution.py:327
  (65 shorter events, 12.3 us)
Async XLA Ops:
  6.5 4.5 %collective-permute-start.3 = (bf16[224,1024]{1,0:T(8,128)(2,1)}, bf16[224,1024]{1,0:T(8,128)(2,1)S(1)}, u32[]{:S(2)}, u32[]{:S(2)}) collective-permute-start(bf16[224,1024]{1,0:T(8,128)(2,1)} %bitcast.22), channel_id=1, source_target_pairs={{0,1},{1,0},{2,3},{3,2},{4,5},{5,4},{6,7},{7,6},{8,9},{9,8},{10,11... | collective-permute-start | bytes 1376264 | tf_op jit(solution)/shard_map/ppermute | solution.py:32
  6.5 4.5 %collective-permute-start.4 = (bf16[224,1024]{1,0:T(8,128)(2,1)}, bf16[224,1024]{1,0:T(8,128)(2,1)S(1)}, u32[]{:S(2)}, u32[]{:S(2)}) collective-permute-start(bf16[224,1024]{1,0:T(8,128)(2,1)} %bitcast.24), channel_id=1, source_target_pairs={{0,1},{1,0},{2,3},{3,2},{4,5},{5,4},{6,7},{7,6},{8,9},{9,8},{10,11... | collective-permute-start | bytes 1376264 | tf_op jit(solution)/shard_map/ppermute | solution.py:32
  7.0 4.0 %collective-permute-start.5 = (bf16[224,1024]{1,0:T(8,128)(2,1)}, bf16[224,1024]{1,0:T(8,128)(2,1)S(1)}, u32[]{:S(2)}, u32[]{:S(2)}) collective-permute-start(bf16[224,1024]{1,0:T(8,128)(2,1)} %w0.1), channel_id=1, source_target_pairs={{0,1},{1,0},{2,3},{3,2},{4,5},{5,4},{6,7},{7,6},{8,9},{9,8},{10,11... | collective-permute-start | bytes 1376264 | tf_op jit(solution)/shard_map/ppermute | solution.py:32
  8.9 1.3 collective-permute-start
  9.5 1.4 collective-permute-start.2
  12.0 21.5 %copy-start.6 = (bf16[64,1024]{1,0:T(8,128)(2,1)S(1)}, bf16[64,1024]{1,0:T(8,128)(2,1)}, u32[]{:S(2)}) copy-start(bf16[64,1024]{1,0:T(8,128)(2,1)} %param.12) | copy-start | bytes 393220
  12.0 39.6 %copy-start.2 = (bf16[1024,224]{0,1:T(8,128)(2,1)S(1)}, bf16[1024,224]{0,1:T(8,128)(2,1)}, u32[]{:S(2)}) copy-start(bf16[1024,224]{0,1:T(8,128)(2,1)} %param.9) | copy-start | bytes 1376260
  12.0 39.6 %copy-start.3 = (bf16[1024,224]{0,1:T(8,128)(2,1)S(1)}, bf16[1024,224]{0,1:T(8,128)(2,1)}, u32[]{:S(2)}) copy-start(bf16[1024,224]{0,1:T(8,128)(2,1)} %param.10) | copy-start | bytes 1376260
  12.0 39.5 %all-to-all-start = ((bf16[32,64,128]{2,1,0:T(8,128)(2,1)}), bf16[32,64,128]{2,1,0:T(8,128)(2,1)S(1)}, u32[]{:S(2)}, u32[]{:S(2)}) async-start(bf16[32,64,128]{2,1,0:T(8,128)(2,1)} %broadcast_in_dim.26), calls=%async_computation | async-start | bytes 1048576 | tf_op jit(solution)/shard_map/all_to_all | solution.py:41
  33.4 74.2 %all-gather.2.cloned.1.call-start = ((), (), s32[]{:S(2)}) async-start(), calls=%async_computation.4 | async-start | bytes 1179648 | tf_op jit(solution)/shard_map/all_gather | solution.py:364
  33.5 0.7 collective-permute-start.1
  34.2 17.3 %copy-start.5 = (bf16[64,1024]{1,0:T(8,128)(2,1)}, bf16[64,1024]{1,0:T(8,128)(2,1)S(1)}, u32[]{:S(2)}) copy-start(bf16[64,1024]{1,0:T(8,128)(2,1)S(1)} %collective-permute-done.1) | copy-start | bytes 393220
  53.0 17.9 %copy-start.4 = (bf16[224,1024]{1,0:T(8,128)(2,1)S(1)}, bf16[224,1024]{1,0:T(8,128)(2,1)}, u32[]{:S(2)}) copy-start(bf16[224,1024]{1,0:T(8,128)(2,1)} %w0.1) | copy-start | bytes 1376260
  53.0 8.0 %collective-permute-start.6 = (bf16[64,1024]{1,0:T(8,128)(2,1)S(1)}, bf16[64,1024]{1,0:T(8,128)(2,1)S(1)}, u32[]{:S(2)}, u32[]{:S(2)}) collective-permute-start(bf16[64,1024]{1,0:T(8,128)(2,1)S(1)} %get-tuple-element.30), channel_id=1, source_target_pairs={{0,64},{64,128},{128,192},{192,0},{1,65},{65,129},{129,193},{193,1... | collective-permute-start | bytes 393224 | tf_op jit(solution)/shard_map/ppermute | solution.py:36
  54.4 6.6 %collective-permute-start.7 = (bf16[64,1024]{1,0:T(8,128)(2,1)S(1)}, bf16[64,1024]{1,0:T(8,128)(2,1)S(1)}, u32[]{:S(2)}, u32[]{:S(2)}) collective-permute-start(bf16[64,1024]{1,0:T(8,128)(2,1)S(1)} %get-tuple-element.31), channel_id=1, source_target_pairs={{0,128},{64,192},{128,0},{192,64},{1,129},{65,193},{129,1},{193,65... | collective-permute-start | bytes 393224 | tf_op jit(solution)/shard_map/ppermute | solution.py:36
  55.7 6.0 %collective-permute-start.8 = (bf16[64,1024]{1,0:T(8,128)(2,1)S(1)}, bf16[64,1024]{1,0:T(8,128)(2,1)S(1)}, u32[]{:S(2)}, u32[]{:S(2)}) collective-permute-start(bf16[64,1024]{1,0:T(8,128)(2,1)S(1)} %get-tuple-element.32), channel_id=1, source_target_pairs={{0,192},{64,0},{128,64},{192,128},{1,193},{65,1},{129,65},{193,129... | collective-permute-start | bytes 393224 | tf_op jit(solution)/shard_map/ppermute | solution.py:36
  61.9 5.1 %collective-permute-start.11 = (bf16[64,512]{1,0:T(8,128)(2,1)S(1)}, bf16[64,512]{1,0:T(8,128)(2,1)S(1)}, u32[]{:S(2)}, u32[]{:S(2)}) collective-permute-start(bf16[64,512]{1,0:T(8,128)(2,1)S(1)} %hidden_units.1.a), channel_id=1, source_target_pairs={{0,192},{64,0},{128,64},{192,128},{1,193},{65,1},{129,65},{193,129... | collective-permute-start | bytes 196616 | tf_op jit(solution)/shard_map/ppermute | solution.py:36
  64.4 5.9 %collective-permute-start.10 = (bf16[64,512]{1,0:T(8,128)(2,1)S(1)}, bf16[64,512]{1,0:T(8,128)(2,1)S(1)}, u32[]{:S(2)}, u32[]{:S(2)}) collective-permute-start(bf16[64,512]{1,0:T(8,128)(2,1)S(1)} %hidden_units.1.a), channel_id=1, source_target_pairs={{0,128},{64,192},{128,0},{192,64},{1,129},{65,193},{129,1},{193,65... | collective-permute-start | bytes 196616 | tf_op jit(solution)/shard_map/ppermute | solution.py:36
  64.6 6.2 %collective-permute-start.9 = (bf16[64,512]{1,0:T(8,128)(2,1)S(1)}, bf16[64,512]{1,0:T(8,128)(2,1)S(1)}, u32[]{:S(2)}, u32[]{:S(2)}) collective-permute-start(bf16[64,512]{1,0:T(8,128)(2,1)S(1)} %hidden_units.1.a), channel_id=1, source_target_pairs={{0,64},{64,128},{128,192},{192,0},{1,65},{65,129},{129,193},{193,1... | collective-permute-start | bytes 196616 | tf_op jit(solution)/shard_map/ppermute | solution.py:36
  72.6 25.1 %all-to-all-start.1 = ((bf16[32,8,1024]{2,1,0:T(8,128)(2,1)}), bf16[32,8,1024]{2,1,0:T(8,128)(2,1)S(1)}, u32[]{:S(2)}, u32[]{:S(2)}) async-start(bf16[32,8,1024]{2,1,0:T(8,128)(2,1)} %bitcast.10), calls=%async_computation.1 | async-start | bytes 1048576 | tf_op jit(solution)/shard_map/all_to_all | solution.py:370
  97.9 4.0 %collective-permute-start.14 = (f32[8,128]{1,0:T(8,128)S(1)}, f32[8,128]{1,0:T(8,128)S(1)}, u32[]{:S(2)}, u32[]{:S(2)}) collective-permute-start(f32[8,128]{1,0:T(8,128)S(1)} %get-tuple-element.35.a), channel_id=1, source_target_pairs={{0,192},{64,0},{128,64},{192,128},{1,193},{65,1},{129,65},{193,129... | collective-permute-start | bytes 12296 | tf_op jit(solution)/shard_map/ppermute | solution.py:36
  99.8 5.1 %collective-permute-start.13 = (f32[8,128]{1,0:T(8,128)S(1)}, f32[8,128]{1,0:T(8,128)S(1)}, u32[]{:S(2)}, u32[]{:S(2)}) collective-permute-start(f32[8,128]{1,0:T(8,128)S(1)} %get-tuple-element.35.a), channel_id=1, source_target_pairs={{0,128},{64,192},{128,0},{192,64},{1,129},{65,193},{129,1},{193,65... | collective-permute-start | bytes 12296 | tf_op jit(solution)/shard_map/ppermute | solution.py:36
  100.8 4.8 %collective-permute-start.12 = (f32[8,128]{1,0:T(8,128)S(1)}, f32[8,128]{1,0:T(8,128)S(1)}, u32[]{:S(2)}, u32[]{:S(2)}) collective-permute-start(f32[8,128]{1,0:T(8,128)S(1)} %get-tuple-element.35.a), channel_id=1, source_target_pairs={{0,64},{64,128},{128,192},{192,0},{1,65},{65,129},{129,193},{193,1... | collective-permute-start | bytes 12296 | tf_op jit(solution)/shard_map/ppermute | solution.py:36
  106.4 1.2 collective-permute-start.15
  107.6 1.2 copy-start.1
  109.6 25.0 %copy-start = (bf16[512,1024]{1,0:T(8,128)(2,1)S(1)}, bf16[512,1024]{1,0:T(8,128)(2,1)}, u32[]{:S(2)}) copy-start(bf16[512,1024]{1,0:T(8,128)(2,1)} %refs_3_.1) | copy-start | bytes 3145732
  109.6 1.4 collective-permute-start.16
  133.4 1.3 collective-permute-start.17
  138.6 1.3 collective-permute-start.18
  140.9 4.9 %collective-permute-start.19 = (f32[4,128]{1,0:T(4,128)S(1)}, f32[4,128]{1,0:T(4,128)S(1)}, u32[]{:S(2)}, u32[]{:S(2)}) collective-permute-start(f32[4,128]{1,0:T(4,128)S(1)} %get-tuple-element.42), channel_id=1, source_target_pairs={{0,64},{64,128},{128,192},{192,0},{1,65},{65,129},{129,193},{193,1... | collective-permute-start | bytes 6152 | tf_op jit(solution)/shard_map/ppermute | solution.py:36
  141.0 5.2 %collective-permute-start.20 = (f32[4,128]{1,0:T(4,128)S(1)}, f32[4,128]{1,0:T(4,128)S(1)}, u32[]{:S(2)}, u32[]{:S(2)}) collective-permute-start(f32[4,128]{1,0:T(4,128)S(1)} %get-tuple-element.43), channel_id=1, source_target_pairs={{0,128},{64,192},{128,0},{192,64},{1,129},{65,193},{129,1},{193,65... | collective-permute-start | bytes 6152 | tf_op jit(solution)/shard_map/ppermute | solution.py:36
  143.1 3.6 %collective-permute-start.21 = (f32[4,128]{1,0:T(4,128)S(1)}, f32[4,128]{1,0:T(4,128)S(1)}, u32[]{:S(2)}, u32[]{:S(2)}) collective-permute-start(f32[4,128]{1,0:T(4,128)S(1)} %get-tuple-element.44), channel_id=1, source_target_pairs={{0,192},{64,0},{128,64},{192,128},{1,193},{65,1},{129,65},{193,129... | collective-permute-start | bytes 6152 | tf_op jit(solution)/shard_map/ppermute | solution.py:36
  (1 other events, 0.7 us)
Sparse Core Ops, SparseCore 0:
  51.6 38.2 all-gather.1

commit v3 on v2

--- a/solution.py
+++ b/solution.py
@@ -43,6 +43,31 @@
 
 def lanes(like):
     return lax.broadcasted_iota(jnp.int32, like, 1)
+
+
+def pack_kernel(place, lengths, h, own, other):
+    k = place[1]
+    for q in range(4):
+        one = h[q * 32 : q * 32 + 16, :]
+        two = h[q * 32 + 16 : q * 32 + 32, :]
+        own[q * 16 : q * 16 + 16, :] = jnp.where(k == 0, one, two)
+        other[q * 16 : q * 16 + 16, :] = jnp.where(k == 0, two, one)
+    query = lax.broadcasted_iota(jnp.int32, (16, 64), 0) // 4
+    counts = jnp.zeros((16, 64), jnp.int32)
+    for q in range(4):
+        counts = jnp.where(query == q, lengths[q], counts)
+    own[64:80, :] = counts.astype(F32).astype(BF16)
+
+
+def pack(place, lengths, h):
+    return pl.pallas_call(
+        pack_kernel,
+        out_shape=(shape((80, 64), BF16), shape((64, 64), BF16)),
+        in_specs=[SMEM, SMEM, VMEM],
+        out_specs=(VMEM,) * 2,
+        compiler_params=PARAMS,
+        name="pack",
+    )(place, lengths, h)
 
 
 def gate_up_kernel(place, h, g0, u0, g1, u1, o0, o1, o2, o3, lhs, wide):
@@ -182,29 +207,35 @@
     )(place, counts, res, *sqs)
 
 
-def code_kernel(place, a, b, w, keep, send):
-    k = place[1]
+def code_kernel(place, a, b, w0, w1, w2, w3, keep, send, left):
+    k, zh = place[1], place[5]
     pooled = a[...] + b[...]
     top = pooled.astype(BF16).astype(F32)
     row = lax.broadcasted_iota(jnp.int32, (8, 512), 0)
-    left = jnp.where(row == 0, top, jnp.where(row == 1, pooled - top, 0.0)).astype(BF16)
-    both = jnp.dot(left, w[...], preferred_element_type=F32)
-    part = both[0:1] + both[1:2]
+    both = jnp.where(row == 0, top, jnp.where(row == 1, pooled - top, 0.0))
+    for t in range(4):
+        left[t] = both[:, t * 128 : t * 128 + 128]
+    total = jnp.zeros((8, 1024), F32)
+    for d, w in enumerate((w0, w1, w2, w3)):
+        piece = left[(zh - d + 4) % 4].astype(BF16)
+        total += jnp.dot(piece, w[...], preferred_element_type=F32)
+    part = total[0:1] + total[1:2]
     low, high = part[:, 0:512], part[:, 512:1024]
     keep[...] = jnp.where(k == 0, low, high)
     send[...] = jnp.where(k == 0, high, low)
 
 
-def code_part(place, a, b, w):
+def code_part(place, a, b, ws):
     half = shape((1, 512), F32)
     return pl.pallas_call(
         code_kernel,
         out_shape=(half, half),
-        in_specs=[SMEM] + [VMEM] * 3,
+        in_specs=[SMEM] + [VMEM] * 6,
         out_specs=(VMEM,) * 2,
+        scratch_shapes=[pltpu.VMEM((4, 8, 128), F32)],
         compiler_params=PARAMS,
         name="code_part",
-    )(place, a, b, w)
+    )(place, a, b, *ws)
 
 
 def exchange(x, step, falling):
@@ -336,13 +367,9 @@
 
 def per_device(hidden_in, lengths, gate_weight, up_weight, down_weight, code_weight, corpus_codes):
     y, x, zh, zb, k = (lax.axis_index(a) for a in QUERY_CORPUS)
-    place = jnp.stack([y, k, 16 * k + 8 * zb, zh % 2, 4 * zh]).astype(jnp.int32)
-
-    halves = hidden_in.reshape(4, 2, 16, 64)
-    first, second = halves[:, 0].reshape(64, 64), halves[:, 1].reshape(64, 64)
-    counts = jnp.broadcast_to(jnp.repeat(lengths.astype(BF16), 4)[:, None], (16, 64))
-    own = jnp.concatenate([jnp.where(k == 0, first, second), counts], axis=0)
-    other = jnp.where(k == 0, second, first)
+    place = jnp.stack([y, k, 16 * k + 8 * zb, zh % 2, 4 * zh, zh]).astype(jnp.int32)
+
+    own, other = pack(place, lengths, hidden_in)
     swap = [(a * 4 + b, b * 4 + a) for a in range(4) for b in range(4)]
     straight = [(s * 2 + c, t * 2 + c) for s, t in swap for c in range(2)]
     crossed = [(s * 2 + c, t * 2 + 1 - c) for s, t in swap for c in range(2)]
@@ -359,9 +386,13 @@
     )
     gathered = spread(block, XZ, 32)
 
-    code_rows = lax.ppermute(code_weight, ("y", "x"), swap)
-    code_rows, gathered = lax.optimization_barrier((code_rows, gathered))
-    code_rows = lax.all_gather(code_rows, Z, axis=0, tiled=True)
+    rows = lax.ppermute(code_weight, ("y", "x"), swap)
+    peer = lax.ppermute(rows, "zb", [(0, 1), (1, 0)])
+    rows = jnp.concatenate(
+        [jnp.where(zb == 0, rows, peer), jnp.where(zb == 0, peer, rows)], axis=0
+    )
+    rows, gathered = lax.optimization_barrier((rows, gathered))
+    code_rows = (rows, *(lax.ppermute(rows, "zh", [(i, (i + d) % 4) for i in range(4)]) for d in (1, 2, 3)))
 
     parts = gate_up(place, gathered, gate_rows, up_rows, gate_peer, up_peer)
     units = hidden_of(parts[0], *(shifted(parts[d], d) for d in (1, 2, 3)))

time: 180 us -> 179 us (level)
  between operations: 13.6 us -> 0.24 us
  starting transfers between devices: 48.8 us -> 56.9 us
  waiting for transfers between devices: 54.6 us -> 58.1 us
    ppermute x1 -> x5, waiting for transfers between devices: 0.01 us -> 17.4 us  [the longest x1 13.8 us: per_device(): peer = lax.ppermute(rows, 'zb', [(0, 1), (1, 0)])]
    all_to_all x1, waiting for transfers between devices: 17.3 us -> 3.11 us  [spread(): return lax.all_to_all(copies, axes, 0, 0, tiled=True)]
    ppermute x1 -> x5, starting transfers between devices: 0.67 us -> 8.47 us  [the longest x3 7.48 us: per_device(): lax.ppermute(rows, 'zh', [(i, (i + d) % 4) for i in range(4)])]
    ppermute x12, waiting for transfers between devices: 15.8 us -> 19.7 us  [shifted(): return lax.ppermute(x, 'y', [(i, (i + d) % 4) for i in range(4)])]
    all_to_all x1, waiting for transfers between devices: 16.3 us -> 13.8 us  [per_device(): branch = lax.all_to_all(branch.reshape(32, 8, 1024), XZ, 0, 0, tiled=True)]
  transfers between devices with their start and end apart: 25 -> 28, of which waited for: 17 -> 19; matrix products, arithmetic and copies ran while one was open for 1% -> 0% of each run, Pallas kernels for 2% -> 1%
where the time goes in v3:
time: 179 us; the launch traced here: 178 us
  waiting for transfers between devices  58.1 us (32%)
  starting transfers between devices  56.9 us (32%)
  blocking collectives  44.2 us (25%)
  Pallas kernels  15.6 us (9%)
  local copies, waits for them, and re-layouts  2.66 us (1%)
    all_to_all x1, blocking collectives, spread(): return lax.all_to_all(copies, axes, 0, 0, tiled=True)  23.2 us
    all_to_all x1, starting transfers between devices, spread(): return lax.all_to_all(copies, axes, 0, 0, tiled=True)  21.4 us
    all_to_all x1, blocking collectives, per_device(): arrived = lax.all_to_all(lists, YXZ, 0, 0, tiled=True)  21 us
    ppermute x12, waiting for transfers between devices, shifted(): return lax.ppermute(x, 'y', [(i, (i + d) % 4) for i in range(4)])  19.7 us
    ppermute x12, starting transfers between devices, shifted(): return lax.ppermute(x, 'y', [(i, (i + d) % 4) for i in range(4)])  14.7 us
    ppermute x1, waiting for transfers between devices, per_device(): peer = lax.ppermute(rows, 'zb', [(0, 1), (1, 0)])  13.8 us
    all_to_all x1, waiting for transfers between devices, per_device(): branch = lax.all_to_all(branch.reshape(32, 8, 1024), XZ, 0, 0, tiled=True)  13.8 us
    all_to_all x1, starting transfers between devices, per_device(): branch = lax.all_to_all(branch.reshape(32, 8, 1024), XZ, 0, 0, tiled=True)  10 us
  transfers between devices with their start and end apart: 28, of which 19 were waited for; matrix products, arithmetic and copies ran while one was open for 0% of the time, Pallas kernels for 1%

profile of v3, /device:TPU:32, one launch (start us, length us, event | category | flops | bytes accessed | tf_op | source)
XLA Modules:
  0.0 178.0 jit_solution(6301244795252192253)
XLA Ops:
  5.7 21.4 %all-to-all-start = ((bf16[32,64,128]{2,1,0:T(8,128)(2,1)}), bf16[32,64,128]{2,1,0:T(8,128)(2,1)S(1)}, u32[]{:S(2)}, u32[]{:S(2)}) async-start(bf16[32,64,128]{2,1,0:T(8,128)(2,1)} %broadcast_in_dim.6), calls=%async_computation | async-start | bytes 1048576 | tf_op jit(solution)/shard_map/all_to_all | solution.py:41
  28.2 13.8 %collective-permute-done.2 = bf16[64,1024]{1,0:T(8,128)(2,1)S(1)} collective-permute-done((bf16[64,1024]{1,0:T(8,128)(2,1)S(1)}, bf16[64,1024]{1,0:T(8,128)(2,1)S(1)}, u32[]{:S(2)}, u32[]{:S(2)}) %collective-permute-start.2) | collective-permute-done | bytes 131104 | tf_op jit(solution)/shard_map/ppermute | solution.py:390
  42.1 3.1 %all-to-all-done.h = bf16[32,64,128]{2,1,0:T(8,128)(2,1)S(1)} async-done(((bf16[32,64,128]{2,1,0:T(8,128)(2,1)}), bf16[32,64,128]{2,1,0:T(8,128)(2,1)S(1)}, u32[]{:S(2)}, u32[]{:S(2)}) %all-to-all-start) | async-done | bytes 524320 | tf_op jit(solution)/shard_map/all_to_all | solution.py:41
  45.2 1.4 gate_up.1
  46.6 1.4 collective-permute-start.7
  47.9 5.0 %collective-permute-start.8 = (bf16[64,1024]{1,0:T(8,128)(2,1)S(1)}, bf16[64,1024]{1,0:T(8,128)(2,1)S(1)}, u32[]{:S(2)}, u32[]{:S(2)}) collective-permute-start(bf16[64,1024]{1,0:T(8,128)(2,1)S(1)} %get-tuple-element.35), channel_id=1, source_target_pairs={{0,128},{64,192},{128,0},{192,64},{1,129},{65,193},{129,1},{193,65... | collective-permute-start | bytes 393224 | tf_op jit(solution)/shard_map/ppermute | solution.py:36
  52.9 2.3 %collective-permute-done.7.b = bf16[64,1024]{1,0:T(8,128)(2,1)S(1)} collective-permute-done((bf16[64,1024]{1,0:T(8,128)(2,1)S(1)}, bf16[64,1024]{1,0:T(8,128)(2,1)S(1)}, u32[]{:S(2)}, u32[]{:S(2)}) %collective-permute-start.7) | collective-permute-done | bytes 131104 | tf_op jit(solution)/shard_map/ppermute | solution.py:36
  55.2 3.0 %collective-permute-done.8.c = bf16[64,1024]{1,0:T(8,128)(2,1)S(1)} collective-permute-done((bf16[64,1024]{1,0:T(8,128)(2,1)S(1)}, bf16[64,1024]{1,0:T(8,128)(2,1)S(1)}, u32[]{:S(2)}, u32[]{:S(2)}) %collective-permute-start.8) | collective-permute-done | bytes 131104 | tf_op jit(solution)/shard_map/ppermute | solution.py:36
  58.4 2.2 %collective-permute-start.12 = (bf16[64,512]{1,0:T(8,128)(2,1)S(1)}, bf16[64,512]{1,0:T(8,128)(2,1)S(1)}, u32[]{:S(2)}, u32[]{:S(2)}) collective-permute-start(bf16[64,512]{1,0:T(8,128)(2,1)S(1)} %hidden_units.1.a), channel_id=1, source_target_pairs={{0,192},{64,0},{128,64},{192,128},{1,193},{65,1},{129,65},{193,129... | collective-permute-start | bytes 196616 | tf_op jit(solution)/shard_map/ppermute | solution.py:36
  61.6 1.6 collective-permute-done.12.d
  63.1 3.4 %collective-permute-done.11.c = bf16[64,512]{1,0:T(8,128)(2,1)S(1)} collective-permute-done((bf16[64,512]{1,0:T(8,128)(2,1)S(1)}, bf16[64,512]{1,0:T(8,128)(2,1)S(1)}, u32[]{:S(2)}, u32[]{:S(2)}) %collective-permute-start.11) | collective-permute-done | bytes 65568 | tf_op jit(solution)/shard_map/ppermute | solution.py:36
  66.8 1.8 down.1
  68.6 10.0 %all-to-all-start.1 = ((bf16[32,8,1024]{2,1,0:T(8,128)(2,1)}), bf16[32,8,1024]{2,1,0:T(8,128)(2,1)S(1)}, u32[]{:S(2)}, u32[]{:S(2)}) async-start(bf16[32,8,1024]{2,1,0:T(8,128)(2,1)} %bitcast.8), calls=%async_computation.1 | async-start | bytes 1048576 | tf_op jit(solution)/shard_map/all_to_all | solution.py:401
  78.6 2.8 %collective-permute-start.19 = (bf16[128,1024]{1,0:T(8,128)(2,1)S(1)}, bf16[128,1024]{1,0:T(8,128)(2,1)S(1)}, u32[]{:S(2)}, u32[]{:S(2)}) collective-permute-start(bf16[128,1024]{1,0:T(8,128)(2,1)S(1)} %pad_maximum_fusion.w0), channel_id=1, source_target_pairs={{0,12},{4,0},{8,4},{12,8},{1,13},{5,1},{9,5},{13,9},{2,14},{6,2},{... | collective-permute-start | bytes 786440 | tf_op jit(solution)/shard_map/ppermute | solution.py:395
  81.3 3.3 %collective-permute-start.18 = (bf16[128,1024]{1,0:T(8,128)(2,1)S(1)}, bf16[128,1024]{1,0:T(8,128)(2,1)S(1)}, u32[]{:S(2)}, u32[]{:S(2)}) collective-permute-start(bf16[128,1024]{1,0:T(8,128)(2,1)S(1)} %pad_maximum_fusion.w0), channel_id=1, source_target_pairs={{0,8},{4,12},{8,0},{12,4},{1,9},{5,13},{9,1},{13,5},{2,10},{6,14},... | collective-permute-start | bytes 786440 | tf_op jit(solution)/shard_map/ppermute | solution.py:395
  84.6 1.5 collective-permute-start.17
  86.1 13.8 %all-to-all-done.1.parts = bf16[32,8,1024]{2,1,0:T(8,128)(2,1)S(1)} async-done(((bf16[32,8,1024]{2,1,0:T(8,128)(2,1)}), bf16[32,8,1024]{2,1,0:T(8,128)(2,1)S(1)}, u32[]{:S(2)}, u32[]{:S(2)}) %all-to-all-start.1) | async-done | bytes 524320 | tf_op jit(solution)/shard_map/all_to_all | solution.py:401
  101.5 2.2 %collective-permute-done.15.d = f32[8,128]{1,0:T(8,128)S(1)} collective-permute-done((f32[8,128]{1,0:T(8,128)S(1)}, f32[8,128]{1,0:T(8,128)S(1)}, u32[]{:S(2)}, u32[]{:S(2)}) %collective-permute-start.15) | collective-permute-done | bytes 4128 | tf_op jit(solution)/shard_map/ppermute | solution.py:36
  103.8 2.0 %collective-permute-done.14.c = f32[8,128]{1,0:T(8,128)S(1)} collective-permute-done((f32[8,128]{1,0:T(8,128)S(1)}, f32[8,128]{1,0:T(8,128)S(1)}, u32[]{:S(2)}, u32[]{:S(2)}) %collective-permute-start.14) | collective-permute-done | bytes 4128 | tf_op jit(solution)/shard_map/ppermute | solution.py:36
  105.8 2.8 %collective-permute-done.13.b = f32[8,128]{1,0:T(8,128)S(1)} collective-permute-done((f32[8,128]{1,0:T(8,128)S(1)}, f32[8,128]{1,0:T(8,128)S(1)}, u32[]{:S(2)}, u32[]{:S(2)}) %collective-permute-start.13) | collective-permute-done | bytes 4128 | tf_op jit(solution)/shard_map/ppermute | solution.py:36
  109.5 3.5 %collective-permute-done.18.w2 = bf16[128,1024]{1,0:T(8,128)(2,1)S(1)} collective-permute-done((bf16[128,1024]{1,0:T(8,128)(2,1)S(1)}, bf16[128,1024]{1,0:T(8,128)(2,1)S(1)}, u32[]{:S(2)}, u32[]{:S(2)}) %collective-permute-start.18) | collective-permute-done | bytes 262176 | tf_op jit(solution)/shard_map/ppermute | solution.py:395
  113.9 1.1 collective-permute-done.20
  115.1 23.2 %all_to_all.20 = f32[128,4,128]{2,1,0:T(4,128)S(1)} all-to-all(f32[128,4,128]{2,1,0:T(4,128)S(1)} %broadcast_in_dim.15), channel_id=1, replica_groups=mesh['y'=4,'x'=4,'zh'=4,'zb'=2,'k'=2] {'y','x','zh','zb'}, dimensions={0} | all-to-all | bytes 524288 | tf_op jit(solution)/shard_map/all_to_all | solution.py:41
  138.8 1.2 collective-permute-done.21.refs_2_
  140.0 3.9 %scores.1.a = f32[16,128]{1,0:T(8,128)S(1)} custom-call(s32[6]{0:T(128)S(1)} %stack.27.place.refs_0_, bf16[16,512]{1,0:T(8,128)(2,1)S(1)} %convert_element_type.6.refs_1_, bf16[16,512]{1,0:T(8,128)(2,1)S(1)} %collective-permute-done.21.refs_2_, bf16[512,1024]{1,0:T(8,128)(2,1)S(1)} %copy-done), custom_call_target="tpu_custom_call" | custom-call | tf_op jit(solution)/shard_map/scores/pallas_call | solution.py:290
  145.2 1.0 pair_lists.1
  146.3 2.1 %collective-permute-start.24 = (f32[4,128]{1,0:T(4,128)S(1)}, f32[4,128]{1,0:T(4,128)S(1)}, u32[]{:S(2)}, u32[]{:S(2)}) collective-permute-start(f32[4,128]{1,0:T(4,128)S(1)} %get-tuple-element.47), channel_id=1, source_target_pairs={{0,128},{64,192},{128,0},{192,64},{1,129},{65,193},{129,1},{193,65... | collective-permute-start | bytes 6152 | tf_op jit(solution)/shard_map/ppermute | solution.py:36
  148.4 1.5 collective-permute-start.25
  149.8 1.2 collective-permute-done.23.b
  151.9 1.6 four_lists.1
  153.5 21.0 %all_to_all.21 = f32[128,4,128]{2,1,0:T(4,128)S(1)} all-to-all(f32[128,4,128]{2,1,0:T(4,128)S(1)} %four_lists.1), channel_id=1, replica_groups=mesh['y'=4,'x'=4,'zh'=4,'zb'=2,'k'=2] {'y','x','zh','zb'}, dimensions={0} | all-to-all | bytes 524288 | tf_op jit(solution)/shard_map/all_to_all | solution.py:418
  174.5 3.5 %final_lists.1 = f32[16,100]{1,0:T(8,128)} custom-call(f32[512,128]{1,0:T(8,128)S(1)} %bitcast.19), custom_call_target="tpu_custom_call" | custom-call | tf_op jit(solution)/shard_map/final_lists/pallas_call | solution.py:358
  (65 shorter events, 14.3 us)
Async XLA Ops:
  0.0 4.8 %collective-permute-start.4 = (bf16[224,1024]{1,0:T(8,128)(2,1)}, bf16[224,1024]{1,0:T(8,128)(2,1)S(1)}, u32[]{:S(2)}, u32[]{:S(2)}) collective-permute-start(bf16[224,1024]{1,0:T(8,128)(2,1)} %bitcast.20), channel_id=1, source_target_pairs={{0,1},{1,0},{2,3},{3,2},{4,5},{5,4},{6,7},{7,6},{8,9},{9,8},{10,11... | collective-permute-start | bytes 1376264 | tf_op jit(solution)/shard_map/ppermute | solution.py:32
  0.0 4.8 %collective-permute-start.5 = (bf16[224,1024]{1,0:T(8,128)(2,1)}, bf16[224,1024]{1,0:T(8,128)(2,1)S(1)}, u32[]{:S(2)}, u32[]{:S(2)}) collective-permute-start(bf16[224,1024]{1,0:T(8,128)(2,1)} %bitcast.22), channel_id=1, source_target_pairs={{0,1},{1,0},{2,3},{3,2},{4,5},{5,4},{6,7},{7,6},{8,9},{9,8},{10,11... | collective-permute-start | bytes 1376264 | tf_op jit(solution)/shard_map/ppermute | solution.py:32
  0.5 4.3 %collective-permute-start.6 = (bf16[224,1024]{1,0:T(8,128)(2,1)}, bf16[224,1024]{1,0:T(8,128)(2,1)S(1)}, u32[]{:S(2)}, u32[]{:S(2)}) collective-permute-start(bf16[224,1024]{1,0:T(8,128)(2,1)} %w0.1), channel_id=1, source_target_pairs={{0,1},{1,0},{2,3},{3,2},{4,5},{5,4},{6,7},{7,6},{8,9},{9,8},{10,11... | collective-permute-start | bytes 1376264 | tf_op jit(solution)/shard_map/ppermute | solution.py:32
  2.6 1.3 collective-permute-start
  3.3 1.4 collective-permute-start.3
  5.7 21.4 %copy-start.6 = (bf16[64,1024]{1,0:T(8,128)(2,1)S(1)}, bf16[64,1024]{1,0:T(8,128)(2,1)}, u32[]{:S(2)}) copy-start(bf16[64,1024]{1,0:T(8,128)(2,1)} %param.12) | copy-start | bytes 393220
  5.7 39.5 %all-to-all-start = ((bf16[32,64,128]{2,1,0:T(8,128)(2,1)}), bf16[32,64,128]{2,1,0:T(8,128)(2,1)S(1)}, u32[]{:S(2)}, u32[]{:S(2)}) async-start(bf16[32,64,128]{2,1,0:T(8,128)(2,1)} %broadcast_in_dim.6), calls=%async_computation | async-start | bytes 1048576 | tf_op jit(solution)/shard_map/all_to_all | solution.py:41
  27.2 0.7 collective-permute-start.1
  27.8 14.2 %collective-permute-start.2 = (bf16[64,1024]{1,0:T(8,128)(2,1)S(1)}, bf16[64,1024]{1,0:T(8,128)(2,1)S(1)}, u32[]{:S(2)}, u32[]{:S(2)}) collective-permute-start(bf16[64,1024]{1,0:T(8,128)(2,1)S(1)} %collective-permute-done.1), channel_id=1, source_target_pairs={{0,2},{2,0},{1,3},{3,1},{4,6},{6,4},{5,7},{7,5},{8,10},{10,8},{9,1... | collective-permute-start | bytes 393224 | tf_op jit(solution)/shard_map/ppermute | solution.py:390
  28.2 17.0 %copy-start.2 = (bf16[1024,224]{0,1:T(8,128)(2,1)S(1)}, bf16[1024,224]{0,1:T(8,128)(2,1)}, u32[]{:S(2)}) copy-start(bf16[1024,224]{0,1:T(8,128)(2,1)} %param.10) | copy-start | bytes 1376260
  46.6 20.2 %copy-start.3 = (bf16[224,1024]{1,0:T(8,128)(2,1)S(1)}, bf16[224,1024]{1,0:T(8,128)(2,1)}, u32[]{:S(2)}) copy-start(bf16[224,1024]{1,0:T(8,128)(2,1)} %w0.1) | copy-start | bytes 1376260
  46.6 8.7 %collective-permute-start.7 = (bf16[64,1024]{1,0:T(8,128)(2,1)S(1)}, bf16[64,1024]{1,0:T(8,128)(2,1)S(1)}, u32[]{:S(2)}, u32[]{:S(2)}) collective-permute-start(bf16[64,1024]{1,0:T(8,128)(2,1)S(1)} %get-tuple-element.34), channel_id=1, source_target_pairs={{0,64},{64,128},{128,192},{192,0},{1,65},{65,129},{129,193},{193,1... | collective-permute-start | bytes 393224 | tf_op jit(solution)/shard_map/ppermute | solution.py:36
  47.9 10.3 %collective-permute-start.8 = (bf16[64,1024]{1,0:T(8,128)(2,1)S(1)}, bf16[64,1024]{1,0:T(8,128)(2,1)S(1)}, u32[]{:S(2)}, u32[]{:S(2)}) collective-permute-start(bf16[64,1024]{1,0:T(8,128)(2,1)S(1)} %get-tuple-element.35), channel_id=1, source_target_pairs={{0,128},{64,192},{128,0},{192,64},{1,129},{65,193},{129,1},{193,65... | collective-permute-start | bytes 393224 | tf_op jit(solution)/shard_map/ppermute | solution.py:36
  52.9 5.3 %collective-permute-start.9 = (bf16[64,1024]{1,0:T(8,128)(2,1)S(1)}, bf16[64,1024]{1,0:T(8,128)(2,1)S(1)}, u32[]{:S(2)}, u32[]{:S(2)}) collective-permute-start(bf16[64,1024]{1,0:T(8,128)(2,1)S(1)} %get-tuple-element.36), channel_id=1, source_target_pairs={{0,192},{64,0},{128,64},{192,128},{1,193},{65,1},{129,65},{193,129... | collective-permute-start | bytes 393224 | tf_op jit(solution)/shard_map/ppermute | solution.py:36
  58.4 4.8 %collective-permute-start.12 = (bf16[64,512]{1,0:T(8,128)(2,1)S(1)}, bf16[64,512]{1,0:T(8,128)(2,1)S(1)}, u32[]{:S(2)}, u32[]{:S(2)}) collective-permute-start(bf16[64,512]{1,0:T(8,128)(2,1)S(1)} %hidden_units.1.a), channel_id=1, source_target_pairs={{0,192},{64,0},{128,64},{192,128},{1,193},{65,1},{129,65},{193,129... | collective-permute-start | bytes 196616 | tf_op jit(solution)/shard_map/ppermute | solution.py:36
  60.6 5.9 %collective-permute-start.11 = (bf16[64,512]{1,0:T(8,128)(2,1)S(1)}, bf16[64,512]{1,0:T(8,128)(2,1)S(1)}, u32[]{:S(2)}, u32[]{:S(2)}) collective-permute-start(bf16[64,512]{1,0:T(8,128)(2,1)S(1)} %hidden_units.1.a), channel_id=1, source_target_pairs={{0,128},{64,192},{128,0},{192,64},{1,129},{65,193},{129,1},{193,65... | collective-permute-start | bytes 196616 | tf_op jit(solution)/shard_map/ppermute | solution.py:36
  60.6 6.2 %collective-permute-start.10 = (bf16[64,512]{1,0:T(8,128)(2,1)S(1)}, bf16[64,512]{1,0:T(8,128)(2,1)S(1)}, u32[]{:S(2)}, u32[]{:S(2)}) collective-permute-start(bf16[64,512]{1,0:T(8,128)(2,1)S(1)} %hidden_units.1.a), channel_id=1, source_target_pairs={{0,64},{64,128},{128,192},{192,0},{1,65},{65,129},{129,193},{193,1... | collective-permute-start | bytes 196616 | tf_op jit(solution)/shard_map/ppermute | solution.py:36
  68.6 31.3 %all-to-all-start.1 = ((bf16[32,8,1024]{2,1,0:T(8,128)(2,1)}), bf16[32,8,1024]{2,1,0:T(8,128)(2,1)S(1)}, u32[]{:S(2)}, u32[]{:S(2)}) async-start(bf16[32,8,1024]{2,1,0:T(8,128)(2,1)} %bitcast.8), calls=%async_computation.1 | async-start | bytes 1048576 | tf_op jit(solution)/shard_map/all_to_all | solution.py:401
  78.6 30.9 %collective-permute-start.19 = (bf16[128,1024]{1,0:T(8,128)(2,1)S(1)}, bf16[128,1024]{1,0:T(8,128)(2,1)S(1)}, u32[]{:S(2)}, u32[]{:S(2)}) collective-permute-start(bf16[128,1024]{1,0:T(8,128)(2,1)S(1)} %pad_maximum_fusion.w0), channel_id=1, source_target_pairs={{0,12},{4,0},{8,4},{12,8},{1,13},{5,1},{9,5},{13,9},{2,14},{6,2},{... | collective-permute-start | bytes 786440 | tf_op jit(solution)/shard_map/ppermute | solution.py:395
  81.3 31.7 %collective-permute-start.18 = (bf16[128,1024]{1,0:T(8,128)(2,1)S(1)}, bf16[128,1024]{1,0:T(8,128)(2,1)S(1)}, u32[]{:S(2)}, u32[]{:S(2)}) collective-permute-start(bf16[128,1024]{1,0:T(8,128)(2,1)S(1)} %pad_maximum_fusion.w0), channel_id=1, source_target_pairs={{0,8},{4,12},{8,0},{12,4},{1,9},{5,13},{9,1},{13,5},{2,10},{6,14},... | collective-permute-start | bytes 786440 | tf_op jit(solution)/shard_map/ppermute | solution.py:395
  84.6 28.4 %collective-permute-start.17 = (bf16[128,1024]{1,0:T(8,128)(2,1)S(1)}, bf16[128,1024]{1,0:T(8,128)(2,1)S(1)}, u32[]{:S(2)}, u32[]{:S(2)}) collective-permute-start(bf16[128,1024]{1,0:T(8,128)(2,1)S(1)} %pad_maximum_fusion.w0), channel_id=1, source_target_pairs={{0,4},{4,8},{8,12},{12,0},{1,5},{5,9},{9,13},{13,1},{2,6},{6,10},{... | collective-permute-start | bytes 786440 | tf_op jit(solution)/shard_map/ppermute | solution.py:395
  100.0 3.8 %collective-permute-start.15 = (f32[8,128]{1,0:T(8,128)S(1)}, f32[8,128]{1,0:T(8,128)S(1)}, u32[]{:S(2)}, u32[]{:S(2)}) collective-permute-start(f32[8,128]{1,0:T(8,128)S(1)} %get-tuple-element.39.a), channel_id=1, source_target_pairs={{0,192},{64,0},{128,64},{192,128},{1,193},{65,1},{129,65},{193,129... | collective-permute-start | bytes 12296 | tf_op jit(solution)/shard_map/ppermute | solution.py:36
  100.7 5.1 %collective-permute-start.14 = (f32[8,128]{1,0:T(8,128)S(1)}, f32[8,128]{1,0:T(8,128)S(1)}, u32[]{:S(2)}, u32[]{:S(2)}) collective-permute-start(f32[8,128]{1,0:T(8,128)S(1)} %get-tuple-element.39.a), channel_id=1, source_target_pairs={{0,128},{64,192},{128,0},{192,64},{1,129},{65,193},{129,1},{193,65... | collective-permute-start | bytes 12296 | tf_op jit(solution)/shard_map/ppermute | solution.py:36
  103.8 4.8 %collective-permute-start.13 = (f32[8,128]{1,0:T(8,128)S(1)}, f32[8,128]{1,0:T(8,128)S(1)}, u32[]{:S(2)}, u32[]{:S(2)}) collective-permute-start(f32[8,128]{1,0:T(8,128)S(1)} %get-tuple-element.39.a), channel_id=1, source_target_pairs={{0,64},{64,128},{128,192},{192,0},{1,65},{65,129},{129,193},{193,1... | collective-permute-start | bytes 12296 | tf_op jit(solution)/shard_map/ppermute | solution.py:36
  109.4 3.6 %collective-permute-start.16 = (f32[1,512]{1,0:T(1,128)S(1)}, f32[1,512]{1,0:T(1,128)S(1)}, u32[]{:S(2)}, u32[]{:S(2)}) collective-permute-start(f32[1,512]{1,0:T(1,128)S(1)} %get-tuple-element.41), channel_id=1, source_target_pairs={{0,1},{1,0},{2,3},{3,2},{4,5},{5,4},{6,7},{7,6},{8,9},{9,8},{10,11... | collective-permute-start | bytes 6152 | tf_op jit(solution)/shard_map/ppermute | solution.py:32
  113.8 26.1 %copy-start = (bf16[512,1024]{1,0:T(8,128)(2,1)S(1)}, bf16[512,1024]{1,0:T(8,128)(2,1)}, u32[]{:S(2)}) copy-start(bf16[512,1024]{1,0:T(8,128)(2,1)} %refs_3_.1) | copy-start | bytes 3145732
  113.8 1.2 collective-permute-start.20
  138.7 1.3 collective-permute-start.21
  143.9 1.3 collective-permute-start.22
  146.2 4.9 %collective-permute-start.23 = (f32[4,128]{1,0:T(4,128)S(1)}, f32[4,128]{1,0:T(4,128)S(1)}, u32[]{:S(2)}, u32[]{:S(2)}) collective-permute-start(f32[4,128]{1,0:T(4,128)S(1)} %get-tuple-element.46), channel_id=1, source_target_pairs={{0,64},{64,128},{128,192},{192,0},{1,65},{65,129},{129,193},{193,1... | collective-permute-start | bytes 6152 | tf_op jit(solution)/shard_map/ppermute | solution.py:36
  146.3 5.2 %collective-permute-start.24 = (f32[4,128]{1,0:T(4,128)S(1)}, f32[4,128]{1,0:T(4,128)S(1)}, u32[]{:S(2)}, u32[]{:S(2)}) collective-permute-start(f32[4,128]{1,0:T(4,128)S(1)} %get-tuple-element.47), channel_id=1, source_target_pairs={{0,128},{64,192},{128,0},{192,64},{1,129},{65,193},{129,1},{193,65... | collective-permute-start | bytes 6152 | tf_op jit(solution)/shard_map/ppermute | solution.py:36
  148.4 3.6 %collective-permute-start.25 = (f32[4,128]{1,0:T(4,128)S(1)}, f32[4,128]{1,0:T(4,128)S(1)}, u32[]{:S(2)}, u32[]{:S(2)}) collective-permute-start(f32[4,128]{1,0:T(4,128)S(1)} %get-tuple-element.48), channel_id=1, source_target_pairs={{0,192},{64,0},{128,64},{192,128},{1,193},{65,1},{129,65},{193,129... | collective-permute-start | bytes 6152 | tf_op jit(solution)/shard_map/ppermute | solution.py:36
  (3 other events, 18.4 us)

commit v4 on v3

--- a/solution.py
+++ b/solution.py
@@ -176,8 +176,8 @@
     )(parts, h)
 
 
-def pool_kernel(place, counts, res, a, b, c, d, keep, send):
-    k, first, row = place[1], place[2], place[4]
+def pool_kernel(place, counts, res, a, b, c, d, o0, o1, o2, o3):
+    k, first, row, zb = place[1], place[2], place[4], place[6]
     sq = (a[...] + b[...] + c[...] + d[...])[:, 0:1]
     slots = lax.broadcasted_iota(jnp.int32, (8, 1), 0) + first
     held = counts[...].astype(F32)
@@ -185,57 +185,48 @@
     count = jnp.max(jnp.max(held, axis=1, keepdims=True), axis=0, keepdims=True)
     weight = jnp.where(slots.astype(F32) < count, lax.rsqrt(sq / D + EPS), 0.0)
     pooled = jnp.sum(res[...] * weight, axis=0, keepdims=True) / count
-    low = lanes((1, 128)) < 64
-    for t in range(4):
-        one = pooled[:, t * 256 : t * 256 + 128]
-        two = pooled[:, t * 256 + 128 : t * 256 + 256]
-        even = jnp.where(low, one, pltpu.roll(two, 64, 1))
-        odd = jnp.where(low, pltpu.roll(one, 64, 1), two)
-        keep[:, t * 128 : t * 128 + 128] = jnp.where(k == 0, even, odd)
-        send[:, t * 128 : t * 128 + 128] = jnp.where(k == 0, odd, even)
+    ahead = jnp.concatenate([pooled[:, t * 256 : t * 256 + 128] for t in range(4)], axis=0)
+    behind = jnp.concatenate([pooled[:, t * 256 + 128 : t * 256 + 256] for t in range(4)], axis=0)
+    for r, out in enumerate((o0, o1, o2, o3)):
+        part = jnp.where(zb == r // 2, ahead, behind)
+        out[...] = jnp.where(k == r % 2, part, pltpu.roll(part, 64, 1))
 
 
 def pool(place, counts, res, sqs):
-    half = shape((1, 512), F32)
+    part = shape((4, 128), F32)
     return pl.pallas_call(
         pool_kernel,
-        out_shape=(half, half),
+        out_shape=(part,) * 4,
         in_specs=[SMEM] + [VMEM] * 6,
-        out_specs=(VMEM,) * 2,
+        out_specs=(VMEM,) * 4,
         compiler_params=PARAMS,
         name="pool",
     )(place, counts, res, *sqs)
 
 
-def code_kernel(place, a, b, w0, w1, w2, w3, keep, send, left):
+def code_kernel(place, a, b, c, d, w0, w1, w2, w3, keep, send, left):
     k, zh = place[1], place[5]
-    pooled = a[...] + b[...]
-    top = pooled.astype(BF16).astype(F32)
-    row = lax.broadcasted_iota(jnp.int32, (8, 512), 0)
-    both = jnp.where(row == 0, top, jnp.where(row == 1, pooled - top, 0.0))
-    for t in range(4):
-        left[t] = both[:, t * 128 : t * 128 + 128]
+    left[...] = a[...] + b[...] + c[...] + d[...]
     total = jnp.zeros((8, 1024), F32)
-    for d, w in enumerate((w0, w1, w2, w3)):
-        piece = left[(zh - d + 4) % 4].astype(BF16)
-        total += jnp.dot(piece, w[...], preferred_element_type=F32)
-    part = total[0:1] + total[1:2]
-    low, high = part[:, 0:512], part[:, 512:1024]
+    for s, w in enumerate((w0, w1, w2, w3)):
+        piece = jnp.broadcast_to(left[pl.ds((zh - s + 4) % 4, 1), :], (8, 128))
+        total += jnp.dot(piece[:, 0:64].astype(BF16), w[...], preferred_element_type=F32)
+    low, high = total[0:1, 0:512], total[0:1, 512:1024]
     keep[...] = jnp.where(k == 0, low, high)
     send[...] = jnp.where(k == 0, high, low)
 
 
-def code_part(place, a, b, ws):
+def code_part(place, pieces, ws):
     half = shape((1, 512), F32)
     return pl.pallas_call(
         code_kernel,
         out_shape=(half, half),
-        in_specs=[SMEM] + [VMEM] * 6,
+        in_specs=[SMEM] + [VMEM] * 8,
         out_specs=(VMEM,) * 2,
-        scratch_shapes=[pltpu.VMEM((4, 8, 128), F32)],
+        scratch_shapes=[pltpu.VMEM((4, 128), F32)],
         compiler_params=PARAMS,
         name="code_part",
-    )(place, a, b, *ws)
+    )(place, *pieces, *ws)
 
 
 def exchange(x, step, falling):
@@ -367,7 +358,7 @@
 
 def per_device(hidden_in, lengths, gate_weight, up_weight, down_weight, code_weight, corpus_codes):
     y, x, zh, zb, k = (lax.axis_index(a) for a in QUERY_CORPUS)
-    place = jnp.stack([y, k, 16 * k + 8 * zb, zh % 2, 4 * zh, zh]).astype(jnp.int32)
+    place = jnp.stack([y, k, 16 * k + 8 * zb, zh % 2, 4 * zh, zh, zb]).astype(jnp.int32)
 
     own, other = pack(place, lengths, hidden_in)
     swap = [(a * 4 + b, b * 4 + a) for a in range(4) for b in range(4)]
@@ -387,16 +378,14 @@
     gathered = spread(block, XZ, 32)
 
     rows = lax.ppermute(code_weight, ("y", "x"), swap)
-    peer = lax.ppermute(rows, "zb", [(0, 1), (1, 0)])
-    rows = jnp.concatenate(
-        [jnp.where(zb == 0, rows, peer), jnp.where(zb == 0, peer, rows)], axis=0
-    )
     rows, gathered = lax.optimization_barrier((rows, gathered))
-    code_rows = (rows, *(lax.ppermute(rows, "zh", [(i, (i + d) % 4) for i in range(4)]) for d in (1, 2, 3)))
+    turned = [[(i, (i + d) % 4) for i in range(4)] for d in range(4)]
+    code_rows = (rows, *(lax.ppermute(rows, "zh", turned[d]) for d in (1, 2, 3)))
 
     parts = gate_up(place, gathered, gate_rows, up_rows, gate_peer, up_peer)
     units = hidden_of(parts[0], *(shifted(parts[d], d) for d in (1, 2, 3)))
     groups = (units, *(shifted(units, d) for d in (1, 2, 3)))
+    groups, code_rows = lax.optimization_barrier((groups, code_rows))
     branch = down(place, groups, down_weight, down_peer)
     branch = lax.all_to_all(branch.reshape(32, 8, 1024), XZ, 0, 0, tiled=True)
     here = lax.dynamic_slice(
@@ -405,8 +394,10 @@
     here = jnp.moveaxis(here, 0, 1).reshape(8, 1024)
     res, sq = residual_of(branch, here)
     sqs = (sq, *(shifted(sq, d) for d in (1, 2, 3)))
-    keep, send = pool(place, counts, res, sqs)
-    keep, send = code_part(place, keep, to_peer(send), code_rows)
+    mine = pool(place, counts, res, sqs)
+    flips = [[(i, i ^ r) for i in range(4)] for r in range(4)]
+    pieces = (mine[0], *(lax.ppermute(mine[r], ("zb", "k"), flips[r]) for r in (1, 2, 3)))
+    keep, send = code_part(place, pieces, code_rows)
     part = (keep + to_peer(send)).reshape(4, 128)
     codes = spread(part, YXZ, 128).reshape(4, 4, 4, 2, 512).sum(axis=(0, 3))
     codes = codes.reshape(16, 512).astype(BF16)

time: 179 us -> 170 us (0.950)
  waiting for transfers between devices: 58.1 us -> 54.4 us
  starting transfers between devices: 56.9 us -> 54 us
  blocking collectives: 44.2 us -> 42.2 us
    all_to_all x1, waiting for transfers between devices: 3.11 us -> 17.3 us  [spread(): return lax.all_to_all(copies, axes, 0, 0, tiled=True)]
    ppermute x12, waiting for transfers between devices: 19.7 us -> 7.68 us  [shifted(): return lax.ppermute(x, 'y', [(i, (i + d) % 4) for i in range(4)])]
    ppermute x4 -> x6, waiting for transfers between devices: 17.4 us -> 8.29 us  [the longest x3 6.48 us: per_device(): lax.ppermute(rows, 'zh', turned[d])]
    all_to_all x1, starting transfers between devices: 10 us -> 6.65 us  [per_device(): branch = lax.all_to_all(branch.reshape(32, 8, 1024), XZ, 0, 0, tiled=True)]
    all_to_all x1, waiting for transfers between devices: 13.8 us -> 17 us  [per_device(): branch = lax.all_to_all(branch.reshape(32, 8, 1024), XZ, 0, 0, tiled=True)]
    all_to_all x1, blocking collectives: 23.2 us -> 21.2 us  [spread(): return lax.all_to_all(copies, axes, 0, 0, tiled=True)]
    ppermute x4 -> x6, starting transfers between devices: 7.8 us -> 7.86 us  [the longest x3 5.97 us: per_device(): lax.ppermute(rows, 'zh', turned[d])]
  transfers between devices with their start and end apart: 28 -> 29, of which waited for: 19 -> 15; matrix products, arithmetic and copies ran while one was open for 0% -> 0% of each run, Pallas kernels for 1% -> 0%
where the time goes in v4:
time: 170 us; the launch traced here: 169 us
  waiting for transfers between devices  54.4 us (32%)
  starting transfers between devices  54 us (32%)
  blocking collectives  42.2 us (25%)
  Pallas kernels  15.5 us (9%)
  local copies, waits for them, and re-layouts  2.66 us (2%)
    all_to_all x1, starting transfers between devices, spread(): return lax.all_to_all(copies, axes, 0, 0, tiled=True)  21.4 us
    all_to_all x1, blocking collectives, spread(): return lax.all_to_all(copies, axes, 0, 0, tiled=True)  21.2 us
    all_to_all x1, blocking collectives, per_device(): arrived = lax.all_to_all(lists, YXZ, 0, 0, tiled=True)  21 us
    all_to_all x1, waiting for transfers between devices, spread(): return lax.all_to_all(copies, axes, 0, 0, tiled=True)  17.3 us
    all_to_all x1, waiting for transfers between devices, per_device(): branch = lax.all_to_all(branch.reshape(32, 8, 1024), XZ, 0, 0, tiled=True)  17 us
    ppermute x12, starting transfers between devices, shifted(): return lax.ppermute(x, 'y', [(i, (i + d) % 4) for i in range(4)])  15.1 us
    ppermute x12, waiting for transfers between devices, shifted(): return lax.ppermute(x, 'y', [(i, (i + d) % 4) for i in range(4)])  7.68 us
    all_to_all x1, starting transfers between devices, per_device(): branch = lax.all_to_all(branch.reshape(32, 8, 1024), XZ, 0, 0, tiled=True)  6.65 us
  transfers between devices with their start and end apart: 29, of which 15 were waited for; matrix products, arithmetic and copies ran while one was open for 0% of the time, Pallas kernels for 0%

profile of v4, /device:TPU:32, one launch (start us, length us, event | category | flops | bytes accessed | tf_op | source)
XLA Modules:
  0.0 169.2 jit_solution(9783887888500593841)
XLA Ops:
  5.7 21.4 %all-to-all-start = ((bf16[32,64,128]{2,1,0:T(8,128)(2,1)}), bf16[32,64,128]{2,1,0:T(8,128)(2,1)S(1)}, u32[]{:S(2)}, u32[]{:S(2)}) async-start(bf16[32,64,128]{2,1,0:T(8,128)(2,1)} %broadcast_in_dim.6), calls=%async_computation | async-start | bytes 1048576 | tf_op jit(solution)/shard_map/all_to_all | solution.py:41
  27.8 17.3 %all-to-all-done.h = bf16[32,64,128]{2,1,0:T(8,128)(2,1)S(1)} async-done(((bf16[32,64,128]{2,1,0:T(8,128)(2,1)}), bf16[32,64,128]{2,1,0:T(8,128)(2,1)S(1)}, u32[]{:S(2)}, u32[]{:S(2)}) %all-to-all-start) | async-done | bytes 524320 | tf_op jit(solution)/shard_map/all_to_all | solution.py:41
  45.2 1.4 gate_up.1
  46.6 1.4 collective-permute-start.6
  47.9 1.3 collective-permute-start.7
  49.2 1.5 collective-permute-start.8
  51.0 4.4 %collective-permute-start.13 = (bf16[64,1024]{1,0:T(8,128)(2,1)S(1)}, bf16[64,1024]{1,0:T(8,128)(2,1)S(1)}, u32[]{:S(2)}, u32[]{:S(2)}) collective-permute-start(bf16[64,1024]{1,0:T(8,128)(2,1)S(1)} %collective-permute-done.1.w0), channel_id=1, source_target_pairs={{0,8},{4,12},{8,0},{12,4},{1,9},{5,13},{9,1},{13,5},{2,10},{6,14},... | collective-permute-start | bytes 393224 | tf_op jit(solution)/shard_map/ppermute | solution.py:383
  55.4 1.3 collective-permute-start.12
  56.8 1.1 collective-permute-start.11
  58.0 2.1 %collective-permute-start.10 = (bf16[64,512]{1,0:T(8,128)(2,1)S(1)}, bf16[64,512]{1,0:T(8,128)(2,1)S(1)}, u32[]{:S(2)}, u32[]{:S(2)}) collective-permute-start(bf16[64,512]{1,0:T(8,128)(2,1)S(1)} %hidden_units.1.a), channel_id=1, source_target_pairs={{0,128},{64,192},{128,0},{192,64},{1,129},{65,193},{129,1},{193,65... | collective-permute-start | bytes 196616 | tf_op jit(solution)/shard_map/ppermute | solution.py:36
  60.1 2.9 %collective-permute-done.14.w3 = bf16[64,1024]{1,0:T(8,128)(2,1)S(1)} collective-permute-done((bf16[64,1024]{1,0:T(8,128)(2,1)S(1)}, bf16[64,1024]{1,0:T(8,128)(2,1)S(1)}, u32[]{:S(2)}, u32[]{:S(2)}) %collective-permute-start.14) | collective-permute-done | bytes 131104 | tf_op jit(solution)/shard_map/ppermute | solution.py:383
  63.0 3.6 %collective-permute-done.12.w1 = bf16[64,1024]{1,0:T(8,128)(2,1)S(1)} collective-permute-done((bf16[64,1024]{1,0:T(8,128)(2,1)S(1)}, bf16[64,1024]{1,0:T(8,128)(2,1)S(1)}, u32[]{:S(2)}, u32[]{:S(2)}) %collective-permute-start.12) | collective-permute-done | bytes 131104 | tf_op jit(solution)/shard_map/ppermute | solution.py:383
  66.5 1.9 %collective-permute-done.9.b = bf16[64,512]{1,0:T(8,128)(2,1)S(1)} collective-permute-done((bf16[64,512]{1,0:T(8,128)(2,1)S(1)}, bf16[64,512]{1,0:T(8,128)(2,1)S(1)}, u32[]{:S(2)}, u32[]{:S(2)}) %collective-permute-start.9) | collective-permute-done | bytes 65568 | tf_op jit(solution)/shard_map/ppermute | solution.py:36
  68.4 1.8 %down.1 = bf16[256,1024]{1,0:T(8,128)(2,1)} custom-call(s32[7]{0:T(128)S(1)} %stack.31.place.refs_0_, bf16[64,512]{1,0:T(8,128)(2,1)S(1)} %hidden_units.1.a, bf16[64,512]{1,0:T(8,128)(2,1)S(1)} %collective-permute-done.9.b, bf16[64,512]{1,0:T(8,128)(2,1)S(1)} %collective-permute-done.10.c, bf16[64,512]{1,0:T(8,128)(2,1)S(1)} %collective-permute-done.11.d, ...), custom_call_target="tpu_custom_call" | custom-call | tf_op jit(solution)/shard_map/down/pallas_call | solution.py:149
  70.2 6.6 %all-to-all-start.1 = ((bf16[32,8,1024]{2,1,0:T(8,128)(2,1)}), bf16[32,8,1024]{2,1,0:T(8,128)(2,1)S(1)}, u32[]{:S(2)}, u32[]{:S(2)}) async-start(bf16[32,8,1024]{2,1,0:T(8,128)(2,1)} %bitcast.9), calls=%async_computation.1 | async-start | bytes 1048576 | tf_op jit(solution)/shard_map/all_to_all | solution.py:390
  76.9 17.0 %all-to-all-done.1.parts = bf16[32,8,1024]{2,1,0:T(8,128)(2,1)S(1)} async-done(((bf16[32,8,1024]{2,1,0:T(8,128)(2,1)}), bf16[32,8,1024]{2,1,0:T(8,128)(2,1)S(1)}, u32[]{:S(2)}, u32[]{:S(2)}) %all-to-all-start.1) | async-done | bytes 524320 | tf_op jit(solution)/shard_map/all_to_all | solution.py:390
  94.9 2.2 %collective-permute-start.16 = (f32[8,128]{1,0:T(8,128)S(1)}, f32[8,128]{1,0:T(8,128)S(1)}, u32[]{:S(2)}, u32[]{:S(2)}) collective-permute-start(f32[8,128]{1,0:T(8,128)S(1)} %get-tuple-element.54.a), channel_id=1, source_target_pairs={{0,128},{64,192},{128,0},{192,64},{1,129},{65,193},{129,1},{193,65... | collective-permute-start | bytes 12296 | tf_op jit(solution)/shard_map/ppermute | solution.py:36
  97.0 1.1 collective-permute-start.15
  98.2 1.8 %collective-permute-done.16.c = f32[8,128]{1,0:T(8,128)S(1)} collective-permute-done((f32[8,128]{1,0:T(8,128)S(1)}, f32[8,128]{1,0:T(8,128)S(1)}, u32[]{:S(2)}, u32[]{:S(2)}) %collective-permute-start.16) | collective-permute-done | bytes 4128 | tf_op jit(solution)/shard_map/ppermute | solution.py:36
  100.0 1.9 %collective-permute-done.15.b = f32[8,128]{1,0:T(8,128)S(1)} collective-permute-done((f32[8,128]{1,0:T(8,128)S(1)}, f32[8,128]{1,0:T(8,128)S(1)}, u32[]{:S(2)}, u32[]{:S(2)}) %collective-permute-start.15) | collective-permute-done | bytes 4128 | tf_op jit(solution)/shard_map/ppermute | solution.py:36
  102.8 1.8 %collective-permute-start.20 = (f32[4,128]{1,0:T(4,128)S(1)}, f32[4,128]{1,0:T(4,128)S(1)}, u32[]{:S(2)}, u32[]{:S(2)}) collective-permute-start(f32[4,128]{1,0:T(4,128)S(1)} %get-tuple-element.58), channel_id=1, source_target_pairs={{0,3},{1,2},{2,1},{3,0},{4,7},{5,6},{6,5},{7,4},{8,11},{9,10},{10,... | collective-permute-start | bytes 6152 | tf_op jit(solution)/shard_map/ppermute | solution.py:399
  104.6 1.8 %collective-permute-done.19.c = f32[4,128]{1,0:T(4,128)S(1)} collective-permute-done((f32[4,128]{1,0:T(4,128)S(1)}, f32[4,128]{1,0:T(4,128)S(1)}, u32[]{:S(2)}, u32[]{:S(2)}) %collective-permute-start.19) | collective-permute-done | bytes 2080 | tf_op jit(solution)/shard_map/ppermute | solution.py:399
  107.2 1.0 collective-permute-done.21
  108.3 21.2 %all_to_all.20 = f32[128,4,128]{2,1,0:T(4,128)S(1)} all-to-all(f32[128,4,128]{2,1,0:T(4,128)S(1)} %broadcast_in_dim.15), channel_id=1, replica_groups=mesh['y'=4,'x'=4,'zh'=4,'zb'=2,'k'=2] {'y','x','zh','zb'}, dimensions={0} | all-to-all | bytes 524288 | tf_op jit(solution)/shard_map/all_to_all | solution.py:41
  130.0 1.2 collective-permute-done.22.refs_2_
  131.2 3.9 %scores.1.a = f32[16,128]{1,0:T(8,128)S(1)} custom-call(s32[7]{0:T(128)S(1)} %stack.31.place.refs_0_, bf16[16,512]{1,0:T(8,128)(2,1)S(1)} %convert_element_type.6.refs_1_, bf16[16,512]{1,0:T(8,128)(2,1)S(1)} %collective-permute-done.22.refs_2_, bf16[512,1024]{1,0:T(8,128)(2,1)S(1)} %copy-done), custom_call_target="tpu_custom_call" | custom-call | tf_op jit(solution)/shard_map/scores/pallas_call | solution.py:281
  137.5 2.1 %collective-permute-start.25 = (f32[4,128]{1,0:T(4,128)S(1)}, f32[4,128]{1,0:T(4,128)S(1)}, u32[]{:S(2)}, u32[]{:S(2)}) collective-permute-start(f32[4,128]{1,0:T(4,128)S(1)} %get-tuple-element.67), channel_id=1, source_target_pairs={{0,128},{64,192},{128,0},{192,64},{1,129},{65,193},{129,1},{193,65... | collective-permute-start | bytes 6152 | tf_op jit(solution)/shard_map/ppermute | solution.py:36
  139.6 1.5 collective-permute-start.26
  141.0 1.2 collective-permute-done.24.b
  143.2 1.6 four_lists.1
  144.7 21.0 %all_to_all.21 = f32[128,4,128]{2,1,0:T(4,128)S(1)} all-to-all(f32[128,4,128]{2,1,0:T(4,128)S(1)} %four_lists.1), channel_id=1, replica_groups=mesh['y'=4,'x'=4,'zh'=4,'zb'=2,'k'=2] {'y','x','zh','zb'}, dimensions={0} | all-to-all | bytes 524288 | tf_op jit(solution)/shard_map/all_to_all | solution.py:409
  165.7 3.5 %final_lists.1 = f32[16,100]{1,0:T(8,128)} custom-call(f32[512,128]{1,0:T(8,128)S(1)} %bitcast.20), custom_call_target="tpu_custom_call" | custom-call | tf_op jit(solution)/shard_map/final_lists/pallas_call | solution.py:349
  (65 shorter events, 13.3 us)
Async XLA Ops:
  0.0 4.8 %collective-permute-start.3 = (bf16[224,1024]{1,0:T(8,128)(2,1)}, bf16[224,1024]{1,0:T(8,128)(2,1)S(1)}, u32[]{:S(2)}, u32[]{:S(2)}) collective-permute-start(bf16[224,1024]{1,0:T(8,128)(2,1)} %bitcast.21), channel_id=1, source_target_pairs={{0,1},{1,0},{2,3},{3,2},{4,5},{5,4},{6,7},{7,6},{8,9},{9,8},{10,11... | collective-permute-start | bytes 1376264 | tf_op jit(solution)/shard_map/ppermute | solution.py:32
  0.0 4.8 %collective-permute-start.4 = (bf16[224,1024]{1,0:T(8,128)(2,1)}, bf16[224,1024]{1,0:T(8,128)(2,1)S(1)}, u32[]{:S(2)}, u32[]{:S(2)}) collective-permute-start(bf16[224,1024]{1,0:T(8,128)(2,1)} %bitcast.23), channel_id=1, source_target_pairs={{0,1},{1,0},{2,3},{3,2},{4,5},{5,4},{6,7},{7,6},{8,9},{9,8},{10,11... | collective-permute-start | bytes 1376264 | tf_op jit(solution)/shard_map/ppermute | solution.py:32
  0.5 4.3 %collective-permute-start.5 = (bf16[224,1024]{1,0:T(8,128)(2,1)}, bf16[224,1024]{1,0:T(8,128)(2,1)S(1)}, u32[]{:S(2)}, u32[]{:S(2)}) collective-permute-start(bf16[224,1024]{1,0:T(8,128)(2,1)} %w0.1), channel_id=1, source_target_pairs={{0,1},{1,0},{2,3},{3,2},{4,5},{5,4},{6,7},{7,6},{8,9},{9,8},{10,11... | collective-permute-start | bytes 1376264 | tf_op jit(solution)/shard_map/ppermute | solution.py:32
  2.6 1.3 collective-permute-start
  3.3 1.4 collective-permute-start.2
  5.7 39.5 %copy-start.1 = (bf16[1024,224]{0,1:T(8,128)(2,1)S(1)}, bf16[1024,224]{0,1:T(8,128)(2,1)}, u32[]{:S(2)}) copy-start(bf16[1024,224]{0,1:T(8,128)(2,1)} %param.9) | copy-start | bytes 1376260
  5.7 39.5 %copy-start.2 = (bf16[1024,224]{0,1:T(8,128)(2,1)S(1)}, bf16[1024,224]{0,1:T(8,128)(2,1)}, u32[]{:S(2)}) copy-start(bf16[1024,224]{0,1:T(8,128)(2,1)} %param.10) | copy-start | bytes 1376260
  5.7 39.5 %all-to-all-start = ((bf16[32,64,128]{2,1,0:T(8,128)(2,1)}), bf16[32,64,128]{2,1,0:T(8,128)(2,1)S(1)}, u32[]{:S(2)}, u32[]{:S(2)}) async-start(bf16[32,64,128]{2,1,0:T(8,128)(2,1)} %broadcast_in_dim.6), calls=%async_computation | async-start | bytes 1048576 | tf_op jit(solution)/shard_map/all_to_all | solution.py:41
  27.2 0.7 collective-permute-start.1
  46.6 8.9 %collective-permute-start.6 = (bf16[64,1024]{1,0:T(8,128)(2,1)S(1)}, bf16[64,1024]{1,0:T(8,128)(2,1)S(1)}, u32[]{:S(2)}, u32[]{:S(2)}) collective-permute-start(bf16[64,1024]{1,0:T(8,128)(2,1)S(1)} %get-tuple-element.44), channel_id=1, source_target_pairs={{0,64},{64,128},{128,192},{192,0},{1,65},{65,129},{129,193},{193,1... | collective-permute-start | bytes 393224 | tf_op jit(solution)/shard_map/ppermute | solution.py:36
  47.9 8.7 %collective-permute-start.7 = (bf16[64,1024]{1,0:T(8,128)(2,1)S(1)}, bf16[64,1024]{1,0:T(8,128)(2,1)S(1)}, u32[]{:S(2)}, u32[]{:S(2)}) collective-permute-start(bf16[64,1024]{1,0:T(8,128)(2,1)S(1)} %get-tuple-element.45), channel_id=1, source_target_pairs={{0,128},{64,192},{128,0},{192,64},{1,129},{65,193},{129,1},{193,65... | collective-permute-start | bytes 393224 | tf_op jit(solution)/shard_map/ppermute | solution.py:36
  49.2 7.5 %collective-permute-start.8 = (bf16[64,1024]{1,0:T(8,128)(2,1)S(1)}, bf16[64,1024]{1,0:T(8,128)(2,1)S(1)}, u32[]{:S(2)}, u32[]{:S(2)}) collective-permute-start(bf16[64,1024]{1,0:T(8,128)(2,1)S(1)} %get-tuple-element.46), channel_id=1, source_target_pairs={{0,192},{64,0},{128,64},{192,128},{1,193},{65,1},{129,65},{193,129... | collective-permute-start | bytes 393224 | tf_op jit(solution)/shard_map/ppermute | solution.py:36
  50.7 12.2 %collective-permute-start.14 = (bf16[64,1024]{1,0:T(8,128)(2,1)S(1)}, bf16[64,1024]{1,0:T(8,128)(2,1)S(1)}, u32[]{:S(2)}, u32[]{:S(2)}) collective-permute-start(bf16[64,1024]{1,0:T(8,128)(2,1)S(1)} %collective-permute-done.1.w0), channel_id=1, source_target_pairs={{0,12},{4,0},{8,4},{12,8},{1,13},{5,1},{9,5},{13,9},{2,14},{6,2},{... | collective-permute-start | bytes 393224 | tf_op jit(solution)/shard_map/ppermute | solution.py:383
  51.0 11.9 %collective-permute-start.13 = (bf16[64,1024]{1,0:T(8,128)(2,1)S(1)}, bf16[64,1024]{1,0:T(8,128)(2,1)S(1)}, u32[]{:S(2)}, u32[]{:S(2)}) collective-permute-start(bf16[64,1024]{1,0:T(8,128)(2,1)S(1)} %collective-permute-done.1.w0), channel_id=1, source_target_pairs={{0,8},{4,12},{8,0},{12,4},{1,9},{5,13},{9,1},{13,5},{2,10},{6,14},... | collective-permute-start | bytes 393224 | tf_op jit(solution)/shard_map/ppermute | solution.py:383
  55.4 11.1 %collective-permute-start.12 = (bf16[64,1024]{1,0:T(8,128)(2,1)S(1)}, bf16[64,1024]{1,0:T(8,128)(2,1)S(1)}, u32[]{:S(2)}, u32[]{:S(2)}) collective-permute-start(bf16[64,1024]{1,0:T(8,128)(2,1)S(1)} %collective-permute-done.1.w0), channel_id=1, source_target_pairs={{0,4},{4,8},{8,12},{12,0},{1,5},{5,9},{9,13},{13,1},{2,6},{6,10},{... | collective-permute-start | bytes 393224 | tf_op jit(solution)/shard_map/ppermute | solution.py:383
  56.8 9.7 %collective-permute-start.11 = (bf16[64,512]{1,0:T(8,128)(2,1)S(1)}, bf16[64,512]{1,0:T(8,128)(2,1)S(1)}, u32[]{:S(2)}, u32[]{:S(2)}) collective-permute-start(bf16[64,512]{1,0:T(8,128)(2,1)S(1)} %hidden_units.1.a), channel_id=1, source_target_pairs={{0,192},{64,0},{128,64},{192,128},{1,193},{65,1},{129,65},{193,129... | collective-permute-start | bytes 196616 | tf_op jit(solution)/shard_map/ppermute | solution.py:36
  58.0 8.6 %collective-permute-start.10 = (bf16[64,512]{1,0:T(8,128)(2,1)S(1)}, bf16[64,512]{1,0:T(8,128)(2,1)S(1)}, u32[]{:S(2)}, u32[]{:S(2)}) collective-permute-start(bf16[64,512]{1,0:T(8,128)(2,1)S(1)} %hidden_units.1.a), channel_id=1, source_target_pairs={{0,128},{64,192},{128,0},{192,64},{1,129},{65,193},{129,1},{193,65... | collective-permute-start | bytes 196616 | tf_op jit(solution)/shard_map/ppermute | solution.py:36
  62.9 5.5 %collective-permute-start.9 = (bf16[64,512]{1,0:T(8,128)(2,1)S(1)}, bf16[64,512]{1,0:T(8,128)(2,1)S(1)}, u32[]{:S(2)}, u32[]{:S(2)}) collective-permute-start(bf16[64,512]{1,0:T(8,128)(2,1)S(1)} %hidden_units.1.a), channel_id=1, source_target_pairs={{0,64},{64,128},{128,192},{192,0},{1,65},{65,129},{129,193},{193,1... | collective-permute-start | bytes 196616 | tf_op jit(solution)/shard_map/ppermute | solution.py:36
  70.2 23.7 %all-to-all-start.1 = ((bf16[32,8,1024]{2,1,0:T(8,128)(2,1)}), bf16[32,8,1024]{2,1,0:T(8,128)(2,1)S(1)}, u32[]{:S(2)}, u32[]{:S(2)}) async-start(bf16[32,8,1024]{2,1,0:T(8,128)(2,1)} %bitcast.9), calls=%async_computation.1 | async-start | bytes 1048576 | tf_op jit(solution)/shard_map/all_to_all | solution.py:390
  94.1 4.1 %collective-permute-start.17 = (f32[8,128]{1,0:T(8,128)S(1)}, f32[8,128]{1,0:T(8,128)S(1)}, u32[]{:S(2)}, u32[]{:S(2)}) collective-permute-start(f32[8,128]{1,0:T(8,128)S(1)} %get-tuple-element.54.a), channel_id=1, source_target_pairs={{0,192},{64,0},{128,64},{192,128},{1,193},{65,1},{129,65},{193,129... | collective-permute-start | bytes 12296 | tf_op jit(solution)/shard_map/ppermute | solution.py:36
  94.9 5.1 %collective-permute-start.16 = (f32[8,128]{1,0:T(8,128)S(1)}, f32[8,128]{1,0:T(8,128)S(1)}, u32[]{:S(2)}, u32[]{:S(2)}) collective-permute-start(f32[8,128]{1,0:T(8,128)S(1)} %get-tuple-element.54.a), channel_id=1, source_target_pairs={{0,128},{64,192},{128,0},{192,64},{1,129},{65,193},{129,1},{193,65... | collective-permute-start | bytes 12296 | tf_op jit(solution)/shard_map/ppermute | solution.py:36
  97.0 4.8 %collective-permute-start.15 = (f32[8,128]{1,0:T(8,128)S(1)}, f32[8,128]{1,0:T(8,128)S(1)}, u32[]{:S(2)}, u32[]{:S(2)}) collective-permute-start(f32[8,128]{1,0:T(8,128)S(1)} %get-tuple-element.54.a), channel_id=1, source_target_pairs={{0,64},{64,128},{128,192},{192,0},{1,65},{65,129},{129,193},{193,1... | collective-permute-start | bytes 12296 | tf_op jit(solution)/shard_map/ppermute | solution.py:36
  102.7 1.9 %collective-permute-start.18 = (f32[4,128]{1,0:T(4,128)S(1)}, f32[4,128]{1,0:T(4,128)S(1)}, u32[]{:S(2)}, u32[]{:S(2)}) collective-permute-start(f32[4,128]{1,0:T(4,128)S(1)} %get-tuple-element.56), channel_id=1, source_target_pairs={{0,1},{1,0},{2,3},{3,2},{4,5},{5,4},{6,7},{7,6},{8,9},{9,8},{10,11... | collective-permute-start | bytes 6152 | tf_op jit(solution)/shard_map/ppermute | solution.py:399
  102.7 3.7 %collective-permute-start.19 = (f32[4,128]{1,0:T(4,128)S(1)}, f32[4,128]{1,0:T(4,128)S(1)}, u32[]{:S(2)}, u32[]{:S(2)}) collective-permute-start(f32[4,128]{1,0:T(4,128)S(1)} %get-tuple-element.57), channel_id=1, source_target_pairs={{0,2},{1,3},{2,0},{3,1},{4,6},{5,7},{6,4},{7,5},{8,10},{9,11},{10,... | collective-permute-start | bytes 6152 | tf_op jit(solution)/shard_map/ppermute | solution.py:399
  102.8 3.6 %collective-permute-start.20 = (f32[4,128]{1,0:T(4,128)S(1)}, f32[4,128]{1,0:T(4,128)S(1)}, u32[]{:S(2)}, u32[]{:S(2)}) collective-permute-start(f32[4,128]{1,0:T(4,128)S(1)} %get-tuple-element.58), channel_id=1, source_target_pairs={{0,3},{1,2},{2,1},{3,0},{4,7},{5,6},{6,5},{7,4},{8,11},{9,10},{10,... | collective-permute-start | bytes 6152 | tf_op jit(solution)/shard_map/ppermute | solution.py:399
  106.4 24.8 %copy-start = (bf16[512,1024]{1,0:T(8,128)(2,1)S(1)}, bf16[512,1024]{1,0:T(8,128)(2,1)}, u32[]{:S(2)}) copy-start(bf16[512,1024]{1,0:T(8,128)(2,1)} %refs_3_.1) | copy-start | bytes 3145732
  107.1 1.2 collective-permute-start.21
  129.9 1.3 collective-permute-start.22
  135.1 1.3 collective-permute-start.23
  137.4 4.9 %collective-permute-start.24 = (f32[4,128]{1,0:T(4,128)S(1)}, f32[4,128]{1,0:T(4,128)S(1)}, u32[]{:S(2)}, u32[]{:S(2)}) collective-permute-start(f32[4,128]{1,0:T(4,128)S(1)} %get-tuple-element.66), channel_id=1, source_target_pairs={{0,64},{64,128},{128,192},{192,0},{1,65},{65,129},{129,193},{193,1... | collective-permute-start | bytes 6152 | tf_op jit(solution)/shard_map/ppermute | solution.py:36
  137.5 5.2 %collective-permute-start.25 = (f32[4,128]{1,0:T(4,128)S(1)}, f32[4,128]{1,0:T(4,128)S(1)}, u32[]{:S(2)}, u32[]{:S(2)}) collective-permute-start(f32[4,128]{1,0:T(4,128)S(1)} %get-tuple-element.67), channel_id=1, source_target_pairs={{0,128},{64,192},{128,0},{192,64},{1,129},{65,193},{129,1},{193,65... | collective-permute-start | bytes 6152 | tf_op jit(solution)/shard_map/ppermute | solution.py:36
  139.6 3.6 %collective-permute-start.26 = (f32[4,128]{1,0:T(4,128)S(1)}, f32[4,128]{1,0:T(4,128)S(1)}, u32[]{:S(2)}, u32[]{:S(2)}) collective-permute-start(f32[4,128]{1,0:T(4,128)S(1)} %get-tuple-element.68), channel_id=1, source_target_pairs={{0,192},{64,0},{128,64},{192,128},{1,193},{65,1},{129,65},{193,129... | collective-permute-start | bytes 6152 | tf_op jit(solution)/shard_map/ppermute | solution.py:36
  (4 other events, 44.7 us)

commit v5 on v4

--- a/solution.py
+++ b/solution.py
@@ -176,8 +176,8 @@
     )(parts, h)
 
 
-def pool_kernel(place, counts, res, a, b, c, d, o0, o1, o2, o3):
-    k, first, row, zb = place[1], place[2], place[4], place[6]
+def pool_kernel(place, counts, res, a, b, c, d, same, other):
+    first, row, zb = place[2], place[4], place[6]
     sq = (a[...] + b[...] + c[...] + d[...])[:, 0:1]
     slots = lax.broadcasted_iota(jnp.int32, (8, 1), 0) + first
     held = counts[...].astype(F32)
@@ -187,42 +187,40 @@
     pooled = jnp.sum(res[...] * weight, axis=0, keepdims=True) / count
     ahead = jnp.concatenate([pooled[:, t * 256 : t * 256 + 128] for t in range(4)], axis=0)
     behind = jnp.concatenate([pooled[:, t * 256 + 128 : t * 256 + 256] for t in range(4)], axis=0)
-    for r, out in enumerate((o0, o1, o2, o3)):
-        part = jnp.where(zb == r // 2, ahead, behind)
-        out[...] = jnp.where(k == r % 2, part, pltpu.roll(part, 64, 1))
+    same[...] = jnp.where(zb == 0, ahead, behind)
+    other[...] = jnp.where(zb == 0, behind, ahead)
 
 
 def pool(place, counts, res, sqs):
     part = shape((4, 128), F32)
     return pl.pallas_call(
         pool_kernel,
-        out_shape=(part,) * 4,
+        out_shape=(part,) * 2,
         in_specs=[SMEM] + [VMEM] * 6,
-        out_specs=(VMEM,) * 4,
+        out_specs=(VMEM,) * 2,
         compiler_params=PARAMS,
         name="pool",
     )(place, counts, res, *sqs)
 
 
-def code_kernel(place, a, b, c, d, w0, w1, w2, w3, keep, send, left):
-    k, zh = place[1], place[5]
+def code_kernel(place, a, b, c, d, w0, w1, w2, w3, out, left):
+    zh = place[5]
     left[...] = a[...] + b[...] + c[...] + d[...]
-    total = jnp.zeros((8, 1024), F32)
+    total = jnp.zeros((8, 512), F32)
     for s, w in enumerate((w0, w1, w2, w3)):
         piece = jnp.broadcast_to(left[pl.ds((zh - s + 4) % 4, 1), :], (8, 128))
-        total += jnp.dot(piece[:, 0:64].astype(BF16), w[...], preferred_element_type=F32)
-    low, high = total[0:1, 0:512], total[0:1, 512:1024]
-    keep[...] = jnp.where(k == 0, low, high)
-    send[...] = jnp.where(k == 0, high, low)
+        total += jnp.dot(piece.astype(BF16), w[...], preferred_element_type=F32)
+    for t in range(4):
+        left[t : t + 1, :] = total[0:1, t * 128 : t * 128 + 128]
+    out[...] = jnp.broadcast_to(left[...][None], (128, 4, 128))
 
 
 def code_part(place, pieces, ws):
-    half = shape((1, 512), F32)
     return pl.pallas_call(
         code_kernel,
-        out_shape=(half, half),
+        out_shape=shape((128, 4, 128), F32),
         in_specs=[SMEM] + [VMEM] * 8,
-        out_specs=(VMEM,) * 2,
+        out_specs=VMEM,
         scratch_shapes=[pltpu.VMEM((4, 128), F32)],
         compiler_params=PARAMS,
         name="code_part",
@@ -253,6 +251,74 @@
     return x
 
 
+def halves_far(v, apart, falling):
+    out = list(v)
+    for i in range(len(v)):
+        if i & apart == 0:
+            high, low = jnp.maximum(v[i], v[i + apart]), jnp.minimum(v[i], v[i + apart])
+            way = falling(i)
+            if way is True:
+                out[i], out[i + apart] = high, low
+            elif way is False:
+                out[i], out[i + apart] = low, high
+            else:
+                out[i] = jnp.where(way, high, low)
+                out[i + apart] = jnp.where(way, low, high)
+    return out
+
+
+def halves_near(v, step, falling):
+    upper = (rows_of((8, 128)) & step) != 0
+    out = []
+    for i, x in enumerate(v):
+        other = pltpu.roll(x, step, 0)
+        if step != 4:
+            other = jnp.where(upper, other, pltpu.roll(x, 8 - step, 0))
+        way = falling(i)
+        if way is True:
+            take = ~upper
+        elif way is False:
+            take = upper
+        else:
+            take = upper ^ way
+        out.append(jnp.where(take, jnp.maximum(x, other), jnp.minimum(x, other)))
+    return out
+
+
+def column_step(v, step, falling):
+    if step >= 8:
+        return halves_far(v, step // 8, falling)
+    return halves_near(v, step, falling)
+
+
+def column_merge(v, falling):
+    for step in (64, 32, 16, 8, 4, 2, 1):
+        v = column_step(v, step, lambda i: falling)
+    return v
+
+
+def column_sort(v, falling):
+    sub = rows_of((8, 128))
+    for size in (2, 4, 8, 16, 32, 64, 128):
+
+        def way(i, size=size):
+            if size == 128:
+                return falling
+            if size >= 8:
+                return (i * 8) & size == 0
+            return (sub & size) == 0
+
+        step = size // 2
+        while step:
+            v = column_step(v, step, way)
+            step //= 2
+    return v
+
+
+def columns_of(x):
+    return [x[i * 8 : i * 8 + 8] for i in range(16)]
+
+
 def rows_of(like):
     return lax.broadcasted_iota(jnp.int32, like, 0)
 
@@ -266,12 +332,14 @@
     scores = lax.dot_general(low, docs[:, 0:512], dims, preferred_element_type=F32)
     scores += lax.dot_general(high, docs[:, 512:1024], dims, preferred_element_type=F32)
     scores = scores * scale
-    x = jnp.concatenate([scores[:, c * 128 : c * 128 + 128] for c in range(4)], axis=0)
-    x = bitonic_sort(x, rows_of((64, 128)) < 32)
-    x = jnp.maximum(x[0:32], x[32:64])
-    x = bitonic_merge(x, rows_of((32, 128)) < 16)
-    x = jnp.maximum(x[0:16], x[16:32])
-    lists[...] = bitonic_merge(x, rows_of((16, 128)) * 0 + k == 0)
+    x = jnp.concatenate([scores[:, c * 128 : c * 128 + 128] for c in range(4)] * 2, axis=0)
+    lane = lanes((8, 128))
+    v = column_sort(columns_of(x.T), lane & 32 == 0)
+    v = [jnp.maximum(a, pltpu.roll(a, 96, 1)) for a in v]
+    v = column_merge(v, lane & 16 == 0)
+    v = [jnp.maximum(a, pltpu.roll(a, 112, 1)) for a in v]
+    v = column_merge(v, lane * 0 + k == 0)
+    lists[...] = jnp.concatenate(v, axis=0).T[0:16]
 
 
 def local_lists(place, mine, theirs, docs):
@@ -333,16 +401,30 @@
 
 
 def final_kernel(x_ref, out):
-    x = x_ref[...]
-    for groups in (32, 16, 8, 4):
-        x = x.reshape(groups, 2, 8, 128)
-        x = jnp.maximum(x[:, 0], x[:, 1]).reshape(groups * 8, 128)
-        row = rows_of(x.shape)
-        x = bitonic_merge(x, row % 8 < 4 if groups == 4 else (row // 8) % 2 == 0)
-    x = jnp.maximum(x, pltpu.roll(x, 4, 0))
-    x = bitonic_merge(x, rows_of(x.shape) >= 0)
+    lane = lanes((8, 128))
+    tiles = []
     for y in range(4):
-        out[y * 4 : y * 4 + 4, :] = x[y * 8 + 4 : y * 8 + 8, 0:TOPK]
+        v = columns_of(x_ref[y * 128 : y * 128 + 128, :].T)
+        tiles.append([jnp.maximum(a, pltpu.roll(a, 64, 1)) for a in v])
+    first = [jnp.where(lane < 64, a, b) for a, b in zip(tiles[0], tiles[1])]
+    second = [jnp.where(lane < 64, a, b) for a, b in zip(tiles[2], tiles[3])]
+    first = column_merge(first, lane & 32 == 0)
+    second = column_merge(second, lane & 32 == 0)
+    v = [
+        jnp.where(
+            lane & 32 == 0,
+            jnp.maximum(a, pltpu.roll(a, 96, 1)),
+            jnp.maximum(b, pltpu.roll(b, 32, 1)),
+        )
+        for a, b in zip(first, second)
+    ]
+    for near in (16, 8, 4):
+        v = column_merge(v, lane & near == 0)
+        v = [jnp.maximum(a, pltpu.roll(a, 128 - near, 1)) for a in v]
+    v = column_merge(v, True)
+    x = jnp.concatenate(v, axis=0).T
+    for y, row in enumerate((0, 64, 32, 96)):
+        out[y * 4 : y * 4 + 4, :] = x[row : row + 4, 0:TOPK]
 
 
 def final_lists(x):
@@ -358,7 +440,7 @@
 
 def per_device(hidden_in, lengths, gate_weight, up_weight, down_weight, code_weight, corpus_codes):
     y, x, zh, zb, k = (lax.axis_index(a) for a in QUERY_CORPUS)
-    place = jnp.stack([y, k, 16 * k + 8 * zb, zh % 2, 4 * zh, zh, zb]).astype(jnp.int32)
+    place = jnp.stack([y, k, 16 * k + 8 * zb, x // 2, 4 * zh, zh, zb]).astype(jnp.int32)
 
     own, other = pack(place, lengths, hidden_in)
     swap = [(a * 4 + b, b * 4 + a) for a in range(4) for b in range(4)]
@@ -377,7 +459,12 @@
     )
     gathered = spread(block, XZ, 32)
 
-    rows = lax.ppermute(code_weight, ("y", "x"), swap)
+    low, high = code_weight[:, :512], code_weight[:, 512:]
+    mine = lax.ppermute(jnp.where(k == 0, low, high), ("y", "x", "k"), straight)
+    theirs = lax.ppermute(jnp.where(k == 0, high, low), ("y", "x", "k"), crossed)
+    rows = jnp.concatenate(
+        [jnp.where(k == 0, mine, theirs), jnp.where(k == 0, theirs, mine)], axis=0
+    )
     rows, gathered = lax.optimization_barrier((rows, gathered))
     turned = [[(i, (i + d) % 4) for i in range(4)] for d in range(4)]
     code_rows = (rows, *(lax.ppermute(rows, "zh", turned[d]) for d in (1, 2, 3)))
@@ -385,7 +472,6 @@
     parts = gate_up(place, gathered, gate_rows, up_rows, gate_peer, up_peer)
     units = hidden_of(parts[0], *(shifted(parts[d], d) for d in (1, 2, 3)))
     groups = (units, *(shifted(units, d) for d in (1, 2, 3)))
-    groups, code_rows = lax.optimization_barrier((groups, code_rows))
     branch = down(place, groups, down_weight, down_peer)
     branch = lax.all_to_all(branch.reshape(32, 8, 1024), XZ, 0, 0, tiled=True)
     here = lax.dynamic_slice(
@@ -394,12 +480,13 @@
     here = jnp.moveaxis(here, 0, 1).reshape(8, 1024)
     res, sq = residual_of(branch, here)
     sqs = (sq, *(shifted(sq, d) for d in (1, 2, 3)))
-    mine = pool(place, counts, res, sqs)
+    same, other = pool(place, counts, res, sqs)
     flips = [[(i, i ^ r) for i in range(4)] for r in range(4)]
-    pieces = (mine[0], *(lax.ppermute(mine[r], ("zb", "k"), flips[r]) for r in (1, 2, 3)))
-    keep, send = code_part(place, pieces, code_rows)
-    part = (keep + to_peer(send)).reshape(4, 128)
-    codes = spread(part, YXZ, 128).reshape(4, 4, 4, 2, 512).sum(axis=(0, 3))
+    sent = ((same, 1), (other, 2), (other, 3))
+    pieces = (same, *(lax.ppermute(a, ("zb", "k"), flips[r]) for a, r in sent))
+    part = code_part(place, pieces, code_rows)
+    codes = lax.all_to_all(part, YXZ, 0, 0, tiled=True)
+    codes = codes.reshape(4, 4, 4, 2, 512).sum(axis=(0, 3))
     codes = codes.reshape(16, 512).astype(BF16)
 
     lists = local_lists(place, codes, to_peer(codes), corpus_codes)

time: 170 us -> 167 us (0.982)
  Pallas kernels: 15.5 us -> 11 us
  starting transfers between devices: 54 us -> 56.2 us
    ppermute x12, waiting for transfers between devices: 7.68 us -> 18.5 us  [shifted(): return lax.ppermute(x, 'y', [(i, (i + d) % 4) for i in range(4)])]
    ppermute x3, waiting for transfers between devices: 6.48 us -> 0.01 us  [per_device(): lax.ppermute(rows, 'zh', turned[d])]
    all_to_all x1, waiting for transfers between devices: 17 us -> 12.9 us  [per_device(): branch = lax.all_to_all(branch.reshape(32, 8, 1024), XZ, 0, 0, tiled=True)]
    pallas_call x1, Pallas kernels: 3.95 us -> 1.51 us  [local_lists(): pl.pallas_call(body, out_shape=shape((16, 128), F32), in_specs=[SMEM] + [...]
    pallas_call x1, Pallas kernels: 3.47 us -> 1.42 us  [final_lists(): pl.pallas_call(final_kernel, out_shape=shape((16, TOPK), F32), in_specs=[...]
    all_to_all x1, starting transfers between devices: 6.65 us -> 8.63 us  [per_device(): branch = lax.all_to_all(branch.reshape(32, 8, 1024), XZ, 0, 0, tiled=True)]
  transfers between devices with their start and end apart: 29 -> 29, of which waited for: 15 -> 20; matrix products, arithmetic and copies ran while one was open for 0% -> 0% of each run, Pallas kernels for 0% -> 1%
where the time goes in v5:
time: 167 us; the launch traced here: 166 us
  starting transfers between devices  56.2 us (34%)
  waiting for transfers between devices  53.1 us (32%)
  blocking collectives  42.8 us (26%)
  Pallas kernels  11 us (7%)
  local copies, waits for them, and re-layouts  2.62 us (2%)
    all_to_all x1, blocking collectives, per_device(): codes = lax.all_to_all(part, YXZ, 0, 0, tiled=True)  21.8 us
    all_to_all x1, starting transfers between devices, spread(): return lax.all_to_all(copies, axes, 0, 0, tiled=True)  21.4 us
    all_to_all x1, blocking collectives, per_device(): arrived = lax.all_to_all(lists, YXZ, 0, 0, tiled=True)  21 us
    ppermute x12, waiting for transfers between devices, shifted(): return lax.ppermute(x, 'y', [(i, (i + d) % 4) for i in range(4)])  18.5 us
    all_to_all x1, waiting for transfers between devices, spread(): return lax.all_to_all(copies, axes, 0, 0, tiled=True)  15.8 us
    ppermute x12, starting transfers between devices, shifted(): return lax.ppermute(x, 'y', [(i, (i + d) % 4) for i in range(4)])  13.5 us
    all_to_all x1, waiting for transfers between devices, per_device(): branch = lax.all_to_all(branch.reshape(32, 8, 1024), XZ, 0, 0, tiled=True)  12.9 us
    all_to_all x1, starting transfers between devices, per_device(): branch = lax.all_to_all(branch.reshape(32, 8, 1024), XZ, 0, 0, tiled=True)  8.63 us
  transfers between devices with their start and end apart: 29, of which 20 were waited for; matrix products, arithmetic and copies ran while one was open for 0% of the time, Pallas kernels for 1%

profile of v5, /device:TPU:32, one launch (start us, length us, event | category | flops | bytes accessed | tf_op | source)
XLA Modules:
  0.0 166.3 jit_solution(8598966669808360450)
XLA Ops:
  5.7 21.4 %all-to-all-start = ((bf16[32,64,128]{2,1,0:T(8,128)(2,1)}), bf16[32,64,128]{2,1,0:T(8,128)(2,1)S(1)}, u32[]{:S(2)}, u32[]{:S(2)}) async-start(bf16[32,64,128]{2,1,0:T(8,128)(2,1)} %broadcast_in_dim.2), calls=%async_computation | async-start | bytes 1048576 | tf_op jit(solution)/shard_map/all_to_all | solution.py:41
  28.1 1.2 collective-permute-done.2
  29.4 15.8 %all-to-all-done.h = bf16[32,64,128]{2,1,0:T(8,128)(2,1)S(1)} async-done(((bf16[32,64,128]{2,1,0:T(8,128)(2,1)}), bf16[32,64,128]{2,1,0:T(8,128)(2,1)S(1)}, u32[]{:S(2)}, u32[]{:S(2)}) %all-to-all-start) | async-done | bytes 524320 | tf_op jit(solution)/shard_map/all_to_all | solution.py:41
  45.2 1.4 gate_up.1
  46.6 1.4 collective-permute-start.7
  47.9 1.3 collective-permute-start.8
  49.2 1.5 collective-permute-start.9
  50.7 2.2 %collective-permute-done.7.b = bf16[64,1024]{1,0:T(8,128)(2,1)S(1)} collective-permute-done((bf16[64,1024]{1,0:T(8,128)(2,1)S(1)}, bf16[64,1024]{1,0:T(8,128)(2,1)S(1)}, u32[]{:S(2)}, u32[]{:S(2)}) %collective-permute-start.7) | collective-permute-done | bytes 131104 | tf_op jit(solution)/shard_map/ppermute | solution.py:36
  52.9 1.5 collective-permute-done.8.c
  55.5 2.5 %collective-permute-start.12 = (bf16[64,512]{1,0:T(8,128)(2,1)S(1)}, bf16[64,512]{1,0:T(8,128)(2,1)S(1)}, u32[]{:S(2)}, u32[]{:S(2)}) collective-permute-start(bf16[64,512]{1,0:T(8,128)(2,1)S(1)} %hidden_units.1.a), channel_id=1, source_target_pairs={{0,192},{64,0},{128,64},{192,128},{1,193},{65,1},{129,65},{193,129... | collective-permute-start | bytes 196616 | tf_op jit(solution)/shard_map/ppermute | solution.py:36
  58.9 1.6 collective-permute-done.12.d
  60.5 3.4 %collective-permute-done.11.c = bf16[64,512]{1,0:T(8,128)(2,1)S(1)} collective-permute-done((bf16[64,512]{1,0:T(8,128)(2,1)S(1)}, bf16[64,512]{1,0:T(8,128)(2,1)S(1)}, u32[]{:S(2)}, u32[]{:S(2)}) %collective-permute-start.11) | collective-permute-done | bytes 65568 | tf_op jit(solution)/shard_map/ppermute | solution.py:36
  64.4 1.8 %down.1 = bf16[256,1024]{1,0:T(8,128)(2,1)} custom-call(s32[7]{0:T(128)S(1)} %stack.31.place.refs_0_, bf16[64,512]{1,0:T(8,128)(2,1)S(1)} %hidden_units.1.a, bf16[64,512]{1,0:T(8,128)(2,1)S(1)} %collective-permute-done.10.b, bf16[64,512]{1,0:T(8,128)(2,1)S(1)} %collective-permute-done.11.c, bf16[64,512]{1,0:T(8,128)(2,1)S(1)} %collective-permute-done.12.d, ...), custom_call_target="tpu_custom_call" | custom-call | tf_op jit(solution)/shard_map/down/pallas_call | solution.py:149
  66.2 8.6 %all-to-all-start.1 = ((bf16[32,8,1024]{2,1,0:T(8,128)(2,1)}), bf16[32,8,1024]{2,1,0:T(8,128)(2,1)S(1)}, u32[]{:S(2)}, u32[]{:S(2)}) async-start(bf16[32,8,1024]{2,1,0:T(8,128)(2,1)} %bitcast.9), calls=%async_computation.1 | async-start | bytes 1048576 | tf_op jit(solution)/shard_map/all_to_all | solution.py:476
  74.8 2.8 %collective-permute-start.21 = (bf16[128,512]{1,0:T(8,128)(2,1)S(1)}, bf16[128,512]{1,0:T(8,128)(2,1)S(1)}, u32[]{:S(2)}, u32[]{:S(2)}) collective-permute-start(bf16[128,512]{1,0:T(8,128)(2,1)S(1)} %pad_maximum_fusion.w0), channel_id=1, source_target_pairs={{0,12},{4,0},{8,4},{12,8},{1,13},{5,1},{9,5},{13,9},{2,14},{6,2},{... | collective-permute-start | bytes 393224 | tf_op jit(solution)/shard_map/ppermute | solution.py:470
  77.6 3.3 %collective-permute-start.20 = (bf16[128,512]{1,0:T(8,128)(2,1)S(1)}, bf16[128,512]{1,0:T(8,128)(2,1)S(1)}, u32[]{:S(2)}, u32[]{:S(2)}) collective-permute-start(bf16[128,512]{1,0:T(8,128)(2,1)S(1)} %pad_maximum_fusion.w0), channel_id=1, source_target_pairs={{0,8},{4,12},{8,0},{12,4},{1,9},{5,13},{9,1},{13,5},{2,10},{6,14},... | collective-permute-start | bytes 393224 | tf_op jit(solution)/shard_map/ppermute | solution.py:470
  80.8 1.5 collective-permute-start.19
  82.3 12.9 %all-to-all-done.1.parts = bf16[32,8,1024]{2,1,0:T(8,128)(2,1)S(1)} async-done(((bf16[32,8,1024]{2,1,0:T(8,128)(2,1)}), bf16[32,8,1024]{2,1,0:T(8,128)(2,1)S(1)}, u32[]{:S(2)}, u32[]{:S(2)}) %all-to-all-start.1) | async-done | bytes 524320 | tf_op jit(solution)/shard_map/all_to_all | solution.py:476
  95.4 1.4 collective-permute-start.15
  97.6 1.6 collective-permute-done.15.d
  99.2 2.7 %collective-permute-done.14.c = f32[8,128]{1,0:T(8,128)S(1)} collective-permute-done((f32[8,128]{1,0:T(8,128)S(1)}, f32[8,128]{1,0:T(8,128)S(1)}, u32[]{:S(2)}, u32[]{:S(2)}) %collective-permute-start.14) | collective-permute-done | bytes 4128 | tf_op jit(solution)/shard_map/ppermute | solution.py:36
  101.8 2.1 %collective-permute-done.13.b = f32[8,128]{1,0:T(8,128)S(1)} collective-permute-done((f32[8,128]{1,0:T(8,128)S(1)}, f32[8,128]{1,0:T(8,128)S(1)}, u32[]{:S(2)}, u32[]{:S(2)}) %collective-permute-start.13) | collective-permute-done | bytes 4128 | tf_op jit(solution)/shard_map/ppermute | solution.py:36
  104.9 2.0 %collective-permute-start.17 = (f32[4,128]{1,0:T(4,128)S(1)}, f32[4,128]{1,0:T(4,128)S(1)}, u32[]{:S(2)}, u32[]{:S(2)}) collective-permute-start(f32[4,128]{1,0:T(4,128)S(1)} %get-tuple-element.39), channel_id=1, source_target_pairs={{0,2},{1,3},{2,0},{3,1},{4,6},{5,7},{6,4},{7,5},{8,10},{9,11},{10,... | collective-permute-start | bytes 6152 | tf_op jit(solution)/shard_map/ppermute | solution.py:486
  109.4 21.8 %all_to_all.20 = f32[128,4,128]{2,1,0:T(4,128)S(1)} all-to-all(f32[128,4,128]{2,1,0:T(4,128)S(1)} %code_part.1), channel_id=1, replica_groups=mesh['y'=4,'x'=4,'zh'=4,'zb'=2,'k'=2] {'y','x','zh','zb'}, dimensions={0} | all-to-all | bytes 524288 | tf_op jit(solution)/shard_map/all_to_all | solution.py:488
  131.6 1.2 collective-permute-done.22.refs_2_
  132.8 1.5 scores.1.a
  136.6 2.1 %collective-permute-start.25 = (f32[4,128]{1,0:T(4,128)S(1)}, f32[4,128]{1,0:T(4,128)S(1)}, u32[]{:S(2)}, u32[]{:S(2)}) collective-permute-start(f32[4,128]{1,0:T(4,128)S(1)} %get-tuple-element.43), channel_id=1, source_target_pairs={{0,128},{64,192},{128,0},{192,64},{1,129},{65,193},{129,1},{193,65... | collective-permute-start | bytes 6152 | tf_op jit(solution)/shard_map/ppermute | solution.py:36
  138.7 1.5 collective-permute-start.26
  140.2 1.2 collective-permute-done.24.b
  142.3 1.6 four_lists.1
  143.9 21.0 %all_to_all.21 = f32[128,4,128]{2,1,0:T(4,128)S(1)} all-to-all(f32[128,4,128]{2,1,0:T(4,128)S(1)} %four_lists.1), channel_id=1, replica_groups=mesh['y'=4,'x'=4,'zh'=4,'zb'=2,'k'=2] {'y','x','zh','zb'}, dimensions={0} | all-to-all | bytes 524288 | tf_op jit(solution)/shard_map/all_to_all | solution.py:496
  164.9 1.4 final_lists.1
  (66 shorter events, 17.1 us)
Async XLA Ops:
  0.0 4.8 %collective-permute-start.4 = (bf16[224,1024]{1,0:T(8,128)(2,1)}, bf16[224,1024]{1,0:T(8,128)(2,1)S(1)}, u32[]{:S(2)}, u32[]{:S(2)}) collective-permute-start(bf16[224,1024]{1,0:T(8,128)(2,1)} %bitcast.20), channel_id=1, source_target_pairs={{0,1},{1,0},{2,3},{3,2},{4,5},{5,4},{6,7},{7,6},{8,9},{9,8},{10,11... | collective-permute-start | bytes 1376264 | tf_op jit(solution)/shard_map/ppermute | solution.py:32
  0.0 4.8 %collective-permute-start.5 = (bf16[224,1024]{1,0:T(8,128)(2,1)}, bf16[224,1024]{1,0:T(8,128)(2,1)S(1)}, u32[]{:S(2)}, u32[]{:S(2)}) collective-permute-start(bf16[224,1024]{1,0:T(8,128)(2,1)} %bitcast.22), channel_id=1, source_target_pairs={{0,1},{1,0},{2,3},{3,2},{4,5},{5,4},{6,7},{7,6},{8,9},{9,8},{10,11... | collective-permute-start | bytes 1376264 | tf_op jit(solution)/shard_map/ppermute | solution.py:32
  0.5 4.3 %collective-permute-start.6 = (bf16[224,1024]{1,0:T(8,128)(2,1)}, bf16[224,1024]{1,0:T(8,128)(2,1)S(1)}, u32[]{:S(2)}, u32[]{:S(2)}) collective-permute-start(bf16[224,1024]{1,0:T(8,128)(2,1)} %w0.1), channel_id=1, source_target_pairs={{0,1},{1,0},{2,3},{3,2},{4,5},{5,4},{6,7},{7,6},{8,9},{9,8},{10,11... | collective-permute-start | bytes 1376264 | tf_op jit(solution)/shard_map/ppermute | solution.py:32
  2.6 1.3 collective-permute-start
  3.3 1.4 collective-permute-start.3
  5.7 21.4 %copy-start.5 = (bf16[64,1024]{1,0:T(8,128)(2,1)S(1)}, bf16[64,1024]{1,0:T(8,128)(2,1)}, u32[]{:S(2)}) copy-start(bf16[64,1024]{1,0:T(8,128)(2,1)} %param.12) | copy-start | bytes 393220
  5.7 39.5 %copy-start.2 = (bf16[1024,224]{0,1:T(8,128)(2,1)S(1)}, bf16[1024,224]{0,1:T(8,128)(2,1)}, u32[]{:S(2)}) copy-start(bf16[1024,224]{0,1:T(8,128)(2,1)} %param.10) | copy-start | bytes 1376260
  5.7 39.5 %all-to-all-start = ((bf16[32,64,128]{2,1,0:T(8,128)(2,1)}), bf16[32,64,128]{2,1,0:T(8,128)(2,1)S(1)}, u32[]{:S(2)}, u32[]{:S(2)}) async-start(bf16[32,64,128]{2,1,0:T(8,128)(2,1)} %broadcast_in_dim.2), calls=%async_computation | async-start | bytes 1048576 | tf_op jit(solution)/shard_map/all_to_all | solution.py:41
  27.2 0.9 collective-permute-start.1
  28.0 1.3 collective-permute-start.2
  46.6 6.4 %collective-permute-start.7 = (bf16[64,1024]{1,0:T(8,128)(2,1)S(1)}, bf16[64,1024]{1,0:T(8,128)(2,1)S(1)}, u32[]{:S(2)}, u32[]{:S(2)}) collective-permute-start(bf16[64,1024]{1,0:T(8,128)(2,1)S(1)} %get-tuple-element.32), channel_id=1, source_target_pairs={{0,64},{64,128},{128,192},{192,0},{1,65},{65,129},{129,193},{193,1... | collective-permute-start | bytes 393224 | tf_op jit(solution)/shard_map/ppermute | solution.py:36
  47.9 6.5 %collective-permute-start.8 = (bf16[64,1024]{1,0:T(8,128)(2,1)S(1)}, bf16[64,1024]{1,0:T(8,128)(2,1)S(1)}, u32[]{:S(2)}, u32[]{:S(2)}) collective-permute-start(bf16[64,1024]{1,0:T(8,128)(2,1)S(1)} %get-tuple-element.33), channel_id=1, source_target_pairs={{0,128},{64,192},{128,0},{192,64},{1,129},{65,193},{129,1},{193,65... | collective-permute-start | bytes 393224 | tf_op jit(solution)/shard_map/ppermute | solution.py:36
  49.2 6.1 %collective-permute-start.9 = (bf16[64,1024]{1,0:T(8,128)(2,1)S(1)}, bf16[64,1024]{1,0:T(8,128)(2,1)S(1)}, u32[]{:S(2)}, u32[]{:S(2)}) collective-permute-start(bf16[64,1024]{1,0:T(8,128)(2,1)S(1)} %get-tuple-element.34), channel_id=1, source_target_pairs={{0,192},{64,0},{128,64},{192,128},{1,193},{65,1},{129,65},{193,129... | collective-permute-start | bytes 393224 | tf_op jit(solution)/shard_map/ppermute | solution.py:36
  55.5 5.0 %collective-permute-start.12 = (bf16[64,512]{1,0:T(8,128)(2,1)S(1)}, bf16[64,512]{1,0:T(8,128)(2,1)S(1)}, u32[]{:S(2)}, u32[]{:S(2)}) collective-permute-start(bf16[64,512]{1,0:T(8,128)(2,1)S(1)} %hidden_units.1.a), channel_id=1, source_target_pairs={{0,192},{64,0},{128,64},{192,128},{1,193},{65,1},{129,65},{193,129... | collective-permute-start | bytes 196616 | tf_op jit(solution)/shard_map/ppermute | solution.py:36
  58.0 5.9 %collective-permute-start.11 = (bf16[64,512]{1,0:T(8,128)(2,1)S(1)}, bf16[64,512]{1,0:T(8,128)(2,1)S(1)}, u32[]{:S(2)}, u32[]{:S(2)}) collective-permute-start(bf16[64,512]{1,0:T(8,128)(2,1)S(1)} %hidden_units.1.a), channel_id=1, source_target_pairs={{0,128},{64,192},{128,0},{192,64},{1,129},{65,193},{129,1},{193,65... | collective-permute-start | bytes 196616 | tf_op jit(solution)/shard_map/ppermute | solution.py:36
  58.2 6.2 %collective-permute-start.10 = (bf16[64,512]{1,0:T(8,128)(2,1)S(1)}, bf16[64,512]{1,0:T(8,128)(2,1)S(1)}, u32[]{:S(2)}, u32[]{:S(2)}) collective-permute-start(bf16[64,512]{1,0:T(8,128)(2,1)S(1)} %hidden_units.1.a), channel_id=1, source_target_pairs={{0,64},{64,128},{128,192},{192,0},{1,65},{65,129},{129,193},{193,1... | collective-permute-start | bytes 196616 | tf_op jit(solution)/shard_map/ppermute | solution.py:36
  66.2 29.0 %all-to-all-start.1 = ((bf16[32,8,1024]{2,1,0:T(8,128)(2,1)}), bf16[32,8,1024]{2,1,0:T(8,128)(2,1)S(1)}, u32[]{:S(2)}, u32[]{:S(2)}) async-start(bf16[32,8,1024]{2,1,0:T(8,128)(2,1)} %bitcast.9), calls=%async_computation.1 | async-start | bytes 1048576 | tf_op jit(solution)/shard_map/all_to_all | solution.py:476
  74.8 30.1 %collective-permute-start.21 = (bf16[128,512]{1,0:T(8,128)(2,1)S(1)}, bf16[128,512]{1,0:T(8,128)(2,1)S(1)}, u32[]{:S(2)}, u32[]{:S(2)}) collective-permute-start(bf16[128,512]{1,0:T(8,128)(2,1)S(1)} %pad_maximum_fusion.w0), channel_id=1, source_target_pairs={{0,12},{4,0},{8,4},{12,8},{1,13},{5,1},{9,5},{13,9},{2,14},{6,2},{... | collective-permute-start | bytes 393224 | tf_op jit(solution)/shard_map/ppermute | solution.py:470
  77.6 29.4 %collective-permute-start.20 = (bf16[128,512]{1,0:T(8,128)(2,1)S(1)}, bf16[128,512]{1,0:T(8,128)(2,1)S(1)}, u32[]{:S(2)}, u32[]{:S(2)}) collective-permute-start(bf16[128,512]{1,0:T(8,128)(2,1)S(1)} %pad_maximum_fusion.w0), channel_id=1, source_target_pairs={{0,8},{4,12},{8,0},{12,4},{1,9},{5,13},{9,1},{13,5},{2,10},{6,14},... | collective-permute-start | bytes 393224 | tf_op jit(solution)/shard_map/ppermute | solution.py:470
  80.8 26.1 %collective-permute-start.19 = (bf16[128,512]{1,0:T(8,128)(2,1)S(1)}, bf16[128,512]{1,0:T(8,128)(2,1)S(1)}, u32[]{:S(2)}, u32[]{:S(2)}) collective-permute-start(bf16[128,512]{1,0:T(8,128)(2,1)S(1)} %pad_maximum_fusion.w0), channel_id=1, source_target_pairs={{0,4},{4,8},{8,12},{12,0},{1,5},{5,9},{9,13},{13,1},{2,6},{6,10},{... | collective-permute-start | bytes 393224 | tf_op jit(solution)/shard_map/ppermute | solution.py:470
  95.4 3.8 %collective-permute-start.15 = (f32[8,128]{1,0:T(8,128)S(1)}, f32[8,128]{1,0:T(8,128)S(1)}, u32[]{:S(2)}, u32[]{:S(2)}) collective-permute-start(f32[8,128]{1,0:T(8,128)S(1)} %get-tuple-element.37.a), channel_id=1, source_target_pairs={{0,192},{64,0},{128,64},{192,128},{1,193},{65,1},{129,65},{193,129... | collective-permute-start | bytes 12296 | tf_op jit(solution)/shard_map/ppermute | solution.py:36
  96.7 5.1 %collective-permute-start.14 = (f32[8,128]{1,0:T(8,128)S(1)}, f32[8,128]{1,0:T(8,128)S(1)}, u32[]{:S(2)}, u32[]{:S(2)}) collective-permute-start(f32[8,128]{1,0:T(8,128)S(1)} %get-tuple-element.37.a), channel_id=1, source_target_pairs={{0,128},{64,192},{128,0},{192,64},{1,129},{65,193},{129,1},{193,65... | collective-permute-start | bytes 12296 | tf_op jit(solution)/shard_map/ppermute | solution.py:36
  99.2 4.8 %collective-permute-start.13 = (f32[8,128]{1,0:T(8,128)S(1)}, f32[8,128]{1,0:T(8,128)S(1)}, u32[]{:S(2)}, u32[]{:S(2)}) collective-permute-start(f32[8,128]{1,0:T(8,128)S(1)} %get-tuple-element.37.a), channel_id=1, source_target_pairs={{0,64},{64,128},{128,192},{192,0},{1,65},{65,129},{129,193},{193,1... | collective-permute-start | bytes 12296 | tf_op jit(solution)/shard_map/ppermute | solution.py:36
  104.7 2.3 %collective-permute-start.16 = (f32[4,128]{1,0:T(4,128)S(1)}, f32[4,128]{1,0:T(4,128)S(1)}, u32[]{:S(2)}, u32[]{:S(2)}) collective-permute-start(f32[4,128]{1,0:T(4,128)S(1)} %get-tuple-element.38.a), channel_id=1, source_target_pairs={{0,1},{1,0},{2,3},{3,2},{4,5},{5,4},{6,7},{7,6},{8,9},{9,8},{10,11... | collective-permute-start | bytes 6152 | tf_op jit(solution)/shard_map/ppermute | solution.py:486
  104.8 28.0 %copy-start = (bf16[512,1024]{1,0:T(8,128)(2,1)S(1)}, bf16[512,1024]{1,0:T(8,128)(2,1)}, u32[]{:S(2)}) copy-start(bf16[512,1024]{1,0:T(8,128)(2,1)} %refs_3_.1) | copy-start | bytes 3145732
  104.8 3.1 %collective-permute-start.18 = (f32[4,128]{1,0:T(4,128)S(1)}, f32[4,128]{1,0:T(4,128)S(1)}, u32[]{:S(2)}, u32[]{:S(2)}) collective-permute-start(f32[4,128]{1,0:T(4,128)S(1)} %get-tuple-element.39), channel_id=1, source_target_pairs={{0,3},{1,2},{2,1},{3,0},{4,7},{5,6},{6,5},{7,4},{8,11},{9,10},{10,... | collective-permute-start | bytes 6152 | tf_op jit(solution)/shard_map/ppermute | solution.py:486
  104.9 3.7 %collective-permute-start.17 = (f32[4,128]{1,0:T(4,128)S(1)}, f32[4,128]{1,0:T(4,128)S(1)}, u32[]{:S(2)}, u32[]{:S(2)}) collective-permute-start(f32[4,128]{1,0:T(4,128)S(1)} %get-tuple-element.39), channel_id=1, source_target_pairs={{0,2},{1,3},{2,0},{3,1},{4,6},{5,7},{6,4},{7,5},{8,10},{9,11},{10,... | collective-permute-start | bytes 6152 | tf_op jit(solution)/shard_map/ppermute | solution.py:486
  131.5 1.3 collective-permute-start.22
  134.3 1.2 collective-permute-start.23
  136.6 4.9 %collective-permute-start.24 = (f32[4,128]{1,0:T(4,128)S(1)}, f32[4,128]{1,0:T(4,128)S(1)}, u32[]{:S(2)}, u32[]{:S(2)}) collective-permute-start(f32[4,128]{1,0:T(4,128)S(1)} %get-tuple-element.42), channel_id=1, source_target_pairs={{0,64},{64,128},{128,192},{192,0},{1,65},{65,129},{129,193},{193,1... | collective-permute-start | bytes 6152 | tf_op jit(solution)/shard_map/ppermute | solution.py:36
  136.6 5.2 %collective-permute-start.25 = (f32[4,128]{1,0:T(4,128)S(1)}, f32[4,128]{1,0:T(4,128)S(1)}, u32[]{:S(2)}, u32[]{:S(2)}) collective-permute-start(f32[4,128]{1,0:T(4,128)S(1)} %get-tuple-element.43), channel_id=1, source_target_pairs={{0,128},{64,192},{128,0},{192,64},{1,129},{65,193},{129,1},{193,65... | collective-permute-start | bytes 6152 | tf_op jit(solution)/shard_map/ppermute | solution.py:36
  138.7 3.6 %collective-permute-start.26 = (f32[4,128]{1,0:T(4,128)S(1)}, f32[4,128]{1,0:T(4,128)S(1)}, u32[]{:S(2)}, u32[]{:S(2)}) collective-permute-start(f32[4,128]{1,0:T(4,128)S(1)} %get-tuple-element.44), channel_id=1, source_target_pairs={{0,192},{64,0},{128,64},{192,128},{1,193},{65,1},{129,65},{193,129... | collective-permute-start | bytes 6152 | tf_op jit(solution)/shard_map/ppermute | solution.py:36
  (4 other events, 37.3 us)

commit v6 on v5

--- a/solution.py
+++ b/solution.py
@@ -45,32 +45,29 @@
     return lax.broadcasted_iota(jnp.int32, like, 1)
 
 
-def pack_kernel(place, lengths, h, own, other):
+def pack_kernel(place, h, own, other):
     k = place[1]
+    x = h[...].astype(F32).T
     for q in range(4):
-        one = h[q * 32 : q * 32 + 16, :]
-        two = h[q * 32 + 16 : q * 32 + 32, :]
-        own[q * 16 : q * 16 + 16, :] = jnp.where(k == 0, one, two)
-        other[q * 16 : q * 16 + 16, :] = jnp.where(k == 0, two, one)
-    query = lax.broadcasted_iota(jnp.int32, (16, 64), 0) // 4
-    counts = jnp.zeros((16, 64), jnp.int32)
-    for q in range(4):
-        counts = jnp.where(query == q, lengths[q], counts)
-    own[64:80, :] = counts.astype(F32).astype(BF16)
-
-
-def pack(place, lengths, h):
+        one = x[q * 32 : q * 32 + 16, :]
+        two = x[q * 32 + 16 : q * 32 + 32, :]
+        own[q * 16 : q * 16 + 16, :] = jnp.where(k == 0, one, two).astype(BF16)
+        other[q * 16 : q * 16 + 16, :] = jnp.where(k == 0, two, one).astype(BF16)
+
+
+def pack(place, h):
+    part = shape((64, 64), BF16)
     return pl.pallas_call(
         pack_kernel,
-        out_shape=(shape((80, 64), BF16), shape((64, 64), BF16)),
-        in_specs=[SMEM, SMEM, VMEM],
+        out_shape=(part, part),
+        in_specs=[SMEM, VMEM],
         out_specs=(VMEM,) * 2,
         compiler_params=PARAMS,
         name="pack",
-    )(place, lengths, h)
-
-
-def gate_up_kernel(place, h, g0, u0, g1, u1, o0, o1, o2, o3, lhs, wide):
+    )(place, h)
+
+
+def gate_up_kernel(place, lengths, h, g0, u0, g1, u1, o0, o1, o2, o3, lhs, wide):
     y = place[0]
     for d in range(4):
         i = (y + d) % 4
@@ -93,25 +90,32 @@
             block = jnp.where(col == 224, top, block)
             block = jnp.where(col == 225, mid, block)
             block = jnp.where(col == 226, low, block)
+            for q in range(4):
+                block = jnp.where(col == 228 + q, lengths[q].astype(F32), block)
         block = block.astype(BF16)
         for d, o in enumerate((o0, o1, o2, o3)):
             o[:, b * 256 : b * 256 + 256] = block[d * 64 : d * 64 + 64]
 
 
-def gate_up(place, h, g0, u0, g1, u1):
+def gate_up(place, lengths, h, g0, u0, g1, u1):
     part = shape((64, 1024), BF16)
     return pl.pallas_call(
         gate_up_kernel,
         out_shape=(part,) * 4,
-        in_specs=[SMEM] + [VMEM] * 5,
+        in_specs=[SMEM] * 2 + [VMEM] * 5,
         out_specs=(VMEM,) * 4,
         scratch_shapes=[pltpu.VMEM((256, 1024), BF16), pltpu.VMEM((256, 256), F32)],
         compiler_params=PARAMS,
         name="gate_up",
-    )(place, h, g0, u0, g1, u1)
-
-
-def hidden_kernel(a, b, c, d, out):
+    )(place, lengths, h, g0, u0, g1, u1)
+
+
+def hidden_kernel(place, a, b, c, d, out, counts):
+    y, x = place[0], place[7]
+    held = jnp.zeros((8, 128), F32)
+    for s, part in enumerate((a, b, c, d)):
+        held = jnp.where((y - s + 4) % 4 == x, part[0:8, 128:256].astype(F32), held)
+    counts[...] = held
     total = a[...].astype(F32) + b[...].astype(F32) + c[...].astype(F32) + d[...].astype(F32)
     col = lanes((64, 256))
     first = total[:, 0:256]
@@ -124,15 +128,15 @@
         out[:, b * 256 : b * 256 + 256] = jnp.where(col < 224, units, 0.0).astype(BF16)
 
 
-def hidden_of(a, b, c, d):
+def hidden_of(place, a, b, c, d):
     return pl.pallas_call(
         hidden_kernel,
-        out_shape=shape((64, 512), BF16),
-        in_specs=[VMEM] * 4,
-        out_specs=VMEM,
+        out_shape=(shape((64, 512), BF16), shape((8, 128), F32)),
+        in_specs=[SMEM] + [VMEM] * 4,
+        out_specs=(VMEM,) * 2,
         compiler_params=PARAMS,
         name="hidden_units",
-    )(a, b, c, d)
+    )(place, a, b, c, d)
 
 
 def down_kernel(place, a, b, c, d, w0, w1, out, lhs):
@@ -176,28 +180,30 @@
     )(parts, h)
 
 
-def pool_kernel(place, counts, res, a, b, c, d, same, other):
-    first, row, zb = place[2], place[4], place[6]
+def pool_kernel(place, counts, res, a, b, c, d, o0, o1, o2, o3):
+    k, first, zh, zb = place[1], place[2], place[5], place[6]
     sq = (a[...] + b[...] + c[...] + d[...])[:, 0:1]
     slots = lax.broadcasted_iota(jnp.int32, (8, 1), 0) + first
-    held = counts[...].astype(F32)
-    held = jnp.where(lax.broadcasted_iota(jnp.int32, (16, 64), 0) == row, held, 0.0)
-    count = jnp.max(jnp.max(held, axis=1, keepdims=True), axis=0, keepdims=True)
+    held = jnp.where(lanes((1, 128)) == 100 + zh, counts[0:1, :], 0.0)
+    count = jnp.max(held, axis=1, keepdims=True)
     weight = jnp.where(slots.astype(F32) < count, lax.rsqrt(sq / D + EPS), 0.0)
     pooled = jnp.sum(res[...] * weight, axis=0, keepdims=True) / count
     ahead = jnp.concatenate([pooled[:, t * 256 : t * 256 + 128] for t in range(4)], axis=0)
     behind = jnp.concatenate([pooled[:, t * 256 + 128 : t * 256 + 256] for t in range(4)], axis=0)
-    same[...] = jnp.where(zb == 0, ahead, behind)
-    other[...] = jnp.where(zb == 0, behind, ahead)
+    for r, out in enumerate((o0, o1, o2, o3)):
+        one = jnp.where(zb == r // 2, ahead, behind)
+        two = jnp.where(zb == r // 2, behind, ahead)
+        part = jnp.concatenate([one, two], axis=0)
+        out[...] = jnp.where(k == r % 2, part, pltpu.roll(part, 64, 1))
 
 
 def pool(place, counts, res, sqs):
-    part = shape((4, 128), F32)
+    part = shape((8, 128), F32)
     return pl.pallas_call(
         pool_kernel,
-        out_shape=(part,) * 2,
+        out_shape=(part,) * 4,
         in_specs=[SMEM] + [VMEM] * 6,
-        out_specs=(VMEM,) * 2,
+        out_specs=(VMEM,) * 4,
         compiler_params=PARAMS,
         name="pool",
     )(place, counts, res, *sqs)
@@ -206,22 +212,25 @@
 def code_kernel(place, a, b, c, d, w0, w1, w2, w3, out, left):
     zh = place[5]
     left[...] = a[...] + b[...] + c[...] + d[...]
-    total = jnp.zeros((8, 512), F32)
+    total = jnp.zeros((8, 256), F32)
     for s, w in enumerate((w0, w1, w2, w3)):
-        piece = jnp.broadcast_to(left[pl.ds((zh - s + 4) % 4, 1), :], (8, 128))
-        total += jnp.dot(piece.astype(BF16), w[...], preferred_element_type=F32)
-    for t in range(4):
+        row = (zh - s + 4) % 4
+        one = jnp.broadcast_to(left[pl.ds(row, 1), :], (8, 128))
+        two = jnp.broadcast_to(left[pl.ds(row + 4, 1), :], (8, 128))
+        piece = jnp.concatenate([one, two], axis=1).astype(BF16)
+        total += jnp.dot(piece, w[...], preferred_element_type=F32)
+    for t in range(2):
         left[t : t + 1, :] = total[0:1, t * 128 : t * 128 + 128]
-    out[...] = jnp.broadcast_to(left[...][None], (128, 4, 128))
+    out[...] = jnp.broadcast_to(left[0:2][None], (64, 2, 128))
 
 
 def code_part(place, pieces, ws):
     return pl.pallas_call(
         code_kernel,
-        out_shape=shape((128, 4, 128), F32),
+        out_shape=shape((64, 2, 128), F32),
         in_specs=[SMEM] + [VMEM] * 8,
         out_specs=VMEM,
-        scratch_shapes=[pltpu.VMEM((4, 128), F32)],
+        scratch_shapes=[pltpu.VMEM((8, 128), F32)],
         compiler_params=PARAMS,
         name="code_part",
     )(place, *pieces, *ws)
@@ -323,14 +332,17 @@
     return lax.broadcasted_iota(jnp.int32, like, 0)
 
 
-def score_kernel(place, mine, theirs, docs, lists, *, scale):
-    k = place[1]
-    own, peer = mine[...], theirs[...]
-    low = jnp.where(k == 0, own, peer)
-    high = jnp.where(k == 0, peer, own)
+def score_kernel(place, c0, c1, c2, c3, docs, lists, *, scale):
+    k, zb = place[1], place[6]
+    at = zb * 2 + k
     dims = (((1,), (1,)), ((), ()))
-    scores = lax.dot_general(low, docs[:, 0:512], dims, preferred_element_type=F32)
-    scores += lax.dot_general(high, docs[:, 512:1024], dims, preferred_element_type=F32)
+    scores = jnp.zeros((16, 512), F32)
+    for j in range(4):
+        piece = c0[...]
+        for r, c in ((1, c1), (2, c2), (3, c3)):
+            piece = jnp.where(at == j ^ r, c[...], piece)
+        part = docs[:, j * 256 : j * 256 + 256]
+        scores += lax.dot_general(piece, part, dims, preferred_element_type=F32)
     scores = scores * scale
     x = jnp.concatenate([scores[:, c * 128 : c * 128 + 128] for c in range(4)] * 2, axis=0)
     lane = lanes((8, 128))
@@ -342,18 +354,18 @@
     lists[...] = jnp.concatenate(v, axis=0).T[0:16]
 
 
-def local_lists(place, mine, theirs, docs):
+def local_lists(place, pieces, docs):
     def body(*refs):
         score_kernel(*refs, scale=1.0 / math.sqrt(docs.shape[1]))
 
     return pl.pallas_call(
         body,
         out_shape=shape((16, 128), F32),
-        in_specs=[SMEM] + [VMEM] * 3,
+        in_specs=[SMEM] + [VMEM] * 5,
         out_specs=VMEM,
         compiler_params=PARAMS,
         name="scores",
-    )(place, mine, theirs, docs)
+    )(place, *pieces, docs)
 
 
 def pair_kernel(place, a, b, o0, o1, o2, o3, held):
@@ -440,15 +452,14 @@
 
 def per_device(hidden_in, lengths, gate_weight, up_weight, down_weight, code_weight, corpus_codes):
     y, x, zh, zb, k = (lax.axis_index(a) for a in QUERY_CORPUS)
-    place = jnp.stack([y, k, 16 * k + 8 * zb, x // 2, 4 * zh, zh, zb]).astype(jnp.int32)
-
-    own, other = pack(place, lengths, hidden_in)
+    place = jnp.stack([y, k, 16 * k + 8 * zb, x // 2, 4 * zh, zh, zb, x]).astype(jnp.int32)
+
+    own, other = pack(place, hidden_in.T)
     swap = [(a * 4 + b, b * 4 + a) for a in range(4) for b in range(4)]
     straight = [(s * 2 + c, t * 2 + c) for s, t in swap for c in range(2)]
     crossed = [(s * 2 + c, t * 2 + 1 - c) for s, t in swap for c in range(2)]
     own = lax.ppermute(own, ("y", "x", "k"), straight)
     other = lax.ppermute(other, ("y", "x", "k"), crossed)
-    counts, own = own[64:], own[:64]
     block = jnp.where(
         k == 0, jnp.concatenate([own, other], axis=1), jnp.concatenate([other, own], axis=1)
     )
@@ -459,18 +470,19 @@
     )
     gathered = spread(block, XZ, 32)
 
-    low, high = code_weight[:, :512], code_weight[:, 512:]
-    mine = lax.ppermute(jnp.where(k == 0, low, high), ("y", "x", "k"), straight)
-    theirs = lax.ppermute(jnp.where(k == 0, high, low), ("y", "x", "k"), crossed)
-    rows = jnp.concatenate(
-        [jnp.where(k == 0, mine, theirs), jnp.where(k == 0, theirs, mine)], axis=0
-    )
+    at = 2 * zb + k
+    flipped = []
+    for r in range(4):
+        bits = lax.dynamic_slice_in_dim(code_weight, (at ^ r) * 256, 256, axis=1)
+        pairs = [(s * 4 + c, t * 4 + (c ^ r)) for s, t in swap for c in range(4)]
+        flipped.append(lax.ppermute(bits, ("y", "x", "zb", "k"), pairs))
+    rows = jnp.concatenate(flipped, axis=0)
     rows, gathered = lax.optimization_barrier((rows, gathered))
     turned = [[(i, (i + d) % 4) for i in range(4)] for d in range(4)]
     code_rows = (rows, *(lax.ppermute(rows, "zh", turned[d]) for d in (1, 2, 3)))
 
-    parts = gate_up(place, gathered, gate_rows, up_rows, gate_peer, up_peer)
-    units = hidden_of(parts[0], *(shifted(parts[d], d) for d in (1, 2, 3)))
+    parts = gate_up(place, lengths, gathered, gate_rows, up_rows, gate_peer, up_peer)
+    units, counts = hidden_of(place, parts[0], *(shifted(parts[d], d) for d in (1, 2, 3)))
     groups = (units, *(shifted(units, d) for d in (1, 2, 3)))
     branch = down(place, groups, down_weight, down_peer)
     branch = lax.all_to_all(branch.reshape(32, 8, 1024), XZ, 0, 0, tiled=True)
@@ -480,16 +492,14 @@
     here = jnp.moveaxis(here, 0, 1).reshape(8, 1024)
     res, sq = residual_of(branch, here)
     sqs = (sq, *(shifted(sq, d) for d in (1, 2, 3)))
-    same, other = pool(place, counts, res, sqs)
+    mine = pool(place, counts, res, sqs)
     flips = [[(i, i ^ r) for i in range(4)] for r in range(4)]
-    sent = ((same, 1), (other, 2), (other, 3))
-    pieces = (same, *(lax.ppermute(a, ("zb", "k"), flips[r]) for a, r in sent))
+    pieces = (mine[0], *(lax.ppermute(mine[r], ("zb", "k"), flips[r]) for r in (1, 2, 3)))
     part = code_part(place, pieces, code_rows)
-    codes = lax.all_to_all(part, YXZ, 0, 0, tiled=True)
-    codes = codes.reshape(4, 4, 4, 2, 512).sum(axis=(0, 3))
-    codes = codes.reshape(16, 512).astype(BF16)
-
-    lists = local_lists(place, codes, to_peer(codes), corpus_codes)
+    codes = lax.all_to_all(part, ("y", "x", "zh"), 0, 0, tiled=True)
+    codes = codes.reshape(4, 16, 256).sum(axis=0).astype(BF16)
+    codes = (codes, *(lax.ppermute(codes, ("zb", "k"), flips[r]) for r in (1, 2, 3)))
+    lists = local_lists(place, codes, corpus_codes)
     lists = pair_lists(place, lists, to_peer(lists))
     lists = (lists[0], *(shifted(lists[d], d) for d in (1, 2, 3)))
     lists = four_lists(place, lists)

time: 167 us -> 167 us (level)
  starting transfers between devices: 56.2 us -> 67.3 us
  waiting for transfers between devices: 53.1 us -> 45 us
  blocking collectives: 42.8 us -> 40.7 us
    ppermute x5 -> x10, waiting for transfers between devices: 2.88 us -> 13.9 us  [the longest x4 9.99 us: per_device(): flipped.append(lax.ppermute(bits, ('y', 'x', 'zb', 'k'), pairs))]
    all_to_all x1, waiting for transfers between devices: 15.8 us -> 5.23 us  [spread(): return lax.all_to_all(copies, axes, 0, 0, tiled=True)]
    ppermute x12, starting transfers between devices: 13.5 us -> 19.7 us  [shifted(): return lax.ppermute(x, 'y', [(i, (i + d) % 4) for i in range(4)])]
    ppermute x12, waiting for transfers between devices: 18.5 us -> 13.2 us  [shifted(): return lax.ppermute(x, 'y', [(i, (i + d) % 4) for i in range(4)])]
    ppermute x5 -> x10, starting transfers between devices: 3.11 us -> 6.61 us  [the longest x4 2.75 us: per_device(): flipped.append(lax.ppermute(bits, ('y', 'x', 'zb', 'k'), pairs))]
    all_to_all x1, waiting for transfers between devices: 12.9 us -> 10.8 us  [per_device(): branch = lax.all_to_all(branch.reshape(32, 8, 1024), XZ, 0, 0, tiled=True)]
  transfers between devices with their start and end apart: 29 -> 33, of which waited for: 20 -> 20; matrix products, arithmetic and copies ran while one was open for 0% -> 0% of each run, Pallas kernels for 1% -> 1%
where the time goes in v6:
time: 167 us
  starting transfers between devices  67.3 us (40%)
  waiting for transfers between devices  45 us (27%)
  blocking collectives  40.7 us (24%)
  Pallas kernels  11.7 us (7%)
  local copies, waits for them, and re-layouts  1.76 us (1%)
    all_to_all x1, starting transfers between devices, spread(): return lax.all_to_all(copies, axes, 0, 0, tiled=True)  21.4 us
    all_to_all x1, blocking collectives, per_device(): arrived = lax.all_to_all(lists, YXZ, 0, 0, tiled=True)  20.4 us
    all_to_all x1, blocking collectives, per_device(): codes = lax.all_to_all(part, ('y', 'x', 'zh'), 0, 0, tiled=True)  20.3 us
    ppermute x12, starting transfers between devices, shifted(): return lax.ppermute(x, 'y', [(i, (i + d) % 4) for i in range(4)])  19.7 us
    ppermute x12, waiting for transfers between devices, shifted(): return lax.ppermute(x, 'y', [(i, (i + d) % 4) for i in range(4)])  13.2 us
    all_to_all x1, waiting for transfers between devices, per_device(): branch = lax.all_to_all(branch.reshape(32, 8, 1024), XZ, 0, 0, tiled=True)  10.8 us
    ppermute x4, waiting for transfers between devices, per_device(): flipped.append(lax.ppermute(bits, ('y', 'x', 'zb', 'k'), pairs))  9.99 us
    all_to_all x1, starting transfers between devices, per_device(): branch = lax.all_to_all(branch.reshape(32, 8, 1024), XZ, 0, 0, tiled=True)  8.88 us
  transfers between devices with their start and end apart: 33, of which 20 were waited for; matrix products, arithmetic and copies ran while one was open for 0% of the time, Pallas kernels for 1%

profile of v6, /device:TPU:32, one launch (start us, length us, event | category | flops | bytes accessed | tf_op | source)
XLA Modules:
  0.0 166.8 jit_solution(7184762556564287082)
XLA Ops:
  5.0 21.4 %all-to-all-start = ((bf16[32,64,128]{2,1,0:T(8,128)(2,1)}), bf16[32,64,128]{2,1,0:T(8,128)(2,1)S(1)}, u32[]{:S(2)}, u32[]{:S(2)}) async-start(bf16[32,64,128]{2,1,0:T(8,128)(2,1)} %broadcast_in_dim.2), calls=%async_computation | async-start | bytes 1048576 | tf_op jit(solution)/shard_map/all_to_all | solution.py:41
  27.8 1.5 collective-permute-start.3
  29.3 9.8 %collective-permute-done.2 = bf16[64,256]{1,0:T(8,128)(2,1)S(1)} collective-permute-done((bf16[64,256]{1,0:T(8,128)(2,1)S(1)}, bf16[64,256]{1,0:T(8,128)(2,1)S(1)}, u32[]{:S(2)}, u32[]{:S(2)}) %collective-permute-start.2) | collective-permute-done | bytes 32800 | tf_op jit(solution)/shard_map/ppermute | solution.py:478
  39.3 5.2 %all-to-all-done.h = bf16[32,64,128]{2,1,0:T(8,128)(2,1)S(1)} async-done(((bf16[32,64,128]{2,1,0:T(8,128)(2,1)}), bf16[32,64,128]{2,1,0:T(8,128)(2,1)S(1)}, u32[]{:S(2)}, u32[]{:S(2)}) %all-to-all-start) | async-done | bytes 524320 | tf_op jit(solution)/shard_map/all_to_all | solution.py:41
  44.6 1.4 gate_up.1
  46.0 3.4 %collective-permute-start.10 = (bf16[64,1024]{1,0:T(8,128)(2,1)S(1)}, bf16[64,1024]{1,0:T(8,128)(2,1)S(1)}, u32[]{:S(2)}, u32[]{:S(2)}) collective-permute-start(bf16[64,1024]{1,0:T(8,128)(2,1)S(1)} %get-tuple-element.37), channel_id=1, source_target_pairs={{0,128},{64,192},{128,0},{192,64},{1,129},{65,193},{129,1},{193,65... | collective-permute-start | bytes 393224 | tf_op jit(solution)/shard_map/ppermute | solution.py:36
  49.9 1.5 collective-permute-start.9
  51.4 2.5 %collective-permute-done.10.c = bf16[64,1024]{1,0:T(8,128)(2,1)S(1)} collective-permute-done((bf16[64,1024]{1,0:T(8,128)(2,1)S(1)}, bf16[64,1024]{1,0:T(8,128)(2,1)S(1)}, u32[]{:S(2)}, u32[]{:S(2)}) %collective-permute-start.10) | collective-permute-done | bytes 131104 | tf_op jit(solution)/shard_map/ppermute | solution.py:36
  53.9 1.6 collective-permute-done.11.d
  57.3 1.8 %collective-permute-start.12 = (bf16[64,512]{1,0:T(8,128)(2,1)S(1)}, bf16[64,512]{1,0:T(8,128)(2,1)S(1)}, u32[]{:S(2)}, u32[]{:S(2)}) collective-permute-start(bf16[64,512]{1,0:T(8,128)(2,1)S(1)} %get-tuple-element.40.a), channel_id=1, source_target_pairs={{0,64},{64,128},{128,192},{192,0},{1,65},{65,129},{129,193},{193,1... | collective-permute-start | bytes 196616 | tf_op jit(solution)/shard_map/ppermute | solution.py:36
  59.1 1.6 collective-permute-start.13
  60.7 2.5 %collective-permute-start.14 = (bf16[64,512]{1,0:T(8,128)(2,1)S(1)}, bf16[64,512]{1,0:T(8,128)(2,1)S(1)}, u32[]{:S(2)}, u32[]{:S(2)}) collective-permute-start(bf16[64,512]{1,0:T(8,128)(2,1)S(1)} %get-tuple-element.40.a), channel_id=1, source_target_pairs={{0,192},{64,0},{128,64},{192,128},{1,193},{65,1},{129,65},{193,129... | collective-permute-start | bytes 196616 | tf_op jit(solution)/shard_map/ppermute | solution.py:36
  63.2 1.7 %collective-permute-done.13.c = bf16[64,512]{1,0:T(8,128)(2,1)S(1)} collective-permute-done((bf16[64,512]{1,0:T(8,128)(2,1)S(1)}, bf16[64,512]{1,0:T(8,128)(2,1)S(1)}, u32[]{:S(2)}, u32[]{:S(2)}) %collective-permute-start.13) | collective-permute-done | bytes 65568 | tf_op jit(solution)/shard_map/ppermute | solution.py:36
  65.1 1.8 %down.1 = bf16[256,1024]{1,0:T(8,128)(2,1)} custom-call(s32[8]{0:T(128)S(1)} %stack.35.place.refs_0_, bf16[64,512]{1,0:T(8,128)(2,1)S(1)} %get-tuple-element.40.a, bf16[64,512]{1,0:T(8,128)(2,1)S(1)} %collective-permute-done.12.b, bf16[64,512]{1,0:T(8,128)(2,1)S(1)} %collective-permute-done.13.c, bf16[64,512]{1,0:T(8,128)(2,1)S(1)} %collective-permute-done.14.d, ...), custom_call_target="tpu_custom_call" | custom-call | tf_op jit(solution)/shard_map/down/pallas_call | solution.py:153
  66.9 8.9 %all-to-all-start.1 = ((bf16[32,8,1024]{2,1,0:T(8,128)(2,1)}), bf16[32,8,1024]{2,1,0:T(8,128)(2,1)S(1)}, u32[]{:S(2)}, u32[]{:S(2)}) async-start(bf16[32,8,1024]{2,1,0:T(8,128)(2,1)} %bitcast.11), calls=%async_computation.1 | async-start | bytes 1048576 | tf_op jit(solution)/shard_map/all_to_all | solution.py:488
  75.8 2.4 %collective-permute-start.21 = (bf16[256,256]{1,0:T(8,128)(2,1)S(1)}, bf16[256,256]{1,0:T(8,128)(2,1)S(1)}, u32[]{:S(2)}, u32[]{:S(2)}) collective-permute-start(bf16[256,256]{1,0:T(8,128)(2,1)S(1)} %pad_maximum_fusion.w0), channel_id=1, source_target_pairs={{0,4},{4,8},{8,12},{12,0},{1,5},{5,9},{9,13},{13,1},{2,6},{6,10},{... | collective-permute-start | bytes 393224 | tf_op jit(solution)/shard_map/ppermute | solution.py:482
  78.3 2.7 %collective-permute-start.22 = (bf16[256,256]{1,0:T(8,128)(2,1)S(1)}, bf16[256,256]{1,0:T(8,128)(2,1)S(1)}, u32[]{:S(2)}, u32[]{:S(2)}) collective-permute-start(bf16[256,256]{1,0:T(8,128)(2,1)S(1)} %pad_maximum_fusion.w0), channel_id=1, source_target_pairs={{0,8},{4,12},{8,0},{12,4},{1,9},{5,13},{9,1},{13,5},{2,10},{6,14},... | collective-permute-start | bytes 393224 | tf_op jit(solution)/shard_map/ppermute | solution.py:482
  80.9 3.6 %collective-permute-start.23 = (bf16[256,256]{1,0:T(8,128)(2,1)S(1)}, bf16[256,256]{1,0:T(8,128)(2,1)S(1)}, u32[]{:S(2)}, u32[]{:S(2)}) collective-permute-start(bf16[256,256]{1,0:T(8,128)(2,1)S(1)} %pad_maximum_fusion.w0), channel_id=1, source_target_pairs={{0,12},{4,0},{8,4},{12,8},{1,13},{5,1},{9,5},{13,9},{2,14},{6,2},{... | collective-permute-start | bytes 393224 | tf_op jit(solution)/shard_map/ppermute | solution.py:482
  84.5 10.8 %all-to-all-done.1.parts = bf16[32,8,1024]{2,1,0:T(8,128)(2,1)S(1)} async-done(((bf16[32,8,1024]{2,1,0:T(8,128)(2,1)}), bf16[32,8,1024]{2,1,0:T(8,128)(2,1)S(1)}, u32[]{:S(2)}, u32[]{:S(2)}) %all-to-all-start.1) | async-done | bytes 524320 | tf_op jit(solution)/shard_map/all_to_all | solution.py:488
  96.0 3.0 %collective-permute-start.16 = (f32[8,128]{1,0:T(8,128)S(1)}, f32[8,128]{1,0:T(8,128)S(1)}, u32[]{:S(2)}, u32[]{:S(2)}) collective-permute-start(f32[8,128]{1,0:T(8,128)S(1)} %get-tuple-element.43.a), channel_id=1, source_target_pairs={{0,128},{64,192},{128,0},{192,64},{1,129},{65,193},{129,1},{193,65... | collective-permute-start | bytes 12296 | tf_op jit(solution)/shard_map/ppermute | solution.py:36
  99.1 1.2 collective-permute-done.15.b
  101.2 2.7 %collective-permute-done.17.d = f32[8,128]{1,0:T(8,128)S(1)} collective-permute-done((f32[8,128]{1,0:T(8,128)S(1)}, f32[8,128]{1,0:T(8,128)S(1)}, u32[]{:S(2)}, u32[]{:S(2)}) %collective-permute-start.17) | collective-permute-done | bytes 4128 | tf_op jit(solution)/shard_map/ppermute | solution.py:36
  105.4 1.1 collective-permute-start.20
  106.6 1.8 %collective-permute-done.19.c = f32[8,128]{1,0:T(8,128)S(1)} collective-permute-done((f32[8,128]{1,0:T(8,128)S(1)}, f32[8,128]{1,0:T(8,128)S(1)}, u32[]{:S(2)}, u32[]{:S(2)}) %collective-permute-start.19) | collective-permute-done | bytes 4128 | tf_op jit(solution)/shard_map/ppermute | solution.py:497
  109.2 20.3 %all_to_all.20 = f32[64,2,128]{2,1,0:T(2,128)S(1)} all-to-all(f32[64,2,128]{2,1,0:T(2,128)S(1)} %code_part.1), channel_id=1, replica_groups=mesh['y'=4,'x'=4,'zh'=4,'zb'=2,'k'=2] {'y','x','zh'}, dimensions={0} | all-to-all | bytes 131072 | tf_op jit(solution)/shard_map/all_to_all | solution.py:499
  131.6 1.9 %collective-permute-done.25.refs_3_ = bf16[16,256]{1,0:T(8,128)(2,1)S(1)} collective-permute-done((bf16[16,256]{1,0:T(8,128)(2,1)S(1)}, bf16[16,256]{1,0:T(8,128)(2,1)S(1)}, u32[]{:S(2)}, u32[]{:S(2)}) %collective-permute-start.25) | collective-permute-done | bytes 8224 | tf_op jit(solution)/shard_map/ppermute | solution.py:501
  133.6 1.5 scores.1.a
  138.0 1.8 %collective-permute-start.29 = (f32[4,128]{1,0:T(4,128)S(1)}, f32[4,128]{1,0:T(4,128)S(1)}, u32[]{:S(2)}, u32[]{:S(2)}) collective-permute-start(f32[4,128]{1,0:T(4,128)S(1)} %get-tuple-element.51), channel_id=1, source_target_pairs={{0,128},{64,192},{128,0},{192,64},{1,129},{65,193},{129,1},{193,65... | collective-permute-start | bytes 6152 | tf_op jit(solution)/shard_map/ppermute | solution.py:36
  139.8 1.3 collective-permute-start.30
  143.4 1.6 four_lists.1
  145.0 20.4 %all_to_all.21 = f32[128,4,128]{2,1,0:T(4,128)S(1)} all-to-all(f32[128,4,128]{2,1,0:T(4,128)S(1)} %four_lists.1), channel_id=1, replica_groups=mesh['y'=4,'x'=4,'zh'=4,'zb'=2,'k'=2] {'y','x','zh','zb'}, dimensions={0} | all-to-all | bytes 524288 | tf_op jit(solution)/shard_map/all_to_all | solution.py:506
  165.4 1.4 final_lists.1
  (69 shorter events, 20.3 us)
Async XLA Ops:
  0.0 4.1 %collective-permute-start.6 = (bf16[224,1024]{1,0:T(8,128)(2,1)}, bf16[224,1024]{1,0:T(8,128)(2,1)S(1)}, u32[]{:S(2)}, u32[]{:S(2)}) collective-permute-start(bf16[224,1024]{1,0:T(8,128)(2,1)} %bitcast.22), channel_id=1, source_target_pairs={{0,1},{1,0},{2,3},{3,2},{4,5},{5,4},{6,7},{7,6},{8,9},{9,8},{10,11... | collective-permute-start | bytes 1376264 | tf_op jit(solution)/shard_map/ppermute | solution.py:32
  0.0 4.1 %collective-permute-start.7 = (bf16[224,1024]{1,0:T(8,128)(2,1)}, bf16[224,1024]{1,0:T(8,128)(2,1)S(1)}, u32[]{:S(2)}, u32[]{:S(2)}) collective-permute-start(bf16[224,1024]{1,0:T(8,128)(2,1)} %bitcast.24), channel_id=1, source_target_pairs={{0,1},{1,0},{2,3},{3,2},{4,5},{5,4},{6,7},{7,6},{8,9},{9,8},{10,11... | collective-permute-start | bytes 1376264 | tf_op jit(solution)/shard_map/ppermute | solution.py:32
  0.5 3.6 %collective-permute-start.8 = (bf16[224,1024]{1,0:T(8,128)(2,1)}, bf16[224,1024]{1,0:T(8,128)(2,1)S(1)}, u32[]{:S(2)}, u32[]{:S(2)}) collective-permute-start(bf16[224,1024]{1,0:T(8,128)(2,1)} %w0.1), channel_id=1, source_target_pairs={{0,1},{1,0},{2,3},{3,2},{4,5},{5,4},{6,7},{7,6},{8,9},{9,8},{10,11... | collective-permute-start | bytes 1376264 | tf_op jit(solution)/shard_map/ppermute | solution.py:32
  1.9 1.3 collective-permute-start.4
  2.5 1.4 collective-permute-start.5
  5.0 39.5 %all-to-all-start = ((bf16[32,64,128]{2,1,0:T(8,128)(2,1)}), bf16[32,64,128]{2,1,0:T(8,128)(2,1)S(1)}, u32[]{:S(2)}, u32[]{:S(2)}) async-start(bf16[32,64,128]{2,1,0:T(8,128)(2,1)} %broadcast_in_dim.2), calls=%async_computation | async-start | bytes 1048576 | tf_op jit(solution)/shard_map/all_to_all | solution.py:41
  26.5 2.8 %collective-permute-start = (bf16[64,256]{1,0:T(8,128)(2,1)S(1)}, bf16[64,256]{1,0:T(8,128)(2,1)S(1)}, u32[]{:S(2)}, u32[]{:S(2)}) collective-permute-start(bf16[64,256]{1,0:T(8,128)(2,1)S(1)} %get-tuple-element.53), channel_id=1, source_target_pairs={{0,0},{1,1},{2,2},{3,3},{16,64},{17,65},{18,66},{19,67},{32,128},{... | collective-permute-start | bytes 98312 | tf_op jit(solution)/shard_map/ppermute | solution.py:478
  27.3 2.0 %collective-permute-start.1 = (bf16[64,256]{1,0:T(8,128)(2,1)S(1)}, bf16[64,256]{1,0:T(8,128)(2,1)S(1)}, u32[]{:S(2)}, u32[]{:S(2)}) collective-permute-start(bf16[64,256]{1,0:T(8,128)(2,1)S(1)} %get-tuple-element.54), channel_id=1, source_target_pairs={{0,1},{1,0},{2,3},{3,2},{16,65},{17,64},{18,67},{19,66},{32,129},{... | collective-permute-start | bytes 98312 | tf_op jit(solution)/shard_map/ppermute | solution.py:478
  27.4 11.7 %collective-permute-start.2 = (bf16[64,256]{1,0:T(8,128)(2,1)S(1)}, bf16[64,256]{1,0:T(8,128)(2,1)S(1)}, u32[]{:S(2)}, u32[]{:S(2)}) collective-permute-start(bf16[64,256]{1,0:T(8,128)(2,1)S(1)} %get-tuple-element.56), channel_id=1, source_target_pairs={{0,2},{1,3},{2,0},{3,1},{16,66},{17,67},{18,64},{19,65},{32,130},{... | collective-permute-start | bytes 98312 | tf_op jit(solution)/shard_map/ppermute | solution.py:478
  27.8 11.5 %collective-permute-start.3 = (bf16[64,256]{1,0:T(8,128)(2,1)S(1)}, bf16[64,256]{1,0:T(8,128)(2,1)S(1)}, u32[]{:S(2)}, u32[]{:S(2)}) collective-permute-start(bf16[64,256]{1,0:T(8,128)(2,1)S(1)} %get-tuple-element.55), channel_id=1, source_target_pairs={{0,3},{1,2},{2,1},{3,0},{16,67},{17,66},{18,65},{19,64},{32,131},{... | collective-permute-start | bytes 98312 | tf_op jit(solution)/shard_map/ppermute | solution.py:478
  46.0 8.0 %collective-permute-start.10 = (bf16[64,1024]{1,0:T(8,128)(2,1)S(1)}, bf16[64,1024]{1,0:T(8,128)(2,1)S(1)}, u32[]{:S(2)}, u32[]{:S(2)}) collective-permute-start(bf16[64,1024]{1,0:T(8,128)(2,1)S(1)} %get-tuple-element.37), channel_id=1, source_target_pairs={{0,128},{64,192},{128,0},{192,64},{1,129},{65,193},{129,1},{193,65... | collective-permute-start | bytes 393224 | tf_op jit(solution)/shard_map/ppermute | solution.py:36
  49.4 6.2 %collective-permute-start.11 = (bf16[64,1024]{1,0:T(8,128)(2,1)S(1)}, bf16[64,1024]{1,0:T(8,128)(2,1)S(1)}, u32[]{:S(2)}, u32[]{:S(2)}) collective-permute-start(bf16[64,1024]{1,0:T(8,128)(2,1)S(1)} %get-tuple-element.38), channel_id=1, source_target_pairs={{0,192},{64,0},{128,64},{192,128},{1,193},{65,1},{129,65},{193,129... | collective-permute-start | bytes 393224 | tf_op jit(solution)/shard_map/ppermute | solution.py:36
  49.9 6.6 %collective-permute-start.9 = (bf16[64,1024]{1,0:T(8,128)(2,1)S(1)}, bf16[64,1024]{1,0:T(8,128)(2,1)S(1)}, u32[]{:S(2)}, u32[]{:S(2)}) collective-permute-start(bf16[64,1024]{1,0:T(8,128)(2,1)S(1)} %get-tuple-element.36), channel_id=1, source_target_pairs={{0,64},{64,128},{128,192},{192,0},{1,65},{65,129},{129,193},{193,1... | collective-permute-start | bytes 393224 | tf_op jit(solution)/shard_map/ppermute | solution.py:36
  57.3 5.9 %collective-permute-start.12 = (bf16[64,512]{1,0:T(8,128)(2,1)S(1)}, bf16[64,512]{1,0:T(8,128)(2,1)S(1)}, u32[]{:S(2)}, u32[]{:S(2)}) collective-permute-start(bf16[64,512]{1,0:T(8,128)(2,1)S(1)} %get-tuple-element.40.a), channel_id=1, source_target_pairs={{0,64},{64,128},{128,192},{192,0},{1,65},{65,129},{129,193},{193,1... | collective-permute-start | bytes 196616 | tf_op jit(solution)/shard_map/ppermute | solution.py:36
  59.1 5.8 %collective-permute-start.13 = (bf16[64,512]{1,0:T(8,128)(2,1)S(1)}, bf16[64,512]{1,0:T(8,128)(2,1)S(1)}, u32[]{:S(2)}, u32[]{:S(2)}) collective-permute-start(bf16[64,512]{1,0:T(8,128)(2,1)S(1)} %get-tuple-element.40.a), channel_id=1, source_target_pairs={{0,128},{64,192},{128,0},{192,64},{1,129},{65,193},{129,1},{193,65... | collective-permute-start | bytes 196616 | tf_op jit(solution)/shard_map/ppermute | solution.py:36
  60.7 4.4 %collective-permute-start.14 = (bf16[64,512]{1,0:T(8,128)(2,1)S(1)}, bf16[64,512]{1,0:T(8,128)(2,1)S(1)}, u32[]{:S(2)}, u32[]{:S(2)}) collective-permute-start(bf16[64,512]{1,0:T(8,128)(2,1)S(1)} %get-tuple-element.40.a), channel_id=1, source_target_pairs={{0,192},{64,0},{128,64},{192,128},{1,193},{65,1},{129,65},{193,129... | collective-permute-start | bytes 196616 | tf_op jit(solution)/shard_map/ppermute | solution.py:36
  66.9 28.4 %all-to-all-start.1 = ((bf16[32,8,1024]{2,1,0:T(8,128)(2,1)}), bf16[32,8,1024]{2,1,0:T(8,128)(2,1)S(1)}, u32[]{:S(2)}, u32[]{:S(2)}) async-start(bf16[32,8,1024]{2,1,0:T(8,128)(2,1)} %bitcast.11), calls=%async_computation.1 | async-start | bytes 1048576 | tf_op jit(solution)/shard_map/all_to_all | solution.py:488
  75.8 29.6 %collective-permute-start.21 = (bf16[256,256]{1,0:T(8,128)(2,1)S(1)}, bf16[256,256]{1,0:T(8,128)(2,1)S(1)}, u32[]{:S(2)}, u32[]{:S(2)}) collective-permute-start(bf16[256,256]{1,0:T(8,128)(2,1)S(1)} %pad_maximum_fusion.w0), channel_id=1, source_target_pairs={{0,4},{4,8},{8,12},{12,0},{1,5},{5,9},{9,13},{13,1},{2,6},{6,10},{... | collective-permute-start | bytes 393224 | tf_op jit(solution)/shard_map/ppermute | solution.py:482
  78.3 28.3 %collective-permute-start.22 = (bf16[256,256]{1,0:T(8,128)(2,1)S(1)}, bf16[256,256]{1,0:T(8,128)(2,1)S(1)}, u32[]{:S(2)}, u32[]{:S(2)}) collective-permute-start(bf16[256,256]{1,0:T(8,128)(2,1)S(1)} %pad_maximum_fusion.w0), channel_id=1, source_target_pairs={{0,8},{4,12},{8,0},{12,4},{1,9},{5,13},{9,1},{13,5},{2,10},{6,14},... | collective-permute-start | bytes 393224 | tf_op jit(solution)/shard_map/ppermute | solution.py:482
  80.9 25.6 %collective-permute-start.23 = (bf16[256,256]{1,0:T(8,128)(2,1)S(1)}, bf16[256,256]{1,0:T(8,128)(2,1)S(1)}, u32[]{:S(2)}, u32[]{:S(2)}) collective-permute-start(bf16[256,256]{1,0:T(8,128)(2,1)S(1)} %pad_maximum_fusion.w0), channel_id=1, source_target_pairs={{0,12},{4,0},{8,4},{12,8},{1,13},{5,1},{9,5},{13,9},{2,14},{6,2},{... | collective-permute-start | bytes 393224 | tf_op jit(solution)/shard_map/ppermute | solution.py:482
  95.4 4.8 %collective-permute-start.15 = (f32[8,128]{1,0:T(8,128)S(1)}, f32[8,128]{1,0:T(8,128)S(1)}, u32[]{:S(2)}, u32[]{:S(2)}) collective-permute-start(f32[8,128]{1,0:T(8,128)S(1)} %get-tuple-element.43.a), channel_id=1, source_target_pairs={{0,64},{64,128},{128,192},{192,0},{1,65},{65,129},{129,193},{193,1... | collective-permute-start | bytes 12296 | tf_op jit(solution)/shard_map/ppermute | solution.py:36
  96.0 5.2 %collective-permute-start.16 = (f32[8,128]{1,0:T(8,128)S(1)}, f32[8,128]{1,0:T(8,128)S(1)}, u32[]{:S(2)}, u32[]{:S(2)}) collective-permute-start(f32[8,128]{1,0:T(8,128)S(1)} %get-tuple-element.43.a), channel_id=1, source_target_pairs={{0,128},{64,192},{128,0},{192,64},{1,129},{65,193},{129,1},{193,65... | collective-permute-start | bytes 12296 | tf_op jit(solution)/shard_map/ppermute | solution.py:36
  100.3 3.6 %collective-permute-start.17 = (f32[8,128]{1,0:T(8,128)S(1)}, f32[8,128]{1,0:T(8,128)S(1)}, u32[]{:S(2)}, u32[]{:S(2)}) collective-permute-start(f32[8,128]{1,0:T(8,128)S(1)} %get-tuple-element.43.a), channel_id=1, source_target_pairs={{0,192},{64,0},{128,64},{192,128},{1,193},{65,1},{129,65},{193,129... | collective-permute-start | bytes 12296 | tf_op jit(solution)/shard_map/ppermute | solution.py:36
  104.6 1.9 %collective-permute-start.18 = (f32[8,128]{1,0:T(8,128)S(1)}, f32[8,128]{1,0:T(8,128)S(1)}, u32[]{:S(2)}, u32[]{:S(2)}) collective-permute-start(f32[8,128]{1,0:T(8,128)S(1)} %get-tuple-element.45), channel_id=1, source_target_pairs={{0,1},{1,0},{2,3},{3,2},{4,5},{5,4},{6,7},{7,6},{8,9},{9,8},{10,11... | collective-permute-start | bytes 12296 | tf_op jit(solution)/shard_map/ppermute | solution.py:497
  104.7 3.7 %collective-permute-start.19 = (f32[8,128]{1,0:T(8,128)S(1)}, f32[8,128]{1,0:T(8,128)S(1)}, u32[]{:S(2)}, u32[]{:S(2)}) collective-permute-start(f32[8,128]{1,0:T(8,128)S(1)} %get-tuple-element.46), channel_id=1, source_target_pairs={{0,2},{1,3},{2,0},{3,1},{4,6},{5,7},{6,4},{7,5},{8,10},{9,11},{10,... | collective-permute-start | bytes 12296 | tf_op jit(solution)/shard_map/ppermute | solution.py:497
  105.4 3.0 %collective-permute-start.20 = (f32[8,128]{1,0:T(8,128)S(1)}, f32[8,128]{1,0:T(8,128)S(1)}, u32[]{:S(2)}, u32[]{:S(2)}) collective-permute-start(f32[8,128]{1,0:T(8,128)S(1)} %get-tuple-element.47), channel_id=1, source_target_pairs={{0,3},{1,2},{2,1},{3,0},{4,7},{5,6},{6,5},{7,4},{8,11},{9,10},{10,... | collective-permute-start | bytes 12296 | tf_op jit(solution)/shard_map/ppermute | solution.py:497
  129.6 2.0 %collective-permute-start.24 = (bf16[16,256]{1,0:T(8,128)(2,1)S(1)}, bf16[16,256]{1,0:T(8,128)(2,1)S(1)}, u32[]{:S(2)}, u32[]{:S(2)}) collective-permute-start(bf16[16,256]{1,0:T(8,128)(2,1)S(1)} %reduce_sum.9.refs_1_), channel_id=1, source_target_pairs={{0,1},{1,0},{2,3},{3,2},{4,5},{5,4},{6,7},{7,6},{8,9},{9,8},{10,11... | collective-permute-start | bytes 24584 | tf_op jit(solution)/shard_map/ppermute | solution.py:501
  129.7 3.7 %collective-permute-start.25 = (bf16[16,256]{1,0:T(8,128)(2,1)S(1)}, bf16[16,256]{1,0:T(8,128)(2,1)S(1)}, u32[]{:S(2)}, u32[]{:S(2)}) collective-permute-start(bf16[16,256]{1,0:T(8,128)(2,1)S(1)} %reduce_sum.9.refs_1_), channel_id=1, source_target_pairs={{0,2},{1,3},{2,0},{3,1},{4,6},{5,7},{6,4},{7,5},{8,10},{9,11},{10,... | collective-permute-start | bytes 24584 | tf_op jit(solution)/shard_map/ppermute | solution.py:501
  130.5 3.1 %collective-permute-start.26 = (bf16[16,256]{1,0:T(8,128)(2,1)S(1)}, bf16[16,256]{1,0:T(8,128)(2,1)S(1)}, u32[]{:S(2)}, u32[]{:S(2)}) collective-permute-start(bf16[16,256]{1,0:T(8,128)(2,1)S(1)} %reduce_sum.9.refs_1_), channel_id=1, source_target_pairs={{0,3},{1,2},{2,1},{3,0},{4,7},{5,6},{6,5},{7,4},{8,11},{9,10},{10,... | collective-permute-start | bytes 24584 | tf_op jit(solution)/shard_map/ppermute | solution.py:501
  137.4 4.9 %collective-permute-start.28 = (f32[4,128]{1,0:T(4,128)S(1)}, f32[4,128]{1,0:T(4,128)S(1)}, u32[]{:S(2)}, u32[]{:S(2)}) collective-permute-start(f32[4,128]{1,0:T(4,128)S(1)} %get-tuple-element.50), channel_id=1, source_target_pairs={{0,64},{64,128},{128,192},{192,0},{1,65},{65,129},{129,193},{193,1... | collective-permute-start | bytes 6152 | tf_op jit(solution)/shard_map/ppermute | solution.py:36
  138.0 5.1 %collective-permute-start.29 = (f32[4,128]{1,0:T(4,128)S(1)}, f32[4,128]{1,0:T(4,128)S(1)}, u32[]{:S(2)}, u32[]{:S(2)}) collective-permute-start(f32[4,128]{1,0:T(4,128)S(1)} %get-tuple-element.51), channel_id=1, source_target_pairs={{0,128},{64,192},{128,0},{192,64},{1,129},{65,193},{129,1},{193,65... | collective-permute-start | bytes 6152 | tf_op jit(solution)/shard_map/ppermute | solution.py:36
  139.8 3.6 %collective-permute-start.30 = (f32[4,128]{1,0:T(4,128)S(1)}, f32[4,128]{1,0:T(4,128)S(1)}, u32[]{:S(2)}, u32[]{:S(2)}) collective-permute-start(f32[4,128]{1,0:T(4,128)S(1)} %get-tuple-element.52), channel_id=1, source_target_pairs={{0,192},{64,0},{128,64},{192,128},{1,193},{65,1},{129,65},{193,129... | collective-permute-start | bytes 6152 | tf_op jit(solution)/shard_map/ppermute | solution.py:36
  (8 other events, 174.8 us)

commit v7 on v6

--- a/solution.py
+++ b/solution.py
@@ -45,26 +45,49 @@
     return lax.broadcasted_iota(jnp.int32, like, 1)
 
 
-def pack_kernel(place, h, own, other):
-    k = place[1]
+def pack_kernel(place, h, w, own, other, w0, w1, w2, w3):
+    k, zb = place[1], place[6]
     x = h[...].astype(F32).T
     for q in range(4):
         one = x[q * 32 : q * 32 + 16, :]
         two = x[q * 32 + 16 : q * 32 + 32, :]
         own[q * 16 : q * 16 + 16, :] = jnp.where(k == 0, one, two).astype(BF16)
         other[q * 16 : q * 16 + 16, :] = jnp.where(k == 0, two, one).astype(BF16)
-
-
-def pack(place, h):
-    part = shape((64, 64), BF16)
+    for r, out in enumerate((w0, w1, w2, w3)):
+        at = (zb * 2 + k) ^ r
+        out[...] = w[:, pl.ds(pl.multiple_of(at * 256, 256), 256)]
+
+
+def pack(place, h, w):
+    part, quarter = shape((64, 64), BF16), shape((64, 256), BF16)
     return pl.pallas_call(
         pack_kernel,
-        out_shape=(part, part),
-        in_specs=[SMEM, VMEM],
-        out_specs=(VMEM,) * 2,
+        out_shape=(part,) * 2 + (quarter,) * 4,
+        in_specs=[SMEM, VMEM, VMEM],
+        out_specs=(VMEM,) * 6,
         compiler_params=PARAMS,
         name="pack",
-    )(place, h)
+    )(place, h, w)
+
+
+def fan_kernel(place, own, other, out):
+    k = place[1]
+    a, b = own[...].astype(F32), other[...].astype(F32)
+    one, two = jnp.where(k == 0, a, b), jnp.where(k == 0, b, a)
+    block = jnp.concatenate([one, two], axis=1).astype(BF16)
+    for p in range(32):
+        out[p] = block
+
+
+def fan(place, own, other):
+    return pl.pallas_call(
+        fan_kernel,
+        out_shape=shape((32, 64, 128), BF16),
+        in_specs=[SMEM, VMEM, VMEM],
+        out_specs=VMEM,
+        compiler_params=PARAMS,
+        name="fan",
+    )(place, own, other)
 
 
 def gate_up_kernel(place, lengths, h, g0, u0, g1, u1, o0, o1, o2, o3, lhs, wide):
@@ -454,37 +477,34 @@
     y, x, zh, zb, k = (lax.axis_index(a) for a in QUERY_CORPUS)
     place = jnp.stack([y, k, 16 * k + 8 * zb, x // 2, 4 * zh, zh, zb, x]).astype(jnp.int32)
 
-    own, other = pack(place, hidden_in.T)
+    own, other, *quarters = pack(place, hidden_in.T, code_weight)
     swap = [(a * 4 + b, b * 4 + a) for a in range(4) for b in range(4)]
     straight = [(s * 2 + c, t * 2 + c) for s, t in swap for c in range(2)]
     crossed = [(s * 2 + c, t * 2 + 1 - c) for s, t in swap for c in range(2)]
     own = lax.ppermute(own, ("y", "x", "k"), straight)
     other = lax.ppermute(other, ("y", "x", "k"), crossed)
-    block = jnp.where(
-        k == 0, jnp.concatenate([own, other], axis=1), jnp.concatenate([other, own], axis=1)
-    )
     gate_rows, up_rows = gate_weight.T, up_weight.T
     gate_peer, up_peer, down_peer = (to_peer(w) for w in (gate_rows, up_rows, down_weight))
-    block, gate_peer, up_peer, down_peer = lax.optimization_barrier(
-        (block, gate_peer, up_peer, down_peer)
+    flips = [[(i, i ^ r) for i in range(4)] for r in range(4)]
+    quarters[1:] = [lax.ppermute(quarters[r], ("zb", "k"), flips[r]) for r in (1, 2, 3)]
+    own, other, gate_peer, up_peer, down_peer, quarters = lax.optimization_barrier(
+        (own, other, gate_peer, up_peer, down_peer, quarters)
     )
-    gathered = spread(block, XZ, 32)
-
-    at = 2 * zb + k
-    flipped = []
-    for r in range(4):
-        bits = lax.dynamic_slice_in_dim(code_weight, (at ^ r) * 256, 256, axis=1)
-        pairs = [(s * 4 + c, t * 4 + (c ^ r)) for s, t in swap for c in range(4)]
-        flipped.append(lax.ppermute(bits, ("y", "x", "zb", "k"), pairs))
-    rows = jnp.concatenate(flipped, axis=0)
+    gathered = lax.all_to_all(fan(place, own, other), XZ, 0, 0, tiled=True)
+
+    rows = lax.ppermute(jnp.concatenate(quarters, axis=0), ("y", "x"), swap)
     rows, gathered = lax.optimization_barrier((rows, gathered))
     turned = [[(i, (i + d) % 4) for i in range(4)] for d in range(4)]
-    code_rows = (rows, *(lax.ppermute(rows, "zh", turned[d]) for d in (1, 2, 3)))
+    code_rows = [rows, *(lax.ppermute(rows, "zh", turned[d]) for d in (1, 2, 3))]
 
     parts = gate_up(place, lengths, gathered, gate_rows, up_rows, gate_peer, up_peer)
     units, counts = hidden_of(place, parts[0], *(shifted(parts[d], d) for d in (1, 2, 3)))
     groups = (units, *(shifted(units, d) for d in (1, 2, 3)))
+    groups, code_rows[2] = lax.optimization_barrier((groups, code_rows[2]))
     branch = down(place, groups, down_weight, down_peer)
+    branch, code_rows[1], code_rows[3] = lax.optimization_barrier(
+        (branch, code_rows[1], code_rows[3])
+    )
     branch = lax.all_to_all(branch.reshape(32, 8, 1024), XZ, 0, 0, tiled=True)
     here = lax.dynamic_slice(
         gathered.reshape(4, 8, 64, 128), (x, 0, zh * 16 + zb * 8, 0), (1, 8, 8, 128)
@@ -493,7 +513,6 @@
     res, sq = residual_of(branch, here)
     sqs = (sq, *(shifted(sq, d) for d in (1, 2, 3)))
     mine = pool(place, counts, res, sqs)
-    flips = [[(i, i ^ r) for i in range(4)] for r in range(4)]
     pieces = (mine[0], *(lax.ppermute(mine[r], ("zb", "k"), flips[r]) for r in (1, 2, 3)))
     part = code_part(place, pieces, code_rows)
     codes = lax.all_to_all(part, ("y", "x", "zh"), 0, 0, tiled=True)

time: 167 us -> 171 us (1.024)
  waiting for transfers between devices: 45 us -> 52.1 us
  starting transfers between devices: 67.3 us -> 64.7 us
  blocking collectives: 40.7 us -> 38.9 us
    all_to_all x1, waiting for transfers between devices: 5.23 us -> 17.2 us  [per_device(): gathered = lax.all_to_all(fan(place, own, other), XZ, 0, 0, tiled=True)]
    ppermute x4, waiting for transfers between devices: 9.99 us -> 3.63 us  [the longest x3 3.62 us: per_device(): lax.ppermute(quarters[r], ('zb', 'k'), flips[r])]
    all_to_all x1, waiting for transfers between devices: 10.8 us -> 15.6 us  [per_device(): branch = lax.all_to_all(branch.reshape(32, 8, 1024), XZ, 0, 0, tiled=True)]
    ppermute x12, waiting for transfers between devices: 13.2 us -> 9.35 us  [shifted(): return lax.ppermute(x, 'y', [(i, (i + d) % 4) for i in range(4)])]
    all_to_all x1, starting transfers between devices: 21.4 us -> 25.1 us  [per_device(): gathered = lax.all_to_all(fan(place, own, other), XZ, 0, 0, tiled=True)]
    ppermute x3, starting transfers between devices: 8.69 us -> 5.07 us  [per_device(): lax.ppermute(rows, 'zh', turned[d])]
    ppermute x12, starting transfers between devices: 19.7 us -> 16.8 us  [shifted(): return lax.ppermute(x, 'y', [(i, (i + d) % 4) for i in range(4)])]
    all_to_all x1, blocking collectives: 20.3 us -> 18.3 us  [per_device(): codes = lax.all_to_all(part, ('y', 'x', 'zh'), 0, 0, tiled=True)]
  transfers between devices with their start and end apart: 33 -> 33, of which waited for: 20 -> 18; matrix products, arithmetic and copies ran while one was open for 0% -> 0% of each run, Pallas kernels for 1% -> 2%
where the time goes in v7:
time: 171 us
  starting transfers between devices  64.7 us (38%)
  waiting for transfers between devices  52.1 us (30%)
  blocking collectives  38.9 us (23%)
  Pallas kernels  13.1 us (8%)
  local copies, waits for them, and re-layouts  1.72 us (1%)
    all_to_all x1, starting transfers between devices, per_device(): gathered = lax.all_to_all(fan(place, own, other), XZ, 0, 0, tiled=True)  25.1 us
    all_to_all x1, blocking collectives, per_device(): arrived = lax.all_to_all(lists, YXZ, 0, 0, tiled=True)  20.5 us
    all_to_all x1, blocking collectives, per_device(): codes = lax.all_to_all(part, ('y', 'x', 'zh'), 0, 0, tiled=True)  18.3 us
    all_to_all x1, waiting for transfers between devices, per_device(): gathered = lax.all_to_all(fan(place, own, other), XZ, 0, 0, tiled=True)  17.2 us
    ppermute x12, starting transfers between devices, shifted(): return lax.ppermute(x, 'y', [(i, (i + d) % 4) for i in range(4)])  16.8 us
    all_to_all x1, waiting for transfers between devices, per_device(): branch = lax.all_to_all(branch.reshape(32, 8, 1024), XZ, 0, 0, tiled=True)  15.6 us
    all_to_all x1, starting transfers between devices, per_device(): branch = lax.all_to_all(branch.reshape(32, 8, 1024), XZ, 0, 0, tiled=True)  9.37 us
    ppermute x12, waiting for transfers between devices, shifted(): return lax.ppermute(x, 'y', [(i, (i + d) % 4) for i in range(4)])  9.35 us
  transfers between devices with their start and end apart: 33, of which 18 were waited for; matrix products, arithmetic and copies ran while one was open for 0% of the time, Pallas kernels for 2%

profile of v7, /device:TPU:32, one launch (start us, length us, event | category | flops | bytes accessed | tf_op | source)
XLA Modules:
  0.0 170.8 jit_solution(6081145207102684449)
XLA Ops:
  4.2 1.2 collective-permute-done.1.other
  5.3 1.8 %collective-permute-start.6 = (bf16[64,256]{1,0:T(8,128)(2,1)S(1)}, bf16[64,256]{1,0:T(8,128)(2,1)S(1)}, u32[]{:S(2)}, u32[]{:S(2)}) collective-permute-start(bf16[64,256]{1,0:T(8,128)(2,1)S(1)} %get-tuple-element.50), channel_id=1, source_target_pairs={{0,2},{1,3},{2,0},{3,1},{4,6},{5,7},{6,4},{7,5},{8,10},{9,11},{10,... | collective-permute-start | bytes 98312 | tf_op jit(solution)/shard_map/ppermute | solution.py:489
  7.2 2.1 %collective-permute-done.6 = bf16[64,256]{1,0:T(8,128)(2,1)S(1)} collective-permute-done((bf16[64,256]{1,0:T(8,128)(2,1)S(1)}, bf16[64,256]{1,0:T(8,128)(2,1)S(1)}, u32[]{:S(2)}, u32[]{:S(2)}) %collective-permute-start.6) | collective-permute-done | bytes 32800 | tf_op jit(solution)/shard_map/ppermute | solution.py:489
  9.2 1.6 collective-permute-done.7
  10.8 1.5 fan.1
  12.3 25.1 %all-to-all-start = ((bf16[32,64,128]{2,1,0:T(8,128)(2,1)}), bf16[32,64,128]{2,1,0:T(8,128)(2,1)S(1)}, u32[]{:S(2)}, u32[]{:S(2)}) async-start(bf16[32,64,128]{2,1,0:T(8,128)(2,1)} %fan.1), calls=%async_computation | async-start | bytes 1048576 | tf_op jit(solution)/shard_map/all_to_all | solution.py:493
  38.1 17.2 %all-to-all-done.h = bf16[32,64,128]{2,1,0:T(8,128)(2,1)S(1)} async-done(((bf16[32,64,128]{2,1,0:T(8,128)(2,1)}), bf16[32,64,128]{2,1,0:T(8,128)(2,1)S(1)}, u32[]{:S(2)}, u32[]{:S(2)}) %all-to-all-start) | async-done | bytes 524320 | tf_op jit(solution)/shard_map/all_to_all | solution.py:493
  55.3 1.4 gate_up.1
  56.7 1.4 collective-permute-start.9
  58.1 1.7 %collective-permute-start.10 = (bf16[64,1024]{1,0:T(8,128)(2,1)S(1)}, bf16[64,1024]{1,0:T(8,128)(2,1)S(1)}, u32[]{:S(2)}, u32[]{:S(2)}) collective-permute-start(bf16[64,1024]{1,0:T(8,128)(2,1)S(1)} %get-tuple-element.63), channel_id=1, source_target_pairs={{0,128},{64,192},{128,0},{192,64},{1,129},{65,193},{129,1},{193,65... | collective-permute-start | bytes 393224 | tf_op jit(solution)/shard_map/ppermute | solution.py:36
  60.9 2.1 %collective-permute-start.15 = (bf16[256,256]{1,0:T(8,128)(2,1)S(1)}, bf16[256,256]{1,0:T(8,128)(2,1)S(1)}, u32[]{:S(2)}, u32[]{:S(2)}) collective-permute-start(bf16[256,256]{1,0:T(8,128)(2,1)S(1)} %collective-permute-done.8.w0), channel_id=1, source_target_pairs={{0,8},{4,12},{8,0},{12,4},{1,9},{5,13},{9,1},{13,5},{2,10},{6,14},... | collective-permute-start | bytes 393224 | tf_op jit(solution)/shard_map/ppermute | solution.py:498
  63.0 2.6 %collective-permute-start.17 = (bf16[256,256]{1,0:T(8,128)(2,1)S(1)}, bf16[256,256]{1,0:T(8,128)(2,1)S(1)}, u32[]{:S(2)}, u32[]{:S(2)}) collective-permute-start(bf16[256,256]{1,0:T(8,128)(2,1)S(1)} %collective-permute-done.8.w0), channel_id=1, source_target_pairs={{0,12},{4,0},{8,4},{12,8},{1,13},{5,1},{9,5},{13,9},{2,14},{6,2},{... | collective-permute-start | bytes 393224 | tf_op jit(solution)/shard_map/ppermute | solution.py:498
  66.6 2.0 %collective-permute-start.14 = (bf16[64,512]{1,0:T(8,128)(2,1)S(1)}, bf16[64,512]{1,0:T(8,128)(2,1)S(1)}, u32[]{:S(2)}, u32[]{:S(2)}) collective-permute-start(bf16[64,512]{1,0:T(8,128)(2,1)S(1)} %get-tuple-element.68.a), channel_id=1, source_target_pairs={{0,192},{64,0},{128,64},{192,128},{1,193},{65,1},{129,65},{193,129... | collective-permute-start | bytes 196616 | tf_op jit(solution)/shard_map/ppermute | solution.py:36
  68.6 2.1 %collective-permute-start.13 = (bf16[64,512]{1,0:T(8,128)(2,1)S(1)}, bf16[64,512]{1,0:T(8,128)(2,1)S(1)}, u32[]{:S(2)}, u32[]{:S(2)}) collective-permute-start(bf16[64,512]{1,0:T(8,128)(2,1)S(1)} %get-tuple-element.68.a), channel_id=1, source_target_pairs={{0,128},{64,192},{128,0},{192,64},{1,129},{65,193},{129,1},{193,65... | collective-permute-start | bytes 196616 | tf_op jit(solution)/shard_map/ppermute | solution.py:36
  71.2 2.3 %collective-permute-start.12 = (bf16[64,512]{1,0:T(8,128)(2,1)S(1)}, bf16[64,512]{1,0:T(8,128)(2,1)S(1)}, u32[]{:S(2)}, u32[]{:S(2)}) collective-permute-start(bf16[64,512]{1,0:T(8,128)(2,1)S(1)} %get-tuple-element.68.a), channel_id=1, source_target_pairs={{0,64},{64,128},{128,192},{192,0},{1,65},{65,129},{129,193},{193,1... | collective-permute-start | bytes 196616 | tf_op jit(solution)/shard_map/ppermute | solution.py:36
  74.4 2.3 %collective-permute-done.12.b = bf16[64,512]{1,0:T(8,128)(2,1)S(1)} collective-permute-done((bf16[64,512]{1,0:T(8,128)(2,1)S(1)}, bf16[64,512]{1,0:T(8,128)(2,1)S(1)}, u32[]{:S(2)}, u32[]{:S(2)}) %collective-permute-start.12) | collective-permute-done | bytes 65568 | tf_op jit(solution)/shard_map/ppermute | solution.py:36
  76.7 1.8 %down.1 = bf16[256,1024]{1,0:T(8,128)(2,1)} custom-call(s32[8]{0:T(128)S(1)} %stack.35.place.refs_0_, bf16[64,512]{1,0:T(8,128)(2,1)S(1)} %get-tuple-element.68.a, bf16[64,512]{1,0:T(8,128)(2,1)S(1)} %collective-permute-done.12.b, bf16[64,512]{1,0:T(8,128)(2,1)S(1)} %collective-permute-done.13.c, bf16[64,512]{1,0:T(8,128)(2,1)S(1)} %collective-permute-done.14.d, ...), custom_call_target="tpu_custom_call" | custom-call | tf_op jit(solution)/shard_map/down/pallas_call | solution.py:176
  78.5 9.4 %all-to-all-start.1 = ((bf16[32,8,1024]{2,1,0:T(8,128)(2,1)}), bf16[32,8,1024]{2,1,0:T(8,128)(2,1)S(1)}, u32[]{:S(2)}, u32[]{:S(2)}) async-start(bf16[32,8,1024]{2,1,0:T(8,128)(2,1)} %bitcast.11), calls=%async_computation.1 | async-start | bytes 1048576 | tf_op jit(solution)/shard_map/all_to_all | solution.py:508
  87.9 15.6 %all-to-all-done.1.parts = bf16[32,8,1024]{2,1,0:T(8,128)(2,1)S(1)} async-done(((bf16[32,8,1024]{2,1,0:T(8,128)(2,1)}), bf16[32,8,1024]{2,1,0:T(8,128)(2,1)S(1)}, u32[]{:S(2)}, u32[]{:S(2)}) %all-to-all-start.1) | async-done | bytes 524320 | tf_op jit(solution)/shard_map/all_to_all | solution.py:508
  104.8 1.1 collective-permute-start.18
  105.9 1.3 collective-permute-done.20.d
  107.2 1.6 collective-permute-done.19.c
  110.8 1.8 %collective-permute-start.23 = (f32[8,128]{1,0:T(8,128)S(1)}, f32[8,128]{1,0:T(8,128)S(1)}, u32[]{:S(2)}, u32[]{:S(2)}) collective-permute-start(f32[8,128]{1,0:T(8,128)S(1)} %get-tuple-element.79), channel_id=1, source_target_pairs={{0,3},{1,2},{2,1},{3,0},{4,7},{5,6},{6,5},{7,4},{8,11},{9,10},{10,... | collective-permute-start | bytes 12296 | tf_op jit(solution)/shard_map/ppermute | solution.py:516
  112.6 1.8 %collective-permute-done.22.c = f32[8,128]{1,0:T(8,128)S(1)} collective-permute-done((f32[8,128]{1,0:T(8,128)S(1)}, f32[8,128]{1,0:T(8,128)S(1)}, u32[]{:S(2)}, u32[]{:S(2)}) %collective-permute-start.22) | collective-permute-done | bytes 4128 | tf_op jit(solution)/shard_map/ppermute | solution.py:516
  115.2 18.3 %all_to_all.20 = f32[64,2,128]{2,1,0:T(2,128)S(1)} all-to-all(f32[64,2,128]{2,1,0:T(2,128)S(1)} %code_part.1), channel_id=1, replica_groups=mesh['y'=4,'x'=4,'zh'=4,'zb'=2,'k'=2] {'y','x','zh'}, dimensions={0} | all-to-all | bytes 131072 | tf_op jit(solution)/shard_map/all_to_all | solution.py:518
  135.5 1.2 collective-permute-done.26.refs_4_
  137.5 1.5 scores.1.a
  141.8 1.8 %collective-permute-start.29 = (f32[4,128]{1,0:T(4,128)S(1)}, f32[4,128]{1,0:T(4,128)S(1)}, u32[]{:S(2)}, u32[]{:S(2)}) collective-permute-start(f32[4,128]{1,0:T(4,128)S(1)} %get-tuple-element.85), channel_id=1, source_target_pairs={{0,128},{64,192},{128,0},{192,64},{1,129},{65,193},{129,1},{193,65... | collective-permute-start | bytes 6152 | tf_op jit(solution)/shard_map/ppermute | solution.py:36
  143.7 1.4 collective-permute-start.30
  147.3 1.6 four_lists.1
  148.8 20.5 %all_to_all.21 = f32[128,4,128]{2,1,0:T(4,128)S(1)} all-to-all(f32[128,4,128]{2,1,0:T(4,128)S(1)} %four_lists.1), channel_id=1, replica_groups=mesh['y'=4,'x'=4,'zh'=4,'zb'=2,'k'=2] {'y','x','zh','zb'}, dimensions={0} | all-to-all | bytes 524288 | tf_op jit(solution)/shard_map/all_to_all | solution.py:525
  169.4 1.4 final_lists.1
  (67 shorter events, 20.1 us)
Async XLA Ops:
  0.0 10.8 %collective-permute-start.2 = (bf16[224,1024]{1,0:T(8,128)(2,1)}, bf16[224,1024]{1,0:T(8,128)(2,1)S(1)}, u32[]{:S(2)}, u32[]{:S(2)}) collective-permute-start(bf16[224,1024]{1,0:T(8,128)(2,1)} %bitcast.22), channel_id=1, source_target_pairs={{0,1},{1,0},{2,3},{3,2},{4,5},{5,4},{6,7},{7,6},{8,9},{9,8},{10,11... | collective-permute-start | bytes 1376264 | tf_op jit(solution)/shard_map/ppermute | solution.py:32
  0.0 10.8 %collective-permute-start.3 = (bf16[224,1024]{1,0:T(8,128)(2,1)}, bf16[224,1024]{1,0:T(8,128)(2,1)S(1)}, u32[]{:S(2)}, u32[]{:S(2)}) collective-permute-start(bf16[224,1024]{1,0:T(8,128)(2,1)} %bitcast.24), channel_id=1, source_target_pairs={{0,1},{1,0},{2,3},{3,2},{4,5},{5,4},{6,7},{7,6},{8,9},{9,8},{10,11... | collective-permute-start | bytes 1376264 | tf_op jit(solution)/shard_map/ppermute | solution.py:32
  0.5 10.3 %collective-permute-start.4 = (bf16[224,1024]{1,0:T(8,128)(2,1)}, bf16[224,1024]{1,0:T(8,128)(2,1)S(1)}, u32[]{:S(2)}, u32[]{:S(2)}) collective-permute-start(bf16[224,1024]{1,0:T(8,128)(2,1)} %w0.1), channel_id=1, source_target_pairs={{0,1},{1,0},{2,3},{3,2},{4,5},{5,4},{6,7},{7,6},{8,9},{9,8},{10,11... | collective-permute-start | bytes 1376264 | tf_op jit(solution)/shard_map/ppermute | solution.py:32
  2.8 4.4 %collective-permute-start.5 = (bf16[64,256]{1,0:T(8,128)(2,1)S(1)}, bf16[64,256]{1,0:T(8,128)(2,1)S(1)}, u32[]{:S(2)}, u32[]{:S(2)}) collective-permute-start(bf16[64,256]{1,0:T(8,128)(2,1)S(1)} %get-tuple-element.49), channel_id=1, source_target_pairs={{0,1},{1,0},{2,3},{3,2},{4,5},{5,4},{6,7},{7,6},{8,9},{9,8},{10,11... | collective-permute-start | bytes 98312 | tf_op jit(solution)/shard_map/ppermute | solution.py:489
  4.0 1.3 collective-permute-start.1
  5.3 3.9 %collective-permute-start.6 = (bf16[64,256]{1,0:T(8,128)(2,1)S(1)}, bf16[64,256]{1,0:T(8,128)(2,1)S(1)}, u32[]{:S(2)}, u32[]{:S(2)}) collective-permute-start(bf16[64,256]{1,0:T(8,128)(2,1)S(1)} %get-tuple-element.50), channel_id=1, source_target_pairs={{0,2},{1,3},{2,0},{3,1},{4,6},{5,7},{6,4},{7,5},{8,10},{9,11},{10,... | collective-permute-start | bytes 98312 | tf_op jit(solution)/shard_map/ppermute | solution.py:489
  7.2 3.6 %collective-permute-start.7 = (bf16[64,256]{1,0:T(8,128)(2,1)S(1)}, bf16[64,256]{1,0:T(8,128)(2,1)S(1)}, u32[]{:S(2)}, u32[]{:S(2)}) collective-permute-start(bf16[64,256]{1,0:T(8,128)(2,1)S(1)} %get-tuple-element.51), channel_id=1, source_target_pairs={{0,3},{1,2},{2,1},{3,0},{4,7},{5,6},{6,5},{7,4},{8,11},{9,10},{10,... | collective-permute-start | bytes 98312 | tf_op jit(solution)/shard_map/ppermute | solution.py:489
  12.3 43.0 %all-to-all-start = ((bf16[32,64,128]{2,1,0:T(8,128)(2,1)}), bf16[32,64,128]{2,1,0:T(8,128)(2,1)S(1)}, u32[]{:S(2)}, u32[]{:S(2)}) async-start(bf16[32,64,128]{2,1,0:T(8,128)(2,1)} %fan.1), calls=%async_computation | async-start | bytes 1048576 | tf_op jit(solution)/shard_map/all_to_all | solution.py:493
  37.4 0.7 collective-permute-start.8
  56.7 8.9 %collective-permute-start.9 = (bf16[64,1024]{1,0:T(8,128)(2,1)S(1)}, bf16[64,1024]{1,0:T(8,128)(2,1)S(1)}, u32[]{:S(2)}, u32[]{:S(2)}) collective-permute-start(bf16[64,1024]{1,0:T(8,128)(2,1)S(1)} %get-tuple-element.62), channel_id=1, source_target_pairs={{0,64},{64,128},{128,192},{192,0},{1,65},{65,129},{129,193},{193,1... | collective-permute-start | bytes 393224 | tf_op jit(solution)/shard_map/ppermute | solution.py:36
  58.1 7.9 %collective-permute-start.10 = (bf16[64,1024]{1,0:T(8,128)(2,1)S(1)}, bf16[64,1024]{1,0:T(8,128)(2,1)S(1)}, u32[]{:S(2)}, u32[]{:S(2)}) collective-permute-start(bf16[64,1024]{1,0:T(8,128)(2,1)S(1)} %get-tuple-element.63), channel_id=1, source_target_pairs={{0,128},{64,192},{128,0},{192,64},{1,129},{65,193},{129,1},{193,65... | collective-permute-start | bytes 393224 | tf_op jit(solution)/shard_map/ppermute | solution.py:36
  59.8 6.1 %collective-permute-start.11 = (bf16[64,1024]{1,0:T(8,128)(2,1)S(1)}, bf16[64,1024]{1,0:T(8,128)(2,1)S(1)}, u32[]{:S(2)}, u32[]{:S(2)}) collective-permute-start(bf16[64,1024]{1,0:T(8,128)(2,1)S(1)} %get-tuple-element.64), channel_id=1, source_target_pairs={{0,192},{64,0},{128,64},{192,128},{1,193},{65,1},{129,65},{193,129... | collective-permute-start | bytes 393224 | tf_op jit(solution)/shard_map/ppermute | solution.py:36
  60.9 10.4 %collective-permute-start.15 = (bf16[256,256]{1,0:T(8,128)(2,1)S(1)}, bf16[256,256]{1,0:T(8,128)(2,1)S(1)}, u32[]{:S(2)}, u32[]{:S(2)}) collective-permute-start(bf16[256,256]{1,0:T(8,128)(2,1)S(1)} %collective-permute-done.8.w0), channel_id=1, source_target_pairs={{0,8},{4,12},{8,0},{12,4},{1,9},{5,13},{9,1},{13,5},{2,10},{6,14},... | collective-permute-start | bytes 393224 | tf_op jit(solution)/shard_map/ppermute | solution.py:498
  63.0 15.5 %collective-permute-start.17 = (bf16[256,256]{1,0:T(8,128)(2,1)S(1)}, bf16[256,256]{1,0:T(8,128)(2,1)S(1)}, u32[]{:S(2)}, u32[]{:S(2)}) collective-permute-start(bf16[256,256]{1,0:T(8,128)(2,1)S(1)} %collective-permute-done.8.w0), channel_id=1, source_target_pairs={{0,12},{4,0},{8,4},{12,8},{1,13},{5,1},{9,5},{13,9},{2,14},{6,2},{... | collective-permute-start | bytes 393224 | tf_op jit(solution)/shard_map/ppermute | solution.py:498
  65.6 12.9 %collective-permute-start.16 = (bf16[256,256]{1,0:T(8,128)(2,1)S(1)}, bf16[256,256]{1,0:T(8,128)(2,1)S(1)}, u32[]{:S(2)}, u32[]{:S(2)}) collective-permute-start(bf16[256,256]{1,0:T(8,128)(2,1)S(1)} %collective-permute-done.8.w0), channel_id=1, source_target_pairs={{0,4},{4,8},{8,12},{12,0},{1,5},{5,9},{9,13},{13,1},{2,6},{6,10},{... | collective-permute-start | bytes 393224 | tf_op jit(solution)/shard_map/ppermute | solution.py:498
  66.6 6.9 %collective-permute-start.14 = (bf16[64,512]{1,0:T(8,128)(2,1)S(1)}, bf16[64,512]{1,0:T(8,128)(2,1)S(1)}, u32[]{:S(2)}, u32[]{:S(2)}) collective-permute-start(bf16[64,512]{1,0:T(8,128)(2,1)S(1)} %get-tuple-element.68.a), channel_id=1, source_target_pairs={{0,192},{64,0},{128,64},{192,128},{1,193},{65,1},{129,65},{193,129... | collective-permute-start | bytes 196616 | tf_op jit(solution)/shard_map/ppermute | solution.py:36
  68.6 5.8 %collective-permute-start.13 = (bf16[64,512]{1,0:T(8,128)(2,1)S(1)}, bf16[64,512]{1,0:T(8,128)(2,1)S(1)}, u32[]{:S(2)}, u32[]{:S(2)}) collective-permute-start(bf16[64,512]{1,0:T(8,128)(2,1)S(1)} %get-tuple-element.68.a), channel_id=1, source_target_pairs={{0,128},{64,192},{128,0},{192,64},{1,129},{65,193},{129,1},{193,65... | collective-permute-start | bytes 196616 | tf_op jit(solution)/shard_map/ppermute | solution.py:36
  71.2 5.5 %collective-permute-start.12 = (bf16[64,512]{1,0:T(8,128)(2,1)S(1)}, bf16[64,512]{1,0:T(8,128)(2,1)S(1)}, u32[]{:S(2)}, u32[]{:S(2)}) collective-permute-start(bf16[64,512]{1,0:T(8,128)(2,1)S(1)} %get-tuple-element.68.a), channel_id=1, source_target_pairs={{0,64},{64,128},{128,192},{192,0},{1,65},{65,129},{129,193},{193,1... | collective-permute-start | bytes 196616 | tf_op jit(solution)/shard_map/ppermute | solution.py:36
  78.5 25.0 %all-to-all-start.1 = ((bf16[32,8,1024]{2,1,0:T(8,128)(2,1)}), bf16[32,8,1024]{2,1,0:T(8,128)(2,1)S(1)}, u32[]{:S(2)}, u32[]{:S(2)}) async-start(bf16[32,8,1024]{2,1,0:T(8,128)(2,1)} %bitcast.11), calls=%async_computation.1 | async-start | bytes 1048576 | tf_op jit(solution)/shard_map/all_to_all | solution.py:508
  103.6 3.6 %collective-permute-start.20 = (f32[8,128]{1,0:T(8,128)S(1)}, f32[8,128]{1,0:T(8,128)S(1)}, u32[]{:S(2)}, u32[]{:S(2)}) collective-permute-start(f32[8,128]{1,0:T(8,128)S(1)} %get-tuple-element.75.a), channel_id=1, source_target_pairs={{0,192},{64,0},{128,64},{192,128},{1,193},{65,1},{129,65},{193,129... | collective-permute-start | bytes 12296 | tf_op jit(solution)/shard_map/ppermute | solution.py:36
  103.6 5.2 %collective-permute-start.19 = (f32[8,128]{1,0:T(8,128)S(1)}, f32[8,128]{1,0:T(8,128)S(1)}, u32[]{:S(2)}, u32[]{:S(2)}) collective-permute-start(f32[8,128]{1,0:T(8,128)S(1)} %get-tuple-element.75.a), channel_id=1, source_target_pairs={{0,128},{64,192},{128,0},{192,64},{1,129},{65,193},{129,1},{193,65... | collective-permute-start | bytes 12296 | tf_op jit(solution)/shard_map/ppermute | solution.py:36
  104.8 5.1 %collective-permute-start.18 = (f32[8,128]{1,0:T(8,128)S(1)}, f32[8,128]{1,0:T(8,128)S(1)}, u32[]{:S(2)}, u32[]{:S(2)}) collective-permute-start(f32[8,128]{1,0:T(8,128)S(1)} %get-tuple-element.75.a), channel_id=1, source_target_pairs={{0,64},{64,128},{128,192},{192,0},{1,65},{65,129},{129,193},{193,1... | collective-permute-start | bytes 12296 | tf_op jit(solution)/shard_map/ppermute | solution.py:36
  110.7 1.9 %collective-permute-start.21 = (f32[8,128]{1,0:T(8,128)S(1)}, f32[8,128]{1,0:T(8,128)S(1)}, u32[]{:S(2)}, u32[]{:S(2)}) collective-permute-start(f32[8,128]{1,0:T(8,128)S(1)} %get-tuple-element.77), channel_id=1, source_target_pairs={{0,1},{1,0},{2,3},{3,2},{4,5},{5,4},{6,7},{7,6},{8,9},{9,8},{10,11... | collective-permute-start | bytes 12296 | tf_op jit(solution)/shard_map/ppermute | solution.py:516
  110.7 3.7 %collective-permute-start.22 = (f32[8,128]{1,0:T(8,128)S(1)}, f32[8,128]{1,0:T(8,128)S(1)}, u32[]{:S(2)}, u32[]{:S(2)}) collective-permute-start(f32[8,128]{1,0:T(8,128)S(1)} %get-tuple-element.78), channel_id=1, source_target_pairs={{0,2},{1,3},{2,0},{3,1},{4,6},{5,7},{6,4},{7,5},{8,10},{9,11},{10,... | collective-permute-start | bytes 12296 | tf_op jit(solution)/shard_map/ppermute | solution.py:516
  110.8 3.6 %collective-permute-start.23 = (f32[8,128]{1,0:T(8,128)S(1)}, f32[8,128]{1,0:T(8,128)S(1)}, u32[]{:S(2)}, u32[]{:S(2)}) collective-permute-start(f32[8,128]{1,0:T(8,128)S(1)} %get-tuple-element.79), channel_id=1, source_target_pairs={{0,3},{1,2},{2,1},{3,0},{4,7},{5,6},{6,5},{7,4},{8,11},{9,10},{10,... | collective-permute-start | bytes 12296 | tf_op jit(solution)/shard_map/ppermute | solution.py:516
  133.6 3.2 %collective-permute-start.26 = (bf16[16,256]{1,0:T(8,128)(2,1)S(1)}, bf16[16,256]{1,0:T(8,128)(2,1)S(1)}, u32[]{:S(2)}, u32[]{:S(2)}) collective-permute-start(bf16[16,256]{1,0:T(8,128)(2,1)S(1)} %reduce_sum.9.refs_1_), channel_id=1, source_target_pairs={{0,3},{1,2},{2,1},{3,0},{4,7},{5,6},{6,5},{7,4},{8,11},{9,10},{10,... | collective-permute-start | bytes 24584 | tf_op jit(solution)/shard_map/ppermute | solution.py:520
  133.7 3.8 %collective-permute-start.25 = (bf16[16,256]{1,0:T(8,128)(2,1)S(1)}, bf16[16,256]{1,0:T(8,128)(2,1)S(1)}, u32[]{:S(2)}, u32[]{:S(2)}) collective-permute-start(bf16[16,256]{1,0:T(8,128)(2,1)S(1)} %reduce_sum.9.refs_1_), channel_id=1, source_target_pairs={{0,2},{1,3},{2,0},{3,1},{4,6},{5,7},{6,4},{7,5},{8,10},{9,11},{10,... | collective-permute-start | bytes 24584 | tf_op jit(solution)/shard_map/ppermute | solution.py:520
  134.8 2.7 %collective-permute-start.24 = (bf16[16,256]{1,0:T(8,128)(2,1)S(1)}, bf16[16,256]{1,0:T(8,128)(2,1)S(1)}, u32[]{:S(2)}, u32[]{:S(2)}) collective-permute-start(bf16[16,256]{1,0:T(8,128)(2,1)S(1)} %reduce_sum.9.refs_1_), channel_id=1, source_target_pairs={{0,1},{1,0},{2,3},{3,2},{4,5},{5,4},{6,7},{7,6},{8,9},{9,8},{10,11... | collective-permute-start | bytes 24584 | tf_op jit(solution)/shard_map/ppermute | solution.py:520
  139.0 1.2 collective-permute-start.27
  141.2 4.9 %collective-permute-start.28 = (f32[4,128]{1,0:T(4,128)S(1)}, f32[4,128]{1,0:T(4,128)S(1)}, u32[]{:S(2)}, u32[]{:S(2)}) collective-permute-start(f32[4,128]{1,0:T(4,128)S(1)} %get-tuple-element.84), channel_id=1, source_target_pairs={{0,64},{64,128},{128,192},{192,0},{1,65},{65,129},{129,193},{193,1... | collective-permute-start | bytes 6152 | tf_op jit(solution)/shard_map/ppermute | solution.py:36
  141.8 5.1 %collective-permute-start.29 = (f32[4,128]{1,0:T(4,128)S(1)}, f32[4,128]{1,0:T(4,128)S(1)}, u32[]{:S(2)}, u32[]{:S(2)}) collective-permute-start(f32[4,128]{1,0:T(4,128)S(1)} %get-tuple-element.85), channel_id=1, source_target_pairs={{0,128},{64,192},{128,0},{192,64},{1,129},{65,193},{129,1},{193,65... | collective-permute-start | bytes 6152 | tf_op jit(solution)/shard_map/ppermute | solution.py:36
  143.7 3.6 %collective-permute-start.30 = (f32[4,128]{1,0:T(4,128)S(1)}, f32[4,128]{1,0:T(4,128)S(1)}, u32[]{:S(2)}, u32[]{:S(2)}) collective-permute-start(f32[4,128]{1,0:T(4,128)S(1)} %get-tuple-element.86), channel_id=1, source_target_pairs={{0,192},{64,0},{128,64},{192,128},{1,193},{65,1},{129,65},{193,129... | collective-permute-start | bytes 6152 | tf_op jit(solution)/shard_map/ppermute | solution.py:36
  (8 other events, 175.9 us)

commit v8 on v5

--- a/solution.py
+++ b/solution.py
@@ -45,32 +45,29 @@
     return lax.broadcasted_iota(jnp.int32, like, 1)
 
 
-def pack_kernel(place, lengths, h, own, other):
+def pack_kernel(place, h, own, other):
     k = place[1]
+    x = h[...].astype(F32).T
     for q in range(4):
-        one = h[q * 32 : q * 32 + 16, :]
-        two = h[q * 32 + 16 : q * 32 + 32, :]
-        own[q * 16 : q * 16 + 16, :] = jnp.where(k == 0, one, two)
-        other[q * 16 : q * 16 + 16, :] = jnp.where(k == 0, two, one)
-    query = lax.broadcasted_iota(jnp.int32, (16, 64), 0) // 4
-    counts = jnp.zeros((16, 64), jnp.int32)
-    for q in range(4):
-        counts = jnp.where(query == q, lengths[q], counts)
-    own[64:80, :] = counts.astype(F32).astype(BF16)
-
-
-def pack(place, lengths, h):
+        one = x[q * 32 : q * 32 + 16, :]
+        two = x[q * 32 + 16 : q * 32 + 32, :]
+        own[q * 16 : q * 16 + 16, :] = jnp.where(k == 0, one, two).astype(BF16)
+        other[q * 16 : q * 16 + 16, :] = jnp.where(k == 0, two, one).astype(BF16)
+
+
+def pack(place, h):
+    part = shape((64, 64), BF16)
     return pl.pallas_call(
         pack_kernel,
-        out_shape=(shape((80, 64), BF16), shape((64, 64), BF16)),
-        in_specs=[SMEM, SMEM, VMEM],
+        out_shape=(part, part),
+        in_specs=[SMEM, VMEM],
         out_specs=(VMEM,) * 2,
         compiler_params=PARAMS,
         name="pack",
-    )(place, lengths, h)
-
-
-def gate_up_kernel(place, h, g0, u0, g1, u1, o0, o1, o2, o3, lhs, wide):
+    )(place, h)
+
+
+def gate_up_kernel(place, lengths, h, g0, u0, g1, u1, o0, o1, o2, o3, lhs, wide):
     y = place[0]
     for d in range(4):
         i = (y + d) % 4
@@ -93,25 +90,32 @@
             block = jnp.where(col == 224, top, block)
             block = jnp.where(col == 225, mid, block)
             block = jnp.where(col == 226, low, block)
+            for q in range(4):
+                block = jnp.where(col == 228 + q, lengths[q].astype(F32), block)
         block = block.astype(BF16)
         for d, o in enumerate((o0, o1, o2, o3)):
             o[:, b * 256 : b * 256 + 256] = block[d * 64 : d * 64 + 64]
 
 
-def gate_up(place, h, g0, u0, g1, u1):
+def gate_up(place, lengths, h, g0, u0, g1, u1):
     part = shape((64, 1024), BF16)
     return pl.pallas_call(
         gate_up_kernel,
         out_shape=(part,) * 4,
-        in_specs=[SMEM] + [VMEM] * 5,
+        in_specs=[SMEM] * 2 + [VMEM] * 5,
         out_specs=(VMEM,) * 4,
         scratch_shapes=[pltpu.VMEM((256, 1024), BF16), pltpu.VMEM((256, 256), F32)],
         compiler_params=PARAMS,
         name="gate_up",
-    )(place, h, g0, u0, g1, u1)
-
-
-def hidden_kernel(a, b, c, d, out):
+    )(place, lengths, h, g0, u0, g1, u1)
+
+
+def hidden_kernel(place, a, b, c, d, out, counts):
+    y, x = place[0], place[7]
+    held = jnp.zeros((8, 128), F32)
+    for s, part in enumerate((a, b, c, d)):
+        held = jnp.where((y - s + 4) % 4 == x, part[0:8, 128:256].astype(F32), held)
+    counts[...] = held
     total = a[...].astype(F32) + b[...].astype(F32) + c[...].astype(F32) + d[...].astype(F32)
     col = lanes((64, 256))
     first = total[:, 0:256]
@@ -124,15 +128,15 @@
         out[:, b * 256 : b * 256 + 256] = jnp.where(col < 224, units, 0.0).astype(BF16)
 
 
-def hidden_of(a, b, c, d):
+def hidden_of(place, a, b, c, d):
     return pl.pallas_call(
         hidden_kernel,
-        out_shape=shape((64, 512), BF16),
-        in_specs=[VMEM] * 4,
-        out_specs=VMEM,
+        out_shape=(shape((64, 512), BF16), shape((8, 128), F32)),
+        in_specs=[SMEM] + [VMEM] * 4,
+        out_specs=(VMEM,) * 2,
         compiler_params=PARAMS,
         name="hidden_units",
-    )(a, b, c, d)
+    )(place, a, b, c, d)
 
 
 def down_kernel(place, a, b, c, d, w0, w1, out, lhs):
@@ -177,12 +181,11 @@
 
 
 def pool_kernel(place, counts, res, a, b, c, d, same, other):
-    first, row, zb = place[2], place[4], place[6]
+    first, zh, zb = place[2], place[5], place[6]
     sq = (a[...] + b[...] + c[...] + d[...])[:, 0:1]
     slots = lax.broadcasted_iota(jnp.int32, (8, 1), 0) + first
-    held = counts[...].astype(F32)
-    held = jnp.where(lax.broadcasted_iota(jnp.int32, (16, 64), 0) == row, held, 0.0)
-    count = jnp.max(jnp.max(held, axis=1, keepdims=True), axis=0, keepdims=True)
+    held = jnp.where(lanes((1, 128)) == 100 + zh, counts[0:1, :], 0.0)
+    count = jnp.max(held, axis=1, keepdims=True)
     weight = jnp.where(slots.astype(F32) < count, lax.rsqrt(sq / D + EPS), 0.0)
     pooled = jnp.sum(res[...] * weight, axis=0, keepdims=True) / count
     ahead = jnp.concatenate([pooled[:, t * 256 : t * 256 + 128] for t in range(4)], axis=0)
@@ -211,14 +214,13 @@
         piece = jnp.broadcast_to(left[pl.ds((zh - s + 4) % 4, 1), :], (8, 128))
         total += jnp.dot(piece.astype(BF16), w[...], preferred_element_type=F32)
     for t in range(4):
-        left[t : t + 1, :] = total[0:1, t * 128 : t * 128 + 128]
-    out[...] = jnp.broadcast_to(left[...][None], (128, 4, 128))
+        out[t : t + 1, :] = total[0:1, t * 128 : t * 128 + 128]
 
 
 def code_part(place, pieces, ws):
     return pl.pallas_call(
         code_kernel,
-        out_shape=shape((128, 4, 128), F32),
+        out_shape=shape((4, 128), F32),
         in_specs=[SMEM] + [VMEM] * 8,
         out_specs=VMEM,
         scratch_shapes=[pltpu.VMEM((4, 128), F32)],
@@ -440,15 +442,14 @@
 
 def per_device(hidden_in, lengths, gate_weight, up_weight, down_weight, code_weight, corpus_codes):
     y, x, zh, zb, k = (lax.axis_index(a) for a in QUERY_CORPUS)
-    place = jnp.stack([y, k, 16 * k + 8 * zb, x // 2, 4 * zh, zh, zb]).astype(jnp.int32)
-
-    own, other = pack(place, lengths, hidden_in)
+    place = jnp.stack([y, k, 16 * k + 8 * zb, x // 2, 4 * zh, zh, zb, x]).astype(jnp.int32)
+
+    own, other = pack(place, hidden_in.T)
     swap = [(a * 4 + b, b * 4 + a) for a in range(4) for b in range(4)]
     straight = [(s * 2 + c, t * 2 + c) for s, t in swap for c in range(2)]
     crossed = [(s * 2 + c, t * 2 + 1 - c) for s, t in swap for c in range(2)]
     own = lax.ppermute(own, ("y", "x", "k"), straight)
     other = lax.ppermute(other, ("y", "x", "k"), crossed)
-    counts, own = own[64:], own[:64]
     block = jnp.where(
         k == 0, jnp.concatenate([own, other], axis=1), jnp.concatenate([other, own], axis=1)
     )
@@ -467,12 +468,16 @@
     )
     rows, gathered = lax.optimization_barrier((rows, gathered))
     turned = [[(i, (i + d) % 4) for i in range(4)] for d in range(4)]
-    code_rows = (rows, *(lax.ppermute(rows, "zh", turned[d]) for d in (1, 2, 3)))
-
-    parts = gate_up(place, gathered, gate_rows, up_rows, gate_peer, up_peer)
-    units = hidden_of(parts[0], *(shifted(parts[d], d) for d in (1, 2, 3)))
+    code_rows = [rows, *(lax.ppermute(rows, "zh", turned[d]) for d in (1, 2, 3))]
+
+    parts = gate_up(place, lengths, gathered, gate_rows, up_rows, gate_peer, up_peer)
+    units, counts = hidden_of(place, parts[0], *(shifted(parts[d], d) for d in (1, 2, 3)))
     groups = (units, *(shifted(units, d) for d in (1, 2, 3)))
+    groups, code_rows[2] = lax.optimization_barrier((groups, code_rows[2]))
     branch = down(place, groups, down_weight, down_peer)
+    branch, code_rows[1], code_rows[3] = lax.optimization_barrier(
+        (branch, code_rows[1], code_rows[3])
+    )
     branch = lax.all_to_all(branch.reshape(32, 8, 1024), XZ, 0, 0, tiled=True)
     here = lax.dynamic_slice(
         gathered.reshape(4, 8, 64, 128), (x, 0, zh * 16 + zb * 8, 0), (1, 8, 8, 128)
@@ -485,10 +490,9 @@
     sent = ((same, 1), (other, 2), (other, 3))
     pieces = (same, *(lax.ppermute(a, ("zb", "k"), flips[r]) for a, r in sent))
     part = code_part(place, pieces, code_rows)
-    codes = lax.all_to_all(part, YXZ, 0, 0, tiled=True)
-    codes = codes.reshape(4, 4, 4, 2, 512).sum(axis=(0, 3))
-    codes = codes.reshape(16, 512).astype(BF16)
-
+    part = part + lax.ppermute(part, "zb", [(0, 1), (1, 0)])
+    codes = spread(part, ("y", "x", "zh"), 64)
+    codes = codes.reshape(4, 16, 512).sum(axis=0).astype(BF16)
     lists = local_lists(place, codes, to_peer(codes), corpus_codes)
     lists = pair_lists(place, lists, to_peer(lists))
     lists = (lists[0], *(shifted(lists[d], d) for d in (1, 2, 3)))

time: 167 us -> 164 us (0.982)
  starting transfers between devices: 56.2 us -> 60.8 us
  waiting for transfers between devices: 53.1 us -> 48.7 us
  blocking collectives: 42.8 us -> 40.2 us
    ppermute x12, waiting for transfers between devices: 18.5 us -> 7.16 us  [shifted(): return lax.ppermute(x, 'y', [(i, (i + d) % 4) for i in range(4)])]
    ppermute x12, starting transfers between devices: 13.5 us -> 16.7 us  [shifted(): return lax.ppermute(x, 'y', [(i, (i + d) % 4) for i in range(4)])]
    all_to_all x1, waiting for transfers between devices: 12.9 us -> 16 us  [per_device(): branch = lax.all_to_all(branch.reshape(32, 8, 1024), XZ, 0, 0, tiled=True)]
    all_to_all x1, blocking collectives: 21.8 us -> 19.6 us  [spread(): return lax.all_to_all(copies, axes, 0, 0, tiled=True)]
    ppermute x0 -> x1, waiting for transfers between devices: none -> 2.14 us  [per_device(): part = part + lax.ppermute(part, 'zb', [(0, 1), (1, 0)])]
  transfers between devices with their start and end apart: 29 -> 30, of which waited for: 20 -> 16; matrix products, arithmetic and copies ran while one was open for 0% -> 0% of each run, Pallas kernels for 1% -> 2%
where the time goes in v8:
time: 164 us; the launch traced here: 163 us
  starting transfers between devices  60.8 us (37%)
  waiting for transfers between devices  48.7 us (30%)
  blocking collectives  40.2 us (25%)
  Pallas kernels  11.6 us (7%)
  local copies, waits for them, and re-layouts  1.76 us (1%)
    all_to_all x1, starting transfers between devices, spread(): return lax.all_to_all(copies, axes, 0, 0, tiled=True)  21.4 us
    all_to_all x1, blocking collectives, per_device(): arrived = lax.all_to_all(lists, YXZ, 0, 0, tiled=True)  20.6 us
    all_to_all x1, blocking collectives, spread(): return lax.all_to_all(copies, axes, 0, 0, tiled=True)  19.6 us
    ppermute x12, starting transfers between devices, shifted(): return lax.ppermute(x, 'y', [(i, (i + d) % 4) for i in range(4)])  16.7 us
    all_to_all x1, waiting for transfers between devices, per_device(): branch = lax.all_to_all(branch.reshape(32, 8, 1024), XZ, 0, 0, tiled=True)  16 us
    all_to_all x1, waiting for transfers between devices, spread(): return lax.all_to_all(copies, axes, 0, 0, tiled=True)  15.8 us
    all_to_all x1, starting transfers between devices, per_device(): branch = lax.all_to_all(branch.reshape(32, 8, 1024), XZ, 0, 0, tiled=True)  9.39 us
    ppermute x12, waiting for transfers between devices, shifted(): return lax.ppermute(x, 'y', [(i, (i + d) % 4) for i in range(4)])  7.16 us
  transfers between devices with their start and end apart: 30, of which 16 were waited for; matrix products, arithmetic and copies ran while one was open for 0% of the time, Pallas kernels for 2%

profile of v8, /device:TPU:32, one launch (start us, length us, event | category | flops | bytes accessed | tf_op | source)
XLA Modules:
  0.0 163.4 jit_solution(9356736488108525104)
XLA Ops:
  5.0 21.4 %all-to-all-start = ((bf16[32,64,128]{2,1,0:T(8,128)(2,1)}), bf16[32,64,128]{2,1,0:T(8,128)(2,1)S(1)}, u32[]{:S(2)}, u32[]{:S(2)}) async-start(bf16[32,64,128]{2,1,0:T(8,128)(2,1)} %broadcast_in_dim.4), calls=%async_computation | async-start | bytes 1048576 | tf_op jit(solution)/shard_map/all_to_all | solution.py:41
  27.4 1.2 collective-permute-done.1
  28.7 15.8 %all-to-all-done.h = bf16[32,64,128]{2,1,0:T(8,128)(2,1)S(1)} async-done(((bf16[32,64,128]{2,1,0:T(8,128)(2,1)}), bf16[32,64,128]{2,1,0:T(8,128)(2,1)S(1)}, u32[]{:S(2)}, u32[]{:S(2)}) %all-to-all-start) | async-done | bytes 524320 | tf_op jit(solution)/shard_map/all_to_all | solution.py:41
  44.5 1.4 gate_up.1
  45.9 1.4 collective-permute-start.7
  47.3 1.3 collective-permute-start.8
  48.6 1.5 collective-permute-start.9
  50.0 2.7 %collective-permute-start.13 = (bf16[128,512]{1,0:T(8,128)(2,1)S(1)}, bf16[128,512]{1,0:T(8,128)(2,1)S(1)}, u32[]{:S(2)}, u32[]{:S(2)}) collective-permute-start(bf16[128,512]{1,0:T(8,128)(2,1)S(1)} %pad_maximum_fusion.w0), channel_id=1, source_target_pairs={{0,8},{4,12},{8,0},{12,4},{1,9},{5,13},{9,1},{13,5},{2,10},{6,14},... | collective-permute-start | bytes 393224 | tf_op jit(solution)/shard_map/ppermute | solution.py:471
  53.4 3.5 %collective-permute-start.15 = (bf16[128,512]{1,0:T(8,128)(2,1)S(1)}, bf16[128,512]{1,0:T(8,128)(2,1)S(1)}, u32[]{:S(2)}, u32[]{:S(2)}) collective-permute-start(bf16[128,512]{1,0:T(8,128)(2,1)S(1)} %pad_maximum_fusion.w0), channel_id=1, source_target_pairs={{0,12},{4,0},{8,4},{12,8},{1,13},{5,1},{9,5},{13,9},{2,14},{6,2},{... | collective-permute-start | bytes 393224 | tf_op jit(solution)/shard_map/ppermute | solution.py:471
  57.6 2.1 %collective-permute-start.10 = (bf16[64,512]{1,0:T(8,128)(2,1)S(1)}, bf16[64,512]{1,0:T(8,128)(2,1)S(1)}, u32[]{:S(2)}, u32[]{:S(2)}) collective-permute-start(bf16[64,512]{1,0:T(8,128)(2,1)S(1)} %get-tuple-element.48.a), channel_id=1, source_target_pairs={{0,64},{64,128},{128,192},{192,0},{1,65},{65,129},{129,193},{193,1... | collective-permute-start | bytes 196616 | tf_op jit(solution)/shard_map/ppermute | solution.py:36
  59.7 1.5 collective-permute-done.13.w2
  61.2 1.4 collective-permute-start.12
  63.4 2.1 %collective-permute-done.11.c = bf16[64,512]{1,0:T(8,128)(2,1)S(1)} collective-permute-done((bf16[64,512]{1,0:T(8,128)(2,1)S(1)}, bf16[64,512]{1,0:T(8,128)(2,1)S(1)}, u32[]{:S(2)}, u32[]{:S(2)}) %collective-permute-start.11) | collective-permute-done | bytes 65568 | tf_op jit(solution)/shard_map/ppermute | solution.py:36
  65.5 1.8 %down.1 = bf16[256,1024]{1,0:T(8,128)(2,1)} custom-call(s32[8]{0:T(128)S(1)} %stack.35.place.refs_0_, bf16[64,512]{1,0:T(8,128)(2,1)S(1)} %get-tuple-element.48.a, bf16[64,512]{1,0:T(8,128)(2,1)S(1)} %collective-permute-done.10.b, bf16[64,512]{1,0:T(8,128)(2,1)S(1)} %collective-permute-done.11.c, bf16[64,512]{1,0:T(8,128)(2,1)S(1)} %collective-permute-done.12.d, ...), custom_call_target="tpu_custom_call" | custom-call | tf_op jit(solution)/shard_map/down/pallas_call | solution.py:153
  67.3 9.4 %all-to-all-start.1 = ((bf16[32,8,1024]{2,1,0:T(8,128)(2,1)}), bf16[32,8,1024]{2,1,0:T(8,128)(2,1)S(1)}, u32[]{:S(2)}, u32[]{:S(2)}) async-start(bf16[32,8,1024]{2,1,0:T(8,128)(2,1)} %bitcast.11), calls=%async_computation.1 | async-start | bytes 1048576 | tf_op jit(solution)/shard_map/all_to_all | solution.py:481
  76.7 16.0 %all-to-all-done.1.parts = bf16[32,8,1024]{2,1,0:T(8,128)(2,1)S(1)} async-done(((bf16[32,8,1024]{2,1,0:T(8,128)(2,1)}), bf16[32,8,1024]{2,1,0:T(8,128)(2,1)S(1)}, u32[]{:S(2)}, u32[]{:S(2)}) %all-to-all-start.1) | async-done | bytes 524320 | tf_op jit(solution)/shard_map/all_to_all | solution.py:481
  93.9 2.7 %collective-permute-start.17 = (f32[8,128]{1,0:T(8,128)S(1)}, f32[8,128]{1,0:T(8,128)S(1)}, u32[]{:S(2)}, u32[]{:S(2)}) collective-permute-start(f32[8,128]{1,0:T(8,128)S(1)} %get-tuple-element.55.a), channel_id=1, source_target_pairs={{0,128},{64,192},{128,0},{192,64},{1,129},{65,193},{129,1},{193,65... | collective-permute-start | bytes 12296 | tf_op jit(solution)/shard_map/ppermute | solution.py:36
  96.6 1.6 collective-permute-start.18
  99.0 1.2 collective-permute-done.18.d
  101.1 1.8 %collective-permute-start.21 = (f32[4,128]{1,0:T(4,128)S(1)}, f32[4,128]{1,0:T(4,128)S(1)}, u32[]{:S(2)}, u32[]{:S(2)}) collective-permute-start(f32[4,128]{1,0:T(4,128)S(1)} %get-tuple-element.57), channel_id=1, source_target_pairs={{0,3},{1,2},{2,1},{3,0},{4,7},{5,6},{6,5},{7,4},{8,11},{9,10},{10,... | collective-permute-start | bytes 6152 | tf_op jit(solution)/shard_map/ppermute | solution.py:491
  102.9 1.8 %collective-permute-done.20.c = f32[4,128]{1,0:T(4,128)S(1)} collective-permute-done((f32[4,128]{1,0:T(4,128)S(1)}, f32[4,128]{1,0:T(4,128)S(1)}, u32[]{:S(2)}, u32[]{:S(2)}) %collective-permute-start.20) | collective-permute-done | bytes 2080 | tf_op jit(solution)/shard_map/ppermute | solution.py:491
  105.4 1.5 collective-permute-start.22
  106.9 2.1 %collective-permute-done.22 = f32[4,128]{1,0:T(4,128)S(1)} collective-permute-done((f32[4,128]{1,0:T(4,128)S(1)}, f32[4,128]{1,0:T(4,128)S(1)}, u32[]{:S(2)}, u32[]{:S(2)}) %collective-permute-start.22) | collective-permute-done | bytes 2080 | tf_op jit(solution)/shard_map/ppermute | solution.py:493
  109.0 19.6 %all_to_all.20 = f32[64,4,128]{2,1,0:T(4,128)S(1)} all-to-all(f32[64,4,128]{2,1,0:T(4,128)S(1)} %broadcast_in_dim.5), channel_id=1, replica_groups=mesh['y'=4,'x'=4,'zh'=4,'zb'=2,'k'=2] {'y','x','zh'}, dimensions={0} | all-to-all | bytes 262144 | tf_op jit(solution)/shard_map/all_to_all | solution.py:41
  128.8 1.2 collective-permute-done.23.refs_2_
  129.9 1.5 scores.1.a
  134.3 1.8 %collective-permute-start.26 = (f32[4,128]{1,0:T(4,128)S(1)}, f32[4,128]{1,0:T(4,128)S(1)}, u32[]{:S(2)}, u32[]{:S(2)}) collective-permute-start(f32[4,128]{1,0:T(4,128)S(1)} %get-tuple-element.63), channel_id=1, source_target_pairs={{0,128},{64,192},{128,0},{192,64},{1,129},{65,193},{129,1},{193,65... | collective-permute-start | bytes 6152 | tf_op jit(solution)/shard_map/ppermute | solution.py:36
  136.2 1.3 collective-permute-start.27
  137.4 1.1 collective-permute-done.25.b
  139.8 1.6 four_lists.1
  141.3 20.6 %all_to_all.21 = f32[128,4,128]{2,1,0:T(4,128)S(1)} all-to-all(f32[128,4,128]{2,1,0:T(4,128)S(1)} %four_lists.1), channel_id=1, replica_groups=mesh['y'=4,'x'=4,'zh'=4,'zb'=2,'k'=2] {'y','x','zh','zb'}, dimensions={0} | all-to-all | bytes 524288 | tf_op jit(solution)/shard_map/all_to_all | solution.py:500
  161.9 1.4 final_lists.1
  (66 shorter events, 15.9 us)
Async XLA Ops:
  0.0 4.1 %collective-permute-start.4 = (bf16[224,1024]{1,0:T(8,128)(2,1)}, bf16[224,1024]{1,0:T(8,128)(2,1)S(1)}, u32[]{:S(2)}, u32[]{:S(2)}) collective-permute-start(bf16[224,1024]{1,0:T(8,128)(2,1)} %bitcast.22), channel_id=1, source_target_pairs={{0,1},{1,0},{2,3},{3,2},{4,5},{5,4},{6,7},{7,6},{8,9},{9,8},{10,11... | collective-permute-start | bytes 1376264 | tf_op jit(solution)/shard_map/ppermute | solution.py:32
  0.0 4.1 %collective-permute-start.5 = (bf16[224,1024]{1,0:T(8,128)(2,1)}, bf16[224,1024]{1,0:T(8,128)(2,1)S(1)}, u32[]{:S(2)}, u32[]{:S(2)}) collective-permute-start(bf16[224,1024]{1,0:T(8,128)(2,1)} %bitcast.24), channel_id=1, source_target_pairs={{0,1},{1,0},{2,3},{3,2},{4,5},{5,4},{6,7},{7,6},{8,9},{9,8},{10,11... | collective-permute-start | bytes 1376264 | tf_op jit(solution)/shard_map/ppermute | solution.py:32
  0.5 3.6 %collective-permute-start.6 = (bf16[224,1024]{1,0:T(8,128)(2,1)}, bf16[224,1024]{1,0:T(8,128)(2,1)S(1)}, u32[]{:S(2)}, u32[]{:S(2)}) collective-permute-start(bf16[224,1024]{1,0:T(8,128)(2,1)} %w0.1), channel_id=1, source_target_pairs={{0,1},{1,0},{2,3},{3,2},{4,5},{5,4},{6,7},{7,6},{8,9},{9,8},{10,11... | collective-permute-start | bytes 1376264 | tf_op jit(solution)/shard_map/ppermute | solution.py:32
  1.9 1.3 collective-permute-start.2
  2.5 1.4 collective-permute-start.3
  5.0 39.5 %copy-start.3 = (bf16[1024,224]{0,1:T(8,128)(2,1)S(1)}, bf16[1024,224]{0,1:T(8,128)(2,1)}, u32[]{:S(2)}) copy-start(bf16[1024,224]{0,1:T(8,128)(2,1)} %param.10) | copy-start | bytes 1376260
  5.0 39.5 %all-to-all-start = ((bf16[32,64,128]{2,1,0:T(8,128)(2,1)}), bf16[32,64,128]{2,1,0:T(8,128)(2,1)S(1)}, u32[]{:S(2)}, u32[]{:S(2)}) async-start(bf16[32,64,128]{2,1,0:T(8,128)(2,1)} %broadcast_in_dim.4), calls=%async_computation | async-start | bytes 1048576 | tf_op jit(solution)/shard_map/all_to_all | solution.py:41
  26.5 0.9 collective-permute-start
  27.3 1.3 collective-permute-start.1
  45.9 7.5 %collective-permute-start.7 = (bf16[64,1024]{1,0:T(8,128)(2,1)S(1)}, bf16[64,1024]{1,0:T(8,128)(2,1)S(1)}, u32[]{:S(2)}, u32[]{:S(2)}) collective-permute-start(bf16[64,1024]{1,0:T(8,128)(2,1)S(1)} %get-tuple-element.42), channel_id=1, source_target_pairs={{0,64},{64,128},{128,192},{192,0},{1,65},{65,129},{129,193},{193,1... | collective-permute-start | bytes 393224 | tf_op jit(solution)/shard_map/ppermute | solution.py:36
  47.3 9.6 %collective-permute-start.8 = (bf16[64,1024]{1,0:T(8,128)(2,1)S(1)}, bf16[64,1024]{1,0:T(8,128)(2,1)S(1)}, u32[]{:S(2)}, u32[]{:S(2)}) collective-permute-start(bf16[64,1024]{1,0:T(8,128)(2,1)S(1)} %get-tuple-element.43), channel_id=1, source_target_pairs={{0,128},{64,192},{128,0},{192,64},{1,129},{65,193},{129,1},{193,65... | collective-permute-start | bytes 393224 | tf_op jit(solution)/shard_map/ppermute | solution.py:36
  48.6 8.4 %collective-permute-start.9 = (bf16[64,1024]{1,0:T(8,128)(2,1)S(1)}, bf16[64,1024]{1,0:T(8,128)(2,1)S(1)}, u32[]{:S(2)}, u32[]{:S(2)}) collective-permute-start(bf16[64,1024]{1,0:T(8,128)(2,1)S(1)} %get-tuple-element.44), channel_id=1, source_target_pairs={{0,192},{64,0},{128,64},{192,128},{1,193},{65,1},{129,65},{193,129... | collective-permute-start | bytes 393224 | tf_op jit(solution)/shard_map/ppermute | solution.py:36
  50.0 11.2 %collective-permute-start.13 = (bf16[128,512]{1,0:T(8,128)(2,1)S(1)}, bf16[128,512]{1,0:T(8,128)(2,1)S(1)}, u32[]{:S(2)}, u32[]{:S(2)}) collective-permute-start(bf16[128,512]{1,0:T(8,128)(2,1)S(1)} %pad_maximum_fusion.w0), channel_id=1, source_target_pairs={{0,8},{4,12},{8,0},{12,4},{1,9},{5,13},{9,1},{13,5},{2,10},{6,14},... | collective-permute-start | bytes 393224 | tf_op jit(solution)/shard_map/ppermute | solution.py:471
  52.8 14.5 %collective-permute-start.14 = (bf16[128,512]{1,0:T(8,128)(2,1)S(1)}, bf16[128,512]{1,0:T(8,128)(2,1)S(1)}, u32[]{:S(2)}, u32[]{:S(2)}) collective-permute-start(bf16[128,512]{1,0:T(8,128)(2,1)S(1)} %pad_maximum_fusion.w0), channel_id=1, source_target_pairs={{0,4},{4,8},{8,12},{12,0},{1,5},{5,9},{9,13},{13,1},{2,6},{6,10},{... | collective-permute-start | bytes 393224 | tf_op jit(solution)/shard_map/ppermute | solution.py:471
  53.4 13.9 %collective-permute-start.15 = (bf16[128,512]{1,0:T(8,128)(2,1)S(1)}, bf16[128,512]{1,0:T(8,128)(2,1)S(1)}, u32[]{:S(2)}, u32[]{:S(2)}) collective-permute-start(bf16[128,512]{1,0:T(8,128)(2,1)S(1)} %pad_maximum_fusion.w0), channel_id=1, source_target_pairs={{0,12},{4,0},{8,4},{12,8},{1,13},{5,1},{9,5},{13,9},{2,14},{6,2},{... | collective-permute-start | bytes 393224 | tf_op jit(solution)/shard_map/ppermute | solution.py:471
  57.6 5.8 %collective-permute-start.10 = (bf16[64,512]{1,0:T(8,128)(2,1)S(1)}, bf16[64,512]{1,0:T(8,128)(2,1)S(1)}, u32[]{:S(2)}, u32[]{:S(2)}) collective-permute-start(bf16[64,512]{1,0:T(8,128)(2,1)S(1)} %get-tuple-element.48.a), channel_id=1, source_target_pairs={{0,64},{64,128},{128,192},{192,0},{1,65},{65,129},{129,193},{193,1... | collective-permute-start | bytes 196616 | tf_op jit(solution)/shard_map/ppermute | solution.py:36
  59.7 5.8 %collective-permute-start.11 = (bf16[64,512]{1,0:T(8,128)(2,1)S(1)}, bf16[64,512]{1,0:T(8,128)(2,1)S(1)}, u32[]{:S(2)}, u32[]{:S(2)}) collective-permute-start(bf16[64,512]{1,0:T(8,128)(2,1)S(1)} %get-tuple-element.48.a), channel_id=1, source_target_pairs={{0,128},{64,192},{128,0},{192,64},{1,129},{65,193},{129,1},{193,65... | collective-permute-start | bytes 196616 | tf_op jit(solution)/shard_map/ppermute | solution.py:36
  61.2 4.3 %collective-permute-start.12 = (bf16[64,512]{1,0:T(8,128)(2,1)S(1)}, bf16[64,512]{1,0:T(8,128)(2,1)S(1)}, u32[]{:S(2)}, u32[]{:S(2)}) collective-permute-start(bf16[64,512]{1,0:T(8,128)(2,1)S(1)} %get-tuple-element.48.a), channel_id=1, source_target_pairs={{0,192},{64,0},{128,64},{192,128},{1,193},{65,1},{129,65},{193,129... | collective-permute-start | bytes 196616 | tf_op jit(solution)/shard_map/ppermute | solution.py:36
  67.3 25.4 %all-to-all-start.1 = ((bf16[32,8,1024]{2,1,0:T(8,128)(2,1)}), bf16[32,8,1024]{2,1,0:T(8,128)(2,1)S(1)}, u32[]{:S(2)}, u32[]{:S(2)}) async-start(bf16[32,8,1024]{2,1,0:T(8,128)(2,1)} %bitcast.11), calls=%async_computation.1 | async-start | bytes 1048576 | tf_op jit(solution)/shard_map/all_to_all | solution.py:481
  76.7 53.3 %copy-start = (bf16[512,1024]{1,0:T(8,128)(2,1)S(1)}, bf16[512,1024]{1,0:T(8,128)(2,1)}, u32[]{:S(2)}) copy-start(bf16[512,1024]{1,0:T(8,128)(2,1)} %refs_3_.1) | copy-start | bytes 3145732
  92.9 5.3 %collective-permute-start.16 = (f32[8,128]{1,0:T(8,128)S(1)}, f32[8,128]{1,0:T(8,128)S(1)}, u32[]{:S(2)}, u32[]{:S(2)}) collective-permute-start(f32[8,128]{1,0:T(8,128)S(1)} %get-tuple-element.55.a), channel_id=1, source_target_pairs={{0,64},{64,128},{128,192},{192,0},{1,65},{65,129},{129,193},{193,1... | collective-permute-start | bytes 12296 | tf_op jit(solution)/shard_map/ppermute | solution.py:36
  93.9 5.1 %collective-permute-start.17 = (f32[8,128]{1,0:T(8,128)S(1)}, f32[8,128]{1,0:T(8,128)S(1)}, u32[]{:S(2)}, u32[]{:S(2)}) collective-permute-start(f32[8,128]{1,0:T(8,128)S(1)} %get-tuple-element.55.a), channel_id=1, source_target_pairs={{0,128},{64,192},{128,0},{192,64},{1,129},{65,193},{129,1},{193,65... | collective-permute-start | bytes 12296 | tf_op jit(solution)/shard_map/ppermute | solution.py:36
  96.6 3.6 %collective-permute-start.18 = (f32[8,128]{1,0:T(8,128)S(1)}, f32[8,128]{1,0:T(8,128)S(1)}, u32[]{:S(2)}, u32[]{:S(2)}) collective-permute-start(f32[8,128]{1,0:T(8,128)S(1)} %get-tuple-element.55.a), channel_id=1, source_target_pairs={{0,192},{64,0},{128,64},{192,128},{1,193},{65,1},{129,65},{193,129... | collective-permute-start | bytes 12296 | tf_op jit(solution)/shard_map/ppermute | solution.py:36
  100.9 2.0 %collective-permute-start.19 = (f32[4,128]{1,0:T(4,128)S(1)}, f32[4,128]{1,0:T(4,128)S(1)}, u32[]{:S(2)}, u32[]{:S(2)}) collective-permute-start(f32[4,128]{1,0:T(4,128)S(1)} %get-tuple-element.56.a), channel_id=1, source_target_pairs={{0,1},{1,0},{2,3},{3,2},{4,5},{5,4},{6,7},{7,6},{8,9},{9,8},{10,11... | collective-permute-start | bytes 6152 | tf_op jit(solution)/shard_map/ppermute | solution.py:491
  101.0 3.7 %collective-permute-start.20 = (f32[4,128]{1,0:T(4,128)S(1)}, f32[4,128]{1,0:T(4,128)S(1)}, u32[]{:S(2)}, u32[]{:S(2)}) collective-permute-start(f32[4,128]{1,0:T(4,128)S(1)} %get-tuple-element.57), channel_id=1, source_target_pairs={{0,2},{1,3},{2,0},{3,1},{4,6},{5,7},{6,4},{7,5},{8,10},{9,11},{10,... | collective-permute-start | bytes 6152 | tf_op jit(solution)/shard_map/ppermute | solution.py:491
  101.1 3.6 %collective-permute-start.21 = (f32[4,128]{1,0:T(4,128)S(1)}, f32[4,128]{1,0:T(4,128)S(1)}, u32[]{:S(2)}, u32[]{:S(2)}) collective-permute-start(f32[4,128]{1,0:T(4,128)S(1)} %get-tuple-element.57), channel_id=1, source_target_pairs={{0,3},{1,2},{2,1},{3,0},{4,7},{5,6},{6,5},{7,4},{8,11},{9,10},{10,... | collective-permute-start | bytes 6152 | tf_op jit(solution)/shard_map/ppermute | solution.py:491
  105.4 3.6 %collective-permute-start.22 = (f32[4,128]{1,0:T(4,128)S(1)}, f32[4,128]{1,0:T(4,128)S(1)}, u32[]{:S(2)}, u32[]{:S(2)}) collective-permute-start(f32[4,128]{1,0:T(4,128)S(1)} %code_part.1), channel_id=1, source_target_pairs={{0,2},{2,0},{1,3},{3,1},{4,6},{6,4},{5,7},{7,5},{8,10},{10,8},{9,1... | collective-permute-start | bytes 6152 | tf_op jit(solution)/shard_map/ppermute | solution.py:493
  128.7 1.3 collective-permute-start.23
  131.5 1.2 collective-permute-start.24
  133.7 4.9 %collective-permute-start.25 = (f32[4,128]{1,0:T(4,128)S(1)}, f32[4,128]{1,0:T(4,128)S(1)}, u32[]{:S(2)}, u32[]{:S(2)}) collective-permute-start(f32[4,128]{1,0:T(4,128)S(1)} %get-tuple-element.62), channel_id=1, source_target_pairs={{0,64},{64,128},{128,192},{192,0},{1,65},{65,129},{129,193},{193,1... | collective-permute-start | bytes 6152 | tf_op jit(solution)/shard_map/ppermute | solution.py:36
  134.3 5.1 %collective-permute-start.26 = (f32[4,128]{1,0:T(4,128)S(1)}, f32[4,128]{1,0:T(4,128)S(1)}, u32[]{:S(2)}, u32[]{:S(2)}) collective-permute-start(f32[4,128]{1,0:T(4,128)S(1)} %get-tuple-element.63), channel_id=1, source_target_pairs={{0,128},{64,192},{128,0},{192,64},{1,129},{65,193},{129,1},{193,65... | collective-permute-start | bytes 6152 | tf_op jit(solution)/shard_map/ppermute | solution.py:36
  136.2 3.6 %collective-permute-start.27 = (f32[4,128]{1,0:T(4,128)S(1)}, f32[4,128]{1,0:T(4,128)S(1)}, u32[]{:S(2)}, u32[]{:S(2)}) collective-permute-start(f32[4,128]{1,0:T(4,128)S(1)} %get-tuple-element.64), channel_id=1, source_target_pairs={{0,192},{64,0},{128,64},{192,128},{1,193},{65,1},{129,65},{193,129... | collective-permute-start | bytes 6152 | tf_op jit(solution)/shard_map/ppermute | solution.py:36
  (5 other events, 75.7 us)

commit v9 on v8

--- a/solution.py
+++ b/solution.py
@@ -146,13 +146,15 @@
         lhs[pl.ds(at, 64), :] = part[...]
     total = jnp.dot(lhs[:, 0:224], w0[...], preferred_element_type=F32)
     total += jnp.dot(lhs[:, 256:480], w1[...], preferred_element_type=F32)
-    out[...] = total.astype(BF16)
+    for t in range(8):
+        tile = total[:, t * 128 : t * 128 + 128].reshape(16, 16, 128).astype(BF16)
+        out[:, t % 2, :, (t // 2) * 128 : (t // 2) * 128 + 128] = tile
 
 
 def down(place, parts, w0, w1):
     return pl.pallas_call(
         down_kernel,
-        out_shape=shape((256, 1024), BF16),
+        out_shape=shape((16, 2, 16, 512), BF16),
         in_specs=[SMEM] + [VMEM] * 6,
         out_specs=VMEM,
         scratch_shapes=[pltpu.VMEM((256, 512), BF16)],
@@ -166,13 +168,13 @@
     for p in range(32):
         total += parts[p].astype(F32)
     res[...] = total
-    sq[...] = jnp.broadcast_to(jnp.sum(total * total, axis=1, keepdims=True), (8, 128))
+    sq[...] = jnp.broadcast_to(jnp.sum(total * total, axis=1, keepdims=True), (16, 128))
 
 
 def residual_of(parts, h):
     return pl.pallas_call(
         residual_kernel,
-        out_shape=(shape((8, 1024), F32), shape((8, 128), F32)),
+        out_shape=(shape((16, 512), F32), shape((16, 128), F32)),
         in_specs=[VMEM] * 2,
         out_specs=(VMEM,) * 2,
         compiler_params=PARAMS,
@@ -180,35 +182,32 @@
     )(parts, h)
 
 
-def pool_kernel(place, counts, res, a, b, c, d, same, other):
-    first, zh, zb = place[2], place[5], place[6]
+def pool_kernel(place, counts, res, a, b, c, d, out):
+    first, zh = place[2], place[5]
     sq = (a[...] + b[...] + c[...] + d[...])[:, 0:1]
-    slots = lax.broadcasted_iota(jnp.int32, (8, 1), 0) + first
+    slots = lax.broadcasted_iota(jnp.int32, (16, 1), 0) + first
     held = jnp.where(lanes((1, 128)) == 100 + zh, counts[0:1, :], 0.0)
     count = jnp.max(held, axis=1, keepdims=True)
     weight = jnp.where(slots.astype(F32) < count, lax.rsqrt(sq / D + EPS), 0.0)
     pooled = jnp.sum(res[...] * weight, axis=0, keepdims=True) / count
-    ahead = jnp.concatenate([pooled[:, t * 256 : t * 256 + 128] for t in range(4)], axis=0)
-    behind = jnp.concatenate([pooled[:, t * 256 + 128 : t * 256 + 256] for t in range(4)], axis=0)
-    same[...] = jnp.where(zb == 0, ahead, behind)
-    other[...] = jnp.where(zb == 0, behind, ahead)
+    for t in range(4):
+        out[t : t + 1, :] = pooled[:, t * 128 : t * 128 + 128]
 
 
 def pool(place, counts, res, sqs):
-    part = shape((4, 128), F32)
     return pl.pallas_call(
         pool_kernel,
-        out_shape=(part,) * 2,
+        out_shape=shape((4, 128), F32),
         in_specs=[SMEM] + [VMEM] * 6,
-        out_specs=(VMEM,) * 2,
+        out_specs=VMEM,
         compiler_params=PARAMS,
         name="pool",
     )(place, counts, res, *sqs)
 
 
-def code_kernel(place, a, b, c, d, w0, w1, w2, w3, out, left):
+def code_kernel(place, a, b, w0, w1, w2, w3, out, left):
     zh = place[5]
-    left[...] = a[...] + b[...] + c[...] + d[...]
+    left[...] = a[...] + b[...]
     total = jnp.zeros((8, 512), F32)
     for s, w in enumerate((w0, w1, w2, w3)):
         piece = jnp.broadcast_to(left[pl.ds((zh - s + 4) % 4, 1), :], (8, 128))
@@ -217,16 +216,16 @@
         out[t : t + 1, :] = total[0:1, t * 128 : t * 128 + 128]
 
 
-def code_part(place, pieces, ws):
+def code_part(place, a, b, ws):
     return pl.pallas_call(
         code_kernel,
         out_shape=shape((4, 128), F32),
-        in_specs=[SMEM] + [VMEM] * 8,
+        in_specs=[SMEM] + [VMEM] * 6,
         out_specs=VMEM,
         scratch_shapes=[pltpu.VMEM((4, 128), F32)],
         compiler_params=PARAMS,
         name="code_part",
-    )(place, *pieces, *ws)
+    )(place, a, b, *ws)
 
 
 def exchange(x, step, falling):
@@ -442,7 +441,7 @@
 
 def per_device(hidden_in, lengths, gate_weight, up_weight, down_weight, code_weight, corpus_codes):
     y, x, zh, zb, k = (lax.axis_index(a) for a in QUERY_CORPUS)
-    place = jnp.stack([y, k, 16 * k + 8 * zb, x // 2, 4 * zh, zh, zb, x]).astype(jnp.int32)
+    place = jnp.stack([y, k, 16 * k, x // 2, 4 * zh, zh, zb, x]).astype(jnp.int32)
 
     own, other = pack(place, hidden_in.T)
     swap = [(a * 4 + b, b * 4 + a) for a in range(4) for b in range(4)]
@@ -478,18 +477,16 @@
     branch, code_rows[1], code_rows[3] = lax.optimization_barrier(
         (branch, code_rows[1], code_rows[3])
     )
-    branch = lax.all_to_all(branch.reshape(32, 8, 1024), XZ, 0, 0, tiled=True)
+    branch = lax.all_to_all(branch.reshape(32, 16, 512), XZ, 0, 0, tiled=True)
     here = lax.dynamic_slice(
-        gathered.reshape(4, 8, 64, 128), (x, 0, zh * 16 + zb * 8, 0), (1, 8, 8, 128)
-    )[0]
-    here = jnp.moveaxis(here, 0, 1).reshape(8, 1024)
+        gathered.reshape(4, 4, 2, 64, 128), (x, 0, zb, zh * 16, 0), (1, 4, 1, 16, 128)
+    )
+    here = jnp.moveaxis(here.reshape(4, 16, 128), 0, 1).reshape(16, 512)
     res, sq = residual_of(branch, here)
+    sq = sq + lax.ppermute(sq, "zb", [(0, 1), (1, 0)])
     sqs = (sq, *(shifted(sq, d) for d in (1, 2, 3)))
-    same, other = pool(place, counts, res, sqs)
-    flips = [[(i, i ^ r) for i in range(4)] for r in range(4)]
-    sent = ((same, 1), (other, 2), (other, 3))
-    pieces = (same, *(lax.ppermute(a, ("zb", "k"), flips[r]) for a, r in sent))
-    part = code_part(place, pieces, code_rows)
+    pooled = pool(place, counts, res, sqs)
+    part = code_part(place, pooled, to_peer(pooled), code_rows)
     part = part + lax.ppermute(part, "zb", [(0, 1), (1, 0)])
     codes = spread(part, ("y", "x", "zh"), 64)
     codes = codes.reshape(4, 16, 512).sum(axis=0).astype(BF16)

time: 164 us -> 164 us (level)
  waiting for transfers between devices: 48.7 us -> 53.2 us
  starting transfers between devices: 60.8 us -> 57.4 us
    ppermute x3 -> x1, waiting for transfers between devices: 1.81 us -> 3.64 us  [per_device(): sq = sq + lax.ppermute(sq, 'zb', [(0, 1), (1, 0)])]
    ppermute x3 -> x1, starting transfers between devices: 1.95 us -> 0.2 us  [per_device(): sq = sq + lax.ppermute(sq, 'zb', [(0, 1), (1, 0)])]
    ppermute x5 -> x6, waiting for transfers between devices: 2.19 us -> 3.33 us  [to_peer(): return lax.ppermute(x, 'k', [(0, 1), (1, 0)])]
  transfers between devices with their start and end apart: 30 -> 29, of which waited for: 16 -> 18; matrix products, arithmetic and copies ran while one was open for 0% -> 0% of each run, Pallas kernels for 2% -> 2%
where the time goes in v9:
time: 164 us
  starting transfers between devices  57.4 us (35%)
  waiting for transfers between devices  53.2 us (32%)
  blocking collectives  39.7 us (24%)
  Pallas kernels  11.5 us (7%)
  local copies, waits for them, and re-layouts  1.75 us (1%)
    all_to_all x1, starting transfers between devices, spread(): return lax.all_to_all(copies, axes, 0, 0, tiled=True)  21.4 us
    all_to_all x1, blocking collectives, per_device(): arrived = lax.all_to_all(lists, YXZ, 0, 0, tiled=True)  20.6 us
    all_to_all x1, blocking collectives, spread(): return lax.all_to_all(copies, axes, 0, 0, tiled=True)  19.1 us
    ppermute x12, starting transfers between devices, shifted(): return lax.ppermute(x, 'y', [(i, (i + d) % 4) for i in range(4)])  16.5 us
    all_to_all x1, waiting for transfers between devices, per_device(): branch = lax.all_to_all(branch.reshape(32, 16, 512), XZ, 0, 0, tiled=True)  16 us
    all_to_all x1, waiting for transfers between devices, spread(): return lax.all_to_all(copies, axes, 0, 0, tiled=True)  15.8 us
    all_to_all x1, starting transfers between devices, per_device(): branch = lax.all_to_all(branch.reshape(32, 16, 512), XZ, 0, 0, tiled=True)  9.38 us
    ppermute x12, waiting for transfers between devices, shifted(): return lax.ppermute(x, 'y', [(i, (i + d) % 4) for i in range(4)])  7.26 us
  transfers between devices with their start and end apart: 29, of which 18 were waited for; matrix products, arithmetic and copies ran while one was open for 0% of the time, Pallas kernels for 2%

profile of v9, /device:TPU:32, one launch (start us, length us, event | category | flops | bytes accessed | tf_op | source)
XLA Modules:
  0.0 163.9 jit_solution(10802727022640603860)
XLA Ops:
  5.0 21.4 %all-to-all-start = ((bf16[32,64,128]{2,1,0:T(8,128)(2,1)}), bf16[32,64,128]{2,1,0:T(8,128)(2,1)S(1)}, u32[]{:S(2)}, u32[]{:S(2)}) async-start(bf16[32,64,128]{2,1,0:T(8,128)(2,1)} %broadcast_in_dim.4), calls=%async_computation | async-start | bytes 1048576 | tf_op jit(solution)/shard_map/all_to_all | solution.py:41
  27.4 1.2 collective-permute-done.1
  28.7 15.8 %all-to-all-done.h = bf16[32,64,128]{2,1,0:T(8,128)(2,1)S(1)} async-done(((bf16[32,64,128]{2,1,0:T(8,128)(2,1)}), bf16[32,64,128]{2,1,0:T(8,128)(2,1)S(1)}, u32[]{:S(2)}, u32[]{:S(2)}) %all-to-all-start) | async-done | bytes 524320 | tf_op jit(solution)/shard_map/all_to_all | solution.py:41
  44.5 1.4 gate_up.1
  45.9 1.4 collective-permute-start.7
  47.2 1.3 collective-permute-start.8
  48.5 1.5 collective-permute-start.9
  50.0 2.7 %collective-permute-start.13 = (bf16[128,512]{1,0:T(8,128)(2,1)S(1)}, bf16[128,512]{1,0:T(8,128)(2,1)S(1)}, u32[]{:S(2)}, u32[]{:S(2)}) collective-permute-start(bf16[128,512]{1,0:T(8,128)(2,1)S(1)} %pad_maximum_fusion.w0), channel_id=1, source_target_pairs={{0,8},{4,12},{8,0},{12,4},{1,9},{5,13},{9,1},{13,5},{2,10},{6,14},... | collective-permute-start | bytes 393224 | tf_op jit(solution)/shard_map/ppermute | solution.py:470
  53.4 3.5 %collective-permute-start.15 = (bf16[128,512]{1,0:T(8,128)(2,1)S(1)}, bf16[128,512]{1,0:T(8,128)(2,1)S(1)}, u32[]{:S(2)}, u32[]{:S(2)}) collective-permute-start(bf16[128,512]{1,0:T(8,128)(2,1)S(1)} %pad_maximum_fusion.w0), channel_id=1, source_target_pairs={{0,12},{4,0},{8,4},{12,8},{1,13},{5,1},{9,5},{13,9},{2,14},{6,2},{... | collective-permute-start | bytes 393224 | tf_op jit(solution)/shard_map/ppermute | solution.py:470
  57.6 2.1 %collective-permute-start.10 = (bf16[64,512]{1,0:T(8,128)(2,1)S(1)}, bf16[64,512]{1,0:T(8,128)(2,1)S(1)}, u32[]{:S(2)}, u32[]{:S(2)}) collective-permute-start(bf16[64,512]{1,0:T(8,128)(2,1)S(1)} %get-tuple-element.46.a), channel_id=1, source_target_pairs={{0,64},{64,128},{128,192},{192,0},{1,65},{65,129},{129,193},{193,1... | collective-permute-start | bytes 196616 | tf_op jit(solution)/shard_map/ppermute | solution.py:36
  59.7 1.6 collective-permute-done.13.w2
  61.2 1.4 collective-permute-start.12
  63.3 2.1 %collective-permute-done.11.c = bf16[64,512]{1,0:T(8,128)(2,1)S(1)} collective-permute-done((bf16[64,512]{1,0:T(8,128)(2,1)S(1)}, bf16[64,512]{1,0:T(8,128)(2,1)S(1)}, u32[]{:S(2)}, u32[]{:S(2)}) %collective-permute-start.11) | collective-permute-done | bytes 65568 | tf_op jit(solution)/shard_map/ppermute | solution.py:36
  65.5 1.8 %down.1 = bf16[16,2,16,512]{3,2,1,0:T(8,128)(2,1)} custom-call(s32[8]{0:T(128)S(1)} %stack.35.place.refs_0_, bf16[64,512]{1,0:T(8,128)(2,1)S(1)} %get-tuple-element.46.a, bf16[64,512]{1,0:T(8,128)(2,1)S(1)} %collective-permute-done.10.b, bf16[64,512]{1,0:T(8,128)(2,1)S(1)} %collective-permute-done.11.c, bf16[64,512]{1,0:T(8,128)(2,1)S(1)} %collective-permute-done.12.d, ...), custom_call_target="tpu_custom_call" | custom-call | tf_op jit(solution)/shard_map/down/pallas_call | solution.py:155
  67.3 9.4 %all-to-all-start.1 = ((bf16[32,16,512]{2,1,0:T(8,128)(2,1)}), bf16[32,16,512]{2,1,0:T(8,128)(2,1)S(1)}, u32[]{:S(2)}, u32[]{:S(2)}) async-start(bf16[32,16,512]{2,1,0:T(8,128)(2,1)} %bitcast.11), calls=%async_computation.1 | async-start | bytes 1048576 | tf_op jit(solution)/shard_map/all_to_all | solution.py:480
  76.7 16.0 %all-to-all-done.1.parts = bf16[32,16,512]{2,1,0:T(8,128)(2,1)S(1)} async-done(((bf16[32,16,512]{2,1,0:T(8,128)(2,1)}), bf16[32,16,512]{2,1,0:T(8,128)(2,1)S(1)}, u32[]{:S(2)}, u32[]{:S(2)}) %all-to-all-start.1) | async-done | bytes 524320 | tf_op jit(solution)/shard_map/all_to_all | solution.py:480
  93.0 3.6 %collective-permute-done.16 = f32[16,128]{1,0:T(8,128)S(1)} collective-permute-done((f32[16,128]{1,0:T(8,128)S(1)}, f32[16,128]{1,0:T(8,128)S(1)}, u32[]{:S(2)}, u32[]{:S(2)}) %collective-permute-start.16) | collective-permute-done | bytes 8224 | tf_op jit(solution)/shard_map/ppermute | solution.py:486
  97.5 2.6 %collective-permute-start.18 = (f32[16,128]{1,0:T(8,128)S(1)}, f32[16,128]{1,0:T(8,128)S(1)}, u32[]{:S(2)}, u32[]{:S(2)}) collective-permute-start(f32[16,128]{1,0:T(8,128)S(1)} %add.19.a), channel_id=1, source_target_pairs={{0,128},{64,192},{128,0},{192,64},{1,129},{65,193},{129,1},{193,65... | collective-permute-start | bytes 24584 | tf_op jit(solution)/shard_map/ppermute | solution.py:36
  100.2 1.6 collective-permute-start.19
  102.7 1.1 collective-permute-done.19.d
  104.6 1.1 collective-permute-done.20.b
  106.5 3.6 %collective-permute-done.21 = f32[4,128]{1,0:T(4,128)S(1)} collective-permute-done((f32[4,128]{1,0:T(4,128)S(1)}, f32[4,128]{1,0:T(4,128)S(1)}, u32[]{:S(2)}, u32[]{:S(2)}) %collective-permute-start.21) | collective-permute-done | bytes 2080 | tf_op jit(solution)/shard_map/ppermute | solution.py:490
  110.1 19.1 %all_to_all.20 = f32[64,4,128]{2,1,0:T(4,128)S(1)} all-to-all(f32[64,4,128]{2,1,0:T(4,128)S(1)} %broadcast_in_dim.5), channel_id=1, replica_groups=mesh['y'=4,'x'=4,'zh'=4,'zb'=2,'k'=2] {'y','x','zh'}, dimensions={0} | all-to-all | bytes 262144 | tf_op jit(solution)/shard_map/all_to_all | solution.py:41
  129.4 1.2 collective-permute-done.22.refs_2_
  130.5 1.5 scores.1.a
  133.3 1.0 pair_lists.1
  134.9 1.8 %collective-permute-start.25 = (f32[4,128]{1,0:T(4,128)S(1)}, f32[4,128]{1,0:T(4,128)S(1)}, u32[]{:S(2)}, u32[]{:S(2)}) collective-permute-start(f32[4,128]{1,0:T(4,128)S(1)} %get-tuple-element.59), channel_id=1, source_target_pairs={{0,128},{64,192},{128,0},{192,64},{1,129},{65,193},{129,1},{193,65... | collective-permute-start | bytes 6152 | tf_op jit(solution)/shard_map/ppermute | solution.py:36
  136.8 1.3 collective-permute-start.26
  138.0 1.1 collective-permute-done.24.b
  140.4 1.6 four_lists.1
  141.9 20.6 %all_to_all.21 = f32[128,4,128]{2,1,0:T(4,128)S(1)} all-to-all(f32[128,4,128]{2,1,0:T(4,128)S(1)} %four_lists.1), channel_id=1, replica_groups=mesh['y'=4,'x'=4,'zh'=4,'zb'=2,'k'=2] {'y','x','zh','zb'}, dimensions={0} | all-to-all | bytes 524288 | tf_op jit(solution)/shard_map/all_to_all | solution.py:497
  162.5 1.4 final_lists.1
  (67 shorter events, 14.8 us)
Async XLA Ops:
  0.0 4.1 %collective-permute-start.4 = (bf16[224,1024]{1,0:T(8,128)(2,1)}, bf16[224,1024]{1,0:T(8,128)(2,1)S(1)}, u32[]{:S(2)}, u32[]{:S(2)}) collective-permute-start(bf16[224,1024]{1,0:T(8,128)(2,1)} %bitcast.23), channel_id=1, source_target_pairs={{0,1},{1,0},{2,3},{3,2},{4,5},{5,4},{6,7},{7,6},{8,9},{9,8},{10,11... | collective-permute-start | bytes 1376264 | tf_op jit(solution)/shard_map/ppermute | solution.py:32
  0.0 4.1 %collective-permute-start.5 = (bf16[224,1024]{1,0:T(8,128)(2,1)}, bf16[224,1024]{1,0:T(8,128)(2,1)S(1)}, u32[]{:S(2)}, u32[]{:S(2)}) collective-permute-start(bf16[224,1024]{1,0:T(8,128)(2,1)} %bitcast.25), channel_id=1, source_target_pairs={{0,1},{1,0},{2,3},{3,2},{4,5},{5,4},{6,7},{7,6},{8,9},{9,8},{10,11... | collective-permute-start | bytes 1376264 | tf_op jit(solution)/shard_map/ppermute | solution.py:32
  0.5 3.6 %collective-permute-start.6 = (bf16[224,1024]{1,0:T(8,128)(2,1)}, bf16[224,1024]{1,0:T(8,128)(2,1)S(1)}, u32[]{:S(2)}, u32[]{:S(2)}) collective-permute-start(bf16[224,1024]{1,0:T(8,128)(2,1)} %w0.1), channel_id=1, source_target_pairs={{0,1},{1,0},{2,3},{3,2},{4,5},{5,4},{6,7},{7,6},{8,9},{9,8},{10,11... | collective-permute-start | bytes 1376264 | tf_op jit(solution)/shard_map/ppermute | solution.py:32
  1.9 1.3 collective-permute-start.2
  2.5 1.4 collective-permute-start.3
  5.0 21.4 %copy-start.6 = (bf16[64,1024]{1,0:T(8,128)(2,1)S(1)}, bf16[64,1024]{1,0:T(8,128)(2,1)}, u32[]{:S(2)}) copy-start(bf16[64,1024]{1,0:T(8,128)(2,1)} %param.12) | copy-start | bytes 393220
  5.0 39.5 %copy-start.3 = (bf16[1024,224]{0,1:T(8,128)(2,1)S(1)}, bf16[1024,224]{0,1:T(8,128)(2,1)}, u32[]{:S(2)}) copy-start(bf16[1024,224]{0,1:T(8,128)(2,1)} %param.10) | copy-start | bytes 1376260
  5.0 39.5 %all-to-all-start = ((bf16[32,64,128]{2,1,0:T(8,128)(2,1)}), bf16[32,64,128]{2,1,0:T(8,128)(2,1)S(1)}, u32[]{:S(2)}, u32[]{:S(2)}) async-start(bf16[32,64,128]{2,1,0:T(8,128)(2,1)} %broadcast_in_dim.4), calls=%async_computation | async-start | bytes 1048576 | tf_op jit(solution)/shard_map/all_to_all | solution.py:41
  26.5 0.9 collective-permute-start
  27.3 1.3 collective-permute-start.1
  45.9 7.5 %collective-permute-start.7 = (bf16[64,1024]{1,0:T(8,128)(2,1)S(1)}, bf16[64,1024]{1,0:T(8,128)(2,1)S(1)}, u32[]{:S(2)}, u32[]{:S(2)}) collective-permute-start(bf16[64,1024]{1,0:T(8,128)(2,1)S(1)} %get-tuple-element.40), channel_id=1, source_target_pairs={{0,64},{64,128},{128,192},{192,0},{1,65},{65,129},{129,193},{193,1... | collective-permute-start | bytes 393224 | tf_op jit(solution)/shard_map/ppermute | solution.py:36
  47.2 9.6 %collective-permute-start.8 = (bf16[64,1024]{1,0:T(8,128)(2,1)S(1)}, bf16[64,1024]{1,0:T(8,128)(2,1)S(1)}, u32[]{:S(2)}, u32[]{:S(2)}) collective-permute-start(bf16[64,1024]{1,0:T(8,128)(2,1)S(1)} %get-tuple-element.41), channel_id=1, source_target_pairs={{0,128},{64,192},{128,0},{192,64},{1,129},{65,193},{129,1},{193,65... | collective-permute-start | bytes 393224 | tf_op jit(solution)/shard_map/ppermute | solution.py:36
  48.5 8.4 %collective-permute-start.9 = (bf16[64,1024]{1,0:T(8,128)(2,1)S(1)}, bf16[64,1024]{1,0:T(8,128)(2,1)S(1)}, u32[]{:S(2)}, u32[]{:S(2)}) collective-permute-start(bf16[64,1024]{1,0:T(8,128)(2,1)S(1)} %get-tuple-element.42), channel_id=1, source_target_pairs={{0,192},{64,0},{128,64},{192,128},{1,193},{65,1},{129,65},{193,129... | collective-permute-start | bytes 393224 | tf_op jit(solution)/shard_map/ppermute | solution.py:36
  50.0 11.2 %collective-permute-start.13 = (bf16[128,512]{1,0:T(8,128)(2,1)S(1)}, bf16[128,512]{1,0:T(8,128)(2,1)S(1)}, u32[]{:S(2)}, u32[]{:S(2)}) collective-permute-start(bf16[128,512]{1,0:T(8,128)(2,1)S(1)} %pad_maximum_fusion.w0), channel_id=1, source_target_pairs={{0,8},{4,12},{8,0},{12,4},{1,9},{5,13},{9,1},{13,5},{2,10},{6,14},... | collective-permute-start | bytes 393224 | tf_op jit(solution)/shard_map/ppermute | solution.py:470
  52.7 14.5 %collective-permute-start.14 = (bf16[128,512]{1,0:T(8,128)(2,1)S(1)}, bf16[128,512]{1,0:T(8,128)(2,1)S(1)}, u32[]{:S(2)}, u32[]{:S(2)}) collective-permute-start(bf16[128,512]{1,0:T(8,128)(2,1)S(1)} %pad_maximum_fusion.w0), channel_id=1, source_target_pairs={{0,4},{4,8},{8,12},{12,0},{1,5},{5,9},{9,13},{13,1},{2,6},{6,10},{... | collective-permute-start | bytes 393224 | tf_op jit(solution)/shard_map/ppermute | solution.py:470
  53.4 13.9 %collective-permute-start.15 = (bf16[128,512]{1,0:T(8,128)(2,1)S(1)}, bf16[128,512]{1,0:T(8,128)(2,1)S(1)}, u32[]{:S(2)}, u32[]{:S(2)}) collective-permute-start(bf16[128,512]{1,0:T(8,128)(2,1)S(1)} %pad_maximum_fusion.w0), channel_id=1, source_target_pairs={{0,12},{4,0},{8,4},{12,8},{1,13},{5,1},{9,5},{13,9},{2,14},{6,2},{... | collective-permute-start | bytes 393224 | tf_op jit(solution)/shard_map/ppermute | solution.py:470
  57.6 5.8 %collective-permute-start.10 = (bf16[64,512]{1,0:T(8,128)(2,1)S(1)}, bf16[64,512]{1,0:T(8,128)(2,1)S(1)}, u32[]{:S(2)}, u32[]{:S(2)}) collective-permute-start(bf16[64,512]{1,0:T(8,128)(2,1)S(1)} %get-tuple-element.46.a), channel_id=1, source_target_pairs={{0,64},{64,128},{128,192},{192,0},{1,65},{65,129},{129,193},{193,1... | collective-permute-start | bytes 196616 | tf_op jit(solution)/shard_map/ppermute | solution.py:36
  59.7 5.8 %collective-permute-start.11 = (bf16[64,512]{1,0:T(8,128)(2,1)S(1)}, bf16[64,512]{1,0:T(8,128)(2,1)S(1)}, u32[]{:S(2)}, u32[]{:S(2)}) collective-permute-start(bf16[64,512]{1,0:T(8,128)(2,1)S(1)} %get-tuple-element.46.a), channel_id=1, source_target_pairs={{0,128},{64,192},{128,0},{192,64},{1,129},{65,193},{129,1},{193,65... | collective-permute-start | bytes 196616 | tf_op jit(solution)/shard_map/ppermute | solution.py:36
  61.2 4.3 %collective-permute-start.12 = (bf16[64,512]{1,0:T(8,128)(2,1)S(1)}, bf16[64,512]{1,0:T(8,128)(2,1)S(1)}, u32[]{:S(2)}, u32[]{:S(2)}) collective-permute-start(bf16[64,512]{1,0:T(8,128)(2,1)S(1)} %get-tuple-element.46.a), channel_id=1, source_target_pairs={{0,192},{64,0},{128,64},{192,128},{1,193},{65,1},{129,65},{193,129... | collective-permute-start | bytes 196616 | tf_op jit(solution)/shard_map/ppermute | solution.py:36
  67.3 25.4 %all-to-all-start.1 = ((bf16[32,16,512]{2,1,0:T(8,128)(2,1)}), bf16[32,16,512]{2,1,0:T(8,128)(2,1)S(1)}, u32[]{:S(2)}, u32[]{:S(2)}) async-start(bf16[32,16,512]{2,1,0:T(8,128)(2,1)} %bitcast.11), calls=%async_computation.1 | async-start | bytes 1048576 | tf_op jit(solution)/shard_map/all_to_all | solution.py:480
  76.7 53.9 %copy-start = (bf16[512,1024]{1,0:T(8,128)(2,1)S(1)}, bf16[512,1024]{1,0:T(8,128)(2,1)}, u32[]{:S(2)}) copy-start(bf16[512,1024]{1,0:T(8,128)(2,1)} %refs_3_.1) | copy-start | bytes 3145732
  92.8 3.8 %collective-permute-start.16 = (f32[16,128]{1,0:T(8,128)S(1)}, f32[16,128]{1,0:T(8,128)S(1)}, u32[]{:S(2)}, u32[]{:S(2)}) collective-permute-start(f32[16,128]{1,0:T(8,128)S(1)} %get-tuple-element.53), channel_id=1, source_target_pairs={{0,2},{2,0},{1,3},{3,1},{4,6},{6,4},{5,7},{7,5},{8,10},{10,8},{9,1... | collective-permute-start | bytes 24584 | tf_op jit(solution)/shard_map/ppermute | solution.py:486
  96.7 5.1 %collective-permute-start.17 = (f32[16,128]{1,0:T(8,128)S(1)}, f32[16,128]{1,0:T(8,128)S(1)}, u32[]{:S(2)}, u32[]{:S(2)}) collective-permute-start(f32[16,128]{1,0:T(8,128)S(1)} %add.19.a), channel_id=1, source_target_pairs={{0,64},{64,128},{128,192},{192,0},{1,65},{65,129},{129,193},{193,1... | collective-permute-start | bytes 24584 | tf_op jit(solution)/shard_map/ppermute | solution.py:36
  97.5 5.2 %collective-permute-start.18 = (f32[16,128]{1,0:T(8,128)S(1)}, f32[16,128]{1,0:T(8,128)S(1)}, u32[]{:S(2)}, u32[]{:S(2)}) collective-permute-start(f32[16,128]{1,0:T(8,128)S(1)} %add.19.a), channel_id=1, source_target_pairs={{0,128},{64,192},{128,0},{192,64},{1,129},{65,193},{129,1},{193,65... | collective-permute-start | bytes 24584 | tf_op jit(solution)/shard_map/ppermute | solution.py:36
  100.2 3.7 %collective-permute-start.19 = (f32[16,128]{1,0:T(8,128)S(1)}, f32[16,128]{1,0:T(8,128)S(1)}, u32[]{:S(2)}, u32[]{:S(2)}) collective-permute-start(f32[16,128]{1,0:T(8,128)S(1)} %add.19.a), channel_id=1, source_target_pairs={{0,192},{64,0},{128,64},{192,128},{1,193},{65,1},{129,65},{193,129... | collective-permute-start | bytes 24584 | tf_op jit(solution)/shard_map/ppermute | solution.py:36
  104.5 1.2 collective-permute-start.20
  106.4 3.6 %collective-permute-start.21 = (f32[4,128]{1,0:T(4,128)S(1)}, f32[4,128]{1,0:T(4,128)S(1)}, u32[]{:S(2)}, u32[]{:S(2)}) collective-permute-start(f32[4,128]{1,0:T(4,128)S(1)} %code_part.1), channel_id=1, source_target_pairs={{0,2},{2,0},{1,3},{3,1},{4,6},{6,4},{5,7},{7,5},{8,10},{10,8},{9,1... | collective-permute-start | bytes 6152 | tf_op jit(solution)/shard_map/ppermute | solution.py:490
  129.3 1.3 collective-permute-start.22
  132.0 1.2 collective-permute-start.23
  134.3 4.9 %collective-permute-start.24 = (f32[4,128]{1,0:T(4,128)S(1)}, f32[4,128]{1,0:T(4,128)S(1)}, u32[]{:S(2)}, u32[]{:S(2)}) collective-permute-start(f32[4,128]{1,0:T(4,128)S(1)} %get-tuple-element.58), channel_id=1, source_target_pairs={{0,64},{64,128},{128,192},{192,0},{1,65},{65,129},{129,193},{193,1... | collective-permute-start | bytes 6152 | tf_op jit(solution)/shard_map/ppermute | solution.py:36
  134.9 5.1 %collective-permute-start.25 = (f32[4,128]{1,0:T(4,128)S(1)}, f32[4,128]{1,0:T(4,128)S(1)}, u32[]{:S(2)}, u32[]{:S(2)}) collective-permute-start(f32[4,128]{1,0:T(4,128)S(1)} %get-tuple-element.59), channel_id=1, source_target_pairs={{0,128},{64,192},{128,0},{192,64},{1,129},{65,193},{129,1},{193,65... | collective-permute-start | bytes 6152 | tf_op jit(solution)/shard_map/ppermute | solution.py:36
  136.8 3.6 %collective-permute-start.26 = (f32[4,128]{1,0:T(4,128)S(1)}, f32[4,128]{1,0:T(4,128)S(1)}, u32[]{:S(2)}, u32[]{:S(2)}) collective-permute-start(f32[4,128]{1,0:T(4,128)S(1)} %get-tuple-element.60), channel_id=1, source_target_pairs={{0,192},{64,0},{128,64},{192,128},{1,193},{65,1},{129,65},{193,129... | collective-permute-start | bytes 6152 | tf_op jit(solution)/shard_map/ppermute | solution.py:36
  (4 other events, 54.2 us)

commit v10 on v8

--- a/solution.py
+++ b/solution.py
@@ -475,9 +475,6 @@
     groups = (units, *(shifted(units, d) for d in (1, 2, 3)))
     groups, code_rows[2] = lax.optimization_barrier((groups, code_rows[2]))
     branch = down(place, groups, down_weight, down_peer)
-    branch, code_rows[1], code_rows[3] = lax.optimization_barrier(
-        (branch, code_rows[1], code_rows[3])
-    )
     branch = lax.all_to_all(branch.reshape(32, 8, 1024), XZ, 0, 0, tiled=True)
     here = lax.dynamic_slice(
         gathered.reshape(4, 8, 64, 128), (x, 0, zh * 16 + zb * 8, 0), (1, 8, 8, 128)

time: 164 us -> 165 us (level)
    ppermute x12, waiting for transfers between devices: 7.16 us -> 10.4 us  [shifted(): return lax.ppermute(x, 'y', [(i, (i + d) % 4) for i in range(4)])]
  transfers between devices with their start and end apart: 30 -> 30, of which waited for: 16 -> 20; matrix products, arithmetic and copies ran while one was open for 0% -> 0% of each run, Pallas kernels for 2% -> 1%
where the time goes in v10:
time: 165 us; the launch traced here: 164 us
  starting transfers between devices  60.4 us (37%)
  waiting for transfers between devices  49.5 us (30%)
  blocking collectives  40.6 us (25%)
  Pallas kernels  11.6 us (7%)
  local copies, waits for them, and re-layouts  1.75 us (1%)
    all_to_all x1, starting transfers between devices, spread(): return lax.all_to_all(copies, axes, 0, 0, tiled=True)  21.4 us
    all_to_all x1, blocking collectives, per_device(): arrived = lax.all_to_all(lists, YXZ, 0, 0, tiled=True)  20.6 us
    all_to_all x1, blocking collectives, spread(): return lax.all_to_all(copies, axes, 0, 0, tiled=True)  20 us
    ppermute x12, starting transfers between devices, shifted(): return lax.ppermute(x, 'y', [(i, (i + d) % 4) for i in range(4)])  16.2 us
    all_to_all x1, waiting for transfers between devices, spread(): return lax.all_to_all(copies, axes, 0, 0, tiled=True)  15.8 us
    all_to_all x1, waiting for transfers between devices, per_device(): branch = lax.all_to_all(branch.reshape(32, 8, 1024), XZ, 0, 0, tiled=True)  14.6 us
    ppermute x12, waiting for transfers between devices, shifted(): return lax.ppermute(x, 'y', [(i, (i + d) % 4) for i in range(4)])  10.4 us
    all_to_all x1, starting transfers between devices, per_device(): branch = lax.all_to_all(branch.reshape(32, 8, 1024), XZ, 0, 0, tiled=True)  9.47 us
  transfers between devices with their start and end apart: 30, of which 20 were waited for; matrix products, arithmetic and copies ran while one was open for 0% of the time, Pallas kernels for 1%

profile of v10, /device:TPU:32, one launch (start us, length us, event | category | flops | bytes accessed | tf_op | source)
XLA Modules:
  0.0 164.2 jit_solution(17546298114277866215)
XLA Ops:
  5.0 21.4 %all-to-all-start = ((bf16[32,64,128]{2,1,0:T(8,128)(2,1)}), bf16[32,64,128]{2,1,0:T(8,128)(2,1)S(1)}, u32[]{:S(2)}, u32[]{:S(2)}) async-start(bf16[32,64,128]{2,1,0:T(8,128)(2,1)} %broadcast_in_dim.4), calls=%async_computation | async-start | bytes 1048576 | tf_op jit(solution)/shard_map/all_to_all | solution.py:41
  27.4 1.2 collective-permute-done.1
  28.7 15.8 %all-to-all-done.h = bf16[32,64,128]{2,1,0:T(8,128)(2,1)S(1)} async-done(((bf16[32,64,128]{2,1,0:T(8,128)(2,1)}), bf16[32,64,128]{2,1,0:T(8,128)(2,1)S(1)}, u32[]{:S(2)}, u32[]{:S(2)}) %all-to-all-start) | async-done | bytes 524320 | tf_op jit(solution)/shard_map/all_to_all | solution.py:41
  44.5 1.4 gate_up.1
  45.9 1.4 collective-permute-start.7
  47.3 1.3 collective-permute-start.8
  48.6 1.5 collective-permute-start.9
  50.1 2.7 %collective-permute-start.13 = (bf16[128,512]{1,0:T(8,128)(2,1)S(1)}, bf16[128,512]{1,0:T(8,128)(2,1)S(1)}, u32[]{:S(2)}, u32[]{:S(2)}) collective-permute-start(bf16[128,512]{1,0:T(8,128)(2,1)S(1)} %pad_maximum_fusion.w0), channel_id=1, source_target_pairs={{0,8},{4,12},{8,0},{12,4},{1,9},{5,13},{9,1},{13,5},{2,10},{6,14},... | collective-permute-start | bytes 393224 | tf_op jit(solution)/shard_map/ppermute | solution.py:471
  52.8 1.0 collective-permute-done.8.c
  56.0 3.3 %collective-permute-start.11 = (bf16[64,512]{1,0:T(8,128)(2,1)S(1)}, bf16[64,512]{1,0:T(8,128)(2,1)S(1)}, u32[]{:S(2)}, u32[]{:S(2)}) collective-permute-start(bf16[64,512]{1,0:T(8,128)(2,1)S(1)} %get-tuple-element.45.a), channel_id=1, source_target_pairs={{0,128},{64,192},{128,0},{192,64},{1,129},{65,193},{129,1},{193,65... | collective-permute-start | bytes 196616 | tf_op jit(solution)/shard_map/ppermute | solution.py:36
  60.7 1.6 collective-permute-done.11.c
  62.3 1.3 collective-permute-done.12.d
  63.6 1.8 %down.1 = bf16[256,1024]{1,0:T(8,128)(2,1)} custom-call(s32[8]{0:T(128)S(1)} %stack.35.place.refs_0_, bf16[64,512]{1,0:T(8,128)(2,1)S(1)} %get-tuple-element.45.a, bf16[64,512]{1,0:T(8,128)(2,1)S(1)} %collective-permute-done.10.b, bf16[64,512]{1,0:T(8,128)(2,1)S(1)} %collective-permute-done.11.c, bf16[64,512]{1,0:T(8,128)(2,1)S(1)} %collective-permute-done.12.d, ...), custom_call_target="tpu_custom_call" | custom-call | tf_op jit(solution)/shard_map/down/pallas_call | solution.py:153
  65.4 9.5 %all-to-all-start.1 = ((bf16[32,8,1024]{2,1,0:T(8,128)(2,1)}), bf16[32,8,1024]{2,1,0:T(8,128)(2,1)S(1)}, u32[]{:S(2)}, u32[]{:S(2)}) async-start(bf16[32,8,1024]{2,1,0:T(8,128)(2,1)} %bitcast.11), calls=%async_computation.1 | async-start | bytes 1048576 | tf_op jit(solution)/shard_map/all_to_all | solution.py:478
  74.9 2.4 %collective-permute-start.20 = (bf16[128,512]{1,0:T(8,128)(2,1)S(1)}, bf16[128,512]{1,0:T(8,128)(2,1)S(1)}, u32[]{:S(2)}, u32[]{:S(2)}) collective-permute-start(bf16[128,512]{1,0:T(8,128)(2,1)S(1)} %pad_maximum_fusion.w0), channel_id=1, source_target_pairs={{0,4},{4,8},{8,12},{12,0},{1,5},{5,9},{9,13},{13,1},{2,6},{6,10},{... | collective-permute-start | bytes 393224 | tf_op jit(solution)/shard_map/ppermute | solution.py:471
  77.3 1.8 %collective-permute-start.21 = (bf16[128,512]{1,0:T(8,128)(2,1)S(1)}, bf16[128,512]{1,0:T(8,128)(2,1)S(1)}, u32[]{:S(2)}, u32[]{:S(2)}) collective-permute-start(bf16[128,512]{1,0:T(8,128)(2,1)S(1)} %pad_maximum_fusion.w0), channel_id=1, source_target_pairs={{0,12},{4,0},{8,4},{12,8},{1,13},{5,1},{9,5},{13,9},{2,14},{6,2},{... | collective-permute-start | bytes 393224 | tf_op jit(solution)/shard_map/ppermute | solution.py:471
  79.1 14.6 %all-to-all-done.1.parts = bf16[32,8,1024]{2,1,0:T(8,128)(2,1)S(1)} async-done(((bf16[32,8,1024]{2,1,0:T(8,128)(2,1)}), bf16[32,8,1024]{2,1,0:T(8,128)(2,1)S(1)}, u32[]{:S(2)}, u32[]{:S(2)}) %all-to-all-start.1) | async-done | bytes 524320 | tf_op jit(solution)/shard_map/all_to_all | solution.py:478
  94.0 3.0 %collective-permute-start.15 = (f32[8,128]{1,0:T(8,128)S(1)}, f32[8,128]{1,0:T(8,128)S(1)}, u32[]{:S(2)}, u32[]{:S(2)}) collective-permute-start(f32[8,128]{1,0:T(8,128)S(1)} %get-tuple-element.51.a), channel_id=1, source_target_pairs={{0,128},{64,192},{128,0},{192,64},{1,129},{65,193},{129,1},{193,65... | collective-permute-start | bytes 12296 | tf_op jit(solution)/shard_map/ppermute | solution.py:36
  99.2 1.4 collective-permute-done.16.d
  101.6 1.7 %collective-permute-start.19 = (f32[4,128]{1,0:T(4,128)S(1)}, f32[4,128]{1,0:T(4,128)S(1)}, u32[]{:S(2)}, u32[]{:S(2)}) collective-permute-start(f32[4,128]{1,0:T(4,128)S(1)} %get-tuple-element.53), channel_id=1, source_target_pairs={{0,3},{1,2},{2,1},{3,0},{4,7},{5,6},{6,5},{7,4},{8,11},{9,10},{10,... | collective-permute-start | bytes 6152 | tf_op jit(solution)/shard_map/ppermute | solution.py:488
  103.3 1.8 %collective-permute-done.18.c = f32[4,128]{1,0:T(4,128)S(1)} collective-permute-done((f32[4,128]{1,0:T(4,128)S(1)}, f32[4,128]{1,0:T(4,128)S(1)}, u32[]{:S(2)}, u32[]{:S(2)}) %collective-permute-start.18) | collective-permute-done | bytes 2080 | tf_op jit(solution)/shard_map/ppermute | solution.py:488
  105.8 1.5 collective-permute-start.22
  107.3 2.1 %collective-permute-done.22 = f32[4,128]{1,0:T(4,128)S(1)} collective-permute-done((f32[4,128]{1,0:T(4,128)S(1)}, f32[4,128]{1,0:T(4,128)S(1)}, u32[]{:S(2)}, u32[]{:S(2)}) %collective-permute-start.22) | collective-permute-done | bytes 2080 | tf_op jit(solution)/shard_map/ppermute | solution.py:490
  109.4 20.0 %all_to_all.20 = f32[64,4,128]{2,1,0:T(4,128)S(1)} all-to-all(f32[64,4,128]{2,1,0:T(4,128)S(1)} %broadcast_in_dim.5), channel_id=1, replica_groups=mesh['y'=4,'x'=4,'zh'=4,'zb'=2,'k'=2] {'y','x','zh'}, dimensions={0} | all-to-all | bytes 262144 | tf_op jit(solution)/shard_map/all_to_all | solution.py:41
  129.6 1.2 collective-permute-done.23.refs_2_
  130.8 1.5 scores.1.a
  135.2 1.8 %collective-permute-start.26 = (f32[4,128]{1,0:T(4,128)S(1)}, f32[4,128]{1,0:T(4,128)S(1)}, u32[]{:S(2)}, u32[]{:S(2)}) collective-permute-start(f32[4,128]{1,0:T(4,128)S(1)} %get-tuple-element.57), channel_id=1, source_target_pairs={{0,128},{64,192},{128,0},{192,64},{1,129},{65,193},{129,1},{193,65... | collective-permute-start | bytes 6152 | tf_op jit(solution)/shard_map/ppermute | solution.py:36
  137.0 1.3 collective-permute-start.27
  138.3 1.1 collective-permute-done.25.b
  140.6 1.6 four_lists.1
  142.2 20.6 %all_to_all.21 = f32[128,4,128]{2,1,0:T(4,128)S(1)} all-to-all(f32[128,4,128]{2,1,0:T(4,128)S(1)} %four_lists.1), channel_id=1, replica_groups=mesh['y'=4,'x'=4,'zh'=4,'zb'=2,'k'=2] {'y','x','zh','zb'}, dimensions={0} | all-to-all | bytes 524288 | tf_op jit(solution)/shard_map/all_to_all | solution.py:497
  162.8 1.4 final_lists.1
  (66 shorter events, 18.0 us)
Async XLA Ops:
  0.0 4.1 %collective-permute-start.4 = (bf16[224,1024]{1,0:T(8,128)(2,1)}, bf16[224,1024]{1,0:T(8,128)(2,1)S(1)}, u32[]{:S(2)}, u32[]{:S(2)}) collective-permute-start(bf16[224,1024]{1,0:T(8,128)(2,1)} %bitcast.22), channel_id=1, source_target_pairs={{0,1},{1,0},{2,3},{3,2},{4,5},{5,4},{6,7},{7,6},{8,9},{9,8},{10,11... | collective-permute-start | bytes 1376264 | tf_op jit(solution)/shard_map/ppermute | solution.py:32
  0.0 4.1 %collective-permute-start.5 = (bf16[224,1024]{1,0:T(8,128)(2,1)}, bf16[224,1024]{1,0:T(8,128)(2,1)S(1)}, u32[]{:S(2)}, u32[]{:S(2)}) collective-permute-start(bf16[224,1024]{1,0:T(8,128)(2,1)} %bitcast.24), channel_id=1, source_target_pairs={{0,1},{1,0},{2,3},{3,2},{4,5},{5,4},{6,7},{7,6},{8,9},{9,8},{10,11... | collective-permute-start | bytes 1376264 | tf_op jit(solution)/shard_map/ppermute | solution.py:32
  0.5 3.6 %collective-permute-start.6 = (bf16[224,1024]{1,0:T(8,128)(2,1)}, bf16[224,1024]{1,0:T(8,128)(2,1)S(1)}, u32[]{:S(2)}, u32[]{:S(2)}) collective-permute-start(bf16[224,1024]{1,0:T(8,128)(2,1)} %w0.1), channel_id=1, source_target_pairs={{0,1},{1,0},{2,3},{3,2},{4,5},{5,4},{6,7},{7,6},{8,9},{9,8},{10,11... | collective-permute-start | bytes 1376264 | tf_op jit(solution)/shard_map/ppermute | solution.py:32
  1.9 1.3 collective-permute-start.2
  2.5 1.4 collective-permute-start.3
  5.0 39.5 %copy-start.3 = (bf16[1024,224]{0,1:T(8,128)(2,1)S(1)}, bf16[1024,224]{0,1:T(8,128)(2,1)}, u32[]{:S(2)}) copy-start(bf16[1024,224]{0,1:T(8,128)(2,1)} %param.10) | copy-start | bytes 1376260
  5.0 39.5 %all-to-all-start = ((bf16[32,64,128]{2,1,0:T(8,128)(2,1)}), bf16[32,64,128]{2,1,0:T(8,128)(2,1)S(1)}, u32[]{:S(2)}, u32[]{:S(2)}) async-start(bf16[32,64,128]{2,1,0:T(8,128)(2,1)} %broadcast_in_dim.4), calls=%async_computation | async-start | bytes 1048576 | tf_op jit(solution)/shard_map/all_to_all | solution.py:41
  26.5 0.9 collective-permute-start
  27.3 1.3 collective-permute-start.1
  45.9 6.9 %collective-permute-start.7 = (bf16[64,1024]{1,0:T(8,128)(2,1)S(1)}, bf16[64,1024]{1,0:T(8,128)(2,1)S(1)}, u32[]{:S(2)}, u32[]{:S(2)}) collective-permute-start(bf16[64,1024]{1,0:T(8,128)(2,1)S(1)} %get-tuple-element.39), channel_id=1, source_target_pairs={{0,64},{64,128},{128,192},{192,0},{1,65},{65,129},{129,193},{193,1... | collective-permute-start | bytes 393224 | tf_op jit(solution)/shard_map/ppermute | solution.py:36
  47.3 6.5 %collective-permute-start.8 = (bf16[64,1024]{1,0:T(8,128)(2,1)S(1)}, bf16[64,1024]{1,0:T(8,128)(2,1)S(1)}, u32[]{:S(2)}, u32[]{:S(2)}) collective-permute-start(bf16[64,1024]{1,0:T(8,128)(2,1)S(1)} %get-tuple-element.40), channel_id=1, source_target_pairs={{0,128},{64,192},{128,0},{192,64},{1,129},{65,193},{129,1},{193,65... | collective-permute-start | bytes 393224 | tf_op jit(solution)/shard_map/ppermute | solution.py:36
  48.6 5.8 %collective-permute-start.9 = (bf16[64,1024]{1,0:T(8,128)(2,1)S(1)}, bf16[64,1024]{1,0:T(8,128)(2,1)S(1)}, u32[]{:S(2)}, u32[]{:S(2)}) collective-permute-start(bf16[64,1024]{1,0:T(8,128)(2,1)S(1)} %get-tuple-element.41), channel_id=1, source_target_pairs={{0,192},{64,0},{128,64},{192,128},{1,193},{65,1},{129,65},{193,129... | collective-permute-start | bytes 393224 | tf_op jit(solution)/shard_map/ppermute | solution.py:36
  50.1 9.7 %collective-permute-start.13 = (bf16[128,512]{1,0:T(8,128)(2,1)S(1)}, bf16[128,512]{1,0:T(8,128)(2,1)S(1)}, u32[]{:S(2)}, u32[]{:S(2)}) collective-permute-start(bf16[128,512]{1,0:T(8,128)(2,1)S(1)} %pad_maximum_fusion.w0), channel_id=1, source_target_pairs={{0,8},{4,12},{8,0},{12,4},{1,9},{5,13},{9,1},{13,5},{2,10},{6,14},... | collective-permute-start | bytes 393224 | tf_op jit(solution)/shard_map/ppermute | solution.py:471
  55.1 5.6 %collective-permute-start.10 = (bf16[64,512]{1,0:T(8,128)(2,1)S(1)}, bf16[64,512]{1,0:T(8,128)(2,1)S(1)}, u32[]{:S(2)}, u32[]{:S(2)}) collective-permute-start(bf16[64,512]{1,0:T(8,128)(2,1)S(1)} %get-tuple-element.45.a), channel_id=1, source_target_pairs={{0,64},{64,128},{128,192},{192,0},{1,65},{65,129},{129,193},{193,1... | collective-permute-start | bytes 196616 | tf_op jit(solution)/shard_map/ppermute | solution.py:36
  56.0 6.2 %collective-permute-start.11 = (bf16[64,512]{1,0:T(8,128)(2,1)S(1)}, bf16[64,512]{1,0:T(8,128)(2,1)S(1)}, u32[]{:S(2)}, u32[]{:S(2)}) collective-permute-start(bf16[64,512]{1,0:T(8,128)(2,1)S(1)} %get-tuple-element.45.a), channel_id=1, source_target_pairs={{0,128},{64,192},{128,0},{192,64},{1,129},{65,193},{129,1},{193,65... | collective-permute-start | bytes 196616 | tf_op jit(solution)/shard_map/ppermute | solution.py:36
  59.3 4.3 %collective-permute-start.12 = (bf16[64,512]{1,0:T(8,128)(2,1)S(1)}, bf16[64,512]{1,0:T(8,128)(2,1)S(1)}, u32[]{:S(2)}, u32[]{:S(2)}) collective-permute-start(bf16[64,512]{1,0:T(8,128)(2,1)S(1)} %get-tuple-element.45.a), channel_id=1, source_target_pairs={{0,192},{64,0},{128,64},{192,128},{1,193},{65,1},{129,65},{193,129... | collective-permute-start | bytes 196616 | tf_op jit(solution)/shard_map/ppermute | solution.py:36
  65.4 28.3 %all-to-all-start.1 = ((bf16[32,8,1024]{2,1,0:T(8,128)(2,1)}), bf16[32,8,1024]{2,1,0:T(8,128)(2,1)S(1)}, u32[]{:S(2)}, u32[]{:S(2)}) async-start(bf16[32,8,1024]{2,1,0:T(8,128)(2,1)} %bitcast.11), calls=%async_computation.1 | async-start | bytes 1048576 | tf_op jit(solution)/shard_map/all_to_all | solution.py:478
  74.9 55.9 %copy-start = (bf16[512,1024]{1,0:T(8,128)(2,1)S(1)}, bf16[512,1024]{1,0:T(8,128)(2,1)}, u32[]{:S(2)}) copy-start(bf16[512,1024]{1,0:T(8,128)(2,1)} %refs_3_.1) | copy-start | bytes 3145732
  74.9 28.4 %collective-permute-start.20 = (bf16[128,512]{1,0:T(8,128)(2,1)S(1)}, bf16[128,512]{1,0:T(8,128)(2,1)S(1)}, u32[]{:S(2)}, u32[]{:S(2)}) collective-permute-start(bf16[128,512]{1,0:T(8,128)(2,1)S(1)} %pad_maximum_fusion.w0), channel_id=1, source_target_pairs={{0,4},{4,8},{8,12},{12,0},{1,5},{5,9},{9,13},{13,1},{2,6},{6,10},{... | collective-permute-start | bytes 393224 | tf_op jit(solution)/shard_map/ppermute | solution.py:471
  77.3 26.0 %collective-permute-start.21 = (bf16[128,512]{1,0:T(8,128)(2,1)S(1)}, bf16[128,512]{1,0:T(8,128)(2,1)S(1)}, u32[]{:S(2)}, u32[]{:S(2)}) collective-permute-start(bf16[128,512]{1,0:T(8,128)(2,1)S(1)} %pad_maximum_fusion.w0), channel_id=1, source_target_pairs={{0,12},{4,0},{8,4},{12,8},{1,13},{5,1},{9,5},{13,9},{2,14},{6,2},{... | collective-permute-start | bytes 393224 | tf_op jit(solution)/shard_map/ppermute | solution.py:471
  93.8 5.0 %collective-permute-start.14 = (f32[8,128]{1,0:T(8,128)S(1)}, f32[8,128]{1,0:T(8,128)S(1)}, u32[]{:S(2)}, u32[]{:S(2)}) collective-permute-start(f32[8,128]{1,0:T(8,128)S(1)} %get-tuple-element.51.a), channel_id=1, source_target_pairs={{0,64},{64,128},{128,192},{192,0},{1,65},{65,129},{129,193},{193,1... | collective-permute-start | bytes 12296 | tf_op jit(solution)/shard_map/ppermute | solution.py:36
  94.0 5.2 %collective-permute-start.15 = (f32[8,128]{1,0:T(8,128)S(1)}, f32[8,128]{1,0:T(8,128)S(1)}, u32[]{:S(2)}, u32[]{:S(2)}) collective-permute-start(f32[8,128]{1,0:T(8,128)S(1)} %get-tuple-element.51.a), channel_id=1, source_target_pairs={{0,128},{64,192},{128,0},{192,64},{1,129},{65,193},{129,1},{193,65... | collective-permute-start | bytes 12296 | tf_op jit(solution)/shard_map/ppermute | solution.py:36
  97.0 3.6 %collective-permute-start.16 = (f32[8,128]{1,0:T(8,128)S(1)}, f32[8,128]{1,0:T(8,128)S(1)}, u32[]{:S(2)}, u32[]{:S(2)}) collective-permute-start(f32[8,128]{1,0:T(8,128)S(1)} %get-tuple-element.51.a), channel_id=1, source_target_pairs={{0,192},{64,0},{128,64},{192,128},{1,193},{65,1},{129,65},{193,129... | collective-permute-start | bytes 12296 | tf_op jit(solution)/shard_map/ppermute | solution.py:36
  101.3 2.0 %collective-permute-start.17 = (f32[4,128]{1,0:T(4,128)S(1)}, f32[4,128]{1,0:T(4,128)S(1)}, u32[]{:S(2)}, u32[]{:S(2)}) collective-permute-start(f32[4,128]{1,0:T(4,128)S(1)} %get-tuple-element.52.a), channel_id=1, source_target_pairs={{0,1},{1,0},{2,3},{3,2},{4,5},{5,4},{6,7},{7,6},{8,9},{9,8},{10,11... | collective-permute-start | bytes 6152 | tf_op jit(solution)/shard_map/ppermute | solution.py:488
  101.4 3.7 %collective-permute-start.18 = (f32[4,128]{1,0:T(4,128)S(1)}, f32[4,128]{1,0:T(4,128)S(1)}, u32[]{:S(2)}, u32[]{:S(2)}) collective-permute-start(f32[4,128]{1,0:T(4,128)S(1)} %get-tuple-element.53), channel_id=1, source_target_pairs={{0,2},{1,3},{2,0},{3,1},{4,6},{5,7},{6,4},{7,5},{8,10},{9,11},{10,... | collective-permute-start | bytes 6152 | tf_op jit(solution)/shard_map/ppermute | solution.py:488
  101.6 3.5 %collective-permute-start.19 = (f32[4,128]{1,0:T(4,128)S(1)}, f32[4,128]{1,0:T(4,128)S(1)}, u32[]{:S(2)}, u32[]{:S(2)}) collective-permute-start(f32[4,128]{1,0:T(4,128)S(1)} %get-tuple-element.53), channel_id=1, source_target_pairs={{0,3},{1,2},{2,1},{3,0},{4,7},{5,6},{6,5},{7,4},{8,11},{9,10},{10,... | collective-permute-start | bytes 6152 | tf_op jit(solution)/shard_map/ppermute | solution.py:488
  105.8 3.6 %collective-permute-start.22 = (f32[4,128]{1,0:T(4,128)S(1)}, f32[4,128]{1,0:T(4,128)S(1)}, u32[]{:S(2)}, u32[]{:S(2)}) collective-permute-start(f32[4,128]{1,0:T(4,128)S(1)} %code_part.1), channel_id=1, source_target_pairs={{0,2},{2,0},{1,3},{3,1},{4,6},{6,4},{5,7},{7,5},{8,10},{10,8},{9,1... | collective-permute-start | bytes 6152 | tf_op jit(solution)/shard_map/ppermute | solution.py:490
  129.5 1.3 collective-permute-start.23
  132.3 1.2 collective-permute-start.24
  134.6 4.9 %collective-permute-start.25 = (f32[4,128]{1,0:T(4,128)S(1)}, f32[4,128]{1,0:T(4,128)S(1)}, u32[]{:S(2)}, u32[]{:S(2)}) collective-permute-start(f32[4,128]{1,0:T(4,128)S(1)} %get-tuple-element.56), channel_id=1, source_target_pairs={{0,64},{64,128},{128,192},{192,0},{1,65},{65,129},{129,193},{193,1... | collective-permute-start | bytes 6152 | tf_op jit(solution)/shard_map/ppermute | solution.py:36
  135.2 5.1 %collective-permute-start.26 = (f32[4,128]{1,0:T(4,128)S(1)}, f32[4,128]{1,0:T(4,128)S(1)}, u32[]{:S(2)}, u32[]{:S(2)}) collective-permute-start(f32[4,128]{1,0:T(4,128)S(1)} %get-tuple-element.57), channel_id=1, source_target_pairs={{0,128},{64,192},{128,0},{192,64},{1,129},{65,193},{129,1},{193,65... | collective-permute-start | bytes 6152 | tf_op jit(solution)/shard_map/ppermute | solution.py:36
  137.0 3.6 %collective-permute-start.27 = (f32[4,128]{1,0:T(4,128)S(1)}, f32[4,128]{1,0:T(4,128)S(1)}, u32[]{:S(2)}, u32[]{:S(2)}) collective-permute-start(f32[4,128]{1,0:T(4,128)S(1)} %get-tuple-element.58), channel_id=1, source_target_pairs={{0,192},{64,0},{128,64},{192,128},{1,193},{65,1},{129,65},{193,129... | collective-permute-start | bytes 6152 | tf_op jit(solution)/shard_map/ppermute | solution.py:36
  (5 other events, 73.7 us)

commit v11 on v10

--- a/solution.py
+++ b/solution.py
@@ -206,13 +206,14 @@
     )(place, counts, res, *sqs)
 
 
-def code_kernel(place, a, b, c, d, w0, w1, w2, w3, out, left):
+def code_kernel(place, a, b, c, d, near, far, out, left):
     zh = place[5]
     left[...] = a[...] + b[...] + c[...] + d[...]
     total = jnp.zeros((8, 512), F32)
-    for s, w in enumerate((w0, w1, w2, w3)):
-        piece = jnp.broadcast_to(left[pl.ds((zh - s + 4) % 4, 1), :], (8, 128))
-        total += jnp.dot(piece.astype(BF16), w[...], preferred_element_type=F32)
+    for w, half, flip in ((near, 0, 0), (near, 1, 1), (far, 0, 3), (far, 1, 2)):
+        piece = jnp.broadcast_to(left[pl.ds(zh ^ flip, 1), :], (8, 128)).astype(BF16)
+        rows = w[half * 128 : half * 128 + 128, :]
+        total += jnp.dot(piece, rows, preferred_element_type=F32)
     for t in range(4):
         out[t : t + 1, :] = total[0:1, t * 128 : t * 128 + 128]
 
@@ -221,7 +222,7 @@
     return pl.pallas_call(
         code_kernel,
         out_shape=shape((4, 128), F32),
-        in_specs=[SMEM] + [VMEM] * 8,
+        in_specs=[SMEM] + [VMEM] * 6,
         out_specs=VMEM,
         scratch_shapes=[pltpu.VMEM((4, 128), F32)],
         compiler_params=PARAMS,
@@ -467,14 +468,17 @@
         [jnp.where(k == 0, mine, theirs), jnp.where(k == 0, theirs, mine)], axis=0
     )
     rows, gathered = lax.optimization_barrier((rows, gathered))
-    turned = [[(i, (i + d) % 4) for i in range(4)] for d in range(4)]
-    code_rows = [rows, *(lax.ppermute(rows, "zh", turned[d]) for d in (1, 2, 3))]
 
     parts = gate_up(place, lengths, gathered, gate_rows, up_rows, gate_peer, up_peer)
+    rows, parts = lax.optimization_barrier((rows, parts))
+    near = lax.ppermute(rows, "zh", [(i, i ^ 1) for i in range(4)])
+    near = jnp.concatenate([rows, near], axis=0)
     units, counts = hidden_of(place, parts[0], *(shifted(parts[d], d) for d in (1, 2, 3)))
+    units, near = lax.optimization_barrier((units, near))
+    far = lax.ppermute(near, "zh", [(i, i ^ 3) for i in range(4)])
     groups = (units, *(shifted(units, d) for d in (1, 2, 3)))
-    groups, code_rows[2] = lax.optimization_barrier((groups, code_rows[2]))
     branch = down(place, groups, down_weight, down_peer)
+    branch, far = lax.optimization_barrier((branch, far))
     branch = lax.all_to_all(branch.reshape(32, 8, 1024), XZ, 0, 0, tiled=True)
     here = lax.dynamic_slice(
         gathered.reshape(4, 8, 64, 128), (x, 0, zh * 16 + zb * 8, 0), (1, 8, 8, 128)
@@ -486,7 +490,7 @@
     flips = [[(i, i ^ r) for i in range(4)] for r in range(4)]
     sent = ((same, 1), (other, 2), (other, 3))
     pieces = (same, *(lax.ppermute(a, ("zb", "k"), flips[r]) for a, r in sent))
-    part = code_part(place, pieces, code_rows)
+    part = code_part(place, pieces, (near, far))
     part = part + lax.ppermute(part, "zb", [(0, 1), (1, 0)])
     codes = spread(part, ("y", "x", "zh"), 64)
     codes = codes.reshape(4, 16, 512).sum(axis=0).astype(BF16)

time: 165 us -> 168 us (1.018)
  waiting for transfers between devices: 49.5 us -> 59.3 us
  starting transfers between devices: 60.4 us -> 55.8 us
  blocking collectives: 40.6 us -> 38.9 us
    ppermute x12, waiting for transfers between devices: 10.4 us -> 14.6 us  [shifted(): return lax.ppermute(x, 'y', [(i, (i + d) % 4) for i in range(4)])]
    all_to_all x1, waiting for transfers between devices: 14.6 us -> 17.8 us  [per_device(): branch = lax.all_to_all(branch.reshape(32, 8, 1024), XZ, 0, 0, tiled=True)]
    ppermute x3 -> x2, starting transfers between devices: 6.94 us -> 4.39 us  [the longest x1 3.16 us: per_device(): far = lax.ppermute(near, 'zh', [(i, i ^ 3) for i in range(4)])]
    ppermute x3 -> x2, waiting for transfers between devices: 0.49 us -> 2.9 us  [the longest x1 2.15 us: per_device(): far = lax.ppermute(near, 'zh', [(i, i ^ 3) for i in range(4)])]
    all_to_all x1, blocking collectives: 20 us -> 18.3 us  [spread(): return lax.all_to_all(copies, axes, 0, 0, tiled=True)]
  transfers between devices with their start and end apart: 30 -> 29, of which waited for: 20 -> 22; matrix products, arithmetic and copies ran while one was open for 0% -> 0% of each run, Pallas kernels for 1% -> 1%
where the time goes in v11:
time: 168 us
  waiting for transfers between devices  59.3 us (35%)
  starting transfers between devices  55.8 us (33%)
  blocking collectives  38.9 us (23%)
  Pallas kernels  11.5 us (7%)
  local copies, waits for them, and re-layouts  1.74 us (1%)
    all_to_all x1, starting transfers between devices, spread(): return lax.all_to_all(copies, axes, 0, 0, tiled=True)  21.4 us
    all_to_all x1, blocking collectives, per_device(): arrived = lax.all_to_all(lists, YXZ, 0, 0, tiled=True)  20.6 us
    all_to_all x1, blocking collectives, spread(): return lax.all_to_all(copies, axes, 0, 0, tiled=True)  18.3 us
    all_to_all x1, waiting for transfers between devices, per_device(): branch = lax.all_to_all(branch.reshape(32, 8, 1024), XZ, 0, 0, tiled=True)  17.8 us
    all_to_all x1, waiting for transfers between devices, spread(): return lax.all_to_all(copies, axes, 0, 0, tiled=True)  15.8 us
    ppermute x12, starting transfers between devices, shifted(): return lax.ppermute(x, 'y', [(i, (i + d) % 4) for i in range(4)])  15.6 us
    ppermute x12, waiting for transfers between devices, shifted(): return lax.ppermute(x, 'y', [(i, (i + d) % 4) for i in range(4)])  14.6 us
    all_to_all x1, starting transfers between devices, per_device(): branch = lax.all_to_all(branch.reshape(32, 8, 1024), XZ, 0, 0, tiled=True)  7.99 us
  transfers between devices with their start and end apart: 29, of which 22 were waited for; matrix products, arithmetic and copies ran while one was open for 0% of the time, Pallas kernels for 1%

profile of v11, /device:TPU:32, one launch (start us, length us, event | category | flops | bytes accessed | tf_op | source)
XLA Modules:
  0.0 167.6 jit_solution(16753422595580678605)
XLA Ops:
  5.0 21.4 %all-to-all-start = ((bf16[32,64,128]{2,1,0:T(8,128)(2,1)}), bf16[32,64,128]{2,1,0:T(8,128)(2,1)S(1)}, u32[]{:S(2)}, u32[]{:S(2)}) async-start(bf16[32,64,128]{2,1,0:T(8,128)(2,1)} %broadcast_in_dim.4), calls=%async_computation | async-start | bytes 1048576 | tf_op jit(solution)/shard_map/all_to_all | solution.py:41
  27.4 1.2 collective-permute-done.1
  28.7 15.8 %all-to-all-done.h = bf16[32,64,128]{2,1,0:T(8,128)(2,1)S(1)} async-done(((bf16[32,64,128]{2,1,0:T(8,128)(2,1)}), bf16[32,64,128]{2,1,0:T(8,128)(2,1)S(1)}, u32[]{:S(2)}, u32[]{:S(2)}) %all-to-all-start) | async-done | bytes 524320 | tf_op jit(solution)/shard_map/all_to_all | solution.py:41
  44.5 1.4 gate_up.1
  45.9 1.2 collective-permute-start.10
  47.1 1.3 collective-permute-start.7
  48.4 1.8 %collective-permute-start.8 = (bf16[64,1024]{1,0:T(8,128)(2,1)S(1)}, bf16[64,1024]{1,0:T(8,128)(2,1)S(1)}, u32[]{:S(2)}, u32[]{:S(2)}) collective-permute-start(bf16[64,1024]{1,0:T(8,128)(2,1)S(1)} %get-tuple-element.49), channel_id=1, source_target_pairs={{0,128},{64,192},{128,0},{192,64},{1,129},{65,193},{129,1},{193,65... | collective-permute-start | bytes 393224 | tf_op jit(solution)/shard_map/ppermute | solution.py:36
  51.8 2.5 %collective-permute-done.7.b = bf16[64,1024]{1,0:T(8,128)(2,1)S(1)} collective-permute-done((bf16[64,1024]{1,0:T(8,128)(2,1)S(1)}, bf16[64,1024]{1,0:T(8,128)(2,1)S(1)}, u32[]{:S(2)}, u32[]{:S(2)}) %collective-permute-start.7) | collective-permute-done | bytes 131104 | tf_op jit(solution)/shard_map/ppermute | solution.py:36
  54.3 1.9 %collective-permute-done.8.c = bf16[64,1024]{1,0:T(8,128)(2,1)S(1)} collective-permute-done((bf16[64,1024]{1,0:T(8,128)(2,1)S(1)}, bf16[64,1024]{1,0:T(8,128)(2,1)S(1)}, u32[]{:S(2)}, u32[]{:S(2)}) %collective-permute-start.8) | collective-permute-done | bytes 131104 | tf_op jit(solution)/shard_map/ppermute | solution.py:36
  56.9 3.2 %collective-permute-start.14 = (bf16[256,512]{1,0:T(8,128)(2,1)S(1)}, bf16[256,512]{1,0:T(8,128)(2,1)S(1)}, u32[]{:S(2)}, u32[]{:S(2)}) collective-permute-start(bf16[256,512]{1,0:T(8,128)(2,1)S(1)} %pad_maximum_fusion.near), channel_id=1, source_target_pairs={{0,12},{4,8},{8,4},{12,0},{1,13},{5,9},{9,5},{13,1},{2,14},{6,10},... | collective-permute-start | bytes 786440 | tf_op jit(solution)/shard_map/ppermute | solution.py:478
  60.2 3.4 %collective-permute-start.12 = (bf16[64,512]{1,0:T(8,128)(2,1)S(1)}, bf16[64,512]{1,0:T(8,128)(2,1)S(1)}, u32[]{:S(2)}, u32[]{:S(2)}) collective-permute-start(bf16[64,512]{1,0:T(8,128)(2,1)S(1)} %get-tuple-element.54.a), channel_id=1, source_target_pairs={{0,128},{64,192},{128,0},{192,64},{1,129},{65,193},{129,1},{193,65... | collective-permute-start | bytes 196616 | tf_op jit(solution)/shard_map/ppermute | solution.py:36
  63.6 2.4 %collective-permute-done.11.b = bf16[64,512]{1,0:T(8,128)(2,1)S(1)} collective-permute-done((bf16[64,512]{1,0:T(8,128)(2,1)S(1)}, bf16[64,512]{1,0:T(8,128)(2,1)S(1)}, u32[]{:S(2)}, u32[]{:S(2)}) %collective-permute-start.11) | collective-permute-done | bytes 65568 | tf_op jit(solution)/shard_map/ppermute | solution.py:36
  66.7 1.2 collective-permute-done.13.d
  67.9 1.8 %down.1 = bf16[256,1024]{1,0:T(8,128)(2,1)} custom-call(s32[8]{0:T(128)S(1)} %stack.35.place.refs_0_, bf16[64,512]{1,0:T(8,128)(2,1)S(1)} %get-tuple-element.54.a, bf16[64,512]{1,0:T(8,128)(2,1)S(1)} %collective-permute-done.11.b, bf16[64,512]{1,0:T(8,128)(2,1)S(1)} %collective-permute-done.12.c, bf16[64,512]{1,0:T(8,128)(2,1)S(1)} %collective-permute-done.13.d, ...), custom_call_target="tpu_custom_call" | custom-call | tf_op jit(solution)/shard_map/down/pallas_call | solution.py:153
  69.7 2.2 %collective-permute-done.14.far = bf16[256,512]{1,0:T(8,128)(2,1)S(1)} collective-permute-done((bf16[256,512]{1,0:T(8,128)(2,1)S(1)}, bf16[256,512]{1,0:T(8,128)(2,1)S(1)}, u32[]{:S(2)}, u32[]{:S(2)}) %collective-permute-start.14) | collective-permute-done | bytes 262176 | tf_op jit(solution)/shard_map/ppermute | solution.py:478
  71.8 8.0 %all-to-all-start.1 = ((bf16[32,8,1024]{2,1,0:T(8,128)(2,1)}), bf16[32,8,1024]{2,1,0:T(8,128)(2,1)S(1)}, u32[]{:S(2)}, u32[]{:S(2)}) async-start(bf16[32,8,1024]{2,1,0:T(8,128)(2,1)} %bitcast.11), calls=%async_computation.1 | async-start | bytes 1048576 | tf_op jit(solution)/shard_map/all_to_all | solution.py:482
  79.9 17.8 %all-to-all-done.1.parts = bf16[32,8,1024]{2,1,0:T(8,128)(2,1)S(1)} async-done(((bf16[32,8,1024]{2,1,0:T(8,128)(2,1)}), bf16[32,8,1024]{2,1,0:T(8,128)(2,1)S(1)}, u32[]{:S(2)}, u32[]{:S(2)}) %all-to-all-start.1) | async-done | bytes 524320 | tf_op jit(solution)/shard_map/all_to_all | solution.py:482
  98.7 3.5 %collective-permute-start.16 = (f32[8,128]{1,0:T(8,128)S(1)}, f32[8,128]{1,0:T(8,128)S(1)}, u32[]{:S(2)}, u32[]{:S(2)}) collective-permute-start(f32[8,128]{1,0:T(8,128)S(1)} %get-tuple-element.59.a), channel_id=1, source_target_pairs={{0,128},{64,192},{128,0},{192,64},{1,129},{65,193},{129,1},{193,65... | collective-permute-start | bytes 12296 | tf_op jit(solution)/shard_map/ppermute | solution.py:36
  102.6 1.2 collective-permute-done.16.c
  103.8 2.0 %collective-permute-done.17.d = f32[8,128]{1,0:T(8,128)S(1)} collective-permute-done((f32[8,128]{1,0:T(8,128)S(1)}, f32[8,128]{1,0:T(8,128)S(1)}, u32[]{:S(2)}, u32[]{:S(2)}) %collective-permute-start.17) | collective-permute-done | bytes 4128 | tf_op jit(solution)/shard_map/ppermute | solution.py:36
  106.7 1.8 %collective-permute-start.20 = (f32[4,128]{1,0:T(4,128)S(1)}, f32[4,128]{1,0:T(4,128)S(1)}, u32[]{:S(2)}, u32[]{:S(2)}) collective-permute-start(f32[4,128]{1,0:T(4,128)S(1)} %get-tuple-element.61), channel_id=1, source_target_pairs={{0,3},{1,2},{2,1},{3,0},{4,7},{5,6},{6,5},{7,4},{8,11},{9,10},{10,... | collective-permute-start | bytes 6152 | tf_op jit(solution)/shard_map/ppermute | solution.py:492
  108.5 1.8 %collective-permute-done.19.c = f32[4,128]{1,0:T(4,128)S(1)} collective-permute-done((f32[4,128]{1,0:T(4,128)S(1)}, f32[4,128]{1,0:T(4,128)S(1)}, u32[]{:S(2)}, u32[]{:S(2)}) %collective-permute-start.19) | collective-permute-done | bytes 2080 | tf_op jit(solution)/shard_map/ppermute | solution.py:492
  111.0 1.5 collective-permute-start.21
  112.5 2.1 %collective-permute-done.21 = f32[4,128]{1,0:T(4,128)S(1)} collective-permute-done((f32[4,128]{1,0:T(4,128)S(1)}, f32[4,128]{1,0:T(4,128)S(1)}, u32[]{:S(2)}, u32[]{:S(2)}) %collective-permute-start.21) | collective-permute-done | bytes 2080 | tf_op jit(solution)/shard_map/ppermute | solution.py:494
  114.6 18.3 %all_to_all.20 = f32[64,4,128]{2,1,0:T(4,128)S(1)} all-to-all(f32[64,4,128]{2,1,0:T(4,128)S(1)} %broadcast_in_dim.5), channel_id=1, replica_groups=mesh['y'=4,'x'=4,'zh'=4,'zb'=2,'k'=2] {'y','x','zh'}, dimensions={0} | all-to-all | bytes 262144 | tf_op jit(solution)/shard_map/all_to_all | solution.py:41
  133.1 1.2 collective-permute-done.22.refs_2_
  134.2 1.5 scores.1.a
  138.6 1.8 %collective-permute-start.25 = (f32[4,128]{1,0:T(4,128)S(1)}, f32[4,128]{1,0:T(4,128)S(1)}, u32[]{:S(2)}, u32[]{:S(2)}) collective-permute-start(f32[4,128]{1,0:T(4,128)S(1)} %get-tuple-element.65), channel_id=1, source_target_pairs={{0,128},{64,192},{128,0},{192,64},{1,129},{65,193},{129,1},{193,65... | collective-permute-start | bytes 6152 | tf_op jit(solution)/shard_map/ppermute | solution.py:36
  140.5 1.3 collective-permute-start.26
  144.1 1.6 four_lists.1
  145.6 20.6 %all_to_all.21 = f32[128,4,128]{2,1,0:T(4,128)S(1)} all-to-all(f32[128,4,128]{2,1,0:T(4,128)S(1)} %four_lists.1), channel_id=1, replica_groups=mesh['y'=4,'x'=4,'zh'=4,'zb'=2,'k'=2] {'y','x','zh','zb'}, dimensions={0} | all-to-all | bytes 524288 | tf_op jit(solution)/shard_map/all_to_all | solution.py:501
  166.2 1.4 final_lists.1
  (65 shorter events, 17.6 us)
Async XLA Ops:
  0.0 4.1 %collective-permute-start.4 = (bf16[224,1024]{1,0:T(8,128)(2,1)}, bf16[224,1024]{1,0:T(8,128)(2,1)S(1)}, u32[]{:S(2)}, u32[]{:S(2)}) collective-permute-start(bf16[224,1024]{1,0:T(8,128)(2,1)} %bitcast.22), channel_id=1, source_target_pairs={{0,1},{1,0},{2,3},{3,2},{4,5},{5,4},{6,7},{7,6},{8,9},{9,8},{10,11... | collective-permute-start | bytes 1376264 | tf_op jit(solution)/shard_map/ppermute | solution.py:32
  0.0 4.1 %collective-permute-start.5 = (bf16[224,1024]{1,0:T(8,128)(2,1)}, bf16[224,1024]{1,0:T(8,128)(2,1)S(1)}, u32[]{:S(2)}, u32[]{:S(2)}) collective-permute-start(bf16[224,1024]{1,0:T(8,128)(2,1)} %bitcast.24), channel_id=1, source_target_pairs={{0,1},{1,0},{2,3},{3,2},{4,5},{5,4},{6,7},{7,6},{8,9},{9,8},{10,11... | collective-permute-start | bytes 1376264 | tf_op jit(solution)/shard_map/ppermute | solution.py:32
  0.5 3.6 %collective-permute-start.6 = (bf16[224,1024]{1,0:T(8,128)(2,1)}, bf16[224,1024]{1,0:T(8,128)(2,1)S(1)}, u32[]{:S(2)}, u32[]{:S(2)}) collective-permute-start(bf16[224,1024]{1,0:T(8,128)(2,1)} %w0.1), channel_id=1, source_target_pairs={{0,1},{1,0},{2,3},{3,2},{4,5},{5,4},{6,7},{7,6},{8,9},{9,8},{10,11... | collective-permute-start | bytes 1376264 | tf_op jit(solution)/shard_map/ppermute | solution.py:32
  1.9 1.3 collective-permute-start.2
  2.5 1.4 collective-permute-start.3
  5.0 39.5 %copy-start.3 = (bf16[1024,224]{0,1:T(8,128)(2,1)S(1)}, bf16[1024,224]{0,1:T(8,128)(2,1)}, u32[]{:S(2)}) copy-start(bf16[1024,224]{0,1:T(8,128)(2,1)} %param.10) | copy-start | bytes 1376260
  5.0 39.5 %all-to-all-start = ((bf16[32,64,128]{2,1,0:T(8,128)(2,1)}), bf16[32,64,128]{2,1,0:T(8,128)(2,1)S(1)}, u32[]{:S(2)}, u32[]{:S(2)}) async-start(bf16[32,64,128]{2,1,0:T(8,128)(2,1)} %broadcast_in_dim.4), calls=%async_computation | async-start | bytes 1048576 | tf_op jit(solution)/shard_map/all_to_all | solution.py:41
  26.5 0.9 collective-permute-start
  27.3 1.3 collective-permute-start.1
  45.8 22.1 %copy-start.1 = (bf16[224,1024]{1,0:T(8,128)(2,1)S(1)}, bf16[224,1024]{1,0:T(8,128)(2,1)}, u32[]{:S(2)}) copy-start(bf16[224,1024]{1,0:T(8,128)(2,1)} %w0.1) | copy-start | bytes 1376260
  45.9 6.0 %collective-permute-start.10 = (bf16[128,512]{1,0:T(8,128)(2,1)S(1)}, bf16[128,512]{1,0:T(8,128)(2,1)S(1)}, u32[]{:S(2)}, u32[]{:S(2)}) collective-permute-start(bf16[128,512]{1,0:T(8,128)(2,1)S(1)} %pad_maximum_fusion.1), channel_id=1, source_target_pairs={{0,4},{4,0},{8,12},{12,8},{1,5},{5,1},{9,13},{13,9},{2,6},{6,2},{1... | collective-permute-start | bytes 393224 | tf_op jit(solution)/shard_map/ppermute | solution.py:474
  47.1 7.2 %collective-permute-start.7 = (bf16[64,1024]{1,0:T(8,128)(2,1)S(1)}, bf16[64,1024]{1,0:T(8,128)(2,1)S(1)}, u32[]{:S(2)}, u32[]{:S(2)}) collective-permute-start(bf16[64,1024]{1,0:T(8,128)(2,1)S(1)} %get-tuple-element.48), channel_id=1, source_target_pairs={{0,64},{64,128},{128,192},{192,0},{1,65},{65,129},{129,193},{193,1... | collective-permute-start | bytes 393224 | tf_op jit(solution)/shard_map/ppermute | solution.py:36
  48.4 7.8 %collective-permute-start.8 = (bf16[64,1024]{1,0:T(8,128)(2,1)S(1)}, bf16[64,1024]{1,0:T(8,128)(2,1)S(1)}, u32[]{:S(2)}, u32[]{:S(2)}) collective-permute-start(bf16[64,1024]{1,0:T(8,128)(2,1)S(1)} %get-tuple-element.49), channel_id=1, source_target_pairs={{0,128},{64,192},{128,0},{192,64},{1,129},{65,193},{129,1},{193,65... | collective-permute-start | bytes 393224 | tf_op jit(solution)/shard_map/ppermute | solution.py:36
  50.2 6.0 %collective-permute-start.9 = (bf16[64,1024]{1,0:T(8,128)(2,1)S(1)}, bf16[64,1024]{1,0:T(8,128)(2,1)S(1)}, u32[]{:S(2)}, u32[]{:S(2)}) collective-permute-start(bf16[64,1024]{1,0:T(8,128)(2,1)S(1)} %get-tuple-element.50), channel_id=1, source_target_pairs={{0,192},{64,0},{128,64},{192,128},{1,193},{65,1},{129,65},{193,129... | collective-permute-start | bytes 393224 | tf_op jit(solution)/shard_map/ppermute | solution.py:36
  56.9 14.9 %collective-permute-start.14 = (bf16[256,512]{1,0:T(8,128)(2,1)S(1)}, bf16[256,512]{1,0:T(8,128)(2,1)S(1)}, u32[]{:S(2)}, u32[]{:S(2)}) collective-permute-start(bf16[256,512]{1,0:T(8,128)(2,1)S(1)} %pad_maximum_fusion.near), channel_id=1, source_target_pairs={{0,12},{4,8},{8,4},{12,0},{1,13},{5,9},{9,5},{13,1},{2,14},{6,10},... | collective-permute-start | bytes 786440 | tf_op jit(solution)/shard_map/ppermute | solution.py:478
  60.1 5.9 %collective-permute-start.11 = (bf16[64,512]{1,0:T(8,128)(2,1)S(1)}, bf16[64,512]{1,0:T(8,128)(2,1)S(1)}, u32[]{:S(2)}, u32[]{:S(2)}) collective-permute-start(bf16[64,512]{1,0:T(8,128)(2,1)S(1)} %get-tuple-element.54.a), channel_id=1, source_target_pairs={{0,64},{64,128},{128,192},{192,0},{1,65},{65,129},{129,193},{193,1... | collective-permute-start | bytes 196616 | tf_op jit(solution)/shard_map/ppermute | solution.py:36
  60.2 6.5 %collective-permute-start.12 = (bf16[64,512]{1,0:T(8,128)(2,1)S(1)}, bf16[64,512]{1,0:T(8,128)(2,1)S(1)}, u32[]{:S(2)}, u32[]{:S(2)}) collective-permute-start(bf16[64,512]{1,0:T(8,128)(2,1)S(1)} %get-tuple-element.54.a), channel_id=1, source_target_pairs={{0,128},{64,192},{128,0},{192,64},{1,129},{65,193},{129,1},{193,65... | collective-permute-start | bytes 196616 | tf_op jit(solution)/shard_map/ppermute | solution.py:36
  63.6 4.3 %collective-permute-start.13 = (bf16[64,512]{1,0:T(8,128)(2,1)S(1)}, bf16[64,512]{1,0:T(8,128)(2,1)S(1)}, u32[]{:S(2)}, u32[]{:S(2)}) collective-permute-start(bf16[64,512]{1,0:T(8,128)(2,1)S(1)} %get-tuple-element.54.a), channel_id=1, source_target_pairs={{0,192},{64,0},{128,64},{192,128},{1,193},{65,1},{129,65},{193,129... | collective-permute-start | bytes 196616 | tf_op jit(solution)/shard_map/ppermute | solution.py:36
  71.8 25.8 %all-to-all-start.1 = ((bf16[32,8,1024]{2,1,0:T(8,128)(2,1)}), bf16[32,8,1024]{2,1,0:T(8,128)(2,1)S(1)}, u32[]{:S(2)}, u32[]{:S(2)}) async-start(bf16[32,8,1024]{2,1,0:T(8,128)(2,1)} %bitcast.11), calls=%async_computation.1 | async-start | bytes 1048576 | tf_op jit(solution)/shard_map/all_to_all | solution.py:482
  79.8 54.4 %copy-start = (bf16[512,1024]{1,0:T(8,128)(2,1)S(1)}, bf16[512,1024]{1,0:T(8,128)(2,1)}, u32[]{:S(2)}) copy-start(bf16[512,1024]{1,0:T(8,128)(2,1)} %refs_3_.1) | copy-start | bytes 3145732
  97.8 4.8 %collective-permute-start.15 = (f32[8,128]{1,0:T(8,128)S(1)}, f32[8,128]{1,0:T(8,128)S(1)}, u32[]{:S(2)}, u32[]{:S(2)}) collective-permute-start(f32[8,128]{1,0:T(8,128)S(1)} %get-tuple-element.59.a), channel_id=1, source_target_pairs={{0,64},{64,128},{128,192},{192,0},{1,65},{65,129},{129,193},{193,1... | collective-permute-start | bytes 12296 | tf_op jit(solution)/shard_map/ppermute | solution.py:36
  98.7 5.1 %collective-permute-start.16 = (f32[8,128]{1,0:T(8,128)S(1)}, f32[8,128]{1,0:T(8,128)S(1)}, u32[]{:S(2)}, u32[]{:S(2)}) collective-permute-start(f32[8,128]{1,0:T(8,128)S(1)} %get-tuple-element.59.a), channel_id=1, source_target_pairs={{0,128},{64,192},{128,0},{192,64},{1,129},{65,193},{129,1},{193,65... | collective-permute-start | bytes 12296 | tf_op jit(solution)/shard_map/ppermute | solution.py:36
  102.2 3.6 %collective-permute-start.17 = (f32[8,128]{1,0:T(8,128)S(1)}, f32[8,128]{1,0:T(8,128)S(1)}, u32[]{:S(2)}, u32[]{:S(2)}) collective-permute-start(f32[8,128]{1,0:T(8,128)S(1)} %get-tuple-element.59.a), channel_id=1, source_target_pairs={{0,192},{64,0},{128,64},{192,128},{1,193},{65,1},{129,65},{193,129... | collective-permute-start | bytes 12296 | tf_op jit(solution)/shard_map/ppermute | solution.py:36
  106.5 2.0 %collective-permute-start.18 = (f32[4,128]{1,0:T(4,128)S(1)}, f32[4,128]{1,0:T(4,128)S(1)}, u32[]{:S(2)}, u32[]{:S(2)}) collective-permute-start(f32[4,128]{1,0:T(4,128)S(1)} %get-tuple-element.60.a), channel_id=1, source_target_pairs={{0,1},{1,0},{2,3},{3,2},{4,5},{5,4},{6,7},{7,6},{8,9},{9,8},{10,11... | collective-permute-start | bytes 6152 | tf_op jit(solution)/shard_map/ppermute | solution.py:492
  106.6 3.7 %collective-permute-start.19 = (f32[4,128]{1,0:T(4,128)S(1)}, f32[4,128]{1,0:T(4,128)S(1)}, u32[]{:S(2)}, u32[]{:S(2)}) collective-permute-start(f32[4,128]{1,0:T(4,128)S(1)} %get-tuple-element.61), channel_id=1, source_target_pairs={{0,2},{1,3},{2,0},{3,1},{4,6},{5,7},{6,4},{7,5},{8,10},{9,11},{10,... | collective-permute-start | bytes 6152 | tf_op jit(solution)/shard_map/ppermute | solution.py:492
  106.7 3.6 %collective-permute-start.20 = (f32[4,128]{1,0:T(4,128)S(1)}, f32[4,128]{1,0:T(4,128)S(1)}, u32[]{:S(2)}, u32[]{:S(2)}) collective-permute-start(f32[4,128]{1,0:T(4,128)S(1)} %get-tuple-element.61), channel_id=1, source_target_pairs={{0,3},{1,2},{2,1},{3,0},{4,7},{5,6},{6,5},{7,4},{8,11},{9,10},{10,... | collective-permute-start | bytes 6152 | tf_op jit(solution)/shard_map/ppermute | solution.py:492
  111.0 3.6 %collective-permute-start.21 = (f32[4,128]{1,0:T(4,128)S(1)}, f32[4,128]{1,0:T(4,128)S(1)}, u32[]{:S(2)}, u32[]{:S(2)}) collective-permute-start(f32[4,128]{1,0:T(4,128)S(1)} %code_part.1), channel_id=1, source_target_pairs={{0,2},{2,0},{1,3},{3,1},{4,6},{6,4},{5,7},{7,5},{8,10},{10,8},{9,1... | collective-permute-start | bytes 6152 | tf_op jit(solution)/shard_map/ppermute | solution.py:494
  133.0 1.3 collective-permute-start.22
  135.7 1.2 collective-permute-start.23
  138.0 4.9 %collective-permute-start.24 = (f32[4,128]{1,0:T(4,128)S(1)}, f32[4,128]{1,0:T(4,128)S(1)}, u32[]{:S(2)}, u32[]{:S(2)}) collective-permute-start(f32[4,128]{1,0:T(4,128)S(1)} %get-tuple-element.64), channel_id=1, source_target_pairs={{0,64},{64,128},{128,192},{192,0},{1,65},{65,129},{129,193},{193,1... | collective-permute-start | bytes 6152 | tf_op jit(solution)/shard_map/ppermute | solution.py:36
  138.6 5.1 %collective-permute-start.25 = (f32[4,128]{1,0:T(4,128)S(1)}, f32[4,128]{1,0:T(4,128)S(1)}, u32[]{:S(2)}, u32[]{:S(2)}) collective-permute-start(f32[4,128]{1,0:T(4,128)S(1)} %get-tuple-element.65), channel_id=1, source_target_pairs={{0,128},{64,192},{128,0},{192,64},{1,129},{65,193},{129,1},{193,65... | collective-permute-start | bytes 6152 | tf_op jit(solution)/shard_map/ppermute | solution.py:36
  140.5 3.6 %collective-permute-start.26 = (f32[4,128]{1,0:T(4,128)S(1)}, f32[4,128]{1,0:T(4,128)S(1)}, u32[]{:S(2)}, u32[]{:S(2)}) collective-permute-start(f32[4,128]{1,0:T(4,128)S(1)} %get-tuple-element.66), channel_id=1, source_target_pairs={{0,192},{64,0},{128,64},{192,128},{1,193},{65,1},{129,65},{193,129... | collective-permute-start | bytes 6152 | tf_op jit(solution)/shard_map/ppermute | solution.py:36
  (4 other events, 56.0 us)

commit v12 on v8

--- a/solution.py
+++ b/solution.py
@@ -455,8 +455,8 @@
     )
     gate_rows, up_rows = gate_weight.T, up_weight.T
     gate_peer, up_peer, down_peer = (to_peer(w) for w in (gate_rows, up_rows, down_weight))
-    block, gate_peer, up_peer, down_peer = lax.optimization_barrier(
-        (block, gate_peer, up_peer, down_peer)
+    code_weight, gate_peer, up_peer, down_peer = lax.optimization_barrier(
+        (code_weight, gate_peer, up_peer, down_peer)
     )
     gathered = spread(block, XZ, 32)
 

time: 164 us -> 162 us (0.988)
  starting transfers between devices: 60.8 us -> 58.8 us
  transfers between devices with their start and end apart: 30 -> 30, of which waited for: 16 -> 18; matrix products, arithmetic and copies ran while one was open for 0% -> 1% of each run, Pallas kernels for 2% -> 2%
where the time goes in v12:
time: 162 us
  starting transfers between devices  58.8 us (36%)
  waiting for transfers between devices  49 us (30%)
  blocking collectives  40.2 us (25%)
  Pallas kernels  11.6 us (7%)
  local copies, waits for them, and re-layouts  1.76 us (1%)
    all_to_all x1, starting transfers between devices, spread(): return lax.all_to_all(copies, axes, 0, 0, tiled=True)  21.6 us
    all_to_all x1, blocking collectives, per_device(): arrived = lax.all_to_all(lists, YXZ, 0, 0, tiled=True)  20.6 us
    all_to_all x1, blocking collectives, spread(): return lax.all_to_all(copies, axes, 0, 0, tiled=True)  19.6 us
    all_to_all x1, waiting for transfers between devices, per_device(): branch = lax.all_to_all(branch.reshape(32, 8, 1024), XZ, 0, 0, tiled=True)  15.7 us
    ppermute x12, starting transfers between devices, shifted(): return lax.ppermute(x, 'y', [(i, (i + d) % 4) for i in range(4)])  15.7 us
    all_to_all x1, waiting for transfers between devices, spread(): return lax.all_to_all(copies, axes, 0, 0, tiled=True)  15.1 us
    all_to_all x1, starting transfers between devices, per_device(): branch = lax.all_to_all(branch.reshape(32, 8, 1024), XZ, 0, 0, tiled=True)  8.45 us
    ppermute x12, waiting for transfers between devices, shifted(): return lax.ppermute(x, 'y', [(i, (i + d) % 4) for i in range(4)])  8.38 us
  transfers between devices with their start and end apart: 30, of which 18 were waited for; matrix products, arithmetic and copies ran while one was open for 1% of the time, Pallas kernels for 2%

profile of v12, /device:TPU:32, one launch (start us, length us, event | category | flops | bytes accessed | tf_op | source)
XLA Modules:
  0.0 161.7 jit_solution(15062253837712919571)
XLA Ops:
  4.3 21.6 %all-to-all-start = ((bf16[32,64,128]{2,1,0:T(8,128)(2,1)}), bf16[32,64,128]{2,1,0:T(8,128)(2,1)S(1)}, u32[]{:S(2)}, u32[]{:S(2)}) async-start(bf16[32,64,128]{2,1,0:T(8,128)(2,1)} %broadcast_in_dim.4), calls=%async_computation | async-start | bytes 1048576 | tf_op jit(solution)/shard_map/all_to_all | solution.py:41
  26.9 1.2 collective-permute-done.4
  28.2 15.1 %all-to-all-done.h = bf16[32,64,128]{2,1,0:T(8,128)(2,1)S(1)} async-done(((bf16[32,64,128]{2,1,0:T(8,128)(2,1)}), bf16[32,64,128]{2,1,0:T(8,128)(2,1)S(1)}, u32[]{:S(2)}, u32[]{:S(2)}) %all-to-all-start) | async-done | bytes 524320 | tf_op jit(solution)/shard_map/all_to_all | solution.py:41
  43.3 1.4 gate_up.1
  44.7 1.4 collective-permute-start.7
  46.1 1.3 collective-permute-start.8
  47.4 1.5 collective-permute-start.9
  48.9 2.9 %collective-permute-start.13 = (bf16[128,512]{1,0:T(8,128)(2,1)S(1)}, bf16[128,512]{1,0:T(8,128)(2,1)S(1)}, u32[]{:S(2)}, u32[]{:S(2)}) collective-permute-start(bf16[128,512]{1,0:T(8,128)(2,1)S(1)} %pad_maximum_fusion.w0), channel_id=1, source_target_pairs={{0,8},{4,12},{8,0},{12,4},{1,9},{5,13},{9,1},{13,5},{2,10},{6,14},... | collective-permute-start | bytes 393224 | tf_op jit(solution)/shard_map/ppermute | solution.py:471
  52.7 3.2 %collective-permute-start.15 = (bf16[128,512]{1,0:T(8,128)(2,1)S(1)}, bf16[128,512]{1,0:T(8,128)(2,1)S(1)}, u32[]{:S(2)}, u32[]{:S(2)}) collective-permute-start(bf16[128,512]{1,0:T(8,128)(2,1)S(1)} %pad_maximum_fusion.w0), channel_id=1, source_target_pairs={{0,12},{4,0},{8,4},{12,8},{1,13},{5,1},{9,5},{13,9},{2,14},{6,2},{... | collective-permute-start | bytes 393224 | tf_op jit(solution)/shard_map/ppermute | solution.py:471
  56.6 2.1 %collective-permute-start.10 = (bf16[64,512]{1,0:T(8,128)(2,1)S(1)}, bf16[64,512]{1,0:T(8,128)(2,1)S(1)}, u32[]{:S(2)}, u32[]{:S(2)}) collective-permute-start(bf16[64,512]{1,0:T(8,128)(2,1)S(1)} %get-tuple-element.48.a), channel_id=1, source_target_pairs={{0,64},{64,128},{128,192},{192,0},{1,65},{65,129},{129,193},{193,1... | collective-permute-start | bytes 196616 | tf_op jit(solution)/shard_map/ppermute | solution.py:36
  58.7 2.3 %collective-permute-done.13.w2 = bf16[128,512]{1,0:T(8,128)(2,1)S(1)} collective-permute-done((bf16[128,512]{1,0:T(8,128)(2,1)S(1)}, bf16[128,512]{1,0:T(8,128)(2,1)S(1)}, u32[]{:S(2)}, u32[]{:S(2)}) %collective-permute-start.13) | collective-permute-done | bytes 131104 | tf_op jit(solution)/shard_map/ppermute | solution.py:471
  62.4 2.1 %collective-permute-done.11.c = bf16[64,512]{1,0:T(8,128)(2,1)S(1)} collective-permute-done((bf16[64,512]{1,0:T(8,128)(2,1)S(1)}, bf16[64,512]{1,0:T(8,128)(2,1)S(1)}, u32[]{:S(2)}, u32[]{:S(2)}) %collective-permute-start.11) | collective-permute-done | bytes 65568 | tf_op jit(solution)/shard_map/ppermute | solution.py:36
  65.3 1.8 %down.1 = bf16[256,1024]{1,0:T(8,128)(2,1)} custom-call(s32[8]{0:T(128)S(1)} %stack.35.place.refs_0_, bf16[64,512]{1,0:T(8,128)(2,1)S(1)} %get-tuple-element.48.a, bf16[64,512]{1,0:T(8,128)(2,1)S(1)} %collective-permute-done.10.b, bf16[64,512]{1,0:T(8,128)(2,1)S(1)} %collective-permute-done.11.c, bf16[64,512]{1,0:T(8,128)(2,1)S(1)} %collective-permute-done.12.d, ...), custom_call_target="tpu_custom_call" | custom-call | tf_op jit(solution)/shard_map/down/pallas_call | solution.py:153
  67.1 8.5 %all-to-all-start.1 = ((bf16[32,8,1024]{2,1,0:T(8,128)(2,1)}), bf16[32,8,1024]{2,1,0:T(8,128)(2,1)S(1)}, u32[]{:S(2)}, u32[]{:S(2)}) async-start(bf16[32,8,1024]{2,1,0:T(8,128)(2,1)} %bitcast.11), calls=%async_computation.1 | async-start | bytes 1048576 | tf_op jit(solution)/shard_map/all_to_all | solution.py:481
  75.6 15.7 %all-to-all-done.1.parts = bf16[32,8,1024]{2,1,0:T(8,128)(2,1)S(1)} async-done(((bf16[32,8,1024]{2,1,0:T(8,128)(2,1)}), bf16[32,8,1024]{2,1,0:T(8,128)(2,1)S(1)}, u32[]{:S(2)}, u32[]{:S(2)}) %all-to-all-start.1) | async-done | bytes 524320 | tf_op jit(solution)/shard_map/all_to_all | solution.py:481
  91.4 1.2 collective-permute-start.16
  92.6 2.3 %collective-permute-start.17 = (f32[8,128]{1,0:T(8,128)S(1)}, f32[8,128]{1,0:T(8,128)S(1)}, u32[]{:S(2)}, u32[]{:S(2)}) collective-permute-start(f32[8,128]{1,0:T(8,128)S(1)} %get-tuple-element.55.a), channel_id=1, source_target_pairs={{0,128},{64,192},{128,0},{192,64},{1,129},{65,193},{129,1},{193,65... | collective-permute-start | bytes 12296 | tf_op jit(solution)/shard_map/ppermute | solution.py:36
  94.9 1.7 %collective-permute-start.18 = (f32[8,128]{1,0:T(8,128)S(1)}, f32[8,128]{1,0:T(8,128)S(1)}, u32[]{:S(2)}, u32[]{:S(2)}) collective-permute-start(f32[8,128]{1,0:T(8,128)S(1)} %get-tuple-element.55.a), channel_id=1, source_target_pairs={{0,192},{64,0},{128,64},{192,128},{1,193},{65,1},{129,65},{193,129... | collective-permute-start | bytes 12296 | tf_op jit(solution)/shard_map/ppermute | solution.py:36
  96.6 1.1 collective-permute-done.17.c
  99.4 1.8 %collective-permute-start.21 = (f32[4,128]{1,0:T(4,128)S(1)}, f32[4,128]{1,0:T(4,128)S(1)}, u32[]{:S(2)}, u32[]{:S(2)}) collective-permute-start(f32[4,128]{1,0:T(4,128)S(1)} %get-tuple-element.57), channel_id=1, source_target_pairs={{0,3},{1,2},{2,1},{3,0},{4,7},{5,6},{6,5},{7,4},{8,11},{9,10},{10,... | collective-permute-start | bytes 6152 | tf_op jit(solution)/shard_map/ppermute | solution.py:491
  101.2 1.8 %collective-permute-done.20.c = f32[4,128]{1,0:T(4,128)S(1)} collective-permute-done((f32[4,128]{1,0:T(4,128)S(1)}, f32[4,128]{1,0:T(4,128)S(1)}, u32[]{:S(2)}, u32[]{:S(2)}) %collective-permute-start.20) | collective-permute-done | bytes 2080 | tf_op jit(solution)/shard_map/ppermute | solution.py:491
  103.7 1.5 collective-permute-start.22
  105.2 2.1 %collective-permute-done.22 = f32[4,128]{1,0:T(4,128)S(1)} collective-permute-done((f32[4,128]{1,0:T(4,128)S(1)}, f32[4,128]{1,0:T(4,128)S(1)}, u32[]{:S(2)}, u32[]{:S(2)}) %collective-permute-start.22) | collective-permute-done | bytes 2080 | tf_op jit(solution)/shard_map/ppermute | solution.py:493
  107.3 19.6 %all_to_all.20 = f32[64,4,128]{2,1,0:T(4,128)S(1)} all-to-all(f32[64,4,128]{2,1,0:T(4,128)S(1)} %broadcast_in_dim.5), channel_id=1, replica_groups=mesh['y'=4,'x'=4,'zh'=4,'zb'=2,'k'=2] {'y','x','zh'}, dimensions={0} | all-to-all | bytes 262144 | tf_op jit(solution)/shard_map/all_to_all | solution.py:41
  127.2 1.2 collective-permute-done.23.refs_2_
  128.3 1.5 scores.1.a
  132.7 1.8 %collective-permute-start.26 = (f32[4,128]{1,0:T(4,128)S(1)}, f32[4,128]{1,0:T(4,128)S(1)}, u32[]{:S(2)}, u32[]{:S(2)}) collective-permute-start(f32[4,128]{1,0:T(4,128)S(1)} %get-tuple-element.63), channel_id=1, source_target_pairs={{0,128},{64,192},{128,0},{192,64},{1,129},{65,193},{129,1},{193,65... | collective-permute-start | bytes 6152 | tf_op jit(solution)/shard_map/ppermute | solution.py:36
  134.6 1.3 collective-permute-start.27
  135.8 1.1 collective-permute-done.25.b
  138.2 1.6 four_lists.1
  139.7 20.6 %all_to_all.21 = f32[128,4,128]{2,1,0:T(4,128)S(1)} all-to-all(f32[128,4,128]{2,1,0:T(4,128)S(1)} %four_lists.1), channel_id=1, replica_groups=mesh['y'=4,'x'=4,'zh'=4,'zb'=2,'k'=2] {'y','x','zh','zb'}, dimensions={0} | all-to-all | bytes 524288 | tf_op jit(solution)/shard_map/all_to_all | solution.py:500
  160.3 1.4 final_lists.1
  (66 shorter events, 15.8 us)
Async XLA Ops:
  1.4 1.8 %collective-permute-start.5 = (bf16[64,64]{1,0:T(8,128)(2,1)S(1)}, bf16[64,64]{1,0:T(8,128)(2,1)S(1)}, u32[]{:S(2)}, u32[]{:S(2)}) collective-permute-start(bf16[64,64]{1,0:T(8,128)(2,1)S(1)} %get-tuple-element.36), channel_id=1, source_target_pairs={{0,0},{1,1},{16,64},{17,65},{32,128},{33,129},{48,192},{49,193},{6... | collective-permute-start | bytes 24584 | tf_op jit(solution)/shard_map/ppermute | solution.py:451
  2.0 1.3 collective-permute-start.6
  2.1 23.8 %collective-permute-start = (bf16[224,1024]{1,0:T(8,128)(2,1)}, bf16[224,1024]{1,0:T(8,128)(2,1)S(1)}, u32[]{:S(2)}, u32[]{:S(2)}) collective-permute-start(bf16[224,1024]{1,0:T(8,128)(2,1)} %bitcast.22), channel_id=1, source_target_pairs={{0,1},{1,0},{2,3},{3,2},{4,5},{5,4},{6,7},{7,6},{8,9},{9,8},{10,11... | collective-permute-start | bytes 1376264 | tf_op jit(solution)/shard_map/ppermute | solution.py:32
  2.6 23.3 %collective-permute-start.1 = (bf16[224,1024]{1,0:T(8,128)(2,1)}, bf16[224,1024]{1,0:T(8,128)(2,1)S(1)}, u32[]{:S(2)}, u32[]{:S(2)}) collective-permute-start(bf16[224,1024]{1,0:T(8,128)(2,1)} %bitcast.24), channel_id=1, source_target_pairs={{0,1},{1,0},{2,3},{3,2},{4,5},{5,4},{6,7},{7,6},{8,9},{9,8},{10,11... | collective-permute-start | bytes 1376264 | tf_op jit(solution)/shard_map/ppermute | solution.py:32
  2.7 23.2 %collective-permute-start.2 = (bf16[224,1024]{1,0:T(8,128)(2,1)}, bf16[224,1024]{1,0:T(8,128)(2,1)S(1)}, u32[]{:S(2)}, u32[]{:S(2)}) collective-permute-start(bf16[224,1024]{1,0:T(8,128)(2,1)} %w0.1), channel_id=1, source_target_pairs={{0,1},{1,0},{2,3},{3,2},{4,5},{5,4},{6,7},{7,6},{8,9},{9,8},{10,11... | collective-permute-start | bytes 1376264 | tf_op jit(solution)/shard_map/ppermute | solution.py:32
  4.3 39.0 %copy-start.3 = (bf16[1024,224]{0,1:T(8,128)(2,1)S(1)}, bf16[1024,224]{0,1:T(8,128)(2,1)}, u32[]{:S(2)}) copy-start(bf16[1024,224]{0,1:T(8,128)(2,1)} %param.10) | copy-start | bytes 1376260
  4.3 39.0 %all-to-all-start = ((bf16[32,64,128]{2,1,0:T(8,128)(2,1)}), bf16[32,64,128]{2,1,0:T(8,128)(2,1)S(1)}, u32[]{:S(2)}, u32[]{:S(2)}) async-start(bf16[32,64,128]{2,1,0:T(8,128)(2,1)} %broadcast_in_dim.4), calls=%async_computation | async-start | bytes 1048576 | tf_op jit(solution)/shard_map/all_to_all | solution.py:41
  26.0 0.9 collective-permute-start.3
  26.8 1.3 collective-permute-start.4
  44.7 8.0 %collective-permute-start.7 = (bf16[64,1024]{1,0:T(8,128)(2,1)S(1)}, bf16[64,1024]{1,0:T(8,128)(2,1)S(1)}, u32[]{:S(2)}, u32[]{:S(2)}) collective-permute-start(bf16[64,1024]{1,0:T(8,128)(2,1)S(1)} %get-tuple-element.42), channel_id=1, source_target_pairs={{0,64},{64,128},{128,192},{192,0},{1,65},{65,129},{129,193},{193,1... | collective-permute-start | bytes 393224 | tf_op jit(solution)/shard_map/ppermute | solution.py:36
  46.1 9.8 %collective-permute-start.8 = (bf16[64,1024]{1,0:T(8,128)(2,1)S(1)}, bf16[64,1024]{1,0:T(8,128)(2,1)S(1)}, u32[]{:S(2)}, u32[]{:S(2)}) collective-permute-start(bf16[64,1024]{1,0:T(8,128)(2,1)S(1)} %get-tuple-element.43), channel_id=1, source_target_pairs={{0,128},{64,192},{128,0},{192,64},{1,129},{65,193},{129,1},{193,65... | collective-permute-start | bytes 393224 | tf_op jit(solution)/shard_map/ppermute | solution.py:36
  47.4 8.5 %collective-permute-start.9 = (bf16[64,1024]{1,0:T(8,128)(2,1)S(1)}, bf16[64,1024]{1,0:T(8,128)(2,1)S(1)}, u32[]{:S(2)}, u32[]{:S(2)}) collective-permute-start(bf16[64,1024]{1,0:T(8,128)(2,1)S(1)} %get-tuple-element.44), channel_id=1, source_target_pairs={{0,192},{64,0},{128,64},{192,128},{1,193},{65,1},{129,65},{193,129... | collective-permute-start | bytes 393224 | tf_op jit(solution)/shard_map/ppermute | solution.py:36
  48.9 12.1 %collective-permute-start.13 = (bf16[128,512]{1,0:T(8,128)(2,1)S(1)}, bf16[128,512]{1,0:T(8,128)(2,1)S(1)}, u32[]{:S(2)}, u32[]{:S(2)}) collective-permute-start(bf16[128,512]{1,0:T(8,128)(2,1)S(1)} %pad_maximum_fusion.w0), channel_id=1, source_target_pairs={{0,8},{4,12},{8,0},{12,4},{1,9},{5,13},{9,1},{13,5},{2,10},{6,14},... | collective-permute-start | bytes 393224 | tf_op jit(solution)/shard_map/ppermute | solution.py:471
  51.8 15.3 %collective-permute-start.14 = (bf16[128,512]{1,0:T(8,128)(2,1)S(1)}, bf16[128,512]{1,0:T(8,128)(2,1)S(1)}, u32[]{:S(2)}, u32[]{:S(2)}) collective-permute-start(bf16[128,512]{1,0:T(8,128)(2,1)S(1)} %pad_maximum_fusion.w0), channel_id=1, source_target_pairs={{0,4},{4,8},{8,12},{12,0},{1,5},{5,9},{9,13},{13,1},{2,6},{6,10},{... | collective-permute-start | bytes 393224 | tf_op jit(solution)/shard_map/ppermute | solution.py:471
  52.7 14.3 %collective-permute-start.15 = (bf16[128,512]{1,0:T(8,128)(2,1)S(1)}, bf16[128,512]{1,0:T(8,128)(2,1)S(1)}, u32[]{:S(2)}, u32[]{:S(2)}) collective-permute-start(bf16[128,512]{1,0:T(8,128)(2,1)S(1)} %pad_maximum_fusion.w0), channel_id=1, source_target_pairs={{0,12},{4,0},{8,4},{12,8},{1,13},{5,1},{9,5},{13,9},{2,14},{6,2},{... | collective-permute-start | bytes 393224 | tf_op jit(solution)/shard_map/ppermute | solution.py:471
  56.6 5.7 %collective-permute-start.10 = (bf16[64,512]{1,0:T(8,128)(2,1)S(1)}, bf16[64,512]{1,0:T(8,128)(2,1)S(1)}, u32[]{:S(2)}, u32[]{:S(2)}) collective-permute-start(bf16[64,512]{1,0:T(8,128)(2,1)S(1)} %get-tuple-element.48.a), channel_id=1, source_target_pairs={{0,64},{64,128},{128,192},{192,0},{1,65},{65,129},{129,193},{193,1... | collective-permute-start | bytes 196616 | tf_op jit(solution)/shard_map/ppermute | solution.py:36
  58.7 5.8 %collective-permute-start.11 = (bf16[64,512]{1,0:T(8,128)(2,1)S(1)}, bf16[64,512]{1,0:T(8,128)(2,1)S(1)}, u32[]{:S(2)}, u32[]{:S(2)}) collective-permute-start(bf16[64,512]{1,0:T(8,128)(2,1)S(1)} %get-tuple-element.48.a), channel_id=1, source_target_pairs={{0,128},{64,192},{128,0},{192,64},{1,129},{65,193},{129,1},{193,65... | collective-permute-start | bytes 196616 | tf_op jit(solution)/shard_map/ppermute | solution.py:36
  61.0 4.3 %collective-permute-start.12 = (bf16[64,512]{1,0:T(8,128)(2,1)S(1)}, bf16[64,512]{1,0:T(8,128)(2,1)S(1)}, u32[]{:S(2)}, u32[]{:S(2)}) collective-permute-start(bf16[64,512]{1,0:T(8,128)(2,1)S(1)} %get-tuple-element.48.a), channel_id=1, source_target_pairs={{0,192},{64,0},{128,64},{192,128},{1,193},{65,1},{129,65},{193,129... | collective-permute-start | bytes 196616 | tf_op jit(solution)/shard_map/ppermute | solution.py:36
  67.1 24.2 %all-to-all-start.1 = ((bf16[32,8,1024]{2,1,0:T(8,128)(2,1)}), bf16[32,8,1024]{2,1,0:T(8,128)(2,1)S(1)}, u32[]{:S(2)}, u32[]{:S(2)}) async-start(bf16[32,8,1024]{2,1,0:T(8,128)(2,1)} %bitcast.11), calls=%async_computation.1 | async-start | bytes 1048576 | tf_op jit(solution)/shard_map/all_to_all | solution.py:481
  75.5 52.8 %copy-start = (bf16[512,1024]{1,0:T(8,128)(2,1)S(1)}, bf16[512,1024]{1,0:T(8,128)(2,1)}, u32[]{:S(2)}) copy-start(bf16[512,1024]{1,0:T(8,128)(2,1)} %refs_3_.1) | copy-start | bytes 3145732
  91.4 5.2 %collective-permute-start.16 = (f32[8,128]{1,0:T(8,128)S(1)}, f32[8,128]{1,0:T(8,128)S(1)}, u32[]{:S(2)}, u32[]{:S(2)}) collective-permute-start(f32[8,128]{1,0:T(8,128)S(1)} %get-tuple-element.55.a), channel_id=1, source_target_pairs={{0,64},{64,128},{128,192},{192,0},{1,65},{65,129},{129,193},{193,1... | collective-permute-start | bytes 12296 | tf_op jit(solution)/shard_map/ppermute | solution.py:36
  92.6 5.1 %collective-permute-start.17 = (f32[8,128]{1,0:T(8,128)S(1)}, f32[8,128]{1,0:T(8,128)S(1)}, u32[]{:S(2)}, u32[]{:S(2)}) collective-permute-start(f32[8,128]{1,0:T(8,128)S(1)} %get-tuple-element.55.a), channel_id=1, source_target_pairs={{0,128},{64,192},{128,0},{192,64},{1,129},{65,193},{129,1},{193,65... | collective-permute-start | bytes 12296 | tf_op jit(solution)/shard_map/ppermute | solution.py:36
  94.9 3.6 %collective-permute-start.18 = (f32[8,128]{1,0:T(8,128)S(1)}, f32[8,128]{1,0:T(8,128)S(1)}, u32[]{:S(2)}, u32[]{:S(2)}) collective-permute-start(f32[8,128]{1,0:T(8,128)S(1)} %get-tuple-element.55.a), channel_id=1, source_target_pairs={{0,192},{64,0},{128,64},{192,128},{1,193},{65,1},{129,65},{193,129... | collective-permute-start | bytes 12296 | tf_op jit(solution)/shard_map/ppermute | solution.py:36
  99.2 2.0 %collective-permute-start.19 = (f32[4,128]{1,0:T(4,128)S(1)}, f32[4,128]{1,0:T(4,128)S(1)}, u32[]{:S(2)}, u32[]{:S(2)}) collective-permute-start(f32[4,128]{1,0:T(4,128)S(1)} %get-tuple-element.56.a), channel_id=1, source_target_pairs={{0,1},{1,0},{2,3},{3,2},{4,5},{5,4},{6,7},{7,6},{8,9},{9,8},{10,11... | collective-permute-start | bytes 6152 | tf_op jit(solution)/shard_map/ppermute | solution.py:491
  99.3 3.7 %collective-permute-start.20 = (f32[4,128]{1,0:T(4,128)S(1)}, f32[4,128]{1,0:T(4,128)S(1)}, u32[]{:S(2)}, u32[]{:S(2)}) collective-permute-start(f32[4,128]{1,0:T(4,128)S(1)} %get-tuple-element.57), channel_id=1, source_target_pairs={{0,2},{1,3},{2,0},{3,1},{4,6},{5,7},{6,4},{7,5},{8,10},{9,11},{10,... | collective-permute-start | bytes 6152 | tf_op jit(solution)/shard_map/ppermute | solution.py:491
  99.4 3.6 %collective-permute-start.21 = (f32[4,128]{1,0:T(4,128)S(1)}, f32[4,128]{1,0:T(4,128)S(1)}, u32[]{:S(2)}, u32[]{:S(2)}) collective-permute-start(f32[4,128]{1,0:T(4,128)S(1)} %get-tuple-element.57), channel_id=1, source_target_pairs={{0,3},{1,2},{2,1},{3,0},{4,7},{5,6},{6,5},{7,4},{8,11},{9,10},{10,... | collective-permute-start | bytes 6152 | tf_op jit(solution)/shard_map/ppermute | solution.py:491
  103.7 3.6 %collective-permute-start.22 = (f32[4,128]{1,0:T(4,128)S(1)}, f32[4,128]{1,0:T(4,128)S(1)}, u32[]{:S(2)}, u32[]{:S(2)}) collective-permute-start(f32[4,128]{1,0:T(4,128)S(1)} %code_part.1), channel_id=1, source_target_pairs={{0,2},{2,0},{1,3},{3,1},{4,6},{6,4},{5,7},{7,5},{8,10},{10,8},{9,1... | collective-permute-start | bytes 6152 | tf_op jit(solution)/shard_map/ppermute | solution.py:493
  127.1 1.3 collective-permute-start.23
  129.8 1.2 collective-permute-start.24
  132.1 4.9 %collective-permute-start.25 = (f32[4,128]{1,0:T(4,128)S(1)}, f32[4,128]{1,0:T(4,128)S(1)}, u32[]{:S(2)}, u32[]{:S(2)}) collective-permute-start(f32[4,128]{1,0:T(4,128)S(1)} %get-tuple-element.62), channel_id=1, source_target_pairs={{0,64},{64,128},{128,192},{192,0},{1,65},{65,129},{129,193},{193,1... | collective-permute-start | bytes 6152 | tf_op jit(solution)/shard_map/ppermute | solution.py:36
  132.7 5.1 %collective-permute-start.26 = (f32[4,128]{1,0:T(4,128)S(1)}, f32[4,128]{1,0:T(4,128)S(1)}, u32[]{:S(2)}, u32[]{:S(2)}) collective-permute-start(f32[4,128]{1,0:T(4,128)S(1)} %get-tuple-element.63), channel_id=1, source_target_pairs={{0,128},{64,192},{128,0},{192,64},{1,129},{65,193},{129,1},{193,65... | collective-permute-start | bytes 6152 | tf_op jit(solution)/shard_map/ppermute | solution.py:36
  134.6 3.6 %collective-permute-start.27 = (f32[4,128]{1,0:T(4,128)S(1)}, f32[4,128]{1,0:T(4,128)S(1)}, u32[]{:S(2)}, u32[]{:S(2)}) collective-permute-start(f32[4,128]{1,0:T(4,128)S(1)} %get-tuple-element.64), channel_id=1, source_target_pairs={{0,192},{64,0},{128,64},{192,128},{1,193},{65,1},{129,65},{193,129... | collective-permute-start | bytes 6152 | tf_op jit(solution)/shard_map/ppermute | solution.py:36
  (5 other events, 75.4 us)
